TPU v7x, 32 devices: a whole 2x2x4 slice. The times are simulated.
32 devices in a mesh: ctx: 16 (over z, y, core), head: 2 (over x).
Axes of the slice: x: 2, y: 2, z: 4, core: 2. Of those that a mesh axis runs over, the one named last changes fastest.
Arguments:
- queries: bfloat16 [4096, 512], P('ctx', 'head'), may hold values from -5 to 5
- keys: bfloat16 [4096, 512], P('ctx', 'head'), may hold values from -5 to 5
- values: bfloat16 [4096, 32, 128], P('ctx', 'head'), may hold values from -16 to 16
- win_q: bfloat16 [4096, 32, 128], P('ctx', 'head'), may hold values from -5 to 5
- win_k: bfloat16 [4096, 32, 128], P('ctx', 'head'), may hold values from -5 to 5
- gain: bfloat16 [32, 128], P('head'), may hold values from 0.25 to 1.75
Outputs:
- normed_out: bfloat16 [4096, 32, 128], P('ctx', 'head')
All inputs are finite; a program needn't handle non-finite values.
Results may differ from a plain program's by a relative error of at most 0.00065.
The roundings to bfloat16 on the way count: a program that leaves them out, or rounds other values in their place, can miss the bound.
Values may be sent and summed in bfloat16 or wider, within the bound.
No kernel may reach another device: no remote copies, remote signals or barrier semaphores. Data moves between devices by JAX's collectives and lax.ppermute only.
A program may use at most 192 MiB of HBM per device.

v0:
```python
import math

import jax
import jax.numpy as jnp
from jax import lax
from jax.sharding import PartitionSpec as P

HEADS = 32
DV = 128
WINDOW = 64


exact_precision = lax.Precision.HIGHEST
norm_epsilon = 1e-06


def prefix(part, axis, combine, identity):
    place = lax.axis_index(axis)
    gathered = jax.tree.map(lambda a: lax.all_gather(a, axis), part)
    state = jax.tree.map(lambda a, e: jnp.zeros_like(a) + jnp.asarray(e, a.dtype), part, identity)

    def one(lap, state):
        return combine(
            state, jax.tree.map(lambda a: lax.dynamic_index_in_dim(a, lap, 0, False), gathered)
        )

    return lax.fori_loop(0, place, one, state)


def shifted(value, axis, steps):
    count = lax.axis_size(axis)
    initial, last = (max(0, -steps), min(count, count - steps))
    return lax.ppermute(value, axis, [(source, source + steps) for source in range(initial, last)])


def features(inputs):
    dim_k = inputs.shape[-1]
    outer_part = (inputs[..., :, None] * inputs[..., None, :]).reshape(
        inputs.shape[:-1] + (dim_k * dim_k,)
    )
    ones_part = jnp.ones(inputs.shape[:-1] + (1,), jnp.float32)
    return jnp.concatenate(
        [ones_part, inputs * dim_k ** (-0.25), outer_part / math.sqrt(2.0 * dim_k)], axis=-1
    )


def add_pair(before, after_part):
    return (before[0] + after_part[0], before[1] + after_part[1])


def on_device(queries, keys, values, win_q, win_k, gain):
    tok_rows = values.shape[0]
    head_rows = values.shape[1]
    dim_v = values.shape[2]
    dim_k = queries.shape[1] // head_rows
    base_pos = lax.axis_index("ctx") * tok_rows
    query_in = queries.reshape(tok_rows, head_rows, dim_k).astype(jnp.float32)
    key_in = keys.reshape(tok_rows, head_rows, dim_k).astype(jnp.float32)
    query_features = features(query_in)
    key_features = features(key_in)
    value_full = values.astype(jnp.float32)
    state_blk = jnp.einsum("thf,thd->hfd", key_features, value_full, precision=exact_precision)
    key_total = jnp.sum(key_features, axis=0)
    zero_state = jnp.zeros_like(state_blk)
    zero_total = jnp.zeros_like(key_total)
    prior_state, previous_total = prefix(
        (state_blk, key_total), "ctx", add_pair, (zero_state, zero_total)
    )
    rim_rows = jnp.stack([win_k[tok_rows - WINDOW :], values[tok_rows - WINDOW :]])
    rim_prev = shifted(rim_rows, "ctx", 1)
    ext_keys = jnp.concatenate([rim_prev[0], win_k], axis=0)
    ext_vals = jnp.concatenate([rim_prev[1], values], axis=0)
    span_rows = min(512, tok_rows)
    lower_triangle = jnp.tril(jnp.ones((span_rows, span_rows), jnp.float32))
    row_idx = jnp.arange(span_rows)[:, None]
    col_idx = jnp.arange(span_rows + WINDOW)[None, :]
    kernel = (
        jnp.einsum("iev,dev->eid", query_features, key_features, precision=exact_precision)
        * lower_triangle[None]
    )
    numer = jnp.einsum("hqk,khd->qhd", kernel, value_full, precision=exact_precision)
    numer = numer + jnp.einsum(
        "qhf,hfd->qhd", query_features, prior_state, precision=exact_precision
    )
    denom = jnp.sum(kernel, axis=2).T + jnp.einsum(
        "qhf,hf->qh", query_features, previous_total, precision=exact_precision
    )
    linear = numer / denom[:, :, None]
    scores = jnp.einsum(
        "qhd,khd->hqk", win_q, ext_keys, preferred_element_type=jnp.float32
    ) / math.sqrt(dim_v)
    valid = (
        (col_idx > row_idx) & (col_idx <= row_idx + WINDOW) & (base_pos + 0 + col_idx - WINDOW >= 0)
    )
    scores = jnp.where(valid[None], scores, jnp.float32(-1e30))
    peak = jnp.max(scores, axis=-1, keepdims=True)
    expo = jnp.exp(scores - peak)
    weights = (expo / jnp.sum(expo, axis=-1, keepdims=True)).astype(jnp.bfloat16)
    window = jnp.einsum("hqk,khd->qhd", weights, ext_vals, preferred_element_type=jnp.float32)
    outputs = linear + window
    local_squares = jnp.sum(outputs * outputs, axis=(1, 2))
    all_squares = lax.psum(local_squares, "head")
    mean_square = all_squares / (HEADS * DV)
    scaled = (
        outputs
        * lax.rsqrt(mean_square + norm_epsilon)[:, None, None]
        * gain.astype(jnp.float32)[None]
    )
    return scaled.astype(jnp.bfloat16)


def solution(mesh):
    return jax.shard_map(
        on_device,
        mesh=mesh,
        in_specs=(
            P("ctx", "head"),
            P("ctx", "head"),
            P("ctx", "head", None),
            P("ctx", "head", None),
            P("ctx", "head", None),
            P("head", None),
        ),
        out_specs=P("ctx", "head", None),
        check_vma=False,
    )
```

profile of v0, /device:TPU:31, one launch (start us, length us, event | category | flops | bytes accessed | tf_op | source)
XLA Modules:
  0.0 284.7 jit_solution(4082793158426167904)
XLA Ops:
  6.5 1.1 copy.19
  8.4 1.9 copy-done.2
  10.3 2.9 %fusion.10 = f32[16,273,128]{2,1,0:T(8,128)S(1)} fusion(f32[256,16,256]{0,2,1:T(8,128)S(1)} %bitcast.54, f32[256,16,16]{0,2,1:T(8,128)S(1)} %broadcast_multiply_fusion, f32[273]{0:T(512)S(1)} %pad.9.clone, bf16[256,16,128]{2,1,0:T(8,128)(2,1)S(1)} %copy-done.6), kind=kOutput, calls=%fused_computation.21 | convolution fusion | flops 1719803904 | bytes 7742532 | tf_op jit(solution)/shard_map/thf,thd->hfd/dot_general | solution.py:62
  13.1 1.8 copy.23
  15.3 1.9 copy.25
  17.2 0.8 pad_maximum_fusion.7
  18.1 1.5 collective-permute-start
  19.9 3.4 %fusion.9 = f32[16,273]{1,0:T(8,128)S(1)} fusion(f32[256,16,256]{0,2,1:T(8,128)} %bitcast.55, f32[256,16,16]{0,2,1:T(8,128)} %copy-done.7, f32[273]{0:T(512)S(1)} %pad.9.clone), kind=kLoop, calls=%fused_computation.20 | loop fusion | flops 3350256 | bytes 4475012 | tf_op jit(solution)/shard_map/reduce_sum | solution.py:63
  23.9 11.4 %multiply_reduce_fusion = (f32[16,256]{1,0:T(8,128)S(1)}, f32[16,256,256]{1,2,0:T(8,128)S(1)}) fusion(f32[256,256]{0,1:T(8,128)S(1)} %fusion.30, f32[256,16,256]{0,2,1:T(8,128)S(1)} %bitcast.56, f32[256,16,16]{0,2,1:T(8,128)S(1)} %copy-done.8, f32[273]{0:T(512)S(1)} %pad.9.clone, f32[256,16,256]{0,2,1:T(8,128)S(1)} %bitcast.57, ...), kind=kOutput, calls=%fused_computation.13 | convolution fusion | flops 3441700864 | bytes 13386820 | tf_op jit(solution)/shard_map/iev,dev->eid/dot_general | solution.py:78
  35.3 22.1 %all-gather.1 = f32[256,273]{1,0:T(8,128)} all-gather(f32[16,273]{1,0:T(8,128)S(1)} %fusion.9), channel_id=3, replica_groups=mesh['ctx'=16,'head'=2] {'ctx'}, dimensions={0}, use_global_device_ids=true | all-gather | bytes 297024 | tf_op jit(solution)/shard_map/all_gather | solution.py:19
  57.5 3.4 %fusion.3 = f32[16,256,128]{1,2,0:T(8,128)} fusion(f32[16,256,256]{1,2,0:T(8,128)S(1)} %get-tuple-element.64, f32[256,256]{0,1:T(8,128)S(1)} %fusion.30, bf16[256,16,128]{2,1,0:T(8,128)(2,1)S(1)} %copy-done.6), kind=kOutput, calls=%fused_computation.14 | convolution fusion | flops 1611661312 | bytes 7602176 | tf_op jit(solution)/shard_map/hqk,khd->qhd/dot_general | solution.py:81
  60.9 1.8 slice_bitcast_fusion.1
  62.6 0.9 fusion.23
  63.5 3.8 %fusion.43 = (f32[16,256]{1,0:T(8,128)S(1)}, f32[16,256,320]{1,2,0:T(8,128)}) fusion(f32[16,320,256]{2,1,0:T(8,128)S(1)} %fusion.23, pred[256,320]{0,1:T(8,128)(4,1)S(1)} %fusion.29), kind=kOutput, calls=%fused_computation.72 | output fusion | flops 7864639 | bytes 10584064 | tf_op jit(solution)/shard_map/sub | solution.py:97
  67.3 135.2 %all-gather.4.cloned.1.call-done = f32[256,273,128]{2,0,1:T(8,128)} async-done(((f32[16,273,128]{2,0,1:T(8,128)}), f32[256,273,128]{2,0,1:T(8,128)}) %all-gather.4.cloned.1.call-update) | async-done | bytes 35782672 | tf_op jit(solution)/shard_map/all_gather | solution.py:19
  202.7 54.1 %while.12 = (s32[]{:T(128)}, f32[16,273,128]{2,1,0:T(8,128)S(1)}, f32[16,273]{1,0:T(8,128)S(1)}, s32[]{:T(128)}, f32[16,16,273,128]{3,1,0,2:T(8,128)}, /*index=5...) while((s32[]{:T(128)}, f32[16,273,128]{2,1,0:T(8,128)S(1)}, f32[16,273]{1,0:T(8,128)S(1)}, s32[]{:T(128)}, ...), condition=%wide.region_2.3_spmd, body=%wide.region_1.2_spmd.sunk | while | flops 563477 | bytes 11234631 | solution.py:27
  202.7 1.9 constant_dynamic-slice_fusion.2
  204.6 1.0 fusion.46
  205.6 0.7 bitcast_add_fusion.5
  206.4 1.8 constant_dynamic-slice_fusion.2
  208.2 1.0 fusion.46
  209.2 0.7 bitcast_add_fusion.5
  210.0 1.8 constant_dynamic-slice_fusion.2
  211.8 1.0 fusion.46
  212.8 0.7 bitcast_add_fusion.5
  213.6 1.8 constant_dynamic-slice_fusion.2
  215.4 1.0 fusion.46
  216.4 0.7 bitcast_add_fusion.5
  217.2 1.8 constant_dynamic-slice_fusion.2
  219.0 1.0 fusion.46
  220.0 0.7 bitcast_add_fusion.5
  220.8 1.8 constant_dynamic-slice_fusion.2
  222.6 1.0 fusion.46
  223.6 0.7 bitcast_add_fusion.5
  224.4 1.8 constant_dynamic-slice_fusion.2
  226.2 1.0 fusion.46
  227.2 0.7 bitcast_add_fusion.5
  228.0 1.8 constant_dynamic-slice_fusion.2
  229.8 1.0 fusion.46
  230.8 0.7 bitcast_add_fusion.5
  231.6 1.8 constant_dynamic-slice_fusion.2
  233.4 1.0 fusion.46
  234.5 0.7 bitcast_add_fusion.5
  235.2 1.8 constant_dynamic-slice_fusion.2
  237.0 1.0 fusion.46
  238.1 0.7 bitcast_add_fusion.5
  238.8 1.8 constant_dynamic-slice_fusion.2
  240.6 1.0 fusion.46
  241.7 0.7 bitcast_add_fusion.5
  242.4 1.8 constant_dynamic-slice_fusion.2
  244.2 1.0 fusion.46
  245.3 0.7 bitcast_add_fusion.5
  246.0 1.8 constant_dynamic-slice_fusion.2
  247.8 1.0 fusion.46
  249.6 1.8 constant_dynamic-slice_fusion.2
  251.4 1.0 fusion.46
  253.2 1.8 constant_dynamic-slice_fusion.2
  255.0 1.0 fusion.46
  256.8 5.2 %fusion.12 = f32[16,1,256]{2,1,0:T(1,128)S(1)} fusion(f32[256,16,256]{0,2,1:T(8,128)} %bitcast.58, f32[256,16,16]{0,2,1:T(8,128)S(1)} %copy-done.13, f32[273]{0:T(512)S(1)} %pad.9.clone, f32[16,273,1]{1,0,2:T(8,128)S(1)} %bitcast.65), kind=kOutput, calls=%fused_computation.23 | convolution fusion | flops 15654912 | bytes 4491396 | tf_op jit(solution)/shard_map/qhf,hf->qh/dot_general | solution.py:85
  262.1 5.8 %fusion.13 = f32[16,128,256]{2,1,0:T(8,128)S(1)} fusion(f32[16,273,128]{2,1,0:T(8,128)S(1)} %get-tuple-element.39, f32[256,16,256]{0,2,1:T(8,128)S(1)} %bitcast.59, f32[256,16,16]{0,2,1:T(8,128)S(1)} %copy-done.13, f32[273]{0:T(512)S(1)} %pad.9.clone), kind=kOutput, calls=%fused_computation.24 | convolution fusion | flops 1719803904 | bytes 8791108 | tf_op jit(solution)/shard_map/qhf,hfd->qhd/dot_general | solution.py:82
  268.0 2.3 multiply_reduce_fusion.1
  270.3 3.8 %psum.7 = f32[256]{0:T(256)S(1)} all-reduce(f32[256]{0:T(256)S(1)} %get-tuple-element.65), channel_id=1, replica_groups=mesh['ctx'=16,'head'=2] {'head'}, use_global_device_ids=true, to_apply=%region_7.8 | all-reduce | flops 256 | bytes 2048 | tf_op jit(solution)/shard_map/psum | solution.py:102
  274.1 1.9 multiply_convert_fusion
  276.1 1.8 copy.30
  (59 shorter events, 4.3 us)
Async XLA Ops:
  6.5 56.1 %copy-start = (bf16[256,16,128]{2,1,0:T(8,128)(2,1)S(1)}, bf16[256,16,128]{2,1,0:T(8,128)(2,1)}, u32[]{:S(2)}) copy-start(bf16[256,16,128]{2,1,0:T(8,128)(2,1)} %param.11) | copy-start | bytes 3145732
  6.5 3.7 %copy-start.6 = (bf16[256,16,128]{2,1,0:T(8,128)(2,1)S(1)}, bf16[256,16,128]{2,1,0:T(8,128)(2,1)}, u32[]{:S(2)}) copy-start(bf16[256,16,128]{2,1,0:T(8,128)(2,1)} %param.10) | copy-start | bytes 3145732
  6.5 196.0 %all-gather.4.cloned.1.call-start = ((), (), s32[]{:S(2)}) async-start(), calls=%async_computation | async-start | bytes 38019072 | tf_op jit(solution)/shard_map/all_gather | solution.py:19
  8.3 2.0 copy-start.2
  8.3 4.8 %copy-start.7 = (f32[256,16,16]{0,2,1:T(8,128)}, f32[256,16,16]{0,2,1:T(8,128)S(1)}, u32[]{:S(2)}) copy-start(f32[256,16,16]{0,2,1:T(8,128)S(1)} %broadcast_multiply_fusion) | copy-start | bytes 786436
  15.0 4.6 %copy-start.15 = (bf16[256,256]{1,0:T(8,128)(2,1)S(1)}, bf16[256,256]{1,0:T(8,128)(2,1)}, u32[]{:S(2)}) copy-start(bf16[256,256]{1,0:T(8,128)(2,1)} %param.8) | copy-start | bytes 393220
  15.0 4.7 %copy-start.16 = (bf16[16,128]{1,0:T(8,128)(2,1)S(1)}, bf16[16,128]{1,0:T(8,128)(2,1)}, u32[]{:S(2)}) copy-start(bf16[16,128]{1,0:T(8,128)(2,1)} %param.13) | copy-start | bytes 12292
  15.3 1.9 copy-start.10
  18.1 42.8 %collective-permute-start = (bf16[2,64,16,128]{3,1,2,0:T(8,128)(2,1)}, bf16[2,64,16,128]{3,1,2,0:T(8,128)(2,1)}, u32[]{:S(2)}, u32[]{:S(2)}) collective-permute-start(bf16[2,64,16,128]{3,1,2,0:T(8,128)(2,1)} %pad_maximum_fusion.7), channel_id=1, source_target_pairs={{0,2},{2,4},{4,6},{6,8},{8,10},{10,12},{12,14},{14,16},{16,18},{18... | collective-permute-start | bytes 1572872 | tf_op jit(solution)/shard_map/ppermute | solution.py:33
  19.9 4.0 %copy-start.12 = (f32[256,16,16]{0,2,1:T(8,128)}, f32[256,16,16]{0,2,1:T(8,128)S(1)}, u32[]{:S(2)}) copy-start(f32[256,16,16]{0,2,1:T(8,128)S(1)} %broadcast_multiply_fusion.1) | copy-start | bytes 786436
  19.9 4.0 %copy-start.3 = (f32[256,16,16,16]{0,3,2,1:T(8,128)S(1)}, f32[256,16,16,16]{0,3,2,1:T(8,128)}, u32[]{:S(2)}) copy-start(f32[256,16,16,16]{0,3,2,1:T(8,128)} %copy-done.2) | copy-start | bytes 12582916
  19.9 4.0 %copy-start.8 = (f32[256,16,16]{0,2,1:T(8,128)S(1)}, f32[256,16,16]{0,2,1:T(8,128)}, u32[]{:S(2)}) copy-start(f32[256,16,16]{0,2,1:T(8,128)} %copy-done.7) | copy-start | bytes 786436
  23.9 11.5 %copy-start.4 = (f32[256,16,16,16]{0,3,2,1:T(8,128)}, f32[256,16,16,16]{0,3,2,1:T(8,128)S(1)}, u32[]{:S(2)}) copy-start(f32[256,16,16,16]{0,3,2,1:T(8,128)S(1)} %multiply_multiply_fusion.1) | copy-start | bytes 12582916
  202.7 54.1 %copy-start.13 = (f32[256,16,16]{0,2,1:T(8,128)S(1)}, f32[256,16,16]{0,2,1:T(8,128)}, u32[]{:S(2)}) copy-start(f32[256,16,16]{0,2,1:T(8,128)} %copy-done.12) | copy-start | bytes 786436
  256.8 5.3 %copy-start.5 = (f32[256,16,16,16]{0,3,2,1:T(8,128)S(1)}, f32[256,16,16,16]{0,3,2,1:T(8,128)}, u32[]{:S(2)}) copy-start(f32[256,16,16,16]{0,3,2,1:T(8,128)} %copy-done.4) | copy-start | bytes 12582916
  262.1 5.9 %copy-start.9 = (f32[16,256,128]{1,2,0:T(8,128)S(1)}, f32[16,256,128]{1,2,0:T(8,128)}, u32[]{:S(2)}) copy-start(f32[16,256,128]{1,2,0:T(8,128)} %fusion.3) | copy-start | bytes 6291460
  262.1 5.9 %copy-start.11 = (bf16[256,16,128]{2,0,1:T(8,128)(2,1)S(1)}, bf16[256,16,128]{2,0,1:T(8,128)(2,1)}, u32[]{:S(2)}) copy-start(bf16[256,16,128]{2,0,1:T(8,128)(2,1)} %copy-done.10) | copy-start | bytes 3145732
  262.1 5.9 %copy-start.14 = (bf16[64,16,128]{2,0,1:T(8,128)(2,1)S(1)}, bf16[64,16,128]{2,0,1:T(8,128)(2,1)}, u32[]{:S(2)}) copy-start(bf16[64,16,128]{2,0,1:T(8,128)(2,1)} %get-tuple-element.59) | copy-start | bytes 786436
  262.1 5.9 %copy-start.17 = (f32[16,256,320]{1,2,0:T(8,128)S(1)}, f32[16,256,320]{1,2,0:T(8,128)}, u32[]{:S(2)}) copy-start(f32[16,256,320]{1,2,0:T(8,128)} %get-tuple-element.62) | copy-start | bytes 15728644
  268.0 9.9 %copy-start.1 = (bf16[256,16,128]{2,1,0:T(8,128)(2,1)S(1)}, bf16[256,16,128]{2,1,0:T(8,128)(2,1)}, u32[]{:S(2)}) copy-start(bf16[256,16,128]{2,1,0:T(8,128)(2,1)} %param.11) | copy-start | bytes 3145732
Sparse Core Ops, SparseCore 0:
  15.1 187.3 all-gather.3
where the time goes:
time: 286 us; the launch traced here: 285 us
  waiting for transfers between devices  135 us (47%)
  local copies, waits for them, and re-layouts  38.1 us (13%)
  other arithmetic  38.1 us (13%)
  matrix products  31.9 us (11%)
  blocking collectives  25.9 us (9%)
  between operations  13.8 us (5%)
    all_gather x1, waiting for transfers between devices, prefix(): gathered = jax.tree.map(lambda a: lax.all_gather(a, axis), part)  135 us
    dynamic_slice x15, local copies, waits for them, and re-layouts, one(): lax.dynamic_index_in_dim(a, lap, 0, False)  27.2 us
    add x30, other arithmetic, add_pair(): return (before[0] + after_part[0], before[1] + after_part[1])  26.8 us
    all_gather x1, blocking collectives, prefix(): gathered = jax.tree.map(lambda a: lax.all_gather(a, axis), part)  22.1 us
    dot_general x1, matrix products, on_device(): jnp.einsum('iev,dev->eid', query_features, key_features, precision=exact_...  11.4 us
    dot_general x1, matrix products, on_device(): jnp.einsum('qhf,hfd->qhd', query_features, prior_state, precision=exact_p...  5.82 us
  transfers between devices with their start and end apart: 2, of which 1 were waited for; matrix products, arithmetic and copies ran while one was open for 10% of the time, Pallas kernels for 0%

commit v1 on v0

v1 whole, which is shorter than its diff:
```python
import functools
import math

import jax
import jax.numpy as jnp
import numpy as np
from jax import lax
from jax.experimental import pallas as pl
from jax.experimental.pallas import tpu as pltpu
from jax.sharding import PartitionSpec as P

HEADS = 32
DV = 128
DK = 16
WINDOW = 64
NORM_EPS = 1e-06

ROWS = 160
TOTAL_ROW = 33
WIDE = 40

F32 = jnp.float32
BF16 = jnp.bfloat16
NN = (((1,), (0,)), ((), ()))
NT = (((1,), (1,)), ((), ()))


def pair_tables():
    first = np.zeros((DK, ROWS), np.float32)
    second = np.zeros((DK, ROWS), np.float32)
    add = np.zeros((8, ROWS), np.float32)
    for i in range(DK):
        first[i, i] = 1.0 / 32.0
        second[i, i] = 1.0
        first[i, DK + i] = 0.25
        add[1, DK + i] = 1.0
        for d in range(1, 8):
            row = WIDE + DK * (d - 1) + i
            first[i, row] = 1.0 / 16.0
            second[(i + d) % DK, row] = 1.0
    for i in range(8):
        first[i, 152 + i] = 1.0 / 16.0
        second[i + 8, 152 + i] = 1.0
    add[0, 2 * DK] = 1.0
    add[1, 2 * DK] = 1.0
    return first, second, add


def dot(a, b, dims=NN):
    return lax.dot_general(a, b, dims, preferred_element_type=F32)


def split(x):
    high = x.astype(BF16)
    return high, (x - high.astype(F32)).astype(BF16)


def quarter(place_ref, r):
    low, mid = place_ref[0], place_ref[1]
    half = jnp.where(r >= 2, 1 - low, low)
    part = jnp.where(r % 2 == 1, 1 - mid, mid)
    return half * 2 + part


def state_kernel(place_ref, kt_ref, v_ref, out_ref):
    heads, toks = v_ref.shape[1], v_ref.shape[2]
    ones = jnp.where(lax.broadcasted_iota(jnp.int32, (8, toks), 0) == 0, 1.0, 0.0)
    ones = ones.astype(F32)
    all_ones = jnp.ones((8, toks), BF16)
    for j in range(heads):
        x = kt_ref[0, j * DK : (j + 1) * DK, :].astype(F32)
        parts = [x * x, x, ones]
        for d in range(1, 8):
            parts.append(x * pltpu.roll(x, DK - d, 0))
        parts.append(x[:8] * x[8:])
        high, low = split(jnp.concatenate(parts, axis=0))
        v = v_ref[0, j]
        out_ref[0, j] = dot(high, v) + dot(low, v)
        total = dot(all_ones, high, NT) + dot(all_ones, low, NT)
        out_ref[0, j, TOTAL_ROW : TOTAL_ROW + 1, :] = total[:1, :128]
        out_ref[0, j, TOTAL_ROW + 1 : TOTAL_ROW + 2, : ROWS - 128] = total[:1, 128:]


def states(place, keys_t, values_h):
    quarters, heads, toks, dim = values_h.shape
    return pl.pallas_call(
        state_kernel,
        out_shape=jax.ShapeDtypeStruct((quarters, heads, ROWS, dim), F32),
        grid_spec=pltpu.PrefetchScalarGridSpec(
            num_scalar_prefetch=1,
            grid=(quarters,),
            in_specs=[
                pl.BlockSpec((1, heads * DK, toks), lambda r, p: (quarter(p, r), 0, 0)),
                pl.BlockSpec((1, heads, toks, dim), lambda r, p: (quarter(p, r), 0, 0, 0)),
            ],
            out_specs=pl.BlockSpec((1, heads, ROWS, dim), lambda r, p: (r, 0, 0, 0)),
        ),
        name="states",
    )(place, keys_t, values_h)


def local_kernel(first_ref, q_ref, k_ref, v_ref, wq_ref, wk_ref, rk_ref, rv_ref,
                 num_ref, den_ref, win_ref):
    heads, toks, dim = v_ref.shape[1], v_ref.shape[2], v_ref.shape[3]
    half = toks // 2
    first = first_ref[0]
    row = lax.broadcasted_iota(jnp.int32, (half, half), 0)
    col = lax.broadcasted_iota(jnp.int32, (half, half), 1)
    tri = col <= row
    wrow = lax.broadcasted_iota(jnp.int32, (WINDOW, 2 * WINDOW), 0)
    wcol = lax.broadcasted_iota(jnp.int32, (WINDOW, 2 * WINDOW), 1)
    band = (wcol > wrow) & (wcol <= wrow + WINDOW)
    edge = band & ((wcol >= WINDOW) | (first == 0))
    den_ref[...] = jnp.zeros_like(den_ref)
    for j in range(heads):
        q = q_ref[0, :, j * DK : (j + 1) * DK]
        k = k_ref[0, :, j * DK : (j + 1) * DK]
        v = v_ref[0, j]
        for b in range(2):
            lo = b * half
            s = dot(q[lo : lo + half], k[: lo + half], NT)
            kern = 1.0 + s * 0.25 + s * s * (1.0 / 32.0)
            if b == 0:
                kern = jnp.where(tri, kern, 0.0)
            else:
                kern = jnp.concatenate(
                    [kern[:, :half], jnp.where(tri, kern[:, half:], 0.0)], axis=1
                )
            high, low = split(kern)
            num_ref[0, j, lo : lo + half, :] = dot(high, v[: lo + half]) + dot(low, v[: lo + half])
            den_ref[0, lo : lo + half, j : j + 1] = jnp.sum(kern, axis=1, keepdims=True)
        for b in range(toks // WINDOW):
            lo = b * WINDOW
            if b == 0:
                kk = jnp.concatenate([rk_ref[0, j], wk_ref[0, j, :WINDOW]], axis=0)
                vv = jnp.concatenate([rv_ref[0, j], v[:WINDOW]], axis=0)
                valid = edge
            else:
                kk = wk_ref[0, j, lo - WINDOW : lo + WINDOW]
                vv = v[lo - WINDOW : lo + WINDOW]
                valid = band
            sc = dot(wq_ref[0, j, lo : lo + WINDOW], kk, NT) / math.sqrt(dim)
            sc = jnp.where(valid, sc, -1e30)
            expo = jnp.exp(sc - jnp.max(sc, axis=1, keepdims=True))
            weights = (expo / jnp.sum(expo, axis=1, keepdims=True)).astype(BF16)
            win_ref[0, j, lo : lo + WINDOW, :] = dot(weights, vv)


def local(first, q4, k4, values_h, wq_h, wk_h, rim_k, rim_v):
    quarters, heads, toks, dim = values_h.shape
    full = pl.BlockSpec((1, heads, toks, dim), lambda r, p: (r, 0, 0, 0))
    rim = pl.BlockSpec((1, heads, WINDOW, dim), lambda r, p: (r, 0, 0, 0))
    narrow = pl.BlockSpec((1, toks, heads * DK), lambda r, p: (r, 0, 0))
    return pl.pallas_call(
        local_kernel,
        out_shape=(
            jax.ShapeDtypeStruct((quarters, heads, toks, dim), F32),
            jax.ShapeDtypeStruct((quarters, toks, 128), F32),
            jax.ShapeDtypeStruct((quarters, heads, toks, dim), F32),
        ),
        grid_spec=pltpu.PrefetchScalarGridSpec(
            num_scalar_prefetch=1,
            grid=(quarters,),
            in_specs=[narrow, narrow, full, full, full, rim, rim],
            out_specs=(full, pl.BlockSpec((1, toks, 128), lambda r, p: (r, 0, 0)), full),
        ),
        name="local",
    )(first, q4, k4, values_h, wq_h, wk_h, rim_k, rim_v)


def final_kernel(place_ref, q_ref, prior_ref, num_ref, den_ref, win_ref, e1_ref, e2_ref, add_ref,
                 mixed_ref, sq_ref, acc_ref):
    heads, toks, dim = num_ref.shape[1], num_ref.shape[2], num_ref.shape[3]
    r = pl.program_id(0)
    squares = jnp.zeros((toks, dim), F32)
    for j in range(heads):
        q = q_ref[0, :, j * DK : (j + 1) * DK]
        phi = (dot(q, e1_ref[...]) + add_ref[0:1]) * (dot(q, e2_ref[...]) + add_ref[1:2])
        phi_high, phi_low = split(phi)
        prior = prior_ref[0, j]
        high, low = split(prior)
        both = dot(phi_high, jnp.concatenate([high, low], axis=1))
        numer = num_ref[0, j] + ((both[:, dim:] + dot(phi_low, high)) + both[:, :dim])
        t0 = prior[TOTAL_ROW : TOTAL_ROW + 1, :]
        t1 = prior[TOTAL_ROW + 1 : TOTAL_ROW + 2, : ROWS - 128]
        denom = den_ref[0, :, j : j + 1] + (
            jnp.sum(phi[:, :128] * t0, axis=1, keepdims=True)
            + jnp.sum(phi[:, 128:] * t1, axis=1, keepdims=True)
        )
        mixed = numer / denom + win_ref[0, j]
        mixed_ref[0, j] = mixed
        squares = squares + mixed * mixed

    @pl.when(r == 0)
    def _():
        acc_ref[...] = squares

    @pl.when(r > 0)
    def _():
        acc_ref[...] += squares

    @pl.when(r == pl.num_programs(0) - 1)
    def _():
        sq_ref[...] = lax.dot_general(
            jnp.ones((8, dim), F32), acc_ref[...], NT,
            precision=lax.Precision.HIGHEST, preferred_element_type=F32,
        )


def final(place, q4, prior, num, den, win):
    quarters, heads, toks, dim = num.shape
    first, second, add = pair_tables()
    own = pl.BlockSpec((1, heads, toks, dim), lambda r, p: (quarter(p, r), 0, 0, 0))
    table = pl.BlockSpec((DK, ROWS), lambda r, p: (0, 0))
    return pl.pallas_call(
        final_kernel,
        out_shape=(
            jax.ShapeDtypeStruct((quarters, heads, toks, dim), F32),
            jax.ShapeDtypeStruct((8, toks), F32),
        ),
        grid_spec=pltpu.PrefetchScalarGridSpec(
            num_scalar_prefetch=1,
            grid=(quarters,),
            in_specs=[
                pl.BlockSpec((1, toks, heads * DK), lambda r, p: (quarter(p, r), 0, 0)),
                pl.BlockSpec((1, heads, ROWS, dim), lambda r, p: (r, 0, 0, 0)),
                own,
                pl.BlockSpec((1, toks, 128), lambda r, p: (quarter(p, r), 0, 0)),
                own,
                table,
                table,
                pl.BlockSpec((8, ROWS), lambda r, p: (0, 0)),
            ],
            out_specs=(own, pl.BlockSpec((8, toks), lambda r, p: (0, 0))),
            scratch_shapes=[pltpu.VMEM((toks, dim), F32)],
        ),
        name="final",
    )(place, q4, prior, num, den, win, jnp.asarray(first, BF16), jnp.asarray(second, BF16),
      jnp.asarray(add, F32))


def norm_kernel(mixed_ref, sq_ref, gain_ref, out_ref, turn_ref):
    heads, toks, dim = mixed_ref.shape
    scale = lax.rsqrt(sq_ref[...] / (HEADS * DV) + NORM_EPS)
    column = jnp.transpose(scale, (1, 0))[:, :1]
    for h in range(heads):
        turn_ref[:, h, :] = mixed_ref[h] * column * gain_ref[h : h + 1, :].astype(F32)
    out_ref[...] = turn_ref[...].astype(BF16)


def norm(mixed, squares, gain):
    heads, toks, dim = mixed.shape
    block = 128
    return pl.pallas_call(
        norm_kernel,
        out_shape=jax.ShapeDtypeStruct((toks, heads, dim), BF16),
        grid=(toks // block,),
        in_specs=[
            pl.BlockSpec((heads, block, dim), lambda i: (0, i, 0)),
            pl.BlockSpec((8, block), lambda i: (0, i)),
            pl.BlockSpec((heads, dim), lambda i: (0, 0)),
        ],
        out_specs=pl.BlockSpec((block, heads, dim), lambda i: (i, 0, 0)),
        scratch_shapes=[pltpu.VMEM((block, heads, dim), F32)],
        name="norm",
    )(mixed, squares, gain)


def exclusive_scan(own, count, low, mid):
    def permute(x, pairs):
        return lax.ppermute(x, "ctx", pairs)

    core_swap = [(i, i ^ 1) for i in range(count)]
    pair_swap = [(i, i ^ 2) for i in range(count)]
    other_core = permute(own[2:], core_swap)
    chip = own[:2] + other_core
    other_chip = permute(chip[1], pair_swap)
    plane = chip[0] + other_chip
    groups = count // 4
    before = jnp.zeros_like(plane)
    inclusive = plane
    step = 1
    while step < groups:
        got = permute(inclusive, [(i, i + 4 * step) for i in range(count - 4 * step)])
        before = got if step == 1 else before + got
        inclusive = inclusive + got
        step *= 2
    mine = before + jnp.where(mid == 1, other_chip, 0.0)
    send = before + jnp.where(mid == 0, chip[0], 0.0)
    half = jnp.stack([mine, permute(send, pair_swap)])
    send = half + jnp.where(low == 0, own[:2], 0.0)
    mine = half + jnp.where(low == 1, other_core, 0.0)
    return jnp.concatenate([mine, permute(send, core_swap)], axis=0)


def on_device(queries, keys, values, win_q, win_k, gain):
    toks, heads, dim = values.shape
    count = lax.axis_size("ctx")
    where = lax.axis_index("ctx")
    low, mid = where % 2, (where // 2) % 2
    place = jnp.stack([low, mid]).astype(jnp.int32)
    part = heads // 4

    rim_pairs = [(i, i + 1) for i in range(count - 1)]
    rim_k = lax.ppermute(win_k[toks - WINDOW :], "ctx", rim_pairs)
    rim_v = lax.ppermute(values[toks - WINDOW :], "ctx", rim_pairs)

    def by_head(x):
        return jnp.transpose(x, (1, 0, 2)).reshape(4, part, x.shape[0], dim)

    values_h = by_head(values)
    own = states(place, keys.T.reshape(4, part * DK, toks), values_h)
    prior = exclusive_scan(own, count, low, mid)

    q4 = jnp.transpose(queries.reshape(toks, 4, part * DK), (1, 0, 2))
    k4 = jnp.transpose(keys.reshape(toks, 4, part * DK), (1, 0, 2))
    first = (where == 0).astype(jnp.int32)[None]
    num, den, win = local(
        first, q4, k4, values_h, by_head(win_q), by_head(win_k), by_head(rim_k), by_head(rim_v)
    )
    mixed, squares = final(place, q4, prior, num, den, win)
    squares = lax.psum(squares[:1], "head")
    squares = jnp.broadcast_to(squares, (8, toks))
    return norm(mixed.reshape(heads, toks, dim), squares, gain)


def solution(mesh):
    return jax.shard_map(
        on_device,
        mesh=mesh,
        in_specs=(
            P("ctx", "head"),
            P("ctx", "head"),
            P("ctx", "head", None),
            P("ctx", "head", None),
            P("ctx", "head", None),
            P("head", None),
        ),
        out_specs=P("ctx", "head", None),
        check_vma=False,
    )
```

time: 286 us -> 122 us (0.43)
  the two profiles are of different devices: /device:TPU:31 before, /device:TPU:20 now
where the time goes in v1:
time: 122 us; the launch traced here: 121 us
  waiting for transfers between devices  35.1 us (29%)
  Pallas kernels  34.9 us (29%)
  starting transfers between devices  20.7 us (17%)
  local copies, waits for them, and re-layouts  19.5 us (16%)
  other arithmetic  5.77 us (5%)
  blocking collectives  4.94 us (4%)
    ppermute x6, waiting for transfers between devices, permute(): return lax.ppermute(x, 'ctx', pairs)  35.1 us
    pallas_call x1, Pallas kernels, local(): pl.pallas_call(local_kernel, out_shape=(jax.ShapeDtypeStruct((quarters, h...  17.6 us
    ppermute x1, starting transfers between devices, on_device(): rim_v = lax.ppermute(values[toks - WINDOW:], 'ctx', rim_pairs)  12.5 us
    transpose x5, local copies, waits for them, and re-layouts, by_head(): return jnp.transpose(x, (1, 0, 2)).reshape(4, part, x.shape[0], dim)  8.45 us
    pallas_call x1, Pallas kernels, final(): pl.pallas_call(final_kernel, out_shape=(jax.ShapeDtypeStruct((quarters, h...  8.41 us
    ppermute x6, starting transfers between devices, permute(): return lax.ppermute(x, 'ctx', pairs)  5.93 us
    pallas_call x1, Pallas kernels, states(): pl.pallas_call(state_kernel, out_shape=jax.ShapeDtypeStruct((quarters, he...  5.02 us
    psum x1, blocking collectives, on_device(): squares = lax.psum(squares[:1], 'head')  4.94 us
  transfers between devices with their start and end apart: 8, of which 5 were waited for; matrix products, arithmetic and copies ran while one was open for 9% of the time, Pallas kernels for 15%

profile of v1, /device:TPU:20, one launch (start us, length us, event | category | flops | bytes accessed | tf_op | source)
XLA Modules:
  0.0 121.1 jit_solution(13326300793246941872)
XLA Ops:
  0.0 1.7 %copy.18 = bf16[256,256]{1,0:T(8,128)(2,1)} copy(bf16[256,256]{0,1:T(8,128)(2,1)} %bitcast.47) | data formatting | bytes 262144 | tf_op jit(solution)/shard_map/transpose | solution.py:312
  1.7 2.5 %copy.19 = bf16[16,256,128]{2,1,0:T(8,128)(2,1)} copy(bf16[16,256,128]{2,0,1:T(8,128)(2,1)} %bitcast.39) | data formatting | bytes 2097152 | tf_op jit(solution)/shard_map/transpose | solution.py:309
  4.1 0.6 pad_add_fusion.place_ref
  4.8 5.0 %states.1 = f32[4,4,160,128]{3,2,1,0:T(8,128)} custom-call(s32[2]{0:T(128)} %pad_add_fusion.place_ref, bf16[4,64,256]{2,1,0:T(8,128)(2,1)} %bitcast.48, bf16[4,4,256,128]{3,2,1,0:T(8,128)(2,1)} %bitcast.32), custom_call_target="tpu_custom_call" | custom-call | tf_op jit(solution)/shard_map/states/pallas_call | solution.py:86
  9.8 0.0 copy-start
  9.8 1.2 %slice.31 = f32[2,4,160,128]{3,2,1,0:T(8,128)S(1)} slice(f32[4,4,160,128]{3,2,1,0:T(8,128)} %states.1), slice={[2:4], [0:4], [0:160], [0:128]} | slice | bytes 1310720 | tf_op jit(solution)/shard_map/slice | solution.py:275
  11.0 0.1 collective-permute-start
  11.1 2.1 %collective-permute-done = f32[2,4,160,128]{3,2,1,0:T(8,128)S(1)} collective-permute-done((f32[2,4,160,128]{3,2,1,0:T(8,128)S(1)}, f32[2,4,160,128]{3,2,1,0:T(8,128)S(1)}, u32[]{:S(2)}, u32[]{:S(2)}) %collective-permute-start) | collective-permute-done | bytes 655392 | tf_op jit(solution)/shard_map/ppermute | solution.py:271
  13.2 0.0 copy-done
  13.2 0.1 slice_add_fusion
  13.3 0.6 collective-permute-start.1
  13.9 9.2 %collective-permute-done.1 = f32[4,160,128]{2,1,0:T(8,128)S(1)} collective-permute-done((f32[4,160,128]{2,1,0:T(8,128)S(1)}, f32[4,160,128]{2,1,0:T(8,128)S(1)}, u32[]{:S(2)}, u32[]{:S(2)}) %collective-permute-start.1) | collective-permute-done | bytes 327712 | tf_op jit(solution)/shard_map/ppermute | solution.py:271
  23.1 3.5 %collective-permute-start.2 = (f32[4,160,128]{2,1,0:T(8,128)S(1)}, f32[4,160,128]{2,1,0:T(8,128)S(1)}, u32[]{:S(2)}, u32[]{:S(2)}) collective-permute-start(f32[4,160,128]{2,1,0:T(8,128)S(1)} %fusion), channel_id=1, source_target_pairs={{0,8},{2,10},{4,12},{6,14},{8,16},{10,18},{12,20},{14,22},{16,24},... | collective-permute-start | bytes 983048 | tf_op jit(solution)/shard_map/ppermute | solution.py:271
  26.6 7.3 %collective-permute-done.2 = f32[4,160,128]{2,1,0:T(8,128)S(1)} collective-permute-done((f32[4,160,128]{2,1,0:T(8,128)S(1)}, f32[4,160,128]{2,1,0:T(8,128)S(1)}, u32[]{:S(2)}, u32[]{:S(2)}) %collective-permute-start.2) | collective-permute-done | bytes 327712 | tf_op jit(solution)/shard_map/ppermute | solution.py:271
  34.0 0.0 copy-start.2
  34.0 0.7 copy-done.2
  34.7 1.3 %collective-permute-start.3 = (f32[4,160,128]{2,1,0:T(8,128)S(1)}, f32[4,160,128]{2,1,0:T(8,128)}, u32[]{:S(2)}, u32[]{:S(2)}) collective-permute-start(f32[4,160,128]{2,1,0:T(8,128)S(1)} %add.38), channel_id=1, source_target_pairs={{0,16},{2,18},{4,20},{6,22},{8,24},{10,26},{12,28},{14,30},{1,17},... | collective-permute-start | bytes 983048 | tf_op jit(solution)/shard_map/ppermute | solution.py:271
  36.0 9.7 %collective-permute-done.3 = f32[4,160,128]{2,1,0:T(8,128)} collective-permute-done((f32[4,160,128]{2,1,0:T(8,128)S(1)}, f32[4,160,128]{2,1,0:T(8,128)}, u32[]{:S(2)}, u32[]{:S(2)}) %collective-permute-start.3) | collective-permute-done | bytes 327712 | tf_op jit(solution)/shard_map/ppermute | solution.py:271
  45.7 1.9 %add_bitcast_fusion = (f32[1,4,160,128]{3,2,1,0:T(8,128)S(1)}, f32[4,160,128]{2,1,0:T(8,128)}) fusion(f32[4,160,128]{2,1,0:T(8,128)S(1)} %collective-permute-done.1, pred[]{:T(512)S(6)} %eq.18, f32[4,160,128]{2,1,0:T(8,128)} %copy-done.2, f32[4,160,128]{2,1,0:T(8,128)} %collective-permute-done.3, f32[2,4,160,128]{3,2,1,0:T(8,128)S(1)} %slice_add_fusion, ...), kind=kLoop, calls=%fused_computation.8 | loop fusion | flops 409600 | bytes 1966082 | tf_op jit(solution)/shard_map/stack | solution.py:290
  47.6 0.5 collective-permute-start.4
  48.1 6.8 %collective-permute-done.4 = f32[4,160,128]{2,1,0:T(8,128)S(1)} collective-permute-done((f32[4,160,128]{2,1,0:T(8,128)}, f32[4,160,128]{2,1,0:T(8,128)S(1)}, u32[]{:S(2)}, u32[]{:S(2)}) %collective-permute-start.4) | collective-permute-done | bytes 327712 | tf_op jit(solution)/shard_map/ppermute | solution.py:271
  54.9 0.0 copy-start.5
  54.9 0.7 copy-done.5
  55.6 0.0 copy-start.4
  55.6 2.0 %select_add_fusion.1 = (f32[2,4,160,128]{3,2,1,0:T(8,128)S(1)}, f32[2,4,160,128]{3,2,1,0:T(8,128)}) fusion(f32[2,4,160,128]{3,2,1,0:T(8,128)S(1)} %collective-permute-done, f32[1,4,160,128]{3,2,1,0:T(8,128)} %bitcast.49, f32[1,4,160,128]{3,2,1,0:T(8,128)S(1)} %get-tuple-element.17, pred[]{:T(512)S(6)} %eq.20, f32[4,4,160,128]{3,2,1,0:T(8,128)S(1)} %copy-done, ...), kind=kLoop, calls=%fused_computation.3 | loop fusion | flops 819200 | bytes 3276802 | tf_op jit(solution)/shard_map/add | solution.py:292
  57.6 0.0 copy-start.6
  57.6 0.0 copy-start.3
  57.6 0.0 collective-permute-start.5
  57.6 1.8 %slice.27 = bf16[64,16,128]{2,1,0:T(8,128)(2,1)} slice(bf16[256,16,128]{2,1,0:T(8,128)(2,1)} %param.13), slice={[192:256], [0:16], [0:128]} | slice | bytes 524288 | tf_op jit(solution)/shard_map/slice | solution.py:305
  59.4 2.3 %collective-permute-start.6 = (bf16[64,16,128]{2,1,0:T(8,128)(2,1)}, bf16[64,16,128]{2,1,0:T(8,128)(2,1)}, u32[]{:S(2)}, u32[]{:S(2)}) collective-permute-start(bf16[64,16,128]{2,1,0:T(8,128)(2,1)} %slice.27), channel_id=1, source_target_pairs={{0,2},{2,4},{4,6},{6,8},{8,10},{10,12},{12,14},{14,16},{16,18},{18... | collective-permute-start | bytes 786440 | tf_op jit(solution)/shard_map/ppermute | solution.py:305
  61.7 1.7 %slice.28 = bf16[64,16,128]{2,1,0:T(8,128)(2,1)} slice(bf16[256,16,128]{2,1,0:T(8,128)(2,1)} %param.11), slice={[192:256], [0:16], [0:128]} | slice | bytes 524288 | tf_op jit(solution)/shard_map/slice | solution.py:306
  63.3 12.5 %collective-permute-start.7 = (bf16[64,16,128]{2,1,0:T(8,128)(2,1)}, bf16[64,16,128]{2,1,0:T(8,128)(2,1)}, u32[]{:S(2)}, u32[]{:S(2)}) collective-permute-start(bf16[64,16,128]{2,1,0:T(8,128)(2,1)} %slice.28), channel_id=1, source_target_pairs={{0,2},{2,4},{4,6},{6,8},{8,10},{10,12},{12,14},{14,16},{16,18},{18... | collective-permute-start | bytes 786440 | tf_op jit(solution)/shard_map/ppermute | solution.py:306
  75.8 0.0 copy-done.4
  75.9 0.1 copy.20
  76.0 0.0 copy-done.6
  76.0 0.1 copy.16
  76.1 0.9 copy.17
  77.0 0.0 copy-start.1
  77.0 0.9 copy.21
  77.8 0.0 copy-done.3
  77.8 1.3 %copy.22 = bf16[16,256,128]{2,1,0:T(8,128)(2,1)} copy(bf16[16,256,128]{2,0,1:T(8,128)(2,1)S(1)} %bitcast.44) | data formatting | bytes 2097152 | tf_op jit(solution)/shard_map/transpose | solution.py:309
  79.1 0.0 copy-done.1
  79.1 1.3 %copy.23 = bf16[16,256,128]{2,1,0:T(8,128)(2,1)} copy(bf16[16,256,128]{2,0,1:T(8,128)(2,1)S(1)} %bitcast.40) | data formatting | bytes 2097152 | tf_op jit(solution)/shard_map/transpose | solution.py:309
  80.4 0.0 collective-permute-done.6
  80.4 1.7 %copy.24 = bf16[16,64,128]{2,1,0:T(8,128)(2,1)} copy(bf16[16,64,128]{2,0,1:T(8,128)(2,1)} %bitcast.19) | data formatting | bytes 524288 | tf_op jit(solution)/shard_map/transpose | solution.py:309
  82.1 0.0 collective-permute-done.7
  82.1 1.7 %copy.25 = bf16[16,64,128]{2,1,0:T(8,128)(2,1)} copy(bf16[16,64,128]{2,0,1:T(8,128)(2,1)} %bitcast.21) | data formatting | bytes 524288 | tf_op jit(solution)/shard_map/transpose | solution.py:309
  83.8 17.6 %local.1 = (f32[4,4,256,128]{3,2,1,0:T(8,128)}, f32[4,256,128]{2,1,0:T(8,128)}, f32[4,4,256,128]{3,2,1,0:T(8,128)}) custom-call(s32[1]{0:T(128)} %bitcast.12.first_ref, bf16[4,256,64]{2,1,0:T(8,128)(2,1)} %bitcast.36, bf16[4,256,64]{2,1,0:T(8,128)(2,1)} %bitcast.41, bf16[4,4,256,128]{3,2,1,0:T(8,128)(2,1)} %bitcast.33, bf16[4,4,256,128]{3,2,1,0:T(8,128)(2,1)} %bitcast.34, ...), custom_call_target="tpu_custom_call" | custom-call | tf_op jit(solution)/shard_map/local/pallas_call | solution.py:154
  101.4 0.0 collective-permute-done.5
  101.4 1.1 pad_maximum_fusion.prior_ref
  102.6 8.4 %final.1 = (f32[4,4,256,128]{3,2,1,0:T(8,128)}, f32[8,256]{1,0:T(8,128)}) custom-call(s32[2]{0:T(128)} %pad_add_fusion.place_ref, bf16[4,256,64]{2,1,0:T(8,128)(2,1)} %bitcast.37, f32[4,4,160,128]{3,2,1,0:T(8,128)} %pad_maximum_fusion.prior_ref, f32[4,4,256,128]{3,2,1,0:T(8,128)} %get-tuple-element.10.num_ref, f32[4,256,128]{2,1,0:T(8,128)} %get-tuple-element.11.den_ref, ...), custom_call_target="tpu_custom_call" | custom-call | tf_op jit(solution)/shard_map/final/pallas_call | solution.py:215
  111.0 0.7 slice.29
  111.7 4.9 %psum.7 = f32[256]{0:T(256)S(1)} all-reduce(f32[256]{0:T(256)S(1)} %bitcast.50), channel_id=1, replica_groups=mesh['ctx'=16,'head'=2] {'head'}, use_global_device_ids=true, to_apply=%region_0.1 | all-reduce | flops 256 | bytes 2048 | tf_op jit(solution)/shard_map/psum | solution.py:322
  116.6 0.6 broadcast_in_dim.27.sq_ref
  117.2 3.9 %norm.1 = bf16[256,16,128]{2,1,0:T(8,128)(2,1)} custom-call(f32[16,256,128]{2,1,0:T(8,128)} %bitcast.38, f32[8,256]{1,0:T(8,128)} %broadcast_in_dim.27.sq_ref, bf16[16,128]{1,0:T(8,128)(2,1)} %gain_ref.1), custom_call_target="tpu_custom_call" | custom-call | tf_op jit(solution)/shard_map/norm/pallas_call | solution.py:254
  (3 shorter events, 0.1 us)
Async XLA Ops:
  9.8 3.4 %copy-start = (f32[4,4,160,128]{3,2,1,0:T(8,128)S(1)}, f32[4,4,160,128]{3,2,1,0:T(8,128)}, u32[]{:S(2)}) copy-start(f32[4,4,160,128]{3,2,1,0:T(8,128)} %states.1) | copy-start | bytes 3932164
  11.0 2.2 %collective-permute-start = (f32[2,4,160,128]{3,2,1,0:T(8,128)S(1)}, f32[2,4,160,128]{3,2,1,0:T(8,128)S(1)}, u32[]{:S(2)}, u32[]{:S(2)}) collective-permute-start(f32[2,4,160,128]{3,2,1,0:T(8,128)S(1)} %slice.31), channel_id=1, source_target_pairs={{0,2},{2,0},{4,6},{6,4},{8,10},{10,8},{12,14},{14,12},{16,18},{18,... | collective-permute-start | bytes 1966088 | tf_op jit(solution)/shard_map/ppermute | solution.py:271
  13.3 9.8 %collective-permute-start.1 = (f32[4,160,128]{2,1,0:T(8,128)S(1)}, f32[4,160,128]{2,1,0:T(8,128)S(1)}, u32[]{:S(2)}, u32[]{:S(2)}) collective-permute-start(f32[4,160,128]{2,1,0:T(8,128)S(1)} %slice_bitcast_fusion), channel_id=1, source_target_pairs={{0,4},{2,6},{4,0},{6,2},{8,12},{10,14},{12,8},{14,10},{16,20},{18,... | collective-permute-start | bytes 983048 | tf_op jit(solution)/shard_map/ppermute | solution.py:271
  23.1 10.8 %collective-permute-start.2 = (f32[4,160,128]{2,1,0:T(8,128)S(1)}, f32[4,160,128]{2,1,0:T(8,128)S(1)}, u32[]{:S(2)}, u32[]{:S(2)}) collective-permute-start(f32[4,160,128]{2,1,0:T(8,128)S(1)} %fusion), channel_id=1, source_target_pairs={{0,8},{2,10},{4,12},{6,14},{8,16},{10,18},{12,20},{14,22},{16,24},... | collective-permute-start | bytes 983048 | tf_op jit(solution)/shard_map/ppermute | solution.py:271
  34.0 0.7 copy-start.2
  34.7 11.0 %collective-permute-start.3 = (f32[4,160,128]{2,1,0:T(8,128)S(1)}, f32[4,160,128]{2,1,0:T(8,128)}, u32[]{:S(2)}, u32[]{:S(2)}) collective-permute-start(f32[4,160,128]{2,1,0:T(8,128)S(1)} %add.38), channel_id=1, source_target_pairs={{0,16},{2,18},{4,20},{6,22},{8,24},{10,26},{12,28},{14,30},{1,17},... | collective-permute-start | bytes 983048 | tf_op jit(solution)/shard_map/ppermute | solution.py:271
  47.6 7.3 %collective-permute-start.4 = (f32[4,160,128]{2,1,0:T(8,128)}, f32[4,160,128]{2,1,0:T(8,128)S(1)}, u32[]{:S(2)}, u32[]{:S(2)}) collective-permute-start(f32[4,160,128]{2,1,0:T(8,128)} %get-tuple-element.18), channel_id=1, source_target_pairs={{0,4},{2,6},{4,0},{6,2},{8,12},{10,14},{12,8},{14,10},{16,20},{18,... | collective-permute-start | bytes 983048 | tf_op jit(solution)/shard_map/ppermute | solution.py:271
  54.9 0.7 copy-start.5
  55.6 20.2 %copy-start.4 = (bf16[256,256]{1,0:T(8,128)(2,1)S(1)}, bf16[256,256]{1,0:T(8,128)(2,1)}, u32[]{:S(2)}) copy-start(bf16[256,256]{1,0:T(8,128)(2,1)} %param.10) | copy-start | bytes 393220
  57.6 18.4 %copy-start.6 = (bf16[256,256]{1,0:T(8,128)(2,1)S(1)}, bf16[256,256]{1,0:T(8,128)(2,1)}, u32[]{:S(2)}) copy-start(bf16[256,256]{1,0:T(8,128)(2,1)} %param.9) | copy-start | bytes 393220
  57.6 20.2 %copy-start.3 = (bf16[256,16,128]{2,1,0:T(8,128)(2,1)S(1)}, bf16[256,16,128]{2,1,0:T(8,128)(2,1)}, u32[]{:S(2)}) copy-start(bf16[256,16,128]{2,1,0:T(8,128)(2,1)} %param.12) | copy-start | bytes 3145732
  57.6 43.8 %collective-permute-start.5 = (f32[2,4,160,128]{3,2,1,0:T(8,128)}, f32[2,4,160,128]{3,2,1,0:T(8,128)S(1)}, u32[]{:S(2)}, u32[]{:S(2)}) collective-permute-start(f32[2,4,160,128]{3,2,1,0:T(8,128)} %get-tuple-element.16), channel_id=1, source_target_pairs={{0,2},{2,0},{4,6},{6,4},{8,10},{10,8},{12,14},{14,12},{16,18},{18,... | collective-permute-start | bytes 1966088 | tf_op jit(solution)/shard_map/ppermute | solution.py:271
  59.4 21.0 %collective-permute-start.6 = (bf16[64,16,128]{2,1,0:T(8,128)(2,1)}, bf16[64,16,128]{2,1,0:T(8,128)(2,1)}, u32[]{:S(2)}, u32[]{:S(2)}) collective-permute-start(bf16[64,16,128]{2,1,0:T(8,128)(2,1)} %slice.27), channel_id=1, source_target_pairs={{0,2},{2,4},{4,6},{6,8},{8,10},{10,12},{12,14},{14,16},{16,18},{18... | collective-permute-start | bytes 786440 | tf_op jit(solution)/shard_map/ppermute | solution.py:305
  63.3 18.7 %collective-permute-start.7 = (bf16[64,16,128]{2,1,0:T(8,128)(2,1)}, bf16[64,16,128]{2,1,0:T(8,128)(2,1)}, u32[]{:S(2)}, u32[]{:S(2)}) collective-permute-start(bf16[64,16,128]{2,1,0:T(8,128)(2,1)} %slice.28), channel_id=1, source_target_pairs={{0,2},{2,4},{4,6},{6,8},{8,10},{10,12},{12,14},{14,16},{16,18},{18... | collective-permute-start | bytes 786440 | tf_op jit(solution)/shard_map/ppermute | solution.py:306
  77.0 2.1 %copy-start.1 = (bf16[256,16,128]{2,1,0:T(8,128)(2,1)S(1)}, bf16[256,16,128]{2,1,0:T(8,128)(2,1)}, u32[]{:S(2)}) copy-start(bf16[256,16,128]{2,1,0:T(8,128)(2,1)} %param.13) | copy-start | bytes 3145732

commit v2 on v0

v2 whole, which is shorter than its diff:
```python
import functools
import math

import jax
import jax.numpy as jnp
import numpy as np
from jax import lax
from jax.experimental import pallas as pl
from jax.experimental.pallas import tpu as pltpu
from jax.sharding import PartitionSpec as P

HEADS = 32
DV = 128
DK = 16
WINDOW = 64
NORM_EPS = 1e-06

ROWS = 160
TOTAL_ROW = 33
WIDE = 40
SENT = ROWS + WIDE

F32 = jnp.float32
BF16 = jnp.bfloat16
NN = (((1,), (0,)), ((), ()))
NT = (((1,), (1,)), ((), ()))


def pair_tables(heads):
    first = np.zeros((DK, ROWS), np.float32)
    second = np.zeros((DK, ROWS), np.float32)
    add = np.zeros((8, ROWS), np.float32)
    for i in range(DK):
        first[i, i] = 1.0 / 32.0
        second[i, i] = 1.0
        first[i, DK + i] = 0.25
        add[1, DK + i] = 1.0
        for d in range(1, 8):
            row = WIDE + DK * (d - 1) + i
            first[i, row] = 1.0 / 16.0
            second[(i + d) % DK, row] = 1.0
    for i in range(8):
        first[i, 152 + i] = 1.0 / 16.0
        second[i + 8, 152 + i] = 1.0
    add[0, 2 * DK] = 1.0
    add[1, 2 * DK] = 1.0
    both = []
    for one in (first, second):
        table = np.zeros((heads, heads * DK, ROWS), np.float32)
        for j in range(heads):
            table[j, j * DK : (j + 1) * DK] = one
        both.append(jnp.asarray(table, BF16))
    return both[0], both[1], jnp.asarray(add, F32)


def dot(a, b, dims=NN):
    return lax.dot_general(a, b, dims, preferred_element_type=F32)


def split(x):
    high = x.astype(BF16)
    return high, (x - high.astype(F32)).astype(BF16)


def pack(ref, x):
    high = x.astype(BF16)
    ref[:ROWS] = high
    ref[ROWS:] = (x[:WIDE] - high[:WIDE].astype(F32)).astype(BF16)


def unpack(got):
    wide = got[:WIDE].astype(F32) + got[ROWS:].astype(F32)
    return jnp.concatenate([wide, got[WIDE:ROWS].astype(F32)], axis=0)


def in_vmem(shape, dtype):
    return pltpu.VMEM(shape, dtype)


VMEM_SPEC = pl.BlockSpec(memory_space=pltpu.VMEM)
SMEM_SPEC = pl.BlockSpec(memory_space=pltpu.SMEM)


def call(body, name, outs, *operands, scalars=0, scratch=(), vmem=48 << 20):
    held = [
        x if i < scalars else pltpu.with_memory_space_constraint(x, pltpu.VMEM)
        for i, x in enumerate(operands)
    ]
    many = isinstance(outs, tuple)
    return pl.pallas_call(
        body,
        out_shape=outs,
        in_specs=[SMEM_SPEC] * scalars + [VMEM_SPEC] * (len(operands) - scalars),
        out_specs=tuple(VMEM_SPEC for _ in outs) if many else VMEM_SPEC,
        scratch_shapes=list(scratch),
        compiler_params=pltpu.CompilerParams(vmem_limit_bytes=vmem),
        name=name,
    )(*held)


def one_state(x, v):
    toks = x.shape[1]
    ones = jnp.where(lax.broadcasted_iota(jnp.int32, (8, toks), 0) == 0, 1.0, 0.0).astype(F32)
    parts = [x * x, x, ones]
    for d in range(1, 8):
        parts.append(x * pltpu.roll(x, DK - d, 0))
    parts.append(x[:8] * x[8:])
    high, low = split(jnp.concatenate(parts, axis=0))
    full = jnp.ones((8, toks), BF16)
    total = dot(full, high, NT) + dot(full, low, NT)
    return dot(high, v) + dot(low, v), total


def put_states(out_ref, place_ref, far, kt_ref, vh_ref):
    part = out_ref.shape[1]
    half = place_ref[0] if far == 0 else 1 - place_ref[0]

    def one(r, carry):
        mid = jnp.where(r == 1, 1 - place_ref[1], place_ref[1])
        base = (half * 2 + mid) * part
        for j in range(part):
            x = kt_ref[pl.ds(pl.multiple_of((base + j) * DK, DK), DK), :]
            state, total = one_state(x, vh_ref[base + j])
            out_ref[r, j] = state
            out_ref[r, j, TOTAL_ROW : TOTAL_ROW + 1, :] = total[:1, :128]
            out_ref[r, j, TOTAL_ROW + 1 : TOTAL_ROW + 2, : ROWS - 128] = total[:1, 128:]
        return carry

    lax.fori_loop(0, 2, one, 0)


def far_states_kernel(place_ref, keys_ref, v_ref, out_ref, vh_ref, kt_ref):
    vh_ref[...] = jnp.swapaxes(v_ref[...], 0, 1)
    kt_ref[...] = jnp.transpose(keys_ref[...].astype(F32), (1, 0))
    put_states(out_ref, place_ref, 1, kt_ref, vh_ref)


def near_states_kernel(place_ref, kt_ref, vh_ref, after_ref, out_ref):
    put_states(out_ref, place_ref, 0, kt_ref, vh_ref)


def chip_kernel(own_ref, other_ref, chip_ref, msg_ref):
    for j in range(own_ref.shape[1]):
        far = own_ref[1, j] + other_ref[1, j]
        chip_ref[1, j] = far
        pack(msg_ref.at[j], far)
        chip_ref[0, j] = own_ref[0, j] + other_ref[0, j]


def add_kernel(base_ref, got_ref, *rest):
    sum_ref, msg_ref = rest[-2:]
    for j in range(sum_ref.shape[0]):
        total = base_ref[j] + unpack(got_ref[j])
        sum_ref[j] = total
        pack(msg_ref.at[j], total)


def plane_kernel(chip_ref, got_ref, *rest):
    add_kernel(chip_ref.at[0], got_ref, *rest)


def before_kernel(rounds, place_ref, chip_ref, pair_ref, *rest):
    gots, (mine_ref, msg_ref) = rest[:rounds], rest[-2:]
    mid = place_ref[1]
    for j in range(mine_ref.shape[0]):
        before = unpack(gots[0][j])
        for got in gots[1:]:
            before = before + unpack(got[j])
        mine_ref[j] = before + jnp.where(mid == 1, unpack(pair_ref[j]), 0.0)
        pack(msg_ref.at[j], before + jnp.where(mid == 0, chip_ref[0, j], 0.0))


def half_kernel(place_ref, mine_ref, got_ref, own_ref, other_ref, prior_ref, send_ref):
    low = place_ref[0]
    for r in range(2):
        for j in range(mine_ref.shape[0]):
            half = mine_ref[j] if r == 0 else unpack(got_ref[j])
            send_ref[r, j] = half + jnp.where(low == 0, own_ref[r, j], 0.0)
            prior_ref[r, j] = half + jnp.where(low == 1, other_ref[r, j], 0.0)


def phi_kernel(q_ref, e1_ref, e2_ref, add_ref, after_ref, high_ref, low_ref, q4_ref):
    part = e1_ref.shape[0]
    width = part * DK
    for r in range(4):
        q4_ref[r] = q_ref[:, r * width : (r + 1) * width]

    def one(r, carry):
        q = q4_ref[r]
        for j in range(part):
            a = dot(q, e1_ref[j]) + add_ref[0:1]
            b = dot(q, e2_ref[j]) + add_ref[1:2]
            high, low = split(a * b)
            high_ref[r * part + j] = high
            low_ref[r * part + j] = low
        return carry

    lax.fori_loop(0, 4, one, 0)


def intra_kernel(q_ref, k_ref, vh_ref, after_ref, num_ref, den_ref, q4_ref, k4_ref):
    heads, toks, dim = vh_ref.shape
    part = heads // 4
    width = part * DK
    half = toks // 2
    for r in range(4):
        q4_ref[r] = q_ref[:, r * width : (r + 1) * width]
        k4_ref[r] = k_ref[:, r * width : (r + 1) * width]
    row = lax.broadcasted_iota(jnp.int32, (half, half), 0)
    col = lax.broadcasted_iota(jnp.int32, (half, half), 1)
    tri = col <= row
    lane = lax.broadcasted_iota(jnp.int32, (toks, width), 1) // DK

    def poly(s):
        return 1.0 + s * 0.25 + s * s * (1.0 / 32.0)

    def one(r, carry):
        q, k = q4_ref[r], k4_ref[r]
        tops, lows, rights = [], [], []
        for j in range(part):
            own = jnp.where(lane == j, q, jnp.zeros_like(q))
            tops.append(dot(own[:half], k[:half], NT))
            lows.append(dot(own[half:], k, NT))
        for j in range(part):
            v = vh_ref[r * part + j]
            top = jnp.where(tri, poly(tops[j]), 0.0)
            left = poly(lows[j][:, :half])
            right = jnp.where(tri, poly(lows[j][:, half:]), 0.0)
            high, low = split(top)
            num_ref[r * part + j, :half] = dot(high, v[:half]) + dot(low, v[:half])
            high, low = split(jnp.concatenate([left, right], axis=1))
            num_ref[r * part + j, half:] = dot(high, v) + dot(low, v)
            den_ref[r, :half, j : j + 1] = jnp.sum(top, axis=1, keepdims=True)
            den_ref[r, half:, j : j + 1] = jnp.sum(left + right, axis=1, keepdims=True)
        return carry

    lax.fori_loop(0, 4, one, 0)


def window_kernel(first_ref, wq_ref, wk_ref, vh_ref, rk_ref, rv_ref, after_ref,
                  win_ref, qh_ref, kh_ref, ve_ref):
    heads, toks, dim = vh_ref.shape
    part = heads // 4
    qh_ref[...] = jnp.swapaxes(wq_ref[...], 0, 1)
    kh_ref[:, :WINDOW] = jnp.swapaxes(rk_ref[...], 0, 1)
    kh_ref[:, WINDOW:] = jnp.swapaxes(wk_ref[...], 0, 1)
    ve_ref[:, :WINDOW] = jnp.swapaxes(rv_ref[...], 0, 1)
    ve_ref[:, WINDOW:] = vh_ref[...]
    row = lax.broadcasted_iota(jnp.int32, (WINDOW, 2 * WINDOW), 0)
    col = lax.broadcasted_iota(jnp.int32, (WINDOW, 2 * WINDOW), 1)
    band = (col > row) & (col <= row + WINDOW)
    edge = band & ((col >= WINDOW) | (first_ref[0] == 0))
    blocks = toks // WINDOW

    def one(r, carry):
        scores = []
        for j in range(part):
            head = r * part + j
            for b in range(blocks):
                lo = b * WINDOW
                sc = dot(qh_ref[head, lo : lo + WINDOW], kh_ref[head, lo : lo + 2 * WINDOW], NT)
                scores.append(jnp.where(edge if b == 0 else band, sc / math.sqrt(dim), -1e30))
        sc = jnp.concatenate(scores, axis=0)
        expo = jnp.exp(sc - jnp.max(sc, axis=1, keepdims=True))
        weights = (expo / jnp.sum(expo, axis=1, keepdims=True)).astype(BF16)
        for j in range(part):
            head = r * part + j
            for b in range(blocks):
                lo = b * WINDOW
                at = (j * blocks + b) * WINDOW
                win_ref[head, lo : lo + WINDOW] = dot(
                    weights[at : at + WINDOW], ve_ref[head, lo : lo + 2 * WINDOW]
                )
        return carry

    lax.fori_loop(0, 4, one, 0)


def final_kernel(far, place_ref, prior_ref, high_ref, low_ref, num_ref, den_ref, win_ref, *rest):
    mixed_ref, sq_ref = rest[-2:]
    part = prior_ref.shape[1]
    toks, dim = num_ref.shape[1:]
    half = place_ref[0] if far == 0 else 1 - place_ref[0]
    squares = jnp.zeros((toks, dim), F32)
    for a in range(2):
        r = jnp.where(place_ref[1] == a, 0, 1)
        for j in range(part):
            head = (half * 2 + a) * part + j
            prior = prior_ref[r, j]
            phi_high, phi_low = high_ref[head], low_ref[head]
            high, low = split(prior)
            both = dot(phi_high, jnp.concatenate([high, low], axis=1))
            numer = num_ref[head] + ((both[:, dim:] + dot(phi_low, high)) + both[:, :dim])
            t0 = prior[TOTAL_ROW : TOTAL_ROW + 1, :]
            t1 = prior[TOTAL_ROW + 1 : TOTAL_ROW + 2, : ROWS - 128]
            phi = phi_high.astype(F32) + phi_low.astype(F32)
            denom = den_ref[half * 2 + a, :, j : j + 1] + (
                jnp.sum(phi[:, :128] * t0, axis=1, keepdims=True)
                + jnp.sum(phi[:, 128:] * t1, axis=1, keepdims=True)
            )
            mixed = numer / denom + win_ref[head]
            mixed_ref[:, a * part + j, :] = mixed
            squares = squares + mixed * mixed
    total = lax.dot_general(
        jnp.ones((8, dim), F32), squares, NT,
        precision=lax.Precision.HIGHEST, preferred_element_type=F32,
    )
    sq_ref[...] = total if far == 0 else total + rest[0][...]


def norm_kernel(peers, place_ref, near_ref, far_ref, gain_ref, sq_ref, *rest):
    out_ref = rest[-1]
    half = near_ref.shape[1]
    total = sq_ref[...]
    for got in rest[:peers]:
        total = total + got[...]
    scale = lax.rsqrt(total / (HEADS * DV) + NORM_EPS)
    column = jnp.transpose(scale, (1, 0))[:, :1][:, :, None]
    gain = gain_ref[...].astype(F32)[None]

    def put(left_ref, right_ref):
        left = left_ref[...] * column * gain[:, :half]
        right = right_ref[...] * column * gain[:, half:]
        out_ref[...] = jnp.concatenate([left, right], axis=1).astype(BF16)

    @pl.when(place_ref[0] == 0)
    def _():
        put(near_ref, far_ref)

    @pl.when(place_ref[0] == 1)
    def _():
        put(far_ref, near_ref)


def on_device(queries, keys, values, win_q, win_k, gain):
    toks, heads, dim = values.shape
    count = lax.axis_size("ctx")
    peers = lax.axis_size("head") - 1
    where = lax.axis_index("ctx")
    place = jnp.stack([where & 1, (where >> 1) & 1]).astype(jnp.int32)
    first = (where == 0).astype(jnp.int32)[None]
    part = heads // 4
    core_swap = [(i, i ^ 1) for i in range(count)]
    pair_swap = [(i, i ^ 2) for i in range(count)]
    half_shape = in_vmem((2, part, ROWS, dim), F32)
    quarter_shape = in_vmem((part, ROWS, dim), F32)
    msg_shape = in_vmem((part, SENT, dim), BF16)
    head_wide = in_vmem((heads, toks, dim), F32)

    def permute(x, pairs):
        return lax.ppermute(x, "ctx", pairs)

    rim_pairs = [(i, i + 1) for i in range(count - 1)]
    rim_k = permute(win_k[toks - WINDOW :], rim_pairs)
    rim_v = permute(values[toks - WINDOW :], rim_pairs)

    far_own, values_h, keys_t = call(
        far_states_kernel, "far_states",
        (half_shape, in_vmem((heads, toks, dim), BF16), in_vmem((heads * DK, toks), F32)),
        place, keys, values, scalars=1,
    )
    other = permute(far_own, core_swap)
    own = call(near_states_kernel, "near_states", half_shape,
               place, keys_t, values_h, far_own, scalars=1)
    chip, msg = call(chip_kernel, "chip", (half_shape, msg_shape), own, other)
    pair = permute(msg, pair_swap)
    num, den = call(
        intra_kernel, "intra", (head_wide, in_vmem((4, toks, 128), F32)),
        queries, keys, values_h, msg,
        scratch=[pltpu.VMEM((4, toks, part * DK), BF16)] * 2,
    )
    inclusive, msg = call(plane_kernel, "plane", (quarter_shape, msg_shape), chip, pair, den)

    first_table, second_table, add_table = pair_tables(part)
    gots = []
    step = 1
    phi_high = phi_low = win = None
    while step < count // 4:
        got = permute(msg, [(i, i + 4 * step) for i in range(count - 4 * step)])
        gots.append(got)
        if step == 1:
            phi_high, phi_low = call(
                phi_kernel, "phi", (in_vmem((heads, toks, ROWS), BF16),) * 2,
                queries, first_table, second_table, add_table, msg,
                scratch=[pltpu.VMEM((4, toks, part * DK), BF16)],
            )
        if step == 2:
            win = call(
                window_kernel, "window", head_wide,
                first, win_q, win_k, values_h, rim_k, rim_v, msg, scalars=1,
                scratch=[
                    pltpu.VMEM((heads, toks, dim), BF16),
                    pltpu.VMEM((heads, toks + WINDOW, dim), BF16),
                    pltpu.VMEM((heads, toks + WINDOW, dim), BF16),
                ],
            )
        step *= 2
        if step < count // 4:
            inclusive, msg = call(
                add_kernel, "add", (quarter_shape, msg_shape), inclusive, got, phi_high
            )
    mine, msg = call(
        functools.partial(before_kernel, len(gots)), "before", (quarter_shape, msg_shape),
        place, chip, pair, *gots, win, scalars=1,
    )
    got = permute(msg, pair_swap)
    prior, send = call(half_kernel, "half", (half_shape, half_shape),
                       place, mine, got, own, other, scalars=1)
    far_prior = permute(send, core_swap)

    mixed_shape = in_vmem((toks, heads // 2, dim), F32)
    sq_shape = in_vmem((8, toks), F32)
    near, squares = call(
        functools.partial(final_kernel, 0), "near_final", (mixed_shape, sq_shape),
        place, prior, phi_high, phi_low, num, den, win, send, scalars=1,
    )
    far, squares = call(
        functools.partial(final_kernel, 1), "far_final", (mixed_shape, sq_shape),
        place, far_prior, phi_high, phi_low, num, den, win, squares, scalars=1,
    )
    others = [
        lax.ppermute(squares, "head", [(i, (i + k) % (peers + 1)) for i in range(peers + 1)])
        for k in range(1, peers + 1)
    ]
    return call(
        functools.partial(norm_kernel, peers), "norm",
        jax.ShapeDtypeStruct((toks, heads, dim), BF16),
        place, near, far, gain, squares, *others, scalars=1,
    )


def solution(mesh):
    return jax.shard_map(
        on_device,
        mesh=mesh,
        in_specs=(
            P("ctx", "head"),
            P("ctx", "head"),
            P("ctx", "head", None),
            P("ctx", "head", None),
            P("ctx", "head", None),
            P("head", None),
        ),
        out_specs=P("ctx", "head", None),
        check_vma=False,
    )
```

time: 286 us -> 66.6 us (0.23)
  the two profiles are of different devices: /device:TPU:31 before, /device:TPU:0 now
where the time goes in v2:
time: 66.6 us; the launch traced here: 66.1 us
  Pallas kernels  23.7 us (36%)
  starting transfers between devices  19.5 us (29%)
  local copies, waits for them, and re-layouts  12.1 us (18%)
  waiting for transfers between devices  10.4 us (16%)
    pallas_call x13, Pallas kernels, call(): pl.pallas_call(body, out_shape=outs, in_specs=[SMEM_SPEC] * scalars + [VM...  23.7 us
    ppermute x8, starting transfers between devices, permute(): return lax.ppermute(x, 'ctx', pairs)  17.9 us
    unnamed x56, local copies, waits for them, and re-layouts  8.76 us
    ppermute x8, waiting for transfers between devices, permute(): return lax.ppermute(x, 'ctx', pairs)  8.28 us
    ppermute x1, waiting for transfers between devices, on_device(): lax.ppermute(squares, 'head', [(i, (i + k) % (peers + 1)) for i in range(...  2.16 us
    slice x1, local copies, waits for them, and re-layouts, on_device(): rim_k = permute(win_k[toks - WINDOW:], rim_pairs)  1.68 us
    slice x1, local copies, waits for them, and re-layouts, on_device(): rim_v = permute(values[toks - WINDOW:], rim_pairs)  1.67 us
    ppermute x1, starting transfers between devices, on_device(): lax.ppermute(squares, 'head', [(i, (i + k) % (peers + 1)) for i in range(...  1.52 us
  transfers between devices with their start and end apart: 9, of which 4 were waited for; matrix products, arithmetic and copies ran while one was open for 5% of the time, Pallas kernels for 23%

profile of v2, /device:TPU:0, one launch (start us, length us, event | category | flops | bytes accessed | tf_op | source)
XLA Modules:
  0.0 66.1 jit_solution(4223070161870324350)
XLA Ops:
  0.0 0.1 pad_add_fusion.place_ref
  0.1 1.2 %copy-done.12 = bf16[256,16,128]{2,1,0:T(8,128)(2,1)S(1)} copy-done((bf16[256,16,128]{2,1,0:T(8,128)(2,1)S(1)}, bf16[256,16,128]{2,1,0:T(8,128)(2,1)}, u32[]{:S(2)}) %copy-start.12) | copy-done | bytes 1048600
  1.3 0.9 %copy-done.19 = bf16[256,256]{1,0:T(8,128)(2,1)S(1)} copy-done((bf16[256,256]{1,0:T(8,128)(2,1)S(1)}, bf16[256,256]{1,0:T(8,128)(2,1)}, u32[]{:S(2)}) %copy-start.19) | copy-done | bytes 131096
  2.2 1.8 %far_states.1 = (f32[2,4,160,128]{3,2,1,0:T(8,128)S(1)}, bf16[16,256,128]{2,1,0:T(8,128)(2,1)S(1)}, f32[256,256]{1,0:T(8,128)S(1)}) custom-call(s32[2]{0:T(128)S(1)} %pad_add_fusion.place_ref, bf16[256,256]{1,0:T(8,128)(2,1)S(1)} %copy-done.19, bf16[256,16,128]{2,1,0:T(8,128)(2,1)S(1)} %copy-done.12), custom_call_target="tpu_custom_call" | custom-call | tf_op jit(solution)/shard_map/far_states/pallas_call | solution.py:90
  4.0 0.0 copy-start.20
  4.0 0.0 copy-start.21
  4.1 0.5 collective-permute-start
  4.6 1.4 %near_states.1.own_ref = f32[2,4,160,128]{3,2,1,0:T(8,128)S(1)} custom-call(s32[2]{0:T(128)S(1)} %pad_add_fusion.place_ref, f32[256,256]{1,0:T(8,128)S(1)} %get-tuple-element.25.kt_ref, bf16[16,256,128]{2,1,0:T(8,128)(2,1)S(1)} %get-tuple-element.26.vh_ref, f32[2,4,160,128]{3,2,1,0:T(8,128)S(1)} %get-tuple-element.27.after_ref), custom_call_target="tpu_custom_call" | custom-call | tf_op jit(solution)/shard_map/near_states/pallas_call | solution.py:90
  6.0 0.0 copy-start.4
  6.0 0.3 collective-permute-done.other_ref
  6.3 0.1 chip.1
  6.4 0.0 copy-start.10
  6.4 0.0 copy-start.22
  6.4 0.0 copy-start.23
  6.4 0.0 copy-start.26
  6.4 0.4 copy-done.4
  6.9 0.3 copy-done.8
  7.1 2.9 %collective-permute-start.1 = (bf16[4,200,128]{2,1,0:T(8,128)(2,1)S(1)}, bf16[4,200,128]{2,1,0:T(8,128)(2,1)S(1)}, u32[]{:S(2)}, u32[]{:S(2)}) collective-permute-start(bf16[4,200,128]{2,1,0:T(8,128)(2,1)S(1)} %get-tuple-element.29.after_ref), channel_id=1, source_target_pairs={{0,4},{2,6},{4,0},{6,2},{8,12},{10,14},{12,8},{14,10},{16,20},{18,... | collective-permute-start | bytes 614408 | tf_op jit(solution)/shard_map/ppermute | solution.py:351
  10.0 0.0 copy-done.20
  10.0 0.0 copy-done.21
  10.0 2.7 %intra.1 = (f32[16,256,128]{2,1,0:T(8,128)S(1)}, f32[4,256,128]{2,1,0:T(8,128)S(1)}) custom-call(bf16[256,256]{1,0:T(8,128)(2,1)S(1)} %copy-done.21, bf16[256,256]{1,0:T(8,128)(2,1)S(1)} %copy-done.20, bf16[16,256,128]{2,1,0:T(8,128)(2,1)S(1)} %get-tuple-element.26.vh_ref, bf16[4,200,128]{2,1,0:T(8,128)(2,1)S(1)} %get-tuple-element.29.after_ref), custom_call_target="tpu_custom_call" | custom-call | tf_op jit(solution)/shard_map/intra/pallas_call | solution.py:90
  12.8 0.0 copy-start
  12.8 1.3 %copy-done = f32[16,256,128]{2,1,0:T(8,128)} copy-done((f32[16,256,128]{2,1,0:T(8,128)}, f32[16,256,128]{2,1,0:T(8,128)S(1)}, u32[]{:S(2)}) %copy-start) | copy-done | bytes 2097176
  14.1 1.3 %collective-permute-done.1.got_ref.pair_ref = bf16[4,200,128]{2,1,0:T(8,128)(2,1)S(1)} collective-permute-done((bf16[4,200,128]{2,1,0:T(8,128)(2,1)S(1)}, bf16[4,200,128]{2,1,0:T(8,128)(2,1)S(1)}, u32[]{:S(2)}, u32[]{:S(2)}) %collective-permute-start.1) | collective-permute-done | bytes 204832 | tf_op jit(solution)/shard_map/ppermute | solution.py:351
  15.4 0.1 plane.1
  15.5 3.7 %collective-permute-start.2 = (bf16[4,200,128]{2,1,0:T(8,128)(2,1)S(1)}, bf16[4,200,128]{2,1,0:T(8,128)(2,1)S(1)}, u32[]{:S(2)}, u32[]{:S(2)}) collective-permute-start(bf16[4,200,128]{2,1,0:T(8,128)(2,1)S(1)} %get-tuple-element.31.after_ref), channel_id=1, source_target_pairs={{0,8},{2,10},{4,12},{6,14},{8,16},{10,18},{12,20},{14,22},{16,24},... | collective-permute-start | bytes 614408 | tf_op jit(solution)/shard_map/ppermute | solution.py:351
  19.2 1.7 %slice.6 = bf16[64,16,128]{2,1,0:T(8,128)(2,1)} slice(bf16[256,16,128]{2,1,0:T(8,128)(2,1)} %wk_ref.1), slice={[192:256], [0:16], [0:128]} | slice | bytes 524288 | tf_op jit(solution)/shard_map/slice | solution.py:354
  20.9 2.0 %collective-permute-start.4 = (bf16[64,16,128]{2,1,0:T(8,128)(2,1)}, bf16[64,16,128]{2,1,0:T(8,128)(2,1)}, u32[]{:S(2)}, u32[]{:S(2)}) collective-permute-start(bf16[64,16,128]{2,1,0:T(8,128)(2,1)} %slice.6), channel_id=1, source_target_pairs={{0,2},{2,4},{4,6},{6,8},{8,10},{10,12},{12,14},{14,16},{16,18},{18... | collective-permute-start | bytes 786440 | tf_op jit(solution)/shard_map/ppermute | solution.py:351
  22.9 1.7 %slice.7 = bf16[64,16,128]{2,1,0:T(8,128)(2,1)} slice(bf16[256,16,128]{2,1,0:T(8,128)(2,1)} %v_ref.1), slice={[192:256], [0:16], [0:128]} | slice | bytes 524288 | tf_op jit(solution)/shard_map/slice | solution.py:355
  24.5 0.0 copy-done.6
  24.5 0.0 copy-done.17
  24.5 4.1 %collective-permute-start.5 = (bf16[64,16,128]{2,1,0:T(8,128)(2,1)}, bf16[64,16,128]{2,1,0:T(8,128)(2,1)}, u32[]{:S(2)}, u32[]{:S(2)}) collective-permute-start(bf16[64,16,128]{2,1,0:T(8,128)(2,1)} %slice.7), channel_id=1, source_target_pairs={{0,2},{2,4},{4,6},{6,8},{8,10},{10,12},{12,14},{14,16},{16,18},{18... | collective-permute-start | bytes 786440 | tf_op jit(solution)/shard_map/ppermute | solution.py:351
  28.7 0.0 copy-done.22
  28.7 0.0 copy-done.23
  28.7 0.0 copy-done.26
  28.7 1.8 %phi.1 = (bf16[16,256,160]{2,1,0:T(8,128)(2,1)S(1)}, bf16[16,256,160]{2,1,0:T(8,128)(2,1)S(1)}) custom-call(bf16[256,256]{1,0:T(8,128)(2,1)S(1)} %copy-done.21, bf16[4,64,160]{2,1,0:T(8,128)(2,1)S(1)} %copy-done.22, bf16[4,64,160]{2,1,0:T(8,128)(2,1)S(1)} %copy-done.23, f32[8,160]{1,0:T(8,128)S(1)} %copy-done.26, ...), custom_call_target="tpu_custom_call" | custom-call | tf_op jit(solution)/shard_map/phi/pallas_call | solution.py:90
  30.5 0.0 copy-done.10
  30.5 0.0 copy-start.2
  30.5 1.4 %copy-done.2 = bf16[16,256,160]{2,1,0:T(8,128)(2,1)} copy-done((bf16[16,256,160]{2,1,0:T(8,128)(2,1)}, bf16[16,256,160]{2,1,0:T(8,128)(2,1)S(1)}, u32[]{:S(2)}) %copy-start.2) | copy-done | bytes 1310744
  31.9 0.0 collective-permute-done.2.got_ref.rest_0_
  31.9 0.9 %add.3 = (f32[4,160,128]{2,1,0:T(8,128)}, bf16[4,200,128]{2,1,0:T(8,128)(2,1)}) custom-call(f32[4,160,128]{2,1,0:T(8,128)S(1)} %get-tuple-element.32.base_ref, bf16[4,200,128]{2,1,0:T(8,128)(2,1)S(1)} %collective-permute-done.2.got_ref.rest_0_, bf16[16,256,160]{2,1,0:T(8,128)(2,1)S(1)} %get-tuple-element.33.rest_0_.high_ref), custom_call_target="tpu_custom_call" | custom-call | tf_op jit(solution)/shard_map/add/pallas_call | solution.py:90
  32.8 0.7 %copy-done.15 = bf16[4,200,128]{2,1,0:T(8,128)(2,1)} copy-done((bf16[4,200,128]{2,1,0:T(8,128)(2,1)}, bf16[4,200,128]{2,1,0:T(8,128)(2,1)S(1)}, u32[]{:S(2)}) %copy-start.15) | copy-done | bytes 204824
  33.5 4.5 %collective-permute-start.3 = (bf16[4,200,128]{2,1,0:T(8,128)(2,1)}, bf16[4,200,128]{2,1,0:T(8,128)(2,1)}, u32[]{:S(2)}, u32[]{:S(2)}) collective-permute-start(bf16[4,200,128]{2,1,0:T(8,128)(2,1)} %get-tuple-element.34.after_ref), channel_id=1, source_target_pairs={{0,16},{2,18},{4,20},{6,22},{8,24},{10,26},{12,28},{14,30},{1,17},... | collective-permute-start | bytes 614408 | tf_op jit(solution)/shard_map/ppermute | solution.py:351
  38.0 0.0 collective-permute-done.4.rk_ref
  38.0 0.0 collective-permute-done.5.rv_ref
  38.0 1.2 %copy-done.13 = bf16[256,16,128]{2,1,0:T(8,128)(2,1)S(1)} copy-done((bf16[256,16,128]{2,1,0:T(8,128)(2,1)S(1)}, bf16[256,16,128]{2,1,0:T(8,128)(2,1)}, u32[]{:S(2)}) %copy-start.13) | copy-done | bytes 1048600
  39.3 1.2 %copy-done.14 = bf16[256,16,128]{2,1,0:T(8,128)(2,1)S(1)} copy-done((bf16[256,16,128]{2,1,0:T(8,128)(2,1)S(1)}, bf16[256,16,128]{2,1,0:T(8,128)(2,1)}, u32[]{:S(2)}) %copy-start.14) | copy-done | bytes 1048600
  40.5 0.0 copy-start.9
  40.5 5.3 %window.1.rest_2_.win_ref = f32[16,256,128]{2,1,0:T(8,128)S(1)} custom-call(s32[1]{0:T(128)} %bitcast.2.first_ref, bf16[256,16,128]{2,1,0:T(8,128)(2,1)S(1)} %copy-done.14, bf16[256,16,128]{2,1,0:T(8,128)(2,1)S(1)} %copy-done.13, bf16[16,256,128]{2,1,0:T(8,128)(2,1)S(1)} %get-tuple-element.26.vh_ref, bf16[64,16,128]{2,1,0:T(8,128)(2,1)} %collective-permute-done.4.rk_ref, ...), custom_call_target="tpu_custom_call" | custom-call | tf_op jit(solution)/shard_map/window/pallas_call | solution.py:90
  45.8 0.0 collective-permute-done.3.rest_1_
  45.8 1.2 %before.1 = (f32[4,160,128]{2,1,0:T(8,128)S(1)}, bf16[4,200,128]{2,1,0:T(8,128)(2,1)S(1)}) custom-call(s32[2]{0:T(128)S(1)} %pad_add_fusion.place_ref, f32[2,4,160,128]{3,2,1,0:T(8,128)S(1)} %copy-done.11, bf16[4,200,128]{2,1,0:T(8,128)(2,1)S(1)} %copy-done.18, bf16[4,200,128]{2,1,0:T(8,128)(2,1)S(1)} %copy-done.16, ...), custom_call_target="tpu_custom_call" | custom-call | tf_op jit(solution)/shard_map/before/pallas_call | solution.py:90
  47.0 0.1 collective-permute-start.6
  47.1 6.7 %collective-permute-done.6.got_ref = bf16[4,200,128]{2,1,0:T(8,128)(2,1)S(1)} collective-permute-done((bf16[4,200,128]{2,1,0:T(8,128)(2,1)S(1)}, bf16[4,200,128]{2,1,0:T(8,128)(2,1)S(1)}, u32[]{:S(2)}, u32[]{:S(2)}) %collective-permute-start.6) | collective-permute-done | bytes 204832 | tf_op jit(solution)/shard_map/ppermute | solution.py:351
  53.8 0.0 copy-done.5
  53.8 0.7 %half.1 = (f32[2,4,160,128]{3,2,1,0:T(8,128)S(1)}, f32[2,4,160,128]{3,2,1,0:T(8,128)S(1)}) custom-call(s32[2]{0:T(128)S(1)} %pad_add_fusion.place_ref, f32[4,160,128]{2,1,0:T(8,128)S(1)} %get-tuple-element.35.mine_ref, bf16[4,200,128]{2,1,0:T(8,128)(2,1)S(1)} %collective-permute-done.6.got_ref, f32[2,4,160,128]{3,2,1,0:T(8,128)S(1)} %copy-done.5, ...), custom_call_target="tpu_custom_call" | custom-call | tf_op jit(solution)/shard_map/half/pallas_call | solution.py:90
  54.5 0.1 collective-permute-start.7
  54.7 2.8 %near_final.1 = (f32[256,8,128]{2,1,0:T(8,128)S(1)}, f32[8,256]{1,0:T(8,128)S(1)}) custom-call(s32[2]{0:T(128)} %copy-done.24, f32[2,4,160,128]{3,2,1,0:T(8,128)S(1)} %get-tuple-element.37.prior_ref, bf16[16,256,160]{2,1,0:T(8,128)(2,1)S(1)} %get-tuple-element.33.rest_0_.high_ref, bf16[16,256,160]{2,1,0:T(8,128)(2,1)S(1)} %copy-done.3, ...), custom_call_target="tpu_custom_call" | custom-call | tf_op jit(solution)/shard_map/near_final/pallas_call | solution.py:90
  57.4 0.0 collective-permute-done.7.prior_ref
  57.5 0.0 copy-start.27
  57.5 2.9 %far_final.1 = (f32[256,8,128]{2,1,0:T(8,128)S(1)}, f32[8,256]{1,0:T(8,128)S(1)}) custom-call(s32[2]{0:T(128)} %copy-done.24, f32[2,4,160,128]{3,2,1,0:T(8,128)S(1)} %collective-permute-done.7.prior_ref, bf16[16,256,160]{2,1,0:T(8,128)(2,1)S(1)} %get-tuple-element.33.rest_0_.high_ref, bf16[16,256,160]{2,1,0:T(8,128)(2,1)S(1)} %copy-done.3, ...), custom_call_target="tpu_custom_call" | custom-call | tf_op jit(solution)/shard_map/far_final/pallas_call | solution.py:90
  60.4 1.5 %collective-permute-start.8 = (f32[8,256]{1,0:T(8,128)S(1)}, f32[8,256]{1,0:T(8,128)S(1)}, u32[]{:S(2)}, u32[]{:S(2)}) collective-permute-start(f32[8,256]{1,0:T(8,128)S(1)} %get-tuple-element.44.sq_ref), channel_id=1, source_target_pairs={{0,1},{1,0},{2,3},{3,2},{4,5},{5,4},{6,7},{7,6},{8,9},{9,8},{10,11... | collective-permute-start | bytes 24584 | tf_op jit(solution)/shard_map/ppermute | solution.py:422
  61.9 2.2 %collective-permute-done.8.rest_0_ = f32[8,256]{1,0:T(8,128)S(1)} collective-permute-done((f32[8,256]{1,0:T(8,128)S(1)}, f32[8,256]{1,0:T(8,128)S(1)}, u32[]{:S(2)}, u32[]{:S(2)}) %collective-permute-start.8) | collective-permute-done | bytes 8224 | tf_op jit(solution)/shard_map/ppermute | solution.py:422
  64.1 0.0 copy-done.27
  64.1 2.0 %norm.1 = bf16[256,16,128]{2,1,0:T(8,128)(2,1)} custom-call(s32[2]{0:T(128)S(1)} %copy-done.25, f32[256,8,128]{2,1,0:T(8,128)S(1)} %get-tuple-element.41.near_ref, f32[256,8,128]{2,1,0:T(8,128)S(1)} %get-tuple-element.43.far_ref, bf16[16,128]{1,0:T(8,128)(2,1)S(1)} %copy-done.27, f32[8,256]{1,0:T(8,128)S(1)} %get-tuple-element.44.sq_ref, ...), custom_call_target="tpu_custom_call" | custom-call | tf_op jit(solution)/shard_map/norm/pallas_call | solution.py:90
  (26 shorter events, 0.0 us)
Async XLA Ops:
  0.1 1.2 %copy-start.12 = (bf16[256,16,128]{2,1,0:T(8,128)(2,1)S(1)}, bf16[256,16,128]{2,1,0:T(8,128)(2,1)}, u32[]{:S(2)}) copy-start(bf16[256,16,128]{2,1,0:T(8,128)(2,1)} %v_ref.1) | copy-start | bytes 3145732
  1.3 0.9 %copy-start.19 = (bf16[256,256]{1,0:T(8,128)(2,1)S(1)}, bf16[256,256]{1,0:T(8,128)(2,1)}, u32[]{:S(2)}) copy-start(bf16[256,256]{1,0:T(8,128)(2,1)} %k_ref.1) | copy-start | bytes 393220
  2.2 51.6 %copy-start.24 = (s32[2]{0:T(128)}, s32[2]{0:T(128)S(1)}, u32[]{:S(2)}) copy-start(s32[2]{0:T(128)S(1)} %pad_add_fusion.place_ref) | copy-start | bytes 28
  4.0 6.0 %copy-start.20 = (bf16[256,256]{1,0:T(8,128)(2,1)S(1)}, bf16[256,256]{1,0:T(8,128)(2,1)}, u32[]{:S(2)}) copy-start(bf16[256,256]{1,0:T(8,128)(2,1)} %k_ref.1) | copy-start | bytes 393220
  4.0 6.0 %copy-start.21 = (bf16[256,256]{1,0:T(8,128)(2,1)S(1)}, bf16[256,256]{1,0:T(8,128)(2,1)}, u32[]{:S(2)}) copy-start(bf16[256,256]{1,0:T(8,128)(2,1)} %q_ref.3) | copy-start | bytes 393220
  4.1 2.2 %collective-permute-start = (f32[2,4,160,128]{3,2,1,0:T(8,128)S(1)}, f32[2,4,160,128]{3,2,1,0:T(8,128)S(1)}, u32[]{:S(2)}, u32[]{:S(2)}) collective-permute-start(f32[2,4,160,128]{3,2,1,0:T(8,128)S(1)} %get-tuple-element.27.after_ref), channel_id=1, source_target_pairs={{0,2},{2,0},{4,6},{6,4},{8,10},{10,8},{12,14},{14,12},{16,18},{18,... | collective-permute-start | bytes 1966088 | tf_op jit(solution)/shard_map/ppermute | solution.py:351
  6.0 0.8 %copy-start.4 = (f32[2,4,160,128]{3,2,1,0:T(8,128)}, f32[2,4,160,128]{3,2,1,0:T(8,128)S(1)}, u32[]{:S(2)}) copy-start(f32[2,4,160,128]{3,2,1,0:T(8,128)S(1)} %near_states.1.own_ref) | copy-start | bytes 1966084
  6.3 0.8 %copy-start.8 = (f32[2,4,160,128]{3,2,1,0:T(8,128)}, f32[2,4,160,128]{3,2,1,0:T(8,128)S(1)}, u32[]{:S(2)}) copy-start(f32[2,4,160,128]{3,2,1,0:T(8,128)S(1)} %collective-permute-done.other_ref) | copy-start | bytes 1966084
  6.4 24.1 %copy-start.10 = (f32[2,4,160,128]{3,2,1,0:T(8,128)}, f32[2,4,160,128]{3,2,1,0:T(8,128)S(1)}, u32[]{:S(2)}) copy-start(f32[2,4,160,128]{3,2,1,0:T(8,128)S(1)} %get-tuple-element.28.chip_ref) | copy-start | bytes 1966084
  6.4 22.3 %copy-start.22 = (bf16[4,64,160]{2,1,0:T(8,128)(2,1)S(1)}, bf16[4,64,160]{2,1,0:T(8,128)(2,1)}, u32[]{:S(2)}) copy-start(bf16[4,64,160]{2,1,0:T(8,128)(2,1)} %constant.16.clone.e1_ref) | copy-start | bytes 245764
  6.4 22.3 %copy-start.23 = (bf16[4,64,160]{2,1,0:T(8,128)(2,1)S(1)}, bf16[4,64,160]{2,1,0:T(8,128)(2,1)}, u32[]{:S(2)}) copy-start(bf16[4,64,160]{2,1,0:T(8,128)(2,1)} %constant.17.clone.e2_ref) | copy-start | bytes 245764
  6.4 22.3 %copy-start.26 = (f32[8,160]{1,0:T(8,128)S(1)}, f32[8,160]{1,0:T(8,128)}, u32[]{:S(2)}) copy-start(f32[8,160]{1,0:T(8,128)} %constant.18.clone.add_ref) | copy-start | bytes 15364
  7.1 8.3 %collective-permute-start.1 = (bf16[4,200,128]{2,1,0:T(8,128)(2,1)S(1)}, bf16[4,200,128]{2,1,0:T(8,128)(2,1)S(1)}, u32[]{:S(2)}, u32[]{:S(2)}) collective-permute-start(bf16[4,200,128]{2,1,0:T(8,128)(2,1)S(1)} %get-tuple-element.29.after_ref), channel_id=1, source_target_pairs={{0,4},{2,6},{4,0},{6,2},{8,12},{10,14},{12,8},{14,10},{16,20},{18,... | collective-permute-start | bytes 614408 | tf_op jit(solution)/shard_map/ppermute | solution.py:351
  12.8 1.3 %copy-start = (f32[16,256,128]{2,1,0:T(8,128)}, f32[16,256,128]{2,1,0:T(8,128)S(1)}, u32[]{:S(2)}) copy-start(f32[16,256,128]{2,1,0:T(8,128)S(1)} %get-tuple-element.39.num_ref) | copy-start | bytes 6291460
  14.1 10.4 %copy-start.6 = (f32[4,256,128]{2,1,0:T(8,128)}, f32[4,256,128]{2,1,0:T(8,128)S(1)}, u32[]{:S(2)}) copy-start(f32[4,256,128]{2,1,0:T(8,128)S(1)} %get-tuple-element.30.rest_0_.den_ref) | copy-start | bytes 1572868
  15.4 9.1 %copy-start.17 = (bf16[4,200,128]{2,1,0:T(8,128)(2,1)}, bf16[4,200,128]{2,1,0:T(8,128)(2,1)S(1)}, u32[]{:S(2)}) copy-start(bf16[4,200,128]{2,1,0:T(8,128)(2,1)S(1)} %collective-permute-done.1.got_ref.pair_ref) | copy-start | bytes 614404
  15.5 16.4 %collective-permute-start.2 = (bf16[4,200,128]{2,1,0:T(8,128)(2,1)S(1)}, bf16[4,200,128]{2,1,0:T(8,128)(2,1)S(1)}, u32[]{:S(2)}, u32[]{:S(2)}) collective-permute-start(bf16[4,200,128]{2,1,0:T(8,128)(2,1)S(1)} %get-tuple-element.31.after_ref), channel_id=1, source_target_pairs={{0,8},{2,10},{4,12},{6,14},{8,16},{10,18},{12,20},{14,22},{16,24},... | collective-permute-start | bytes 614408 | tf_op jit(solution)/shard_map/ppermute | solution.py:351
  20.9 17.2 %collective-permute-start.4 = (bf16[64,16,128]{2,1,0:T(8,128)(2,1)}, bf16[64,16,128]{2,1,0:T(8,128)(2,1)}, u32[]{:S(2)}, u32[]{:S(2)}) collective-permute-start(bf16[64,16,128]{2,1,0:T(8,128)(2,1)} %slice.6), channel_id=1, source_target_pairs={{0,2},{2,4},{4,6},{6,8},{8,10},{10,12},{12,14},{14,16},{16,18},{18... | collective-permute-start | bytes 786440 | tf_op jit(solution)/shard_map/ppermute | solution.py:351
  24.5 13.5 %collective-permute-start.5 = (bf16[64,16,128]{2,1,0:T(8,128)(2,1)}, bf16[64,16,128]{2,1,0:T(8,128)(2,1)}, u32[]{:S(2)}, u32[]{:S(2)}) collective-permute-start(bf16[64,16,128]{2,1,0:T(8,128)(2,1)} %slice.7), channel_id=1, source_target_pairs={{0,2},{2,4},{4,6},{6,8},{8,10},{10,12},{12,14},{14,16},{16,18},{18... | collective-permute-start | bytes 786440 | tf_op jit(solution)/shard_map/ppermute | solution.py:351
  30.5 1.4 %copy-start.2 = (bf16[16,256,160]{2,1,0:T(8,128)(2,1)}, bf16[16,256,160]{2,1,0:T(8,128)(2,1)S(1)}, u32[]{:S(2)}) copy-start(bf16[16,256,160]{2,1,0:T(8,128)(2,1)S(1)} %get-tuple-element.38.low_ref) | copy-start | bytes 3932164
  32.8 0.7 %copy-start.15 = (bf16[4,200,128]{2,1,0:T(8,128)(2,1)}, bf16[4,200,128]{2,1,0:T(8,128)(2,1)S(1)}, u32[]{:S(2)}) copy-start(bf16[4,200,128]{2,1,0:T(8,128)(2,1)S(1)} %collective-permute-done.2.got_ref.rest_0_) | copy-start | bytes 614404
  33.5 12.3 %collective-permute-start.3 = (bf16[4,200,128]{2,1,0:T(8,128)(2,1)}, bf16[4,200,128]{2,1,0:T(8,128)(2,1)}, u32[]{:S(2)}, u32[]{:S(2)}) collective-permute-start(bf16[4,200,128]{2,1,0:T(8,128)(2,1)} %get-tuple-element.34.after_ref), channel_id=1, source_target_pairs={{0,16},{2,18},{4,20},{6,22},{8,24},{10,26},{12,28},{14,30},{1,17},... | collective-permute-start | bytes 614408 | tf_op jit(solution)/shard_map/ppermute | solution.py:351
  38.0 1.2 %copy-start.13 = (bf16[256,16,128]{2,1,0:T(8,128)(2,1)S(1)}, bf16[256,16,128]{2,1,0:T(8,128)(2,1)}, u32[]{:S(2)}) copy-start(bf16[256,16,128]{2,1,0:T(8,128)(2,1)} %wk_ref.1) | copy-start | bytes 3145732
  39.3 1.2 %copy-start.14 = (bf16[256,16,128]{2,1,0:T(8,128)(2,1)S(1)}, bf16[256,16,128]{2,1,0:T(8,128)(2,1)}, u32[]{:S(2)}) copy-start(bf16[256,16,128]{2,1,0:T(8,128)(2,1)} %wq_ref.1) | copy-start | bytes 3145732
  40.5 5.3 %copy-start.11 = (f32[2,4,160,128]{3,2,1,0:T(8,128)S(1)}, f32[2,4,160,128]{3,2,1,0:T(8,128)}, u32[]{:S(2)}) copy-start(f32[2,4,160,128]{3,2,1,0:T(8,128)} %copy-done.10) | copy-start | bytes 1966084
  40.5 5.3 %copy-start.16 = (bf16[4,200,128]{2,1,0:T(8,128)(2,1)S(1)}, bf16[4,200,128]{2,1,0:T(8,128)(2,1)}, u32[]{:S(2)}) copy-start(bf16[4,200,128]{2,1,0:T(8,128)(2,1)} %copy-done.15) | copy-start | bytes 614404
  40.5 5.3 %copy-start.18 = (bf16[4,200,128]{2,1,0:T(8,128)(2,1)S(1)}, bf16[4,200,128]{2,1,0:T(8,128)(2,1)}, u32[]{:S(2)}) copy-start(bf16[4,200,128]{2,1,0:T(8,128)(2,1)} %copy-done.17) | copy-start | bytes 614404
  40.5 13.3 %copy-start.5 = (f32[2,4,160,128]{3,2,1,0:T(8,128)S(1)}, f32[2,4,160,128]{3,2,1,0:T(8,128)}, u32[]{:S(2)}) copy-start(f32[2,4,160,128]{3,2,1,0:T(8,128)} %copy-done.4) | copy-start | bytes 1966084
  40.5 13.3 %copy-start.9 = (f32[2,4,160,128]{3,2,1,0:T(8,128)S(1)}, f32[2,4,160,128]{3,2,1,0:T(8,128)}, u32[]{:S(2)}) copy-start(f32[2,4,160,128]{3,2,1,0:T(8,128)} %copy-done.8) | copy-start | bytes 1966084
  45.8 8.9 %copy-start.1 = (f32[16,256,128]{2,1,0:T(8,128)S(1)}, f32[16,256,128]{2,1,0:T(8,128)}, u32[]{:S(2)}) copy-start(f32[16,256,128]{2,1,0:T(8,128)} %copy-done) | copy-start | bytes 6291460
  45.8 8.9 %copy-start.3 = (bf16[16,256,160]{2,1,0:T(8,128)(2,1)S(1)}, bf16[16,256,160]{2,1,0:T(8,128)(2,1)}, u32[]{:S(2)}) copy-start(bf16[16,256,160]{2,1,0:T(8,128)(2,1)} %copy-done.2) | copy-start | bytes 3932164
  45.8 8.9 %copy-start.7 = (f32[4,256,128]{2,1,0:T(8,128)S(1)}, f32[4,256,128]{2,1,0:T(8,128)}, u32[]{:S(2)}) copy-start(f32[4,256,128]{2,1,0:T(8,128)} %copy-done.6) | copy-start | bytes 1572868
  47.0 6.8 %collective-permute-start.6 = (bf16[4,200,128]{2,1,0:T(8,128)(2,1)S(1)}, bf16[4,200,128]{2,1,0:T(8,128)(2,1)S(1)}, u32[]{:S(2)}, u32[]{:S(2)}) collective-permute-start(bf16[4,200,128]{2,1,0:T(8,128)(2,1)S(1)} %get-tuple-element.36), channel_id=1, source_target_pairs={{0,4},{2,6},{4,0},{6,2},{8,12},{10,14},{12,8},{14,10},{16,20},{18,... | collective-permute-start | bytes 614408 | tf_op jit(solution)/shard_map/ppermute | solution.py:351
  54.5 2.9 %collective-permute-start.7 = (f32[2,4,160,128]{3,2,1,0:T(8,128)S(1)}, f32[2,4,160,128]{3,2,1,0:T(8,128)S(1)}, u32[]{:S(2)}, u32[]{:S(2)}) collective-permute-start(f32[2,4,160,128]{3,2,1,0:T(8,128)S(1)} %get-tuple-element.40.rest_0_), channel_id=1, source_target_pairs={{0,2},{2,0},{4,6},{6,4},{8,10},{10,8},{12,14},{14,12},{16,18},{18,... | collective-permute-start | bytes 1966088 | tf_op jit(solution)/shard_map/ppermute | solution.py:351
  57.5 6.6 %copy-start.25 = (s32[2]{0:T(128)S(1)}, s32[2]{0:T(128)}, u32[]{:S(2)}) copy-start(s32[2]{0:T(128)} %copy-done.24) | copy-start | bytes 28
  57.5 6.6 %copy-start.27 = (bf16[16,128]{1,0:T(8,128)(2,1)S(1)}, bf16[16,128]{1,0:T(8,128)(2,1)}, u32[]{:S(2)}) copy-start(bf16[16,128]{1,0:T(8,128)(2,1)} %gain_ref.1) | copy-start | bytes 12292
  60.4 3.7 %collective-permute-start.8 = (f32[8,256]{1,0:T(8,128)S(1)}, f32[8,256]{1,0:T(8,128)S(1)}, u32[]{:S(2)}, u32[]{:S(2)}) collective-permute-start(f32[8,256]{1,0:T(8,128)S(1)} %get-tuple-element.44.sq_ref), channel_id=1, source_target_pairs={{0,1},{1,0},{2,3},{3,2},{4,5},{5,4},{6,7},{7,6},{8,9},{9,8},{10,11... | collective-permute-start | bytes 24584 | tf_op jit(solution)/shard_map/ppermute | solution.py:422

commit v3 on v2

v3 whole, which is shorter than its diff:
```python
import functools
import math

import jax
import jax.numpy as jnp
import numpy as np
from jax import lax
from jax.experimental import pallas as pl
from jax.experimental.pallas import tpu as pltpu
from jax.sharding import PartitionSpec as P

HEADS = 32
DV = 128
DK = 16
WINDOW = 64
NORM_EPS = 1e-06

ROWS = 160
TOTAL_ROW = 33
WIDE = 40
SENT = ROWS + WIDE

F32 = jnp.float32
BF16 = jnp.bfloat16
NN = (((1,), (0,)), ((), ()))
NT = (((1,), (1,)), ((), ()))


def pair_tables(heads):
    first = np.zeros((DK, ROWS), np.float32)
    second = np.zeros((DK, ROWS), np.float32)
    add = np.zeros((8, ROWS), np.float32)
    for i in range(DK):
        first[i, i] = 1.0 / 32.0
        second[i, i] = 1.0
        first[i, DK + i] = 0.25
        add[1, DK + i] = 1.0
        for d in range(1, 8):
            row = WIDE + DK * (d - 1) + i
            first[i, row] = 1.0 / 16.0
            second[(i + d) % DK, row] = 1.0
    for i in range(8):
        first[i, 152 + i] = 1.0 / 16.0
        second[i + 8, 152 + i] = 1.0
    add[0, 2 * DK] = 1.0
    add[1, 2 * DK] = 1.0
    both = []
    for one in (first, second):
        table = np.zeros((heads, heads * DK, ROWS), np.float32)
        for j in range(heads):
            table[j, j * DK : (j + 1) * DK] = one
        both.append(jnp.asarray(table, BF16))
    return both[0], both[1], jnp.asarray(add, F32)


def dot(a, b, dims=NN):
    return lax.dot_general(a, b, dims, preferred_element_type=F32)


def split(x):
    high = x.astype(BF16)
    return high, (x - high.astype(F32)).astype(BF16)


def pack(ref, x):
    high = x.astype(BF16)
    ref[:ROWS] = high
    ref[ROWS:] = (x[:WIDE] - high[:WIDE].astype(F32)).astype(BF16)


def unpack(got):
    wide = got[:WIDE].astype(F32) + got[ROWS:].astype(F32)
    return jnp.concatenate([wide, got[WIDE:ROWS].astype(F32)], axis=0)


VMEM_SPEC = pl.BlockSpec(memory_space=pltpu.VMEM)
SMEM_SPEC = pl.BlockSpec(memory_space=pltpu.SMEM)
VMEM_LIMIT = 12 << 20


def call(body, name, outs, *operands, scalars=0, scratch=(), raw=False, aliases=None):
    held = [
        x if i < scalars else pltpu.with_memory_space_constraint(x, pltpu.HBM if raw else pltpu.VMEM)
        for i, x in enumerate(operands)
    ]
    many = isinstance(outs, tuple)
    spec = pl.BlockSpec(memory_space=pltpu.HBM) if raw else VMEM_SPEC
    return pl.pallas_call(
        body,
        out_shape=outs,
        in_specs=[SMEM_SPEC] * scalars + [spec] * (len(operands) - scalars),
        out_specs=tuple(VMEM_SPEC for _ in outs) if many else VMEM_SPEC,
        scratch_shapes=list(scratch),
        input_output_aliases=aliases or {},
        compiler_params=pltpu.CompilerParams(vmem_limit_bytes=VMEM_LIMIT),
        name=name,
    )(*held)


def one_state(x, v):
    toks = x.shape[1]
    ones = jnp.where(lax.broadcasted_iota(jnp.int32, (8, toks), 0) == 0, 1.0, 0.0).astype(F32)
    parts = [x * x, x, ones]
    for d in range(1, 8):
        parts.append(x * pltpu.roll(x, DK - d, 0))
    parts.append(x[:8] * x[8:])
    high, low = split(jnp.concatenate(parts, axis=0))
    full = jnp.ones((8, toks), BF16)
    total = dot(full, high, NT) + dot(full, low, NT)
    return dot(high, v) + dot(low, v), total


def put_states(out_ref, place_ref, far, other, kt_ref, vh_ref):
    part = out_ref.shape[0]
    half = place_ref[0] if far == 0 else 1 - place_ref[0]
    mid = place_ref[1] if other == 0 else 1 - place_ref[1]
    base = (half * 2 + mid) * part
    for j in range(part):
        x = kt_ref[pl.ds(pl.multiple_of((base + j) * DK, DK), DK), :]
        state, total = one_state(x, vh_ref[base + j])
        out_ref[j] = state
        out_ref[j, TOTAL_ROW : TOTAL_ROW + 1, :] = total[:1, :128]
        out_ref[j, TOTAL_ROW + 1 : TOTAL_ROW + 2, : ROWS - 128] = total[:1, 128:]


def rim_kernel(wk_ref, v_ref, rim_ref, sems):
    rows = pl.ds(wk_ref.shape[0] - WINDOW, WINDOW)
    copies = [
        pltpu.make_async_copy(ref.at[rows], rim_ref.at[i], sems.at[i])
        for i, ref in enumerate((wk_ref, v_ref))
    ]
    for copy in copies:
        copy.start()
    for copy in copies:
        copy.wait()


def first_states_kernel(place_ref, keys_ref, v_ref, after_ref, out_ref, vh_ref, kt_ref):
    vh_ref[...] = jnp.swapaxes(v_ref[...], 0, 1)
    kt_ref[...] = jnp.transpose(keys_ref[...].astype(F32), (1, 0))
    put_states(out_ref, place_ref, 1, 1, kt_ref, vh_ref)


def states_kernel(far, other, place_ref, kt_ref, vh_ref, after_ref, out_ref):
    put_states(out_ref, place_ref, far, other, kt_ref, vh_ref)


def chip_kernel(own_ref, other_ref, msg_ref):
    for j in range(own_ref.shape[0]):
        pack(msg_ref.at[j], own_ref[j] + other_ref[j])


def plane_kernel(own_ref, other_ref, got_ref, after_ref, sum_ref, msg_ref):
    for j in range(sum_ref.shape[0]):
        total = own_ref[j] + other_ref[j] + unpack(got_ref[j])
        sum_ref[j] = total
        pack(msg_ref.at[j], total)


def add_kernel(base_ref, got_ref, *rest):
    sum_ref, msg_ref = rest[-2:]
    for j in range(sum_ref.shape[0]):
        total = base_ref[j] + unpack(got_ref[j])
        sum_ref[j] = total
        pack(msg_ref.at[j], total)


def add_two_kernel(base_ref, got_ref, early_ref, *rest):
    sum_ref, msg_ref = rest[-2:]
    for j in range(sum_ref.shape[0]):
        total = base_ref[j] + (unpack(got_ref[j]) + unpack(early_ref[j]))
        sum_ref[j] = total
        pack(msg_ref.at[j], total)


def before_kernel(count, place_ref, own_ref, other_ref, pair_ref, *rest):
    gots, (prior_ref, send_ref, msg_ref) = rest[:count], rest[-3:]
    low, mid = place_ref[0], place_ref[1]
    for j in range(prior_ref.shape[0]):
        before = unpack(gots[0][j])
        for got in gots[1:]:
            before = before + unpack(got[j])
        own, other = own_ref[j], other_ref[j]
        mine = before + jnp.where(mid == 1, unpack(pair_ref[j]), 0.0)
        pack(msg_ref.at[j], before + jnp.where(mid == 0, own + other, 0.0))
        send_ref[j] = mine + jnp.where(low == 0, own, 0.0)
        prior_ref[j] = mine + jnp.where(low == 1, other, 0.0)


def rest_kernel(place_ref, got_ref, own_ref, other_ref, after_ref, prior_ref, send_ref):
    low = place_ref[0]
    for j in range(prior_ref.shape[0]):
        mine = unpack(got_ref[j])
        send_ref[j] = mine + jnp.where(low == 0, own_ref[j], 0.0)
        prior_ref[j] = mine + jnp.where(low == 1, other_ref[j], 0.0)


def phi_kernel(q_ref, e1_ref, e2_ref, add_ref, gain_ref, after_ref,
               high_ref, low_ref, gain_out_ref, q4_ref):
    for h in range(gain_ref.shape[0]):
        gain_out_ref[h] = gain_ref[h : h + 1].astype(F32)
    part = e1_ref.shape[0]
    width = part * DK
    for r in range(4):
        q4_ref[r] = q_ref[:, r * width : (r + 1) * width]

    def one(r, carry):
        q = q4_ref[r]
        for j in range(part):
            a = dot(q, e1_ref[j]) + add_ref[0:1]
            b = dot(q, e2_ref[j]) + add_ref[1:2]
            high, low = split(a * b)
            high_ref[r * part + j] = high
            low_ref[r * part + j] = low
        return carry

    lax.fori_loop(0, 4, one, 0)


def intra_kernel(q_ref, k_ref, vh_ref, after_ref, num_ref, den_ref, q4_ref, k4_ref):
    heads, toks, dim = vh_ref.shape
    part = heads // 4
    width = part * DK
    half = toks // 2
    for r in range(4):
        q4_ref[r] = q_ref[:, r * width : (r + 1) * width]
        k4_ref[r] = k_ref[:, r * width : (r + 1) * width]
    row = lax.broadcasted_iota(jnp.int32, (half, half), 0)
    col = lax.broadcasted_iota(jnp.int32, (half, half), 1)
    tri = col <= row
    lane = lax.broadcasted_iota(jnp.int32, (toks, width), 1) // DK
    ones = jnp.ones((toks, dim), BF16)

    def poly(s):
        return 1.0 + s * 0.25 + s * s * (1.0 / 32.0)

    def one(r, carry):
        q, k = q4_ref[r], k4_ref[r]
        tops, lows, rights = [], [], []
        for j in range(part):
            own = jnp.where(lane == j, q, jnp.zeros_like(q))
            tops.append(dot(own[:half], k[:half], NT))
            lows.append(dot(own[half:], k, NT))
        for j in range(part):
            head = r * part + j
            v = jnp.concatenate([vh_ref[head], ones], axis=1)
            top = jnp.where(tri, poly(tops[j]), 0.0)
            left = poly(lows[j][:, :half])
            right = jnp.where(tri, poly(lows[j][:, half:]), 0.0)
            high, low = split(top)
            both = dot(high, v[:half]) + dot(low, v[:half])
            num_ref[head, :half] = both[:, :dim]
            den_ref[head, :half] = both[:, dim:]
            high, low = split(jnp.concatenate([left, right], axis=1))
            both = dot(high, v) + dot(low, v)
            num_ref[head, half:] = both[:, :dim]
            den_ref[head, half:] = both[:, dim:]
        return carry

    lax.fori_loop(0, 4, one, 0)


def window_kernel(place_ref, wq_ref, wk_ref, vh_ref, rim_ref, after_ref,
                  win_ref, qh_ref, kh_ref, ve_ref):
    heads, toks, dim = vh_ref.shape
    part = heads // 4
    qh_ref[...] = jnp.swapaxes(wq_ref[...], 0, 1)
    kh_ref[:, :WINDOW] = jnp.swapaxes(rim_ref[0], 0, 1)
    kh_ref[:, WINDOW:] = jnp.swapaxes(wk_ref[...], 0, 1)
    ve_ref[:, :WINDOW] = jnp.swapaxes(rim_ref[1], 0, 1)
    ve_ref[:, WINDOW:] = vh_ref[...]
    row = lax.broadcasted_iota(jnp.int32, (WINDOW, 2 * WINDOW), 0)
    col = lax.broadcasted_iota(jnp.int32, (WINDOW, 2 * WINDOW), 1)
    band = (col > row) & (col <= row + WINDOW)
    edge = band & ((col >= WINDOW) | (place_ref[2] > 0))
    blocks = toks // WINDOW

    def one(r, carry):
        scores = []
        for j in range(part):
            head = r * part + j
            for b in range(blocks):
                lo = b * WINDOW
                sc = dot(qh_ref[head, lo : lo + WINDOW], kh_ref[head, lo : lo + 2 * WINDOW], NT)
                scores.append(jnp.where(edge if b == 0 else band, sc / math.sqrt(dim), -1e30))
        sc = jnp.concatenate(scores, axis=0)
        expo = jnp.exp(sc - jnp.max(sc, axis=1, keepdims=True))
        weights = (expo / jnp.sum(expo, axis=1, keepdims=True)).astype(BF16)
        for j in range(part):
            head = r * part + j
            for b in range(blocks):
                lo = b * WINDOW
                at = (j * blocks + b) * WINDOW
                win_ref[head, lo : lo + WINDOW] = dot(
                    weights[at : at + WINDOW], ve_ref[head, lo : lo + 2 * WINDOW]
                )
        return carry

    lax.fori_loop(0, 4, one, 0)


def final_kernel(far, other, stage, place_ref, prior_ref, high_ref, low_ref, num_ref, den_ref,
                 win_ref, gain_ref, *rest):
    mixed_ref, sq_ref = rest[-2:]
    part = prior_ref.shape[0]
    toks, dim = num_ref.shape[1:]
    half = place_ref[0] if far == 0 else 1 - place_ref[0]
    mid = place_ref[1] if other == 0 else 1 - place_ref[1]
    base = (half * 2 + mid) * part
    squares = jnp.zeros((toks, dim), F32) if stage == 0 else rest[1][...]
    for j in range(part):
        head = base + j
        prior = prior_ref[j]
        phi_high, phi_low = high_ref[head], low_ref[head]
        high, low = split(prior)
        both = dot(phi_high, jnp.concatenate([high, low], axis=1))
        numer = num_ref[head] + ((both[:, dim:] + dot(phi_low, high)) + both[:, :dim])
        total = jnp.concatenate(
            [prior[TOTAL_ROW : TOTAL_ROW + 1], prior[TOTAL_ROW + 1 : TOTAL_ROW + 2, : ROWS - 128]],
            axis=1,
        )
        t_high, t_low = split(jnp.broadcast_to(total, (dim, ROWS)))
        both = dot(phi_high, jnp.concatenate([t_high, t_low], axis=0), NT)
        denom = den_ref[head] + ((both[:, dim:] + dot(phi_low, t_high, NT)) + both[:, :dim])
        mixed = numer / denom + win_ref[head]
        mixed_ref[head] = mixed * gain_ref[head]
        squares = squares + mixed * mixed
    if stage < 3:
        sq_ref[...] = squares
    else:
        sq_ref[...] = lax.dot_general(
            jnp.ones((8, dim), F32), squares, NT,
            precision=lax.Precision.HIGHEST, preferred_element_type=F32,
        )


def norm_kernel(peers, mixed_ref, sq_ref, *rest):
    out_ref = rest[-1]
    total = sq_ref[...]
    for got in rest[:peers]:
        total = total + got[...]
    scale = lax.rsqrt(total / (HEADS * DV) + NORM_EPS)
    column = jnp.transpose(scale, (1, 0))[:, :1]
    wide = jnp.broadcast_to(column, mixed_ref.shape[1:])
    out_ref[...] = jnp.swapaxes((mixed_ref[...] * wide[None]).astype(BF16), 0, 1)


def on_device(queries, keys, values, win_q, win_k, gain):
    toks, heads, dim = values.shape
    count = lax.axis_size("ctx")
    peers = lax.axis_size("head") - 1
    where = lax.axis_index("ctx")
    place = jnp.stack([where & 1, (where >> 1) & 1, where]).astype(jnp.int32)
    part = heads // 4
    core_swap = [(i, i ^ 1) for i in range(count)]
    pair_swap = [(i, i ^ 2) for i in range(count)]
    state_shape = pltpu.VMEM((part, ROWS, dim), F32)
    msg_shape = pltpu.VMEM((part, SENT, dim), BF16)
    head_wide = pltpu.VMEM((heads, toks, dim), F32)

    def permute(x, pairs):
        return lax.ppermute(x, "ctx", pairs)

    rim = call(
        rim_kernel, "rim", pltpu.VMEM((2, WINDOW, heads, dim), BF16), win_k, values,
        raw=True, scratch=[pltpu.SemaphoreType.DMA((2,))],
    )
    rim_prev = permute(rim, [(i, i + 1) for i in range(count - 1)])

    far1, values_h, keys_t = call(
        first_states_kernel, "far1",
        (state_shape, pltpu.VMEM((heads, toks, dim), BF16), pltpu.VMEM((heads * DK, toks), F32)),
        place, keys, values, rim, scalars=1,
    )
    other1 = permute(far1, core_swap)

    def states(name, far, other, after):
        return call(functools.partial(states_kernel, far, other), name, state_shape,
                    place, keys_t, values_h, after, scalars=1)

    far0 = states("far0", 1, 0, far1)
    other0 = permute(far0, core_swap)
    near1 = states("near1", 0, 1, far0)
    msg = call(chip_kernel, "chip", msg_shape, near1, other1)
    pair = permute(msg, pair_swap)
    near0 = states("near0", 0, 0, msg)
    num, den = call(
        intra_kernel, "intra", (head_wide, head_wide), queries, keys, values_h, near0,
        scratch=[pltpu.VMEM((4, toks, part * DK), BF16)] * 2,
    )
    inclusive, msg = call(
        plane_kernel, "plane", (state_shape, msg_shape), near0, other0, pair, den
    )

    first_table, second_table, add_table = pair_tables(part)
    groups = count // 4
    gots = []
    start = msg
    step = 1
    phi_high = phi_low = win = None
    early = {}
    while step < groups:
        if step == 1:
            got = [permute(msg, [(i, i + 4) for i in range(count - 4)])]
            far_step = 2
            while far_step < groups:
                early[far_step] = permute(start, [(i, i + 4 * far_step) for i in range(4)])
                far_step *= 2
            phi_high, phi_low, gain = call(
                phi_kernel, "phi",
                (pltpu.VMEM((heads, toks, ROWS), BF16),) * 2 + (pltpu.VMEM((heads, 1, dim), F32),),
                queries, first_table, second_table, add_table, gain, msg,
                scratch=[pltpu.VMEM((4, toks, part * DK), BF16)],
            )
        else:
            got = [permute(msg, [(i, i + 4 * step) for i in range(4, count - 4 * step)]), early[step]]
        if step == 2:
            win = call(
                window_kernel, "window", head_wide,
                place, win_q, win_k, values_h, rim_prev, msg, scalars=1,
                scratch=[
                    pltpu.VMEM((heads, toks, dim), BF16),
                    pltpu.VMEM((heads, toks + WINDOW, dim), BF16),
                    pltpu.VMEM((heads, toks + WINDOW, dim), BF16),
                ],
            )
        gots.extend(got)
        step *= 2
        if step < groups:
            body = add_kernel if len(got) == 1 else add_two_kernel
            inclusive, msg = call(body, "add", (state_shape, msg_shape), inclusive, *got, phi_high)
    prior, send, msg = call(
        functools.partial(before_kernel, len(gots)), "before",
        (state_shape, state_shape, msg_shape),
        place, near0, other0, pair, *gots, win, scalars=1,
    )
    got = permute(msg, pair_swap)
    far_prior = permute(send, core_swap)

    def final(name, far, other, stage, prior, *held):
        last = pltpu.VMEM((8, toks) if stage == 3 else (toks, dim), F32)
        return call(
            functools.partial(final_kernel, far, other, stage), name, (head_wide, last),
            place, prior, phi_high, phi_low, num, den, win, gain, *held, scalars=1,
            aliases={8: 0} if stage else None,
        )

    mixed, squares = final("final0", 0, 0, 0, prior, msg)
    mixed, squares = final("final1", 1, 0, 1, far_prior, mixed, squares)
    prior, send = call(rest_kernel, "rest", (state_shape, state_shape),
                       place, got, near1, other1, squares, scalars=1)
    far_prior = permute(send, core_swap)
    mixed, squares = final("final2", 0, 1, 2, prior, mixed, squares)
    mixed, squares = final("final3", 1, 1, 3, far_prior, mixed, squares)
    others = [
        lax.ppermute(squares, "head", [(i, (i + k) % (peers + 1)) for i in range(peers + 1)])
        for k in range(1, peers + 1)
    ]
    return call(
        functools.partial(norm_kernel, peers), "norm",
        jax.ShapeDtypeStruct((toks, heads, dim), BF16),
        mixed, squares, *others,
    )


def solution(mesh):
    return jax.shard_map(
        on_device,
        mesh=mesh,
        in_specs=(
            P("ctx", "head"),
            P("ctx", "head"),
            P("ctx", "head", None),
            P("ctx", "head", None),
            P("ctx", "head", None),
            P("head", None),
        ),
        out_specs=P("ctx", "head", None),
        check_vma=False,
    )
```

time: 66.6 us -> 51.1 us (0.77)
  the two profiles are of different devices: /device:TPU:0 before, /device:TPU:22 now
where the time goes in v3:
time: 51.1 us; the launch traced here: 50.9 us
  Pallas kernels  23.7 us (46%)
  starting transfers between devices  13.9 us (27%)
  waiting for transfers between devices  12.7 us (25%)
    pallas_call x18, Pallas kernels, call(): pl.pallas_call(body, out_shape=outs, in_specs=[SMEM_SPEC] * scalars + [sp...  23.7 us
    ppermute x10, starting transfers between devices, permute(): return lax.ppermute(x, 'ctx', pairs)  13.3 us
    ppermute x10, waiting for transfers between devices, permute(): return lax.ppermute(x, 'ctx', pairs)  9.53 us
    ppermute x1, waiting for transfers between devices, on_device(): lax.ppermute(squares, 'head', [(i, (i + k) % (peers + 1)) for i in range(...  3.12 us
  transfers between devices with their start and end apart: 11, of which 5 were waited for; matrix products, arithmetic and copies ran while one was open for 0% of the time, Pallas kernels for 33%

profile of v3, /device:TPU:22, one launch (start us, length us, event | category | flops | bytes accessed | tf_op | source)
XLA Modules:
  0.0 50.9 jit_solution(1207950420455799064)
XLA Ops:
  0.0 0.0 copy-start
  0.0 0.0 copy-start.3
  0.0 1.1 %rim.1.after_ref = bf16[2,64,16,128]{3,2,1,0:T(8,128)(2,1)S(1)} custom-call(bf16[256,16,128]{2,1,0:T(8,128)(2,1)} %wk_ref.3, bf16[256,16,128]{2,1,0:T(8,128)(2,1)} %v_ref.3), custom_call_target="tpu_custom_call" | custom-call | tf_op jit(solution)/shard_map/rim/pallas_call | solution.py:88
  1.2 0.1 pad_add_fusion.place_ref
  1.2 0.1 copy-done
  1.4 0.0 copy-done.3
  1.4 1.4 %far1.1 = (f32[4,160,128]{2,1,0:T(8,128)S(1)}, bf16[16,256,128]{2,1,0:T(8,128)(2,1)S(1)}, f32[256,256]{1,0:T(8,128)S(1)}) custom-call(s32[3]{0:T(128)S(1)} %pad_add_fusion.place_ref, bf16[256,256]{1,0:T(8,128)(2,1)S(1)} %copy-done.3, bf16[256,16,128]{2,1,0:T(8,128)(2,1)S(1)} %copy-done, bf16[2,64,16,128]{3,2,1,0:T(8,128)(2,1)S(1)} %rim.1.after_ref), custom_call_target="tpu_custom_call" | custom-call | tf_op jit(solution)/shard_map/far1/pallas_call | solution.py:88
  2.8 0.1 collective-permute-start
  2.8 1.0 %far0.1.after_ref = f32[4,160,128]{2,1,0:T(8,128)S(1)} custom-call(s32[3]{0:T(128)S(1)} %pad_add_fusion.place_ref, f32[256,256]{1,0:T(8,128)S(1)} %get-tuple-element.29.kt_ref, bf16[16,256,128]{2,1,0:T(8,128)(2,1)S(1)} %get-tuple-element.30.vh_ref, f32[4,160,128]{2,1,0:T(8,128)S(1)} %get-tuple-element.31.after_ref), custom_call_target="tpu_custom_call" | custom-call | tf_op jit(solution)/shard_map/far0/pallas_call | solution.py:88
  3.8 0.0 copy-start.4
  3.8 0.6 %collective-permute-start.1 = (f32[4,160,128]{2,1,0:T(8,128)S(1)}, f32[4,160,128]{2,1,0:T(8,128)S(1)}, u32[]{:S(2)}, u32[]{:S(2)}) collective-permute-start(f32[4,160,128]{2,1,0:T(8,128)S(1)} %far0.1.after_ref), channel_id=1, source_target_pairs={{0,2},{2,0},{4,6},{6,4},{8,10},{10,8},{12,14},{14,12},{16,18},{18,... | collective-permute-start | bytes 983048 | tf_op jit(solution)/shard_map/ppermute | solution.py:362
  4.4 1.0 %near1.1.own_ref = f32[4,160,128]{2,1,0:T(8,128)S(1)} custom-call(s32[3]{0:T(128)S(1)} %pad_add_fusion.place_ref, f32[256,256]{1,0:T(8,128)S(1)} %get-tuple-element.29.kt_ref, bf16[16,256,128]{2,1,0:T(8,128)(2,1)S(1)} %get-tuple-element.30.vh_ref, f32[4,160,128]{2,1,0:T(8,128)S(1)} %far0.1.after_ref), custom_call_target="tpu_custom_call" | custom-call | tf_op jit(solution)/shard_map/near1/pallas_call | solution.py:88
  5.4 0.0 collective-permute-done.other_ref
  5.4 0.6 %collective-permute-start.2 = (bf16[4,200,128]{2,1,0:T(8,128)(2,1)S(1)}, bf16[4,200,128]{2,1,0:T(8,128)(2,1)S(1)}, u32[]{:S(2)}, u32[]{:S(2)}) collective-permute-start(bf16[4,200,128]{2,1,0:T(8,128)(2,1)S(1)} %chip.1.after_ref), channel_id=1, source_target_pairs={{0,4},{2,6},{4,0},{6,2},{8,12},{10,14},{12,8},{14,10},{16,20},{18,... | collective-permute-start | bytes 614408 | tf_op jit(solution)/shard_map/ppermute | solution.py:362
  6.0 1.9 %collective-permute-start.6 = (bf16[2,64,16,128]{3,2,1,0:T(8,128)(2,1)S(1)}, bf16[2,64,16,128]{3,2,1,0:T(8,128)(2,1)S(1)}, u32[]{:S(2)}, u32[]{:S(2)}) collective-permute-start(bf16[2,64,16,128]{3,2,1,0:T(8,128)(2,1)S(1)} %rim.1.after_ref), channel_id=1, source_target_pairs={{0,2},{2,4},{4,6},{6,8},{8,10},{10,12},{12,14},{14,16},{16,18},{18... | collective-permute-start | bytes 1572872 | tf_op jit(solution)/shard_map/ppermute | solution.py:362
  7.9 1.0 %near0.1.after_ref.own_ref = f32[4,160,128]{2,1,0:T(8,128)S(1)} custom-call(s32[3]{0:T(128)S(1)} %pad_add_fusion.place_ref, f32[256,256]{1,0:T(8,128)S(1)} %get-tuple-element.29.kt_ref, bf16[16,256,128]{2,1,0:T(8,128)(2,1)S(1)} %get-tuple-element.30.vh_ref, bf16[4,200,128]{2,1,0:T(8,128)(2,1)S(1)} %chip.1.after_ref), custom_call_target="tpu_custom_call" | custom-call | tf_op jit(solution)/shard_map/near0/pallas_call | solution.py:88
  8.9 0.0 copy-done.4
  8.9 0.0 copy-start.5
  8.9 0.0 copy-start.6
  9.0 0.0 copy-start.7
  9.0 0.0 copy-start.8
  9.0 2.8 %intra.1 = (f32[16,256,128]{2,1,0:T(8,128)S(1)}, f32[16,256,128]{2,1,0:T(8,128)S(1)}) custom-call(bf16[256,256]{1,0:T(8,128)(2,1)S(1)} %copy-done.4, bf16[256,256]{1,0:T(8,128)(2,1)S(1)} %copy-done.3, bf16[16,256,128]{2,1,0:T(8,128)(2,1)S(1)} %get-tuple-element.30.vh_ref, f32[4,160,128]{2,1,0:T(8,128)S(1)} %near0.1.after_ref.own_ref), custom_call_target="tpu_custom_call" | custom-call | tf_op jit(solution)/shard_map/intra/pallas_call | solution.py:88
  11.8 0.0 collective-permute-done.1.other_ref
  11.8 1.6 %collective-permute-done.2.got_ref.pair_ref = bf16[4,200,128]{2,1,0:T(8,128)(2,1)S(1)} collective-permute-done((bf16[4,200,128]{2,1,0:T(8,128)(2,1)S(1)}, bf16[4,200,128]{2,1,0:T(8,128)(2,1)S(1)}, u32[]{:S(2)}, u32[]{:S(2)}) %collective-permute-start.2) | collective-permute-done | bytes 204832 | tf_op jit(solution)/shard_map/ppermute | solution.py:362
  13.4 0.1 plane.1
  13.5 0.0 copy-start.1
  13.5 0.0 copy-start.2
  13.5 3.6 %collective-permute-start.3 = (bf16[4,200,128]{2,1,0:T(8,128)(2,1)S(1)}, bf16[4,200,128]{2,1,0:T(8,128)(2,1)S(1)}, u32[]{:S(2)}, u32[]{:S(2)}) collective-permute-start(bf16[4,200,128]{2,1,0:T(8,128)(2,1)S(1)} %get-tuple-element.33.after_ref), channel_id=1, source_target_pairs={{0,8},{2,10},{4,12},{6,14},{8,16},{10,18},{12,20},{14,22},{16,24},... | collective-permute-start | bytes 614408 | tf_op jit(solution)/shard_map/ppermute | solution.py:362
  17.2 1.3 %collective-permute-start.5 = (bf16[4,200,128]{2,1,0:T(8,128)(2,1)S(1)}, bf16[4,200,128]{2,1,0:T(8,128)(2,1)S(1)}, u32[]{:S(2)}, u32[]{:S(2)}) collective-permute-start(bf16[4,200,128]{2,1,0:T(8,128)(2,1)S(1)} %get-tuple-element.33.after_ref), channel_id=1, source_target_pairs={{0,16},{2,18},{4,20},{6,22},{1,17},{3,19},{5,21},{7,23}} | collective-permute-start | bytes 614408 | tf_op jit(solution)/shard_map/ppermute | solution.py:362
  18.5 0.0 copy-done.5
  18.5 0.0 copy-done.6
  18.5 0.0 copy-done.7
  18.5 0.0 copy-done.8
  18.5 1.8 %phi.1 = (bf16[16,256,160]{2,1,0:T(8,128)(2,1)S(1)}, bf16[16,256,160]{2,1,0:T(8,128)(2,1)S(1)}, f32[16,1,128]{2,1,0:T(1,128)S(1)}) custom-call(bf16[256,256]{1,0:T(8,128)(2,1)S(1)} %copy-done.4, bf16[4,64,160]{2,1,0:T(8,128)(2,1)S(1)} %copy-done.6, bf16[4,64,160]{2,1,0:T(8,128)(2,1)S(1)} %copy-done.5, f32[8,160]{1,0:T(8,128)S(1)} %copy-done.7, ...), custom_call_target="tpu_custom_call" | custom-call | tf_op jit(solution)/shard_map/phi/pallas_call | solution.py:88
  20.3 3.1 %collective-permute-done.3.got_ref.rest_0_ = bf16[4,200,128]{2,1,0:T(8,128)(2,1)S(1)} collective-permute-done((bf16[4,200,128]{2,1,0:T(8,128)(2,1)S(1)}, bf16[4,200,128]{2,1,0:T(8,128)(2,1)S(1)}, u32[]{:S(2)}, u32[]{:S(2)}) %collective-permute-start.3) | collective-permute-done | bytes 204832 | tf_op jit(solution)/shard_map/ppermute | solution.py:362
  23.4 0.8 %add.5 = (f32[4,160,128]{2,1,0:T(8,128)}, bf16[4,200,128]{2,1,0:T(8,128)(2,1)S(1)}) custom-call(f32[4,160,128]{2,1,0:T(8,128)S(1)} %get-tuple-element.34.base_ref, bf16[4,200,128]{2,1,0:T(8,128)(2,1)S(1)} %collective-permute-done.3.got_ref.rest_0_, bf16[16,256,160]{2,1,0:T(8,128)(2,1)S(1)} %get-tuple-element.35.rest_0_.high_ref), custom_call_target="tpu_custom_call" | custom-call | tf_op jit(solution)/shard_map/add/pallas_call | solution.py:88
  24.2 0.7 %collective-permute-start.4 = (bf16[4,200,128]{2,1,0:T(8,128)(2,1)S(1)}, bf16[4,200,128]{2,1,0:T(8,128)(2,1)S(1)}, u32[]{:S(2)}, u32[]{:S(2)}) collective-permute-start(bf16[4,200,128]{2,1,0:T(8,128)(2,1)S(1)} %get-tuple-element.36.after_ref), channel_id=1, source_target_pairs={{8,24},{10,26},{12,28},{14,30},{9,25},{11,27},{13,29},{15,31}} | collective-permute-start | bytes 614408 | tf_op jit(solution)/shard_map/ppermute | solution.py:362
  24.9 0.0 collective-permute-done.6.rim_ref
  24.9 0.0 copy-done.1
  24.9 0.0 copy-done.2
  24.9 4.6 %window.1.rest_3_.win_ref = f32[16,256,128]{2,1,0:T(8,128)S(1)} custom-call(s32[3]{0:T(128)S(1)} %pad_add_fusion.place_ref, bf16[256,16,128]{2,1,0:T(8,128)(2,1)S(1)} %copy-done.2, bf16[256,16,128]{2,1,0:T(8,128)(2,1)S(1)} %copy-done.1, bf16[16,256,128]{2,1,0:T(8,128)(2,1)S(1)} %get-tuple-element.30.vh_ref, ...), custom_call_target="tpu_custom_call" | custom-call | tf_op jit(solution)/shard_map/window/pallas_call | solution.py:88
  29.5 0.0 collective-permute-done.5.rest_2_
  29.5 0.0 collective-permute-done.4.rest_1_
  29.5 0.8 %before.1 = (f32[4,160,128]{2,1,0:T(8,128)S(1)}, f32[4,160,128]{2,1,0:T(8,128)S(1)}, bf16[4,200,128]{2,1,0:T(8,128)(2,1)S(1)}) custom-call(s32[3]{0:T(128)S(1)} %pad_add_fusion.place_ref, f32[4,160,128]{2,1,0:T(8,128)S(1)} %near0.1.after_ref.own_ref, f32[4,160,128]{2,1,0:T(8,128)S(1)} %collective-permute-done.1.other_ref, ...), custom_call_target="tpu_custom_call" | custom-call | tf_op jit(solution)/shard_map/before/pallas_call | solution.py:88
  30.2 4.6 %collective-permute-start.8 = (f32[4,160,128]{2,1,0:T(8,128)S(1)}, f32[4,160,128]{2,1,0:T(8,128)S(1)}, u32[]{:S(2)}, u32[]{:S(2)}) collective-permute-start(f32[4,160,128]{2,1,0:T(8,128)S(1)} %get-tuple-element.38), channel_id=1, source_target_pairs={{0,2},{2,0},{4,6},{6,4},{8,10},{10,8},{12,14},{14,12},{16,18},{18,... | collective-permute-start | bytes 983048 | tf_op jit(solution)/shard_map/ppermute | solution.py:362
  34.8 0.0 collective-permute-start.7
  34.8 1.3 %final0.1 = (f32[16,256,128]{2,1,0:T(8,128)S(1)}, f32[256,128]{1,0:T(8,128)S(1)}) custom-call(s32[3]{0:T(128)S(1)} %pad_add_fusion.place_ref, f32[4,160,128]{2,1,0:T(8,128)S(1)} %get-tuple-element.42.prior_ref, bf16[16,256,160]{2,1,0:T(8,128)(2,1)S(1)} %get-tuple-element.35.rest_0_.high_ref, bf16[16,256,160]{2,1,0:T(8,128)(2,1)S(1)} %get-tuple-element.39.low_ref, ...), custom_call_target="tpu_custom_call" | custom-call | tf_op jit(solution)/shard_map/final0/pallas_call | solution.py:88
  36.1 0.0 collective-permute-done.8.prior_ref
  36.1 1.3 %final1.1 = (f32[16,256,128]{2,1,0:T(8,128)S(1)}, f32[256,128]{1,0:T(8,128)S(1)}) custom-call(s32[3]{0:T(128)S(1)} %pad_add_fusion.place_ref, f32[4,160,128]{2,1,0:T(8,128)S(1)} %collective-permute-done.8.prior_ref, bf16[16,256,160]{2,1,0:T(8,128)(2,1)S(1)} %get-tuple-element.35.rest_0_.high_ref, ...), custom_call_target="tpu_custom_call", output_to_operand_aliasing={{0}: (8, {})} | custom-call | tf_op jit(solution)/shard_map/final1/pallas_call | solution.py:88
  37.4 4.5 %collective-permute-done.7.got_ref = bf16[4,200,128]{2,1,0:T(8,128)(2,1)S(1)} collective-permute-done((bf16[4,200,128]{2,1,0:T(8,128)(2,1)S(1)}, bf16[4,200,128]{2,1,0:T(8,128)(2,1)S(1)}, u32[]{:S(2)}, u32[]{:S(2)}) %collective-permute-start.7) | collective-permute-done | bytes 204832 | tf_op jit(solution)/shard_map/ppermute | solution.py:362
  41.9 0.6 %rest.1 = (f32[4,160,128]{2,1,0:T(8,128)S(1)}, f32[4,160,128]{2,1,0:T(8,128)S(1)}) custom-call(s32[3]{0:T(128)S(1)} %pad_add_fusion.place_ref, bf16[4,200,128]{2,1,0:T(8,128)(2,1)S(1)} %collective-permute-done.7.got_ref, f32[4,160,128]{2,1,0:T(8,128)S(1)} %near1.1.own_ref, f32[4,160,128]{2,1,0:T(8,128)S(1)} %collective-permute-done.other_ref, ...), custom_call_target="tpu_custom_call" | custom-call | tf_op jit(solution)/shard_map/rest/pallas_call | solution.py:88
  42.5 0.1 collective-permute-start.9
  42.6 1.3 %final2.1 = (f32[16,256,128]{2,1,0:T(8,128)S(1)}, f32[256,128]{1,0:T(8,128)S(1)}) custom-call(s32[3]{0:T(128)S(1)} %pad_add_fusion.place_ref, f32[4,160,128]{2,1,0:T(8,128)S(1)} %get-tuple-element.47.prior_ref, bf16[16,256,160]{2,1,0:T(8,128)(2,1)S(1)} %get-tuple-element.35.rest_0_.high_ref, ...), custom_call_target="tpu_custom_call", output_to_operand_aliasing={{0}: (8, {})} | custom-call | tf_op jit(solution)/shard_map/final2/pallas_call | solution.py:88
  43.9 0.3 collective-permute-done.9.prior_ref
  44.2 1.6 %final3.1 = (f32[16,256,128]{2,1,0:T(8,128)S(1)}, f32[8,256]{1,0:T(8,128)S(1)}) custom-call(s32[3]{0:T(128)S(1)} %pad_add_fusion.place_ref, f32[4,160,128]{2,1,0:T(8,128)S(1)} %collective-permute-done.9.prior_ref, bf16[16,256,160]{2,1,0:T(8,128)(2,1)S(1)} %get-tuple-element.35.rest_0_.high_ref, ...), custom_call_target="tpu_custom_call", output_to_operand_aliasing={{0}: (8, {})} | custom-call | tf_op jit(solution)/shard_map/final3/pallas_call | solution.py:88
  45.8 0.6 %collective-permute-start.10 = (f32[8,256]{1,0:T(8,128)S(1)}, f32[8,256]{1,0:T(8,128)S(1)}, u32[]{:S(2)}, u32[]{:S(2)}) collective-permute-start(f32[8,256]{1,0:T(8,128)S(1)} %get-tuple-element.52.sq_ref), channel_id=1, source_target_pairs={{0,1},{1,0},{2,3},{3,2},{4,5},{5,4},{6,7},{7,6},{8,9},{9,8},{10,11... | collective-permute-start | bytes 24584 | tf_op jit(solution)/shard_map/ppermute | solution.py:456
  46.4 3.1 %collective-permute-done.10.rest_0_ = f32[8,256]{1,0:T(8,128)S(1)} collective-permute-done((f32[8,256]{1,0:T(8,128)S(1)}, f32[8,256]{1,0:T(8,128)S(1)}, u32[]{:S(2)}, u32[]{:S(2)}) %collective-permute-start.10) | collective-permute-done | bytes 8224 | tf_op jit(solution)/shard_map/ppermute | solution.py:456
  49.5 1.4 %norm.1 = bf16[256,16,128]{2,1,0:T(8,128)(2,1)} custom-call(f32[16,256,128]{2,1,0:T(8,128)S(1)} %get-tuple-element.51.mixed_ref, f32[8,256]{1,0:T(8,128)S(1)} %get-tuple-element.52.sq_ref, f32[8,256]{1,0:T(8,128)S(1)} %collective-permute-done.10.rest_0_), custom_call_target="tpu_custom_call" | custom-call | tf_op jit(solution)/shard_map/norm/pallas_call | solution.py:88
  (1 shorter events, 0.0 us)
Async XLA Ops:
  0.0 1.4 %copy-start = (bf16[256,16,128]{2,1,0:T(8,128)(2,1)S(1)}, bf16[256,16,128]{2,1,0:T(8,128)(2,1)}, u32[]{:S(2)}) copy-start(bf16[256,16,128]{2,1,0:T(8,128)(2,1)} %v_ref.3) | copy-start | bytes 3145732
  0.0 1.4 %copy-start.3 = (bf16[256,256]{1,0:T(8,128)(2,1)S(1)}, bf16[256,256]{1,0:T(8,128)(2,1)}, u32[]{:S(2)}) copy-start(bf16[256,256]{1,0:T(8,128)(2,1)} %k_ref.1) | copy-start | bytes 393220
  2.8 2.6 %collective-permute-start = (f32[4,160,128]{2,1,0:T(8,128)S(1)}, f32[4,160,128]{2,1,0:T(8,128)S(1)}, u32[]{:S(2)}, u32[]{:S(2)}) collective-permute-start(f32[4,160,128]{2,1,0:T(8,128)S(1)} %get-tuple-element.31.after_ref), channel_id=1, source_target_pairs={{0,2},{2,0},{4,6},{6,4},{8,10},{10,8},{12,14},{14,12},{16,18},{18,... | collective-permute-start | bytes 983048 | tf_op jit(solution)/shard_map/ppermute | solution.py:362
  3.8 5.1 %copy-start.4 = (bf16[256,256]{1,0:T(8,128)(2,1)S(1)}, bf16[256,256]{1,0:T(8,128)(2,1)}, u32[]{:S(2)}) copy-start(bf16[256,256]{1,0:T(8,128)(2,1)} %q_ref.3) | copy-start | bytes 393220
  3.8 8.0 %collective-permute-start.1 = (f32[4,160,128]{2,1,0:T(8,128)S(1)}, f32[4,160,128]{2,1,0:T(8,128)S(1)}, u32[]{:S(2)}, u32[]{:S(2)}) collective-permute-start(f32[4,160,128]{2,1,0:T(8,128)S(1)} %far0.1.after_ref), channel_id=1, source_target_pairs={{0,2},{2,0},{4,6},{6,4},{8,10},{10,8},{12,14},{14,12},{16,18},{18,... | collective-permute-start | bytes 983048 | tf_op jit(solution)/shard_map/ppermute | solution.py:362
  5.4 8.0 %collective-permute-start.2 = (bf16[4,200,128]{2,1,0:T(8,128)(2,1)S(1)}, bf16[4,200,128]{2,1,0:T(8,128)(2,1)S(1)}, u32[]{:S(2)}, u32[]{:S(2)}) collective-permute-start(bf16[4,200,128]{2,1,0:T(8,128)(2,1)S(1)} %chip.1.after_ref), channel_id=1, source_target_pairs={{0,4},{2,6},{4,0},{6,2},{8,12},{10,14},{12,8},{14,10},{16,20},{18,... | collective-permute-start | bytes 614408 | tf_op jit(solution)/shard_map/ppermute | solution.py:362
  6.0 18.9 %collective-permute-start.6 = (bf16[2,64,16,128]{3,2,1,0:T(8,128)(2,1)S(1)}, bf16[2,64,16,128]{3,2,1,0:T(8,128)(2,1)S(1)}, u32[]{:S(2)}, u32[]{:S(2)}) collective-permute-start(bf16[2,64,16,128]{3,2,1,0:T(8,128)(2,1)S(1)} %rim.1.after_ref), channel_id=1, source_target_pairs={{0,2},{2,4},{4,6},{6,8},{8,10},{10,12},{12,14},{14,16},{16,18},{18... | collective-permute-start | bytes 1572872 | tf_op jit(solution)/shard_map/ppermute | solution.py:362
  8.9 9.5 %copy-start.5 = (bf16[4,64,160]{2,1,0:T(8,128)(2,1)S(1)}, bf16[4,64,160]{2,1,0:T(8,128)(2,1)}, u32[]{:S(2)}) copy-start(bf16[4,64,160]{2,1,0:T(8,128)(2,1)} %constant.15.clone.e2_ref) | copy-start | bytes 245764
  8.9 9.5 %copy-start.6 = (bf16[4,64,160]{2,1,0:T(8,128)(2,1)S(1)}, bf16[4,64,160]{2,1,0:T(8,128)(2,1)}, u32[]{:S(2)}) copy-start(bf16[4,64,160]{2,1,0:T(8,128)(2,1)} %constant.14.clone.e1_ref) | copy-start | bytes 245764
  9.0 9.5 %copy-start.7 = (f32[8,160]{1,0:T(8,128)S(1)}, f32[8,160]{1,0:T(8,128)}, u32[]{:S(2)}) copy-start(f32[8,160]{1,0:T(8,128)} %constant.16.clone.add_ref) | copy-start | bytes 15364
  9.0 9.5 %copy-start.8 = (bf16[16,128]{1,0:T(8,128)(2,1)S(1)}, bf16[16,128]{1,0:T(8,128)(2,1)}, u32[]{:S(2)}) copy-start(bf16[16,128]{1,0:T(8,128)(2,1)} %gain_ref.1) | copy-start | bytes 12292
  13.5 11.4 %copy-start.1 = (bf16[256,16,128]{2,1,0:T(8,128)(2,1)S(1)}, bf16[256,16,128]{2,1,0:T(8,128)(2,1)}, u32[]{:S(2)}) copy-start(bf16[256,16,128]{2,1,0:T(8,128)(2,1)} %wk_ref.3) | copy-start | bytes 3145732
  13.5 11.4 %copy-start.2 = (bf16[256,16,128]{2,1,0:T(8,128)(2,1)S(1)}, bf16[256,16,128]{2,1,0:T(8,128)(2,1)}, u32[]{:S(2)}) copy-start(bf16[256,16,128]{2,1,0:T(8,128)(2,1)} %wq_ref.1) | copy-start | bytes 3145732
  13.5 9.9 %collective-permute-start.3 = (bf16[4,200,128]{2,1,0:T(8,128)(2,1)S(1)}, bf16[4,200,128]{2,1,0:T(8,128)(2,1)S(1)}, u32[]{:S(2)}, u32[]{:S(2)}) collective-permute-start(bf16[4,200,128]{2,1,0:T(8,128)(2,1)S(1)} %get-tuple-element.33.after_ref), channel_id=1, source_target_pairs={{0,8},{2,10},{4,12},{6,14},{8,16},{10,18},{12,20},{14,22},{16,24},... | collective-permute-start | bytes 614408 | tf_op jit(solution)/shard_map/ppermute | solution.py:362
  17.2 12.3 %collective-permute-start.5 = (bf16[4,200,128]{2,1,0:T(8,128)(2,1)S(1)}, bf16[4,200,128]{2,1,0:T(8,128)(2,1)S(1)}, u32[]{:S(2)}, u32[]{:S(2)}) collective-permute-start(bf16[4,200,128]{2,1,0:T(8,128)(2,1)S(1)} %get-tuple-element.33.after_ref), channel_id=1, source_target_pairs={{0,16},{2,18},{4,20},{6,22},{1,17},{3,19},{5,21},{7,23}} | collective-permute-start | bytes 614408 | tf_op jit(solution)/shard_map/ppermute | solution.py:362
  24.2 5.3 %collective-permute-start.4 = (bf16[4,200,128]{2,1,0:T(8,128)(2,1)S(1)}, bf16[4,200,128]{2,1,0:T(8,128)(2,1)S(1)}, u32[]{:S(2)}, u32[]{:S(2)}) collective-permute-start(bf16[4,200,128]{2,1,0:T(8,128)(2,1)S(1)} %get-tuple-element.36.after_ref), channel_id=1, source_target_pairs={{8,24},{10,26},{12,28},{14,30},{9,25},{11,27},{13,29},{15,31}} | collective-permute-start | bytes 614408 | tf_op jit(solution)/shard_map/ppermute | solution.py:362
  30.2 5.9 %collective-permute-start.8 = (f32[4,160,128]{2,1,0:T(8,128)S(1)}, f32[4,160,128]{2,1,0:T(8,128)S(1)}, u32[]{:S(2)}, u32[]{:S(2)}) collective-permute-start(f32[4,160,128]{2,1,0:T(8,128)S(1)} %get-tuple-element.38), channel_id=1, source_target_pairs={{0,2},{2,0},{4,6},{6,4},{8,10},{10,8},{12,14},{14,12},{16,18},{18,... | collective-permute-start | bytes 983048 | tf_op jit(solution)/shard_map/ppermute | solution.py:362
  34.8 7.1 %collective-permute-start.7 = (bf16[4,200,128]{2,1,0:T(8,128)(2,1)S(1)}, bf16[4,200,128]{2,1,0:T(8,128)(2,1)S(1)}, u32[]{:S(2)}, u32[]{:S(2)}) collective-permute-start(bf16[4,200,128]{2,1,0:T(8,128)(2,1)S(1)} %get-tuple-element.37.rest_0_), channel_id=1, source_target_pairs={{0,4},{2,6},{4,0},{6,2},{8,12},{10,14},{12,8},{14,10},{16,20},{18,... | collective-permute-start | bytes 614408 | tf_op jit(solution)/shard_map/ppermute | solution.py:362
  42.5 1.7 %collective-permute-start.9 = (f32[4,160,128]{2,1,0:T(8,128)S(1)}, f32[4,160,128]{2,1,0:T(8,128)S(1)}, u32[]{:S(2)}, u32[]{:S(2)}) collective-permute-start(f32[4,160,128]{2,1,0:T(8,128)S(1)} %get-tuple-element.46), channel_id=1, source_target_pairs={{0,2},{2,0},{4,6},{6,4},{8,10},{10,8},{12,14},{14,12},{16,18},{18,... | collective-permute-start | bytes 983048 | tf_op jit(solution)/shard_map/ppermute | solution.py:362
  45.8 3.7 %collective-permute-start.10 = (f32[8,256]{1,0:T(8,128)S(1)}, f32[8,256]{1,0:T(8,128)S(1)}, u32[]{:S(2)}, u32[]{:S(2)}) collective-permute-start(f32[8,256]{1,0:T(8,128)S(1)} %get-tuple-element.52.sq_ref), channel_id=1, source_target_pairs={{0,1},{1,0},{2,3},{3,2},{4,5},{5,4},{6,7},{7,6},{8,9},{9,8},{10,11... | collective-permute-start | bytes 24584 | tf_op jit(solution)/shard_map/ppermute | solution.py:456

commit v4 on v3

v4 whole, which is shorter than its diff:
```python
import functools
import math

import jax
import jax.numpy as jnp
import numpy as np
from jax import lax
from jax.experimental import pallas as pl
from jax.experimental.pallas import tpu as pltpu
from jax.sharding import PartitionSpec as P

HEADS = 32
DV = 128
DK = 16
WINDOW = 64
NORM_EPS = 1e-06

ROWS = 160
TOTAL_ROW = 33
WIDE = 40
HALF_WIDE = 2 * DK
SENT = ROWS + HALF_WIDE
GROUP = 4

F32 = jnp.float32
BF16 = jnp.bfloat16
NN = (((1,), (0,)), ((), ()))
NT = (((1,), (1,)), ((), ()))


def pair_tables(heads):
    first = np.zeros((DK, ROWS), np.float32)
    second = np.zeros((DK, ROWS), np.float32)
    add = np.zeros((8, ROWS), np.float32)
    for i in range(DK):
        first[i, i] = 1.0 / 32.0
        second[i, i] = 1.0
        first[i, DK + i] = 0.25
        add[1, DK + i] = 1.0
        for d in range(1, 8):
            row = WIDE + DK * (d - 1) + i
            first[i, row] = 1.0 / 16.0
            second[(i + d) % DK, row] = 1.0
    for i in range(8):
        first[i, 152 + i] = 1.0 / 16.0
        second[i + 8, 152 + i] = 1.0
    add[0, 2 * DK] = 1.0
    add[1, 2 * DK] = 1.0
    both = []
    for one in (first, second):
        table = np.zeros((heads, heads * DK, ROWS), np.float32)
        for j in range(heads):
            table[j, j * DK : (j + 1) * DK] = one
        both.append(jnp.asarray(table, BF16))
    return both[0], both[1], jnp.asarray(add, F32)


def dot(a, b, dims=NN):
    return lax.dot_general(a, b, dims, preferred_element_type=F32)


def split(x):
    high = x.astype(BF16)
    return high, (x - high.astype(F32)).astype(BF16)


def full(pairs, count):
    sources = [i for i in range(count) if i not in {a for a, _ in pairs}]
    targets = [i for i in range(count) if i not in {b for _, b in pairs}]
    stay = sorted(set(sources) & set(targets))
    moved = zip([i for i in sources if i not in stay], [i for i in targets if i not in stay])
    return list(pairs) + [(i, i) for i in stay] + list(moved)


def plane_index():
    return lax.axis_index("ctx") >> 2


def arrived(got_refs, limits, j):
    total = None
    for ref, (least, most) in zip(got_refs, limits):
        here = plane_index()
        meant = (here >= least) & (here <= most)
        got = jnp.where(meant, unpack(ref[j]), 0.0)
        total = got if total is None else total + got
    return total


def core_bit():
    return lax.axis_index("ctx") & 1


def pair_bit():
    return (lax.axis_index("ctx") >> 1) & 1


def each(count, body):
    group = math.gcd(GROUP, count)

    def step(i, carry):
        for j in range(group):
            body(i * group + j)
        return carry

    if group == count:
        step(0, 0)
    else:
        lax.fori_loop(0, count // group, step, 0)


def pack(ref, x):
    high = x.astype(BF16).astype(F32)
    low = x[:WIDE] - high[:WIDE]
    mid = high[HALF_WIDE:WIDE] + pltpu.roll(low[HALF_WIDE:], 3, 0).astype(BF16).astype(F32)
    ref[...] = jnp.concatenate(
        [high[:HALF_WIDE], mid, high[WIDE:], low[:HALF_WIDE]], axis=0
    ).astype(BF16)


def unpack(got):
    got = got.astype(F32)
    mid = got[HALF_WIDE:WIDE]
    row = lax.broadcasted_iota(jnp.int32, mid.shape, 0)
    mid = jnp.where(row < 3, mid + pltpu.roll(mid, 5, 0), 0.0)
    return jnp.concatenate([got[:HALF_WIDE] + got[ROWS:], mid, got[WIDE:ROWS]], axis=0)


VMEM_SPEC = pl.BlockSpec(memory_space=pltpu.VMEM)
VMEM_LIMIT = 12 << 20
FLOPS_PER_US = 1_150_000_000
EXPECTED_US = {"phi": 1.8, "intra": 2.8, "window": 3.5, "chip": 0.1, "plane": 0.1, "open": 12.0, "pick": 0.1}


def call(body, name, outs, *operands, scratch=(), raw=False, aliases=None):
    held = [
        pltpu.with_memory_space_constraint(x, pltpu.HBM if raw else pltpu.VMEM)
        for x in operands
    ]
    many = isinstance(outs, tuple)
    spec = pl.BlockSpec(memory_space=pltpu.HBM) if raw else VMEM_SPEC
    return pl.pallas_call(
        body,
        out_shape=outs,
        in_specs=[spec] * len(operands),
        out_specs=tuple(VMEM_SPEC for _ in outs) if many else VMEM_SPEC,
        scratch_shapes=list(scratch),
        input_output_aliases=aliases or {},
        cost_estimate=pl.CostEstimate(
            flops=int(EXPECTED_US.get(name, 1.0) * FLOPS_PER_US), bytes_accessed=0, transcendentals=0
        ),
        compiler_params=pltpu.CompilerParams(vmem_limit_bytes=VMEM_LIMIT),
        name=name,
    )(*held)


def one_state(x, v):
    toks = x.shape[1]
    ones = jnp.where(lax.broadcasted_iota(jnp.int32, (8, toks), 0) == 0, 1.0, 0.0).astype(F32)
    parts = [x * x, x, ones]
    for d in range(1, 8):
        parts.append(x * pltpu.roll(x, DK - d, 0))
    parts.append(x[:8] * x[8:])
    high, low = split(jnp.concatenate(parts, axis=0))
    full = jnp.ones((8, toks), BF16)
    total = dot(full, high, NT) + dot(full, low, NT)
    return dot(high, v) + dot(low, v), total


def put_states(out_ref, far, other, kt_ref, vh_ref):
    part = out_ref.shape[0]
    base = first_head(far, other, part)

    def one(j):
        x = kt_ref[pl.ds(pl.multiple_of((base + j) * DK, DK), DK), :]
        state, total = one_state(x, vh_ref[base + j])
        out_ref[j] = state
        out_ref[j, TOTAL_ROW : TOTAL_ROW + 1, :] = total[:1, :128]
        out_ref[j, TOTAL_ROW + 1 : TOTAL_ROW + 2, : ROWS - 128] = total[:1, 128:]

    each(part, one)


def rim_kernel(wk_ref, v_ref, rim_ref, sems):
    rows = pl.ds(wk_ref.shape[0] - WINDOW, WINDOW)
    copies = [
        pltpu.make_async_copy(ref.at[rows], rim_ref.at[i], sems.at[i])
        for i, ref in enumerate((wk_ref, v_ref))
    ]
    for copy in copies:
        copy.start()
    for copy in copies:
        copy.wait()


def first_states_kernel(keys_ref, v_ref, after_ref, out_ref, vh_ref, kt_ref):
    vh_ref[...] = jnp.swapaxes(v_ref[...], 0, 1)
    kt_ref[...] = jnp.transpose(keys_ref[...].astype(F32), (1, 0))
    put_states(out_ref, 1, 1, kt_ref, vh_ref)


def states_kernel(far, other, kt_ref, vh_ref, after_ref, out_ref):
    put_states(out_ref, far, other, kt_ref, vh_ref)


def far_rim_kernel(kt_ref, vh_ref, rim_ref, after_ref, out_ref, rim_out_ref):
    rim_out_ref[...] = rim_ref[...]
    put_states(out_ref, 1, 0, kt_ref, vh_ref)


def chip_kernel(own_ref, other_ref, msg_ref):
    def one(j):
        pack(msg_ref.at[j], own_ref[j] + other_ref[j])

    each(own_ref.shape[0], one)


def open_kernel(got_ref, *rest):
    out_ref = rest[-1]

    def one(j):
        out_ref[j] = unpack(got_ref[j])

    each(got_ref.shape[0], one)


def plane_kernel(own_ref, other_ref, got_ref, *rest):
    total_ref, msg_ref = rest[-2:]

    def one(j):
        total = own_ref[j] + other_ref[j] + got_ref[j]
        total_ref[j] = total
        pack(msg_ref.at[j], total)

    each(own_ref.shape[0], one)


def round_kernel(limits, total_ref, *rest):
    gots, (next_ref, msg_ref) = rest[: len(limits)], rest[-2:]

    def one(j):
        total = total_ref[j] + arrived(gots, limits, j)
        next_ref[j] = total
        pack(msg_ref.at[j], total)

    each(total_ref.shape[0], one)


def before_kernel(limits, own_ref, other_ref, pair_ref, *rest):
    gots, (mine_ref, msg_ref) = rest[: len(limits)], rest[-2:]
    mid = pair_bit()

    def one(j):
        before = arrived(gots, limits, j)
        mine_ref[j] = before + jnp.where(mid == 1, pair_ref[j], 0.0)
        pack(msg_ref.at[j], before + jnp.where(mid == 0, own_ref[j] + other_ref[j], 0.0))

    each(own_ref.shape[0], one)


def pick_kernel(rim_ref, got_ref, after_ref, out_ref):
    last = lax.axis_index("ctx") % 4 == 3

    @pl.when(last)
    def _():
        out_ref[...] = got_ref[...]

    @pl.when(jnp.logical_not(last))
    def _():
        out_ref[...] = rim_ref[...]


def phi_kernel(q_ref, e1_ref, e2_ref, add_ref, gain_ref, after_ref,
               high_ref, low_ref, gain_out_ref, q4_ref):
    for h in range(gain_ref.shape[0]):
        gain_out_ref[h] = gain_ref[h : h + 1].astype(F32)
    part = e1_ref.shape[0]
    width = part * DK
    for r in range(4):
        q4_ref[r] = q_ref[:, r * width : (r + 1) * width]

    def one(r, carry):
        q = q4_ref[r]
        for j in range(part):
            a = dot(q, e1_ref[j]) + add_ref[0:1]
            b = dot(q, e2_ref[j]) + add_ref[1:2]
            high, low = split(a * b)
            high_ref[r * part + j] = high
            low_ref[r * part + j] = low
        return carry

    lax.fori_loop(0, 4, one, 0)


def intra_kernel(q_ref, k_ref, vh_ref, after_ref,
                 num_ref, den_ref, again_ref, token_ref, q4_ref, k4_ref):
    again_ref[...] = after_ref[...]
    token_ref[...] = jnp.zeros_like(token_ref)
    heads, toks, dim = vh_ref.shape
    part = heads // 4
    width = part * DK
    half = toks // 2
    for r in range(4):
        q4_ref[r] = q_ref[:, r * width : (r + 1) * width]
        k4_ref[r] = k_ref[:, r * width : (r + 1) * width]
    row = lax.broadcasted_iota(jnp.int32, (half, half), 0)
    col = lax.broadcasted_iota(jnp.int32, (half, half), 1)
    tri = col <= row
    lane = lax.broadcasted_iota(jnp.int32, (toks, width), 1) // DK
    ones = jnp.ones((toks, dim), BF16)

    def poly(s):
        return 1.0 + s * 0.25 + s * s * (1.0 / 32.0)

    def one(r, carry):
        q, k = q4_ref[r], k4_ref[r]
        tops, lows, rights = [], [], []
        for j in range(part):
            own = jnp.where(lane == j, q, jnp.zeros_like(q))
            tops.append(dot(own[:half], k[:half], NT))
            lows.append(dot(own[half:], k, NT))
        for j in range(part):
            head = r * part + j
            v = jnp.concatenate([vh_ref[head], ones], axis=1)
            top = jnp.where(tri, poly(tops[j]), 0.0)
            left = poly(lows[j][:, :half])
            right = jnp.where(tri, poly(lows[j][:, half:]), 0.0)
            high, low = split(top)
            both = dot(high, v[:half]) + dot(low, v[:half])
            num_ref[head, :half] = both[:, :dim]
            den_ref[head, :half] = both[:, dim:]
            high, low = split(jnp.concatenate([left, right], axis=1))
            both = dot(high, v) + dot(low, v)
            num_ref[head, half:] = both[:, :dim]
            den_ref[head, half:] = both[:, dim:]
        return carry

    lax.fori_loop(0, 4, one, 0)


def softmax_blocks(scores):
    sc = jnp.concatenate(scores, axis=0)
    expo = jnp.exp(sc - jnp.max(sc, axis=1, keepdims=True))
    return (expo / jnp.sum(expo, axis=1, keepdims=True)).astype(BF16)


def band_mask():
    row = lax.broadcasted_iota(jnp.int32, (WINDOW, 2 * WINDOW), 0)
    col = lax.broadcasted_iota(jnp.int32, (WINDOW, 2 * WINDOW), 1)
    return (col > row) & (col <= row + WINDOW), col


def window_kernel(wq_ref, wk_ref, vh_ref, after_ref,
                  win_ref, edge_q_ref, edge_k_ref, token_ref, qh_ref, kh_ref):
    heads, toks, dim = vh_ref.shape
    part = heads // 4
    token_ref[...] = jnp.zeros_like(token_ref)
    qh_ref[...] = jnp.swapaxes(wq_ref[...], 0, 1)
    kh_ref[...] = jnp.swapaxes(wk_ref[...], 0, 1)
    edge_q_ref[...] = qh_ref[:, :WINDOW]
    edge_k_ref[...] = kh_ref[:, :WINDOW]
    band, _ = band_mask()
    blocks = toks // WINDOW - 1

    def one(r, carry):
        scores = []
        for j in range(part):
            head = r * part + j
            for b in range(blocks):
                lo = b * WINDOW
                q = qh_ref[head, lo + WINDOW : lo + 2 * WINDOW]
                sc = dot(q, kh_ref[head, lo : lo + 2 * WINDOW], NT)
                scores.append(jnp.where(band, sc / math.sqrt(dim), -1e30))
        weights = softmax_blocks(scores)
        for j in range(part):
            head = r * part + j
            for b in range(blocks):
                lo = b * WINDOW
                at = (j * blocks + b) * WINDOW
                win_ref[head, lo : lo + WINDOW] = dot(
                    weights[at : at + WINDOW], vh_ref[head, lo : lo + 2 * WINDOW]
                )
        return carry

    lax.fori_loop(0, 4, one, 0)


def edge_kernel(q_ref, k_ref, vh_ref, rim_ref, after_ref, out_ref, rk_ref, rv_ref):
    heads, _, dim = vh_ref.shape
    part = heads // 4
    rk_ref[...] = jnp.swapaxes(rim_ref[0], 0, 1)
    rv_ref[...] = jnp.swapaxes(rim_ref[1], 0, 1)
    band, col = band_mask()
    valid = band & ((col >= WINDOW) | (lax.axis_index("ctx") > 0))

    def one(r, carry):
        scores = []
        for j in range(part):
            head = r * part + j
            k = jnp.concatenate([rk_ref[head], k_ref[head]], axis=0)
            sc = dot(q_ref[head], k, NT)
            scores.append(jnp.where(valid, sc / math.sqrt(dim), -1e30))
        weights = softmax_blocks(scores)
        for j in range(part):
            head = r * part + j
            v = jnp.concatenate([rv_ref[head], vh_ref[head, :WINDOW]], axis=0)
            out_ref[head] = dot(weights[j * WINDOW : (j + 1) * WINDOW], v)
        return carry

    lax.fori_loop(0, 4, one, 0)


def first_head(far, other, part):
    half = core_bit() if far == 0 else 1 - core_bit()
    mid = pair_bit() if other == 0 else 1 - pair_bit()
    return (half * 2 + mid) * part


def mix(first, base_ref, extra_ref, high_ref, low_ref, num_ref, den_ref, edge_ref, win_ref,
        gain_ref, mixed_ref, squares):
    part, dim = base_ref.shape[0], num_ref.shape[2]
    for j in range(part):
        head = first + j
        base = unpack(base_ref[j]) if base_ref.shape[1] == SENT else base_ref[j]
        prior = base + jnp.where(core_bit() == 1, extra_ref[j], 0.0)
        phi_high, phi_low = high_ref[head], low_ref[head]
        high, low = split(prior)
        both = dot(phi_high, jnp.concatenate([high, low], axis=1))
        numer = num_ref[head] + ((both[:, dim:] + dot(phi_low, high)) + both[:, :dim])
        total = jnp.concatenate(
            [prior[TOTAL_ROW : TOTAL_ROW + 1], prior[TOTAL_ROW + 1 : TOTAL_ROW + 2, : ROWS - 128]],
            axis=1,
        )
        t_high, t_low = split(jnp.broadcast_to(total, (dim, ROWS)))
        both = dot(phi_high, jnp.concatenate([t_high, t_low], axis=0), NT)
        denom = den_ref[head] + ((both[:, dim:] + dot(phi_low, t_high, NT)) + both[:, :dim])
        window = jnp.concatenate([edge_ref[head], win_ref[head]], axis=0)
        mixed = numer / denom + window
        mixed_ref[head] = mixed * gain_ref[head]
        squares = squares + mixed * mixed
    return squares


def first_final_kernel(mine_ref, other_ref, far_ref, extra_ref, *rest):
    held, (mixed_ref, sq_ref) = rest[:-2], rest[-2:]
    part = mine_ref.shape[0]
    squares = jnp.zeros(sq_ref.shape, F32)
    squares = mix(first_head(0, 0, part), mine_ref, other_ref, *held, mixed_ref, squares)
    squares = mix(first_head(1, 0, part), far_ref, extra_ref, *held, mixed_ref, squares)
    sq_ref[...] = squares


def next_final_kernel(far, base_ref, extra_ref, *rest):
    held, (squares_ref, mixed_ref, sq_ref) = rest[:7], rest[-3:]
    first = first_head(far, 1, base_ref.shape[0])
    squares = mix(first, base_ref, extra_ref, *held, mixed_ref, squares_ref[...])
    if far == 0:
        sq_ref[...] = squares
    else:
        sq_ref[...] = lax.dot_general(
            jnp.ones((8, squares.shape[1]), F32), squares, NT,
            precision=lax.Precision.HIGHEST, preferred_element_type=F32,
        )


def norm_kernel(peers, mixed_ref, sq_ref, *rest):
    out_ref = rest[-1]
    total = sq_ref[...]
    for got in rest[:peers]:
        total = total + got[...]
    scale = lax.rsqrt(total / (HEADS * DV) + NORM_EPS)
    column = jnp.transpose(scale, (1, 0))[:, :1]
    wide = jnp.broadcast_to(column, mixed_ref.shape[1:])
    out_ref[...] = jnp.swapaxes((mixed_ref[...] * wide[None]).astype(BF16), 0, 1)


def on_device(queries, keys, values, win_q, win_k, gain):
    toks, heads, dim = values.shape
    count = lax.axis_size("ctx")
    peers = lax.axis_size("head") - 1
    part = heads // 4
    core_swap = [(i, i ^ 1) for i in range(count)]
    pair_swap = [(i, i ^ 2) for i in range(count)]
    state_shape = pltpu.VMEM((part, ROWS, dim), F32)
    msg_shape = pltpu.VMEM((part, SENT, dim), BF16)
    head_wide = pltpu.VMEM((heads, toks, dim), F32)
    token_shape = pltpu.VMEM((8, 128), F32)

    def permute(x, pairs):
        return lax.ppermute(x, "ctx", pairs)

    rim = call(
        rim_kernel, "rim", pltpu.VMEM((2, WINDOW, heads, dim), BF16), win_k, values,
        raw=True, scratch=[pltpu.SemaphoreType.DMA((2,))],
    )
    far1, values_h, keys_t = call(
        first_states_kernel, "far1",
        (state_shape, pltpu.VMEM((heads, toks, dim), BF16), pltpu.VMEM((heads * DK, toks), F32)),
        keys, values, rim,
    )
    other1 = permute(far1, core_swap)

    def states(name, far, other, after):
        return call(functools.partial(states_kernel, far, other), name, state_shape,
                    keys_t, values_h, after)

    near1 = states("near1", 0, 1, far1)
    msg = call(chip_kernel, "chip", msg_shape, near1, other1)
    pair = call(open_kernel, "open", state_shape, permute(msg, pair_swap))
    far0, rim = call(
        far_rim_kernel, "far0", (state_shape, pltpu.VMEM(rim.shape, BF16)),
        keys_t, values_h, rim, msg,
    )
    rim_up = permute(rim, full([(i, i + 4) for i in range(3, count - 4, 4)], count))
    other0 = permute(far0, core_swap)
    near0 = states("near0", 0, 0, far0)
    first_table, second_table, add_table = pair_tables(part)
    phi_high, phi_low, gain = call(
        phi_kernel, "phi",
        (pltpu.VMEM((heads, toks, ROWS), BF16),) * 2 + (pltpu.VMEM((heads, 1, dim), F32),),
        queries, first_table, second_table, add_table, gain, near0,
        scratch=[pltpu.VMEM((4, toks, part * DK), BF16)],
    )
    total, msg = call(plane_kernel, "plane", (state_shape, msg_shape), near0, other0, pair, gain)
    groups = count // 4
    gots, limits, early = [], [], {}
    step = 1
    while step < groups:
        if step == 1:
            got = [permute(msg, full([(i, i + 4) for i in range(count - 4)], count))]
            limit = [(1, groups)]
            far_near1 = permute(near1, core_swap)
            num, den, again, token = call(
                intra_kernel, "intra", (head_wide, head_wide, msg_shape, token_shape),
                queries, keys, values_h, msg,
                scratch=[pltpu.VMEM((4, toks, part * DK), BF16)] * 2,
            )
            while 2 * step < groups:
                step *= 2
                early[step] = permute(
                    again, full([(i, i + 4 * step) for i in range(4)], count)
                )
            step = 1
        else:
            pairs = [(i, i + 4 * step) for i in range(4, count - 4 * step)]
            got = [permute(msg, full(pairs, count)), early[step]]
            limit = [(step + 1, groups), (step, step)]
        if step == 2:
            far_near0 = permute(near0, core_swap)
            rim = call(pick_kernel, "pick", pltpu.VMEM(rim.shape, BF16), rim, rim_up, msg)
            rim_prev = permute(rim, [(i, i - i % 4 + (i + 1) % 4) for i in range(count)])
            win, edge_q, edge_k, token = call(
                window_kernel, "window",
                (pltpu.VMEM((heads, toks - WINDOW, dim), F32),)
                + (pltpu.VMEM((heads, WINDOW, dim), BF16),) * 2 + (token_shape,),
                win_q, win_k, values_h, msg,
                scratch=[pltpu.VMEM((heads, toks, dim), BF16)] * 2,
            )
        gots.extend(got)
        limits.extend(limit)
        step *= 2
        if step < groups:
            total, msg = call(
                functools.partial(round_kernel, limit), "round", (state_shape, msg_shape),
                total, *got, token,
            )
    mine, msg = call(
        functools.partial(before_kernel, limits), "before", (state_shape, msg_shape),
        near0, other0, pair, *gots, token,
    )
    got = permute(msg, pair_swap)
    far_mine = permute(mine, core_swap)
    edge = call(edge_kernel, "edge", pltpu.VMEM((heads, WINDOW, dim), F32),
                edge_q, edge_k, values_h, rim_prev, msg,
                scratch=[pltpu.VMEM((heads, WINDOW, dim), BF16)] * 2)

    held = (phi_high, phi_low, num, den, edge, win, gain)
    square_shape = pltpu.VMEM((toks, dim), F32)
    mixed, squares = call(
        first_final_kernel, "final0", (head_wide, square_shape),
        mine, other0, far_mine, far_near0, *held,
    )
    mine = call(open_kernel, "open", state_shape, got, squares)
    got, mine, squares = lax.optimization_barrier((got, mine, squares))
    far_got = permute(got, core_swap)
    mixed, squares = call(
        functools.partial(next_final_kernel, 0), "final1", (head_wide, square_shape),
        mine, other1, *held, mixed, squares, aliases={9: 0},
    )
    mixed, squares = call(
        functools.partial(next_final_kernel, 1), "final2",
        (head_wide, pltpu.VMEM((8, toks), F32)),
        far_got, far_near1, *held, mixed, squares, aliases={9: 0},
    )
    others = [
        lax.ppermute(squares, "head", [(i, (i + k) % (peers + 1)) for i in range(peers + 1)])
        for k in range(1, peers + 1)
    ]
    return call(
        functools.partial(norm_kernel, peers), "norm",
        jax.ShapeDtypeStruct((toks, heads, dim), BF16),
        mixed, squares, *others,
    )


def solution(mesh):
    return jax.shard_map(
        on_device,
        mesh=mesh,
        in_specs=(
            P("ctx", "head"),
            P("ctx", "head"),
            P("ctx", "head", None),
            P("ctx", "head", None),
            P("ctx", "head", None),
            P("head", None),
        ),
        out_specs=P("ctx", "head", None),
        check_vma=False,
    )
```

time: 51.1 us -> 46 us (0.900)
  the two profiles are of different devices: /device:TPU:22 before, /device:TPU:0 now
where the time goes in v4:
time: 46 us; the launch traced here: 45.5 us
  Pallas kernels  19.2 us (42%)
  starting transfers between devices  14 us (30%)
  waiting for transfers between devices  11.7 us (25%)
    pallas_call x20, Pallas kernels, call(): pl.pallas_call(body, out_shape=outs, in_specs=[spec] * len(operands), out...  19.2 us
    ppermute x13, starting transfers between devices, permute(): return lax.ppermute(x, 'ctx', pairs)  12.4 us
    ppermute x13, waiting for transfers between devices, permute(): return lax.ppermute(x, 'ctx', pairs)  9.58 us
    ppermute x1, waiting for transfers between devices, on_device(): lax.ppermute(squares, 'head', [(i, (i + k) % (peers + 1)) for i in range(...  2.15 us
    ppermute x1, starting transfers between devices, on_device(): lax.ppermute(squares, 'head', [(i, (i + k) % (peers + 1)) for i in range(...  1.53 us
  transfers between devices with their start and end apart: 14, of which 7 were waited for; matrix products, arithmetic and copies ran while one was open for 0% of the time, Pallas kernels for 32%

profile of v4, /device:TPU:0, one launch (start us, length us, event | category | flops | bytes accessed | tf_op | source)
XLA Modules:
  0.0 45.5 jit_solution(15306110889289969725)
XLA Ops:
  0.0 0.0 copy-start
  0.0 0.0 copy-start.3
  0.0 1.1 %rim.1.after_ref.rim_ref = bf16[2,64,16,128]{3,2,1,0:T(8,128)(2,1)S(1)} custom-call(bf16[256,16,128]{2,1,0:T(8,128)(2,1)} %wk_ref.3, bf16[256,16,128]{2,1,0:T(8,128)(2,1)} %v_ref.3), custom_call_target="tpu_custom_call" | custom-call | flops 1150000000 | tf_op jit(solution)/shard_map/rim/pallas_call | solution.py:141
  1.2 0.2 copy-done
  1.4 0.0 copy-done.3
  1.4 0.7 %far1.1 = (f32[4,160,128]{2,1,0:T(8,128)S(1)}, bf16[16,256,128]{2,1,0:T(8,128)(2,1)S(1)}, f32[256,256]{1,0:T(8,128)S(1)}) custom-call(bf16[256,256]{1,0:T(8,128)(2,1)S(1)} %copy-done.3, bf16[256,16,128]{2,1,0:T(8,128)(2,1)S(1)} %copy-done, bf16[2,64,16,128]{3,2,1,0:T(8,128)(2,1)S(1)} %rim.1.after_ref.rim_ref), custom_call_target="tpu_custom_call" | custom-call | flops 1150000000 | tf_op jit(solution)/shard_map/far1/pallas_call | solution.py:141
  2.1 0.5 %collective-permute-start = (f32[4,160,128]{2,1,0:T(8,128)S(1)}, f32[4,160,128]{2,1,0:T(8,128)S(1)}, u32[]{:S(2)}, u32[]{:S(2)}) collective-permute-start(f32[4,160,128]{2,1,0:T(8,128)S(1)} %get-tuple-element.37.after_ref), channel_id=1, source_target_pairs={{0,2},{2,0},{4,6},{6,4},{8,10},{10,8},{12,14},{14,12},{16,18},{18,... | collective-permute-start | bytes 983048 | tf_op jit(solution)/shard_map/ppermute | solution.py:489
  2.6 0.4 near1.1.own_ref
  3.1 0.8 %collective-permute-done.other_ref.extra_ref = f32[4,160,128]{2,1,0:T(8,128)S(1)} collective-permute-done((f32[4,160,128]{2,1,0:T(8,128)S(1)}, f32[4,160,128]{2,1,0:T(8,128)S(1)}, u32[]{:S(2)}, u32[]{:S(2)}) %collective-permute-start) | collective-permute-done | bytes 327712 | tf_op jit(solution)/shard_map/ppermute | solution.py:489
  3.9 0.5 %far0.1 = (f32[4,160,128]{2,1,0:T(8,128)S(1)}, bf16[2,64,16,128]{3,2,1,0:T(8,128)(2,1)S(1)}) custom-call(f32[256,256]{1,0:T(8,128)S(1)} %get-tuple-element.35.kt_ref, bf16[16,256,128]{2,1,0:T(8,128)(2,1)S(1)} %get-tuple-element.36.vh_ref, bf16[2,64,16,128]{3,2,1,0:T(8,128)(2,1)S(1)} %rim.1.after_ref.rim_ref, bf16[4,192,128]{2,1,0:T(8,128)(2,1)S(1)} %chip.1.after_ref), custom_call_target="tpu_custom_call" | custom-call | flops 1150000000 | tf_op jit(solution)/shard_map/far0/pallas_call | solution.py:141
  4.4 3.0 %collective-permute-start.2 = (bf16[4,192,128]{2,1,0:T(8,128)(2,1)S(1)}, bf16[4,192,128]{2,1,0:T(8,128)(2,1)S(1)}, u32[]{:S(2)}, u32[]{:S(2)}) collective-permute-start(bf16[4,192,128]{2,1,0:T(8,128)(2,1)S(1)} %chip.1.after_ref), channel_id=1, source_target_pairs={{0,4},{2,6},{4,0},{6,2},{8,12},{10,14},{12,8},{14,10},{16,20},{18,... | collective-permute-start | bytes 589832 | tf_op jit(solution)/shard_map/ppermute | solution.py:489
  7.4 0.0 copy-start.4
  7.4 0.0 copy-start.5
  7.4 0.0 copy-start.6
  7.4 0.0 copy-start.7
  7.4 0.0 copy-start.8
  7.4 0.5 near0.1.after_ref.own_ref
  7.8 0.1 collective-permute-start.1
  7.9 0.5 %collective-permute-start.8 = (f32[4,160,128]{2,1,0:T(8,128)S(1)}, f32[4,160,128]{2,1,0:T(8,128)S(1)}, u32[]{:S(2)}, u32[]{:S(2)}) collective-permute-start(f32[4,160,128]{2,1,0:T(8,128)S(1)} %near0.1.after_ref.own_ref), channel_id=1, source_target_pairs={{0,2},{2,0},{4,6},{6,4},{8,10},{10,8},{12,14},{14,12},{16,18},{18,... | collective-permute-start | bytes 983048 | tf_op jit(solution)/shard_map/ppermute | solution.py:489
  8.4 0.7 %collective-permute-start.9 = (bf16[2,64,16,128]{3,2,1,0:T(8,128)(2,1)S(1)}, bf16[2,64,16,128]{3,2,1,0:T(8,128)(2,1)S(1)}, u32[]{:S(2)}, u32[]{:S(2)}) collective-permute-start(bf16[2,64,16,128]{3,2,1,0:T(8,128)(2,1)S(1)} %get-tuple-element.54.rim_ref), channel_id=1, source_target_pairs={{6,14},{14,22},{22,30},{0,0},{2,2},{4,4},{8,8},{10,10},{12,12},{16... | collective-permute-start | bytes 1572872 | tf_op jit(solution)/shard_map/ppermute | solution.py:489
  9.1 0.0 copy-done.4
  9.1 0.0 copy-done.5
  9.1 0.0 copy-done.6
  9.1 0.0 copy-done.7
  9.1 0.0 copy-done.8
  9.2 1.8 %phi.1 = (bf16[16,256,160]{2,1,0:T(8,128)(2,1)S(1)}, bf16[16,256,160]{2,1,0:T(8,128)(2,1)S(1)}, f32[16,1,128]{2,1,0:T(1,128)S(1)}) custom-call(bf16[256,256]{1,0:T(8,128)(2,1)S(1)} %copy-done.4, bf16[4,64,160]{2,1,0:T(8,128)(2,1)S(1)} %copy-done.6, bf16[4,64,160]{2,1,0:T(8,128)(2,1)S(1)} %copy-done.7, f32[8,160]{1,0:T(8,128)S(1)} %copy-done.8, ...), custom_call_target="tpu_custom_call" | custom-call | flops 2070000000 | tf_op jit(solution)/shard_map/phi/pallas_call | solution.py:141
  11.0 1.6 %collective-permute-done.2.got_ref = bf16[4,192,128]{2,1,0:T(8,128)(2,1)S(1)} collective-permute-done((bf16[4,192,128]{2,1,0:T(8,128)(2,1)S(1)}, bf16[4,192,128]{2,1,0:T(8,128)(2,1)S(1)}, u32[]{:S(2)}, u32[]{:S(2)}) %collective-permute-start.2) | collective-permute-done | bytes 196640 | tf_op jit(solution)/shard_map/ppermute | solution.py:489
  12.6 0.0 collective-permute-done.1.other_ref
  12.6 0.1 plane.1
  12.7 1.9 %collective-permute-start.3 = (bf16[4,192,128]{2,1,0:T(8,128)(2,1)S(1)}, bf16[4,192,128]{2,1,0:T(8,128)(2,1)S(1)}, u32[]{:S(2)}, u32[]{:S(2)}) collective-permute-start(bf16[4,192,128]{2,1,0:T(8,128)(2,1)S(1)} %get-tuple-element.40.after_ref), channel_id=1, source_target_pairs={{0,8},{2,10},{4,12},{6,14},{8,16},{10,18},{12,20},{14,22},{16,24},... | collective-permute-start | bytes 589832 | tf_op jit(solution)/shard_map/ppermute | solution.py:489
  14.5 2.9 %intra.1 = (f32[16,256,128]{2,1,0:T(8,128)S(1)}, f32[16,256,128]{2,1,0:T(8,128)S(1)}, bf16[4,192,128]{2,1,0:T(8,128)(2,1)S(1)}, f32[8,128]{1,0:T(8,128)S(1)}) custom-call(bf16[256,256]{1,0:T(8,128)(2,1)S(1)} %copy-done.4, bf16[256,256]{1,0:T(8,128)(2,1)S(1)} %copy-done.3, bf16[16,256,128]{2,1,0:T(8,128)(2,1)S(1)} %get-tuple-element.36.vh_ref, ...), custom_call_target="tpu_custom_call" | custom-call | flops 3220000000 | tf_op jit(solution)/shard_map/intra/pallas_call | solution.py:141
  17.4 4.5 %collective-permute-start.5 = (bf16[4,192,128]{2,1,0:T(8,128)(2,1)S(1)}, bf16[4,192,128]{2,1,0:T(8,128)(2,1)S(1)}, u32[]{:S(2)}, u32[]{:S(2)}) collective-permute-start(bf16[4,192,128]{2,1,0:T(8,128)(2,1)S(1)} %get-tuple-element.44), channel_id=1, source_target_pairs={{0,16},{2,18},{4,20},{6,22},{8,8},{10,10},{12,12},{14,14},{24,24},... | collective-permute-start | bytes 589832 | tf_op jit(solution)/shard_map/ppermute | solution.py:489
  21.9 0.0 collective-permute-done.3.rest_0_
  21.9 0.0 copy-start.1
  21.9 0.0 copy-start.2
  21.9 0.8 %round.1 = (f32[4,160,128]{2,1,0:T(8,128)}, bf16[4,192,128]{2,1,0:T(8,128)(2,1)S(1)}) custom-call(f32[4,160,128]{2,1,0:T(8,128)S(1)} %get-tuple-element.41.total_ref, bf16[4,192,128]{2,1,0:T(8,128)(2,1)S(1)} %collective-permute-done.3.rest_0_, f32[8,128]{1,0:T(8,128)S(1)} %get-tuple-element.42.rest_1_), custom_call_target="tpu_custom_call" | custom-call | flops 1150000000 | tf_op jit(solution)/shard_map/round/pallas_call | solution.py:141
  22.7 0.7 %collective-permute-start.4 = (bf16[4,192,128]{2,1,0:T(8,128)(2,1)S(1)}, bf16[4,192,128]{2,1,0:T(8,128)(2,1)S(1)}, u32[]{:S(2)}, u32[]{:S(2)}) collective-permute-start(bf16[4,192,128]{2,1,0:T(8,128)(2,1)S(1)} %get-tuple-element.43.after_ref), channel_id=1, source_target_pairs={{8,24},{10,26},{12,28},{14,30},{0,0},{2,2},{4,4},{6,6},{16,16},{18... | collective-permute-start | bytes 589832 | tf_op jit(solution)/shard_map/ppermute | solution.py:489
  23.4 0.0 collective-permute-done.9.got_ref
  23.4 0.1 pick.1
  23.5 0.1 collective-permute-start.10
  23.5 0.0 copy-done.1
  23.5 0.0 copy-done.2
  23.6 3.5 %window.1 = (f32[16,192,128]{2,1,0:T(8,128)S(1)}, bf16[16,64,128]{2,1,0:T(8,128)(2,1)S(1)}, bf16[16,64,128]{2,1,0:T(8,128)(2,1)S(1)}, f32[8,128]{1,0:T(8,128)S(1)}) custom-call(bf16[256,16,128]{2,1,0:T(8,128)(2,1)S(1)} %copy-done.2, bf16[256,16,128]{2,1,0:T(8,128)(2,1)S(1)} %copy-done.1, bf16[16,256,128]{2,1,0:T(8,128)(2,1)S(1)} %get-tuple-element.36.vh_ref, ...), custom_call_target="tpu_custom_call" | custom-call | flops 4024999936 | tf_op jit(solution)/shard_map/window/pallas_call | solution.py:141
  27.1 3.2 %collective-permute-done.5.rest_2_ = bf16[4,192,128]{2,1,0:T(8,128)(2,1)S(1)} collective-permute-done((bf16[4,192,128]{2,1,0:T(8,128)(2,1)S(1)}, bf16[4,192,128]{2,1,0:T(8,128)(2,1)S(1)}, u32[]{:S(2)}, u32[]{:S(2)}) %collective-permute-start.5) | collective-permute-done | bytes 196640 | tf_op jit(solution)/shard_map/ppermute | solution.py:489
  30.2 0.0 collective-permute-done.4.rest_1_
  30.2 0.2 before.1
  30.4 0.1 collective-permute-start.7
  30.5 0.5 %collective-permute-start.12 = (f32[4,160,128]{2,1,0:T(8,128)S(1)}, f32[4,160,128]{2,1,0:T(8,128)S(1)}, u32[]{:S(2)}, u32[]{:S(2)}) collective-permute-start(f32[4,160,128]{2,1,0:T(8,128)S(1)} %near1.1.own_ref), channel_id=1, source_target_pairs={{0,2},{2,0},{4,6},{6,4},{8,10},{10,8},{12,14},{14,12},{16,18},{18,... | collective-permute-start | bytes 983048 | tf_op jit(solution)/shard_map/ppermute | solution.py:489
  31.0 0.0 collective-permute-start.6
  31.0 2.1 %collective-permute-done.10.rim_ref = bf16[2,64,16,128]{3,2,1,0:T(8,128)(2,1)S(1)} collective-permute-done((bf16[2,64,16,128]{3,2,1,0:T(8,128)(2,1)S(1)}, bf16[2,64,16,128]{3,2,1,0:T(8,128)(2,1)S(1)}, u32[]{:S(2)}, u32[]{:S(2)}) %collective-permute-start.10) | collective-permute-done | bytes 524320 | tf_op jit(solution)/shard_map/ppermute | solution.py:489
  33.1 2.1 %edge.1.rest_4_ = f32[16,64,128]{2,1,0:T(8,128)S(1)} custom-call(bf16[16,64,128]{2,1,0:T(8,128)(2,1)S(1)} %get-tuple-element.52.q_ref, bf16[16,64,128]{2,1,0:T(8,128)(2,1)S(1)} %get-tuple-element.53.k_ref, bf16[16,256,128]{2,1,0:T(8,128)(2,1)S(1)} %get-tuple-element.36.vh_ref, bf16[2,64,16,128]{3,2,1,0:T(8,128)(2,1)S(1)} %collective-permute-done.10.rim_ref, ...), custom_call_target="tpu_custom_call" | custom-call | flops 1150000000 | tf_op jit(solution)/shard_map/edge/pallas_call | solution.py:141
  35.3 0.0 collective-permute-done.8.extra_ref
  35.3 0.0 collective-permute-done.7.far_ref
  35.3 1.4 %final0.1 = (f32[16,256,128]{2,1,0:T(8,128)S(1)}, f32[256,128]{1,0:T(8,128)S(1)}) custom-call(f32[4,160,128]{2,1,0:T(8,128)S(1)} %get-tuple-element.47.mine_ref, f32[4,160,128]{2,1,0:T(8,128)S(1)} %collective-permute-done.1.other_ref, f32[4,160,128]{2,1,0:T(8,128)S(1)} %collective-permute-done.7.far_ref, ...), custom_call_target="tpu_custom_call" | custom-call | flops 1150000000 | tf_op jit(solution)/shard_map/final0/pallas_call | solution.py:141
  36.6 1.2 %collective-permute-done.6.got_ref = bf16[4,192,128]{2,1,0:T(8,128)(2,1)S(1)} collective-permute-done((bf16[4,192,128]{2,1,0:T(8,128)(2,1)S(1)}, bf16[4,192,128]{2,1,0:T(8,128)(2,1)S(1)}, u32[]{:S(2)}, u32[]{:S(2)}) %collective-permute-start.6) | collective-permute-done | bytes 196640 | tf_op jit(solution)/shard_map/ppermute | solution.py:489
  37.9 0.1 collective-permute-start.11
  38.0 0.8 %final1.1 = (f32[16,256,128]{2,1,0:T(8,128)S(1)}, f32[256,128]{1,0:T(8,128)S(1)}) custom-call(f32[4,160,128]{2,1,0:T(8,128)S(1)} %open.3.base_ref, f32[4,160,128]{2,1,0:T(8,128)S(1)} %collective-permute-done.other_ref.extra_ref, bf16[16,256,160]{2,1,0:T(8,128)(2,1)S(1)} %get-tuple-element.48.rest_0_, ...), custom_call_target="tpu_custom_call", output_to_operand_aliasing={{0}: (9, {})} | custom-call | flops 1150000000 | tf_op jit(solution)/shard_map/final1/pallas_call | solution.py:141
  38.8 0.0 collective-permute-done.12.extra_ref
  38.8 0.6 %collective-permute-done.11.base_ref = bf16[4,192,128]{2,1,0:T(8,128)(2,1)S(1)} collective-permute-done((bf16[4,192,128]{2,1,0:T(8,128)(2,1)S(1)}, bf16[4,192,128]{2,1,0:T(8,128)(2,1)S(1)}, u32[]{:S(2)}, u32[]{:S(2)}) %collective-permute-start.11) | collective-permute-done | bytes 196640 | tf_op jit(solution)/shard_map/ppermute | solution.py:489
  39.4 1.1 %final2.1 = (f32[16,256,128]{2,1,0:T(8,128)S(1)}, f32[8,256]{1,0:T(8,128)S(1)}) custom-call(bf16[4,192,128]{2,1,0:T(8,128)(2,1)S(1)} %collective-permute-done.11.base_ref, f32[4,160,128]{2,1,0:T(8,128)S(1)} %collective-permute-done.12.extra_ref, bf16[16,256,160]{2,1,0:T(8,128)(2,1)S(1)} %get-tuple-element.48.rest_0_, ...), custom_call_target="tpu_custom_call", output_to_operand_aliasing={{0}: (9, {})} | custom-call | flops 1150000000 | tf_op jit(solution)/shard_map/final2/pallas_call | solution.py:141
  40.5 1.5 %collective-permute-start.13 = (f32[8,256]{1,0:T(8,128)S(1)}, f32[8,256]{1,0:T(8,128)S(1)}, u32[]{:S(2)}, u32[]{:S(2)}) collective-permute-start(f32[8,256]{1,0:T(8,128)S(1)} %get-tuple-element.64.sq_ref), channel_id=1, source_target_pairs={{0,1},{1,0},{2,3},{3,2},{4,5},{5,4},{6,7},{7,6},{8,9},{9,8},{10,11... | collective-permute-start | bytes 24584 | tf_op jit(solution)/shard_map/ppermute | solution.py:595
  42.0 2.2 %collective-permute-done.13.rest_0_ = f32[8,256]{1,0:T(8,128)S(1)} collective-permute-done((f32[8,256]{1,0:T(8,128)S(1)}, f32[8,256]{1,0:T(8,128)S(1)}, u32[]{:S(2)}, u32[]{:S(2)}) %collective-permute-start.13) | collective-permute-done | bytes 8224 | tf_op jit(solution)/shard_map/ppermute | solution.py:595
  44.2 1.4 %norm.1 = bf16[256,16,128]{2,1,0:T(8,128)(2,1)} custom-call(f32[16,256,128]{2,1,0:T(8,128)S(1)} %get-tuple-element.63.mixed_ref, f32[8,256]{1,0:T(8,128)S(1)} %get-tuple-element.64.sq_ref, f32[8,256]{1,0:T(8,128)S(1)} %collective-permute-done.13.rest_0_), custom_call_target="tpu_custom_call" | custom-call | flops 1150000000 | tf_op jit(solution)/shard_map/norm/pallas_call | solution.py:141
  (3 shorter events, 0.1 us)
Async XLA Ops:
  0.0 1.4 %copy-start = (bf16[256,16,128]{2,1,0:T(8,128)(2,1)S(1)}, bf16[256,16,128]{2,1,0:T(8,128)(2,1)}, u32[]{:S(2)}) copy-start(bf16[256,16,128]{2,1,0:T(8,128)(2,1)} %v_ref.3) | copy-start | bytes 3145732
  0.0 1.4 %copy-start.3 = (bf16[256,256]{1,0:T(8,128)(2,1)S(1)}, bf16[256,256]{1,0:T(8,128)(2,1)}, u32[]{:S(2)}) copy-start(bf16[256,256]{1,0:T(8,128)(2,1)} %k_ref.1) | copy-start | bytes 393220
  2.1 1.8 %collective-permute-start = (f32[4,160,128]{2,1,0:T(8,128)S(1)}, f32[4,160,128]{2,1,0:T(8,128)S(1)}, u32[]{:S(2)}, u32[]{:S(2)}) collective-permute-start(f32[4,160,128]{2,1,0:T(8,128)S(1)} %get-tuple-element.37.after_ref), channel_id=1, source_target_pairs={{0,2},{2,0},{4,6},{6,4},{8,10},{10,8},{12,14},{14,12},{16,18},{18,... | collective-permute-start | bytes 983048 | tf_op jit(solution)/shard_map/ppermute | solution.py:489
  4.4 8.2 %collective-permute-start.2 = (bf16[4,192,128]{2,1,0:T(8,128)(2,1)S(1)}, bf16[4,192,128]{2,1,0:T(8,128)(2,1)S(1)}, u32[]{:S(2)}, u32[]{:S(2)}) collective-permute-start(bf16[4,192,128]{2,1,0:T(8,128)(2,1)S(1)} %chip.1.after_ref), channel_id=1, source_target_pairs={{0,4},{2,6},{4,0},{6,2},{8,12},{10,14},{12,8},{14,10},{16,20},{18,... | collective-permute-start | bytes 589832 | tf_op jit(solution)/shard_map/ppermute | solution.py:489
  7.4 1.8 %copy-start.4 = (bf16[256,256]{1,0:T(8,128)(2,1)S(1)}, bf16[256,256]{1,0:T(8,128)(2,1)}, u32[]{:S(2)}) copy-start(bf16[256,256]{1,0:T(8,128)(2,1)} %q_ref.3) | copy-start | bytes 393220
  7.4 1.8 %copy-start.5 = (bf16[16,128]{1,0:T(8,128)(2,1)S(1)}, bf16[16,128]{1,0:T(8,128)(2,1)}, u32[]{:S(2)}) copy-start(bf16[16,128]{1,0:T(8,128)(2,1)} %gain_ref.1) | copy-start | bytes 12292
  7.4 1.8 %copy-start.6 = (bf16[4,64,160]{2,1,0:T(8,128)(2,1)S(1)}, bf16[4,64,160]{2,1,0:T(8,128)(2,1)}, u32[]{:S(2)}) copy-start(bf16[4,64,160]{2,1,0:T(8,128)(2,1)} %constant.6.clone.e1_ref) | copy-start | bytes 245764
  7.4 1.8 %copy-start.7 = (bf16[4,64,160]{2,1,0:T(8,128)(2,1)S(1)}, bf16[4,64,160]{2,1,0:T(8,128)(2,1)}, u32[]{:S(2)}) copy-start(bf16[4,64,160]{2,1,0:T(8,128)(2,1)} %constant.7.clone.e2_ref) | copy-start | bytes 245764
  7.4 1.8 %copy-start.8 = (f32[8,160]{1,0:T(8,128)S(1)}, f32[8,160]{1,0:T(8,128)}, u32[]{:S(2)}) copy-start(f32[8,160]{1,0:T(8,128)} %constant.8.clone.add_ref) | copy-start | bytes 15364
  7.8 4.8 %collective-permute-start.1 = (f32[4,160,128]{2,1,0:T(8,128)S(1)}, f32[4,160,128]{2,1,0:T(8,128)S(1)}, u32[]{:S(2)}, u32[]{:S(2)}) collective-permute-start(f32[4,160,128]{2,1,0:T(8,128)S(1)} %get-tuple-element.38.after_ref), channel_id=1, source_target_pairs={{0,2},{2,0},{4,6},{6,4},{8,10},{10,8},{12,14},{14,12},{16,18},{18,... | collective-permute-start | bytes 983048 | tf_op jit(solution)/shard_map/ppermute | solution.py:489
  7.9 27.3 %collective-permute-start.8 = (f32[4,160,128]{2,1,0:T(8,128)S(1)}, f32[4,160,128]{2,1,0:T(8,128)S(1)}, u32[]{:S(2)}, u32[]{:S(2)}) collective-permute-start(f32[4,160,128]{2,1,0:T(8,128)S(1)} %near0.1.after_ref.own_ref), channel_id=1, source_target_pairs={{0,2},{2,0},{4,6},{6,4},{8,10},{10,8},{12,14},{14,12},{16,18},{18,... | collective-permute-start | bytes 983048 | tf_op jit(solution)/shard_map/ppermute | solution.py:489
  8.4 15.0 %collective-permute-start.9 = (bf16[2,64,16,128]{3,2,1,0:T(8,128)(2,1)S(1)}, bf16[2,64,16,128]{3,2,1,0:T(8,128)(2,1)S(1)}, u32[]{:S(2)}, u32[]{:S(2)}) collective-permute-start(bf16[2,64,16,128]{3,2,1,0:T(8,128)(2,1)S(1)} %get-tuple-element.54.rim_ref), channel_id=1, source_target_pairs={{6,14},{14,22},{22,30},{0,0},{2,2},{4,4},{8,8},{10,10},{12,12},{16... | collective-permute-start | bytes 1572872 | tf_op jit(solution)/shard_map/ppermute | solution.py:489
  12.7 9.3 %collective-permute-start.3 = (bf16[4,192,128]{2,1,0:T(8,128)(2,1)S(1)}, bf16[4,192,128]{2,1,0:T(8,128)(2,1)S(1)}, u32[]{:S(2)}, u32[]{:S(2)}) collective-permute-start(bf16[4,192,128]{2,1,0:T(8,128)(2,1)S(1)} %get-tuple-element.40.after_ref), channel_id=1, source_target_pairs={{0,8},{2,10},{4,12},{6,14},{8,16},{10,18},{12,20},{14,22},{16,24},... | collective-permute-start | bytes 589832 | tf_op jit(solution)/shard_map/ppermute | solution.py:489
  17.4 12.8 %collective-permute-start.5 = (bf16[4,192,128]{2,1,0:T(8,128)(2,1)S(1)}, bf16[4,192,128]{2,1,0:T(8,128)(2,1)S(1)}, u32[]{:S(2)}, u32[]{:S(2)}) collective-permute-start(bf16[4,192,128]{2,1,0:T(8,128)(2,1)S(1)} %get-tuple-element.44), channel_id=1, source_target_pairs={{0,16},{2,18},{4,20},{6,22},{8,8},{10,10},{12,12},{14,14},{24,24},... | collective-permute-start | bytes 589832 | tf_op jit(solution)/shard_map/ppermute | solution.py:489
  21.9 1.6 %copy-start.1 = (bf16[256,16,128]{2,1,0:T(8,128)(2,1)S(1)}, bf16[256,16,128]{2,1,0:T(8,128)(2,1)}, u32[]{:S(2)}) copy-start(bf16[256,16,128]{2,1,0:T(8,128)(2,1)} %wk_ref.3) | copy-start | bytes 3145732
  21.9 1.7 %copy-start.2 = (bf16[256,16,128]{2,1,0:T(8,128)(2,1)S(1)}, bf16[256,16,128]{2,1,0:T(8,128)(2,1)}, u32[]{:S(2)}) copy-start(bf16[256,16,128]{2,1,0:T(8,128)(2,1)} %wq_ref.1) | copy-start | bytes 3145732
  22.7 7.5 %collective-permute-start.4 = (bf16[4,192,128]{2,1,0:T(8,128)(2,1)S(1)}, bf16[4,192,128]{2,1,0:T(8,128)(2,1)S(1)}, u32[]{:S(2)}, u32[]{:S(2)}) collective-permute-start(bf16[4,192,128]{2,1,0:T(8,128)(2,1)S(1)} %get-tuple-element.43.after_ref), channel_id=1, source_target_pairs={{8,24},{10,26},{12,28},{14,30},{0,0},{2,2},{4,4},{6,6},{16,16},{18... | collective-permute-start | bytes 589832 | tf_op jit(solution)/shard_map/ppermute | solution.py:489
  23.5 9.7 %collective-permute-start.10 = (bf16[2,64,16,128]{3,2,1,0:T(8,128)(2,1)S(1)}, bf16[2,64,16,128]{3,2,1,0:T(8,128)(2,1)S(1)}, u32[]{:S(2)}, u32[]{:S(2)}) collective-permute-start(bf16[2,64,16,128]{3,2,1,0:T(8,128)(2,1)S(1)} %pick.1), channel_id=1, source_target_pairs={{0,2},{2,4},{4,6},{6,0},{8,10},{10,12},{12,14},{14,8},{16,18},{18,... | collective-permute-start | bytes 1572872 | tf_op jit(solution)/shard_map/ppermute | solution.py:489
  30.4 4.9 %collective-permute-start.7 = (f32[4,160,128]{2,1,0:T(8,128)S(1)}, f32[4,160,128]{2,1,0:T(8,128)S(1)}, u32[]{:S(2)}, u32[]{:S(2)}) collective-permute-start(f32[4,160,128]{2,1,0:T(8,128)S(1)} %get-tuple-element.47.mine_ref), channel_id=1, source_target_pairs={{0,2},{2,0},{4,6},{6,4},{8,10},{10,8},{12,14},{14,12},{16,18},{18,... | collective-permute-start | bytes 983048 | tf_op jit(solution)/shard_map/ppermute | solution.py:489
  30.5 8.3 %collective-permute-start.12 = (f32[4,160,128]{2,1,0:T(8,128)S(1)}, f32[4,160,128]{2,1,0:T(8,128)S(1)}, u32[]{:S(2)}, u32[]{:S(2)}) collective-permute-start(f32[4,160,128]{2,1,0:T(8,128)S(1)} %near1.1.own_ref), channel_id=1, source_target_pairs={{0,2},{2,0},{4,6},{6,4},{8,10},{10,8},{12,14},{14,12},{16,18},{18,... | collective-permute-start | bytes 983048 | tf_op jit(solution)/shard_map/ppermute | solution.py:489
  31.0 6.9 %collective-permute-start.6 = (bf16[4,192,128]{2,1,0:T(8,128)(2,1)S(1)}, bf16[4,192,128]{2,1,0:T(8,128)(2,1)S(1)}, u32[]{:S(2)}, u32[]{:S(2)}) collective-permute-start(bf16[4,192,128]{2,1,0:T(8,128)(2,1)S(1)} %get-tuple-element.46.after_ref), channel_id=1, source_target_pairs={{0,4},{2,6},{4,0},{6,2},{8,12},{10,14},{12,8},{14,10},{16,20},{18,... | collective-permute-start | bytes 589832 | tf_op jit(solution)/shard_map/ppermute | solution.py:489
  37.9 1.5 %collective-permute-start.11 = (bf16[4,192,128]{2,1,0:T(8,128)(2,1)S(1)}, bf16[4,192,128]{2,1,0:T(8,128)(2,1)S(1)}, u32[]{:S(2)}, u32[]{:S(2)}) collective-permute-start(bf16[4,192,128]{2,1,0:T(8,128)(2,1)S(1)} %collective-permute-done.6.got_ref), channel_id=1, source_target_pairs={{0,2},{2,0},{4,6},{6,4},{8,10},{10,8},{12,14},{14,12},{16,18},{18,... | collective-permute-start | bytes 589832 | tf_op jit(solution)/shard_map/ppermute | solution.py:489
  40.5 3.7 %collective-permute-start.13 = (f32[8,256]{1,0:T(8,128)S(1)}, f32[8,256]{1,0:T(8,128)S(1)}, u32[]{:S(2)}, u32[]{:S(2)}) collective-permute-start(f32[8,256]{1,0:T(8,128)S(1)} %get-tuple-element.64.sq_ref), channel_id=1, source_target_pairs={{0,1},{1,0},{2,3},{3,2},{4,5},{5,4},{6,7},{7,6},{8,9},{9,8},{10,11... | collective-permute-start | bytes 24584 | tf_op jit(solution)/shard_map/ppermute | solution.py:595

commit v5 on v4

--- a/solution.py
+++ b/solution.py
@@ -128,7 +128,7 @@
 VMEM_SPEC = pl.BlockSpec(memory_space=pltpu.VMEM)
 VMEM_LIMIT = 12 << 20
 FLOPS_PER_US = 1_150_000_000
-EXPECTED_US = {"phi": 1.8, "intra": 2.8, "window": 3.5, "chip": 0.1, "plane": 0.1, "open": 12.0, "pick": 0.1}
+EXPECTED_US = {"phi": 1.8, "intra": 2.8, "window": 3.5, "chip": 0.1, "plane": 0.1, "open": 12.0, "pick": 60.0, "turn": 60.0}
 
 
 def call(body, name, outs, *operands, scratch=(), raw=False, aliases=None):
@@ -202,11 +202,6 @@
     put_states(out_ref, far, other, kt_ref, vh_ref)
 
 
-def far_rim_kernel(kt_ref, vh_ref, rim_ref, after_ref, out_ref, rim_out_ref):
-    rim_out_ref[...] = rim_ref[...]
-    put_states(out_ref, 1, 0, kt_ref, vh_ref)
-
-
 def chip_kernel(own_ref, other_ref, msg_ref):
     def one(j):
         pack(msg_ref.at[j], own_ref[j] + other_ref[j])
@@ -257,8 +252,9 @@
     each(own_ref.shape[0], one)
 
 
-def pick_kernel(rim_ref, got_ref, after_ref, out_ref):
+def pick_kernel(rim_ref, got_ref, msg_ref, out_ref, again_ref):
     last = lax.axis_index("ctx") % 4 == 3
+    again_ref[...] = msg_ref[...]
 
     @pl.when(last)
     def _():
@@ -291,9 +287,8 @@
     lax.fori_loop(0, 4, one, 0)
 
 
-def intra_kernel(q_ref, k_ref, vh_ref, after_ref,
-                 num_ref, den_ref, again_ref, token_ref, q4_ref, k4_ref):
-    again_ref[...] = after_ref[...]
+def intra_kernel(q_ref, k_ref, vh_ref, rim_ref, after_ref,
+                 num_ref, den_ref, token_ref, q4_ref, k4_ref):
     token_ref[...] = jnp.zeros_like(token_ref)
     heads, toks, dim = vh_ref.shape
     part = heads // 4
@@ -349,15 +344,24 @@
     return (col > row) & (col <= row + WINDOW), col
 
 
-def window_kernel(wq_ref, wk_ref, vh_ref, after_ref,
-                  win_ref, edge_q_ref, edge_k_ref, token_ref, qh_ref, kh_ref):
+def by_head_kernel(wq_ref, wk_ref, after_ref, qh_ref, kh_ref, token_ref):
+    token_ref[...] = jnp.zeros_like(token_ref)
+    qh_ref[...] = jnp.swapaxes(wq_ref[...], 0, 1)
+    kh_ref[...] = jnp.swapaxes(wk_ref[...], 0, 1)
+
+
+def turn_kernel(rim_ref, after_ref, k_ref, v_ref):
+    k_ref[...] = jnp.swapaxes(rim_ref[0], 0, 1)
+    v_ref[...] = jnp.swapaxes(rim_ref[1], 0, 1)
+
+
+def window_kernel(qh_ref, kh_ref, vh_ref, near0_ref, near1_ref, after_ref,
+                  win_ref, nears_ref, token_ref):
     heads, toks, dim = vh_ref.shape
     part = heads // 4
     token_ref[...] = jnp.zeros_like(token_ref)
-    qh_ref[...] = jnp.swapaxes(wq_ref[...], 0, 1)
-    kh_ref[...] = jnp.swapaxes(wk_ref[...], 0, 1)
-    edge_q_ref[...] = qh_ref[:, :WINDOW]
-    edge_k_ref[...] = kh_ref[:, :WINDOW]
+    nears_ref[0] = near0_ref[...]
+    nears_ref[1] = near1_ref[...]
     band, _ = band_mask()
     blocks = toks // WINDOW - 1
 
@@ -384,11 +388,9 @@
     lax.fori_loop(0, 4, one, 0)
 
 
-def edge_kernel(q_ref, k_ref, vh_ref, rim_ref, after_ref, out_ref, rk_ref, rv_ref):
+def edge_kernel(qh_ref, kh_ref, vh_ref, rk_ref, rv_ref, after_ref, out_ref):
     heads, _, dim = vh_ref.shape
     part = heads // 4
-    rk_ref[...] = jnp.swapaxes(rim_ref[0], 0, 1)
-    rv_ref[...] = jnp.swapaxes(rim_ref[1], 0, 1)
     band, col = band_mask()
     valid = band & ((col >= WINDOW) | (lax.axis_index("ctx") > 0))
 
@@ -396,8 +398,8 @@
         scores = []
         for j in range(part):
             head = r * part + j
-            k = jnp.concatenate([rk_ref[head], k_ref[head]], axis=0)
-            sc = dot(q_ref[head], k, NT)
+            k = jnp.concatenate([rk_ref[head], kh_ref[head, :WINDOW]], axis=0)
+            sc = dot(qh_ref[head, :WINDOW], k, NT)
             scores.append(jnp.where(valid, sc / math.sqrt(dim), -1e30))
         weights = softmax_blocks(scores)
         for j in range(part):
@@ -445,13 +447,15 @@
     part = mine_ref.shape[0]
     squares = jnp.zeros(sq_ref.shape, F32)
     squares = mix(first_head(0, 0, part), mine_ref, other_ref, *held, mixed_ref, squares)
-    squares = mix(first_head(1, 0, part), far_ref, extra_ref, *held, mixed_ref, squares)
+    squares = mix(first_head(1, 0, part), far_ref, extra_ref.at[0], *held, mixed_ref, squares)
     sq_ref[...] = squares
 
 
 def next_final_kernel(far, base_ref, extra_ref, *rest):
     held, (squares_ref, mixed_ref, sq_ref) = rest[:7], rest[-3:]
     first = first_head(far, 1, base_ref.shape[0])
+    if far == 1:
+        extra_ref = extra_ref.at[1]
     squares = mix(first, base_ref, extra_ref, *held, mixed_ref, squares_ref[...])
     if far == 0:
         sq_ref[...] = squares
@@ -492,6 +496,7 @@
         rim_kernel, "rim", pltpu.VMEM((2, WINDOW, heads, dim), BF16), win_k, values,
         raw=True, scratch=[pltpu.SemaphoreType.DMA((2,))],
     )
+    rim_up = permute(rim, full([(i, i + 4) for i in range(3, count - 4, 4)], count))
     far1, values_h, keys_t = call(
         first_states_kernel, "far1",
         (state_shape, pltpu.VMEM((heads, toks, dim), BF16), pltpu.VMEM((heads * DK, toks), F32)),
@@ -506,11 +511,7 @@
     near1 = states("near1", 0, 1, far1)
     msg = call(chip_kernel, "chip", msg_shape, near1, other1)
     pair = call(open_kernel, "open", state_shape, permute(msg, pair_swap))
-    far0, rim = call(
-        far_rim_kernel, "far0", (state_shape, pltpu.VMEM(rim.shape, BF16)),
-        keys_t, values_h, rim, msg,
-    )
-    rim_up = permute(rim, full([(i, i + 4) for i in range(3, count - 4, 4)], count))
+    far0 = states("far0", 1, 0, msg)
     other0 = permute(far0, core_swap)
     near0 = states("near0", 0, 0, far0)
     first_table, second_table, add_table = pair_tables(part)
@@ -520,7 +521,15 @@
         queries, first_table, second_table, add_table, gain, near0,
         scratch=[pltpu.VMEM((4, toks, part * DK), BF16)],
     )
-    total, msg = call(plane_kernel, "plane", (state_shape, msg_shape), near0, other0, pair, gain)
+    wq_h, wk_h, token = call(
+        by_head_kernel, "by_head",
+        (pltpu.VMEM((heads, toks, dim), BF16),) * 2 + (token_shape,), win_q, win_k, gain,
+    )
+    total, msg = call(plane_kernel, "plane", (state_shape, msg_shape), near0, other0, pair, token)
+    rim, again = call(
+        pick_kernel, "pick", (pltpu.VMEM(rim.shape, BF16), msg_shape), rim, rim_up, msg
+    )
+    rim_prev = permute(rim, [(i, i - i % 4 + (i + 1) % 4) for i in range(count)])
     groups = count // 4
     gots, limits, early = [], [], {}
     step = 1
@@ -528,10 +537,9 @@
         if step == 1:
             got = [permute(msg, full([(i, i + 4) for i in range(count - 4)], count))]
             limit = [(1, groups)]
-            far_near1 = permute(near1, core_swap)
-            num, den, again, token = call(
-                intra_kernel, "intra", (head_wide, head_wide, msg_shape, token_shape),
-                queries, keys, values_h, msg,
+            num, den, token = call(
+                intra_kernel, "intra", (head_wide, head_wide, token_shape),
+                queries, keys, values_h, rim, msg,
                 scratch=[pltpu.VMEM((4, toks, part * DK), BF16)] * 2,
             )
             while 2 * step < groups:
@@ -545,15 +553,14 @@
             got = [permute(msg, full(pairs, count)), early[step]]
             limit = [(step + 1, groups), (step, step)]
         if step == 2:
-            far_near0 = permute(near0, core_swap)
-            rim = call(pick_kernel, "pick", pltpu.VMEM(rim.shape, BF16), rim, rim_up, msg)
-            rim_prev = permute(rim, [(i, i - i % 4 + (i + 1) % 4) for i in range(count)])
-            win, edge_q, edge_k, token = call(
+            win, nears, token = call(
                 window_kernel, "window",
-                (pltpu.VMEM((heads, toks - WINDOW, dim), F32),)
-                + (pltpu.VMEM((heads, WINDOW, dim), BF16),) * 2 + (token_shape,),
-                win_q, win_k, values_h, msg,
-                scratch=[pltpu.VMEM((heads, toks, dim), BF16)] * 2,
+                (pltpu.VMEM((heads, toks - WINDOW, dim), F32),
+                 pltpu.VMEM((2, part, ROWS, dim), F32), token_shape),
+                wq_h, wk_h, values_h, near0, near1, msg,
+            )
+            rim_k, rim_v = call(
+                turn_kernel, "turn", (pltpu.VMEM((heads, WINDOW, dim), BF16),) * 2, rim_prev, token
             )
         gots.extend(got)
         limits.extend(limit)
@@ -569,15 +576,15 @@
     )
     got = permute(msg, pair_swap)
     far_mine = permute(mine, core_swap)
+    far_nears = permute(nears, core_swap)
     edge = call(edge_kernel, "edge", pltpu.VMEM((heads, WINDOW, dim), F32),
-                edge_q, edge_k, values_h, rim_prev, msg,
-                scratch=[pltpu.VMEM((heads, WINDOW, dim), BF16)] * 2)
+                wq_h, wk_h, values_h, rim_k, rim_v, msg)
 
     held = (phi_high, phi_low, num, den, edge, win, gain)
     square_shape = pltpu.VMEM((toks, dim), F32)
     mixed, squares = call(
         first_final_kernel, "final0", (head_wide, square_shape),
-        mine, other0, far_mine, far_near0, *held,
+        mine, other0, far_mine, far_nears, *held,
     )
     mine = call(open_kernel, "open", state_shape, got, squares)
     got, mine, squares = lax.optimization_barrier((got, mine, squares))
@@ -589,7 +596,7 @@
     mixed, squares = call(
         functools.partial(next_final_kernel, 1), "final2",
         (head_wide, pltpu.VMEM((8, toks), F32)),
-        far_got, far_near1, *held, mixed, squares, aliases={9: 0},
+        far_got, far_nears, *held, mixed, squares, aliases={9: 0},
     )
     others = [
         lax.ppermute(squares, "head", [(i, (i + k) % (peers + 1)) for i in range(peers + 1)])

time: 46 us -> 43.2 us (0.939)
  waiting for transfers between devices: 11.7 us -> 4.83 us
  starting transfers between devices: 14 us -> 17.5 us
  local copies, waits for them, and re-layouts: 0.31 us -> 1.16 us
    ppermute x13 -> x12, waiting for transfers between devices: 9.58 us -> 2.67 us  [permute(): return lax.ppermute(x, 'ctx', pairs)]
    ppermute x13 -> x12, starting transfers between devices: 12.4 us -> 16 us  [permute(): return lax.ppermute(x, 'ctx', pairs)]
    unnamed x18 -> x26, local copies, waits for them, and re-layouts: 0.31 us -> 1.16 us
    pallas_call x20 -> x22, Pallas kernels: 19.2 us -> 19.2 us  [call(): pl.pallas_call(body, out_shape=outs, in_specs=[spec] * len(operands), out...]
  transfers between devices with their start and end apart: 14 -> 13, of which waited for: 7 -> 3; matrix products, arithmetic and copies ran while one was open for 0% -> 0% of each run, Pallas kernels for 32% -> 34%
where the time goes in v5:
time: 43.2 us; the launch traced here: 43 us
  Pallas kernels  19.2 us (44%)
  starting transfers between devices  17.5 us (41%)
  waiting for transfers between devices  4.83 us (11%)
  local copies, waits for them, and re-layouts  1.16 us (3%)
    pallas_call x22, Pallas kernels, call(): pl.pallas_call(body, out_shape=outs, in_specs=[spec] * len(operands), out...  19.2 us
    ppermute x12, starting transfers between devices, permute(): return lax.ppermute(x, 'ctx', pairs)  16 us
    ppermute x12, waiting for transfers between devices, permute(): return lax.ppermute(x, 'ctx', pairs)  2.67 us
    ppermute x1, waiting for transfers between devices, on_device(): lax.ppermute(squares, 'head', [(i, (i + k) % (peers + 1)) for i in range(...  2.15 us
    ppermute x1, starting transfers between devices, on_device(): lax.ppermute(squares, 'head', [(i, (i + k) % (peers + 1)) for i in range(...  1.53 us
    unnamed x26, local copies, waits for them, and re-layouts  1.16 us
  transfers between devices with their start and end apart: 13, of which 3 were waited for; matrix products, arithmetic and copies ran while one was open for 0% of the time, Pallas kernels for 34%

profile of v5, /device:TPU:0, one launch (start us, length us, event | category | flops | bytes accessed | tf_op | source)
XLA Modules:
  0.0 43.0 jit_solution(11156360912595530241)
XLA Ops:
  0.0 1.1 %rim.1.after_ref.rim_ref = bf16[2,64,16,128]{3,2,1,0:T(8,128)(2,1)S(1)} custom-call(bf16[256,16,128]{2,1,0:T(8,128)(2,1)} %wk_ref.3, bf16[256,16,128]{2,1,0:T(8,128)(2,1)} %v_ref.3), custom_call_target="tpu_custom_call" | custom-call | flops 1150000000 | tf_op jit(solution)/shard_map/rim/pallas_call | solution.py:141
  1.2 0.2 copy-done.4
  1.4 0.0 copy-done.7
  1.4 0.7 %far1.1 = (f32[4,160,128]{2,1,0:T(8,128)S(1)}, bf16[16,256,128]{2,1,0:T(8,128)(2,1)S(1)}, f32[256,256]{1,0:T(8,128)S(1)}) custom-call(bf16[256,256]{1,0:T(8,128)(2,1)S(1)} %copy-done.7, bf16[256,16,128]{2,1,0:T(8,128)(2,1)S(1)} %copy-done.4, bf16[2,64,16,128]{3,2,1,0:T(8,128)(2,1)S(1)} %rim.1.after_ref.rim_ref), custom_call_target="tpu_custom_call" | custom-call | flops 1150000000 | tf_op jit(solution)/shard_map/far1/pallas_call | solution.py:141
  2.1 0.5 %collective-permute-start = (f32[4,160,128]{2,1,0:T(8,128)S(1)}, f32[4,160,128]{2,1,0:T(8,128)S(1)}, u32[]{:S(2)}, u32[]{:S(2)}) collective-permute-start(f32[4,160,128]{2,1,0:T(8,128)S(1)} %get-tuple-element.40.after_ref), channel_id=1, source_target_pairs={{0,2},{2,0},{4,6},{6,4},{8,10},{10,8},{12,14},{14,12},{16,18},{18,... | collective-permute-start | bytes 983048 | tf_op jit(solution)/shard_map/ppermute | solution.py:493
  2.6 0.7 %collective-permute-start.4 = (bf16[2,64,16,128]{3,2,1,0:T(8,128)(2,1)S(1)}, bf16[2,64,16,128]{3,2,1,0:T(8,128)(2,1)S(1)}, u32[]{:S(2)}, u32[]{:S(2)}) collective-permute-start(bf16[2,64,16,128]{3,2,1,0:T(8,128)(2,1)S(1)} %rim.1.after_ref.rim_ref), channel_id=1, source_target_pairs={{6,14},{14,22},{22,30},{0,0},{2,2},{4,4},{8,8},{10,10},{12,12},{16... | collective-permute-start | bytes 1572872 | tf_op jit(solution)/shard_map/ppermute | solution.py:493
  3.3 0.5 %near1.1.own_ref.near1_ref = f32[4,160,128]{2,1,0:T(8,128)S(1)} custom-call(f32[256,256]{1,0:T(8,128)S(1)} %get-tuple-element.38.kt_ref, bf16[16,256,128]{2,1,0:T(8,128)(2,1)S(1)} %get-tuple-element.39.vh_ref, f32[4,160,128]{2,1,0:T(8,128)S(1)} %get-tuple-element.40.after_ref), custom_call_target="tpu_custom_call" | custom-call | flops 1150000000 | tf_op jit(solution)/shard_map/near1/pallas_call | solution.py:141
  3.8 0.1 collective-permute-done.other_ref.extra_ref
  3.9 3.0 %collective-permute-start.2 = (bf16[4,192,128]{2,1,0:T(8,128)(2,1)S(1)}, bf16[4,192,128]{2,1,0:T(8,128)(2,1)S(1)}, u32[]{:S(2)}, u32[]{:S(2)}) collective-permute-start(bf16[4,192,128]{2,1,0:T(8,128)(2,1)S(1)} %chip.1.after_ref), channel_id=1, source_target_pairs={{0,4},{2,6},{4,0},{6,2},{8,12},{10,14},{12,8},{14,10},{16,20},{18,... | collective-permute-start | bytes 589832 | tf_op jit(solution)/shard_map/ppermute | solution.py:493
  6.9 0.4 %far0.1.after_ref = f32[4,160,128]{2,1,0:T(8,128)S(1)} custom-call(f32[256,256]{1,0:T(8,128)S(1)} %get-tuple-element.38.kt_ref, bf16[16,256,128]{2,1,0:T(8,128)(2,1)S(1)} %get-tuple-element.39.vh_ref, bf16[4,192,128]{2,1,0:T(8,128)(2,1)S(1)} %chip.1.after_ref), custom_call_target="tpu_custom_call" | custom-call | flops 1150000000 | tf_op jit(solution)/shard_map/far0/pallas_call | solution.py:141
  7.3 0.0 copy-done
  7.3 0.0 copy-start.8
  7.3 0.0 copy-start.9
  7.4 0.0 copy-start.10
  7.4 0.0 copy-start.11
  7.4 0.0 copy-start.12
  7.4 0.5 %near0.1.after_ref.own_ref.near0_ref = f32[4,160,128]{2,1,0:T(8,128)S(1)} custom-call(f32[256,256]{1,0:T(8,128)S(1)} %get-tuple-element.38.kt_ref, bf16[16,256,128]{2,1,0:T(8,128)(2,1)S(1)} %get-tuple-element.39.vh_ref, f32[4,160,128]{2,1,0:T(8,128)S(1)} %far0.1.after_ref), custom_call_target="tpu_custom_call" | custom-call | flops 1150000000 | tf_op jit(solution)/shard_map/near0/pallas_call | solution.py:141
  7.9 0.0 copy-start.5
  7.9 0.0 copy-start.6
  7.9 2.4 %collective-permute-start.1 = (f32[4,160,128]{2,1,0:T(8,128)S(1)}, f32[4,160,128]{2,1,0:T(8,128)S(1)}, u32[]{:S(2)}, u32[]{:S(2)}) collective-permute-start(f32[4,160,128]{2,1,0:T(8,128)S(1)} %far0.1.after_ref), channel_id=1, source_target_pairs={{0,2},{2,0},{4,6},{6,4},{8,10},{10,8},{12,14},{14,12},{16,18},{18,... | collective-permute-start | bytes 983048 | tf_op jit(solution)/shard_map/ppermute | solution.py:493
  10.2 0.0 copy-done.8
  10.2 0.0 copy-done.9
  10.2 0.0 copy-done.10
  10.2 0.0 copy-done.11
  10.2 0.0 copy-done.12
  10.3 1.8 %phi.1 = (bf16[16,256,160]{2,1,0:T(8,128)(2,1)S(1)}, bf16[16,256,160]{2,1,0:T(8,128)(2,1)S(1)}, f32[16,1,128]{2,1,0:T(1,128)S(1)}) custom-call(bf16[256,256]{1,0:T(8,128)(2,1)S(1)} %copy-done.8, bf16[4,64,160]{2,1,0:T(8,128)(2,1)S(1)} %copy-done.11, bf16[4,64,160]{2,1,0:T(8,128)(2,1)S(1)} %copy-done.10, f32[8,160]{1,0:T(8,128)S(1)} %copy-done.12, ...), custom_call_target="tpu_custom_call" | custom-call | flops 2070000000 | tf_op jit(solution)/shard_map/phi/pallas_call | solution.py:141
  12.1 0.0 copy-start.2
  12.1 0.0 copy-done.5
  12.1 0.6 %by_head.1 = (bf16[16,256,128]{2,1,0:T(8,128)(2,1)S(1)}, bf16[16,256,128]{2,1,0:T(8,128)(2,1)S(1)}, f32[8,128]{1,0:T(8,128)S(1)}) custom-call(bf16[256,16,128]{2,1,0:T(8,128)(2,1)S(1)} %copy-done.6, bf16[256,16,128]{2,1,0:T(8,128)(2,1)S(1)} %copy-done.5, f32[16,1,128]{2,1,0:T(1,128)S(1)} %get-tuple-element.41.after_ref.rest_6_), custom_call_target="tpu_custom_call" | custom-call | flops 1150000000 | tf_op jit(solution)/shard_map/by_head/pallas_call | solution.py:141
  12.7 0.0 collective-permute-done.2.got_ref
  12.7 0.0 collective-permute-done.1.other_ref
  12.8 0.1 plane.1
  12.8 1.6 %collective-permute-start.3 = (bf16[4,192,128]{2,1,0:T(8,128)(2,1)S(1)}, bf16[4,192,128]{2,1,0:T(8,128)(2,1)S(1)}, u32[]{:S(2)}, u32[]{:S(2)}) collective-permute-start(bf16[4,192,128]{2,1,0:T(8,128)(2,1)S(1)} %get-tuple-element.43.msg_ref.after_ref), channel_id=1, source_target_pairs={{0,8},{2,10},{4,12},{6,14},{8,16},{10,18},{12,20},{14,22},{16,24},... | collective-permute-start | bytes 589832 | tf_op jit(solution)/shard_map/ppermute | solution.py:493
  14.5 0.0 collective-permute-done.4.got_ref
  14.5 0.1 pick.1
  14.5 4.8 %collective-permute-start.6 = (bf16[4,192,128]{2,1,0:T(8,128)(2,1)S(1)}, bf16[4,192,128]{2,1,0:T(8,128)(2,1)S(1)}, u32[]{:S(2)}, u32[]{:S(2)}) collective-permute-start(bf16[4,192,128]{2,1,0:T(8,128)(2,1)S(1)} %get-tuple-element.48), channel_id=1, source_target_pairs={{0,16},{2,18},{4,20},{6,22},{8,8},{10,10},{12,12},{14,14},{24,24},... | collective-permute-start | bytes 589832 | tf_op jit(solution)/shard_map/ppermute | solution.py:493
  19.4 0.1 collective-permute-start.10
  19.4 2.8 %intra.1 = (f32[16,256,128]{2,1,0:T(8,128)S(1)}, f32[16,256,128]{2,1,0:T(8,128)S(1)}, f32[8,128]{1,0:T(8,128)S(1)}) custom-call(bf16[256,256]{1,0:T(8,128)(2,1)S(1)} %copy-done.8, bf16[256,256]{1,0:T(8,128)(2,1)S(1)} %copy-done.7, bf16[16,256,128]{2,1,0:T(8,128)(2,1)S(1)} %get-tuple-element.39.vh_ref, ...), custom_call_target="tpu_custom_call" | custom-call | flops 3220000000 | tf_op jit(solution)/shard_map/intra/pallas_call | solution.py:141
  22.3 0.0 collective-permute-done.3.rest_0_
  22.3 0.8 %round.1 = (f32[4,160,128]{2,1,0:T(8,128)}, bf16[4,192,128]{2,1,0:T(8,128)(2,1)S(1)}) custom-call(f32[4,160,128]{2,1,0:T(8,128)S(1)} %get-tuple-element.44.total_ref, bf16[4,192,128]{2,1,0:T(8,128)(2,1)S(1)} %collective-permute-done.3.rest_0_, f32[8,128]{1,0:T(8,128)S(1)} %get-tuple-element.46.rest_1_), custom_call_target="tpu_custom_call" | custom-call | flops 1150000000 | tf_op jit(solution)/shard_map/round/pallas_call | solution.py:141
  23.1 0.7 %collective-permute-start.5 = (bf16[4,192,128]{2,1,0:T(8,128)(2,1)S(1)}, bf16[4,192,128]{2,1,0:T(8,128)(2,1)S(1)}, u32[]{:S(2)}, u32[]{:S(2)}) collective-permute-start(bf16[4,192,128]{2,1,0:T(8,128)(2,1)S(1)} %get-tuple-element.47.after_ref), channel_id=1, source_target_pairs={{8,24},{10,26},{12,28},{14,30},{0,0},{2,2},{4,4},{6,6},{16,16},{18... | collective-permute-start | bytes 589832 | tf_op jit(solution)/shard_map/ppermute | solution.py:493
  23.7 2.8 %window.1 = (f32[16,192,128]{2,1,0:T(8,128)S(1)}, f32[2,4,160,128]{3,2,1,0:T(8,128)S(1)}, f32[8,128]{1,0:T(8,128)S(1)}) custom-call(bf16[16,256,128]{2,1,0:T(8,128)(2,1)S(1)} %get-tuple-element.49.qh_ref, bf16[16,256,128]{2,1,0:T(8,128)(2,1)S(1)} %get-tuple-element.50.kh_ref, bf16[16,256,128]{2,1,0:T(8,128)(2,1)S(1)} %get-tuple-element.39.vh_ref, ...), custom_call_target="tpu_custom_call" | custom-call | flops 4024999936 | tf_op jit(solution)/shard_map/window/pallas_call | solution.py:141
  26.6 1.5 %collective-permute-start.9 = (f32[2,4,160,128]{3,2,1,0:T(8,128)S(1)}, f32[2,4,160,128]{3,2,1,0:T(8,128)S(1)}, u32[]{:S(2)}, u32[]{:S(2)}) collective-permute-start(f32[2,4,160,128]{3,2,1,0:T(8,128)S(1)} %get-tuple-element.54), channel_id=1, source_target_pairs={{0,2},{2,0},{4,6},{6,4},{8,10},{10,8},{12,14},{14,12},{16,18},{18,... | collective-permute-start | bytes 1966088 | tf_op jit(solution)/shard_map/ppermute | solution.py:493
  28.0 0.0 collective-permute-done.6.rest_2_
  28.0 0.0 collective-permute-done.5.rest_1_
  28.0 0.2 before.1
  28.2 0.8 %collective-permute-start.7 = (bf16[4,192,128]{2,1,0:T(8,128)(2,1)S(1)}, bf16[4,192,128]{2,1,0:T(8,128)(2,1)S(1)}, u32[]{:S(2)}, u32[]{:S(2)}) collective-permute-start(bf16[4,192,128]{2,1,0:T(8,128)(2,1)S(1)} %get-tuple-element.52.after_ref), channel_id=1, source_target_pairs={{0,4},{2,6},{4,0},{6,2},{8,12},{10,14},{12,8},{14,10},{16,20},{18,... | collective-permute-start | bytes 589832 | tf_op jit(solution)/shard_map/ppermute | solution.py:493
  29.0 0.0 collective-permute-start.8
  29.0 0.0 collective-permute-done.10.rim_ref
  29.0 0.2 turn.1
  29.2 0.0 copy-start.3
  29.2 2.0 %edge.1.rest_4_ = f32[16,64,128]{2,1,0:T(8,128)S(1)} custom-call(bf16[16,256,128]{2,1,0:T(8,128)(2,1)S(1)} %get-tuple-element.49.qh_ref, bf16[16,256,128]{2,1,0:T(8,128)(2,1)S(1)} %get-tuple-element.50.kh_ref, bf16[16,256,128]{2,1,0:T(8,128)(2,1)S(1)} %get-tuple-element.39.vh_ref, bf16[16,64,128]{2,1,0:T(8,128)(2,1)S(1)} %get-tuple-element.59.rk_ref, ...), custom_call_target="tpu_custom_call" | custom-call | flops 1150000000 | tf_op jit(solution)/shard_map/edge/pallas_call | solution.py:141
  31.2 0.0 collective-permute-done.8.far_ref
  31.2 0.0 collective-permute-done.9.extra_ref
  31.2 1.4 %final0.1 = (f32[16,256,128]{2,1,0:T(8,128)S(1)}, f32[256,128]{1,0:T(8,128)S(1)}) custom-call(f32[4,160,128]{2,1,0:T(8,128)S(1)} %get-tuple-element.53.mine_ref, f32[4,160,128]{2,1,0:T(8,128)S(1)} %collective-permute-done.1.other_ref, f32[4,160,128]{2,1,0:T(8,128)S(1)} %collective-permute-done.8.far_ref, ...), custom_call_target="tpu_custom_call" | custom-call | flops 1150000000 | tf_op jit(solution)/shard_map/final0/pallas_call | solution.py:141
  32.6 2.5 %collective-permute-done.7.got_ref = bf16[4,192,128]{2,1,0:T(8,128)(2,1)S(1)} collective-permute-done((bf16[4,192,128]{2,1,0:T(8,128)(2,1)S(1)}, bf16[4,192,128]{2,1,0:T(8,128)(2,1)S(1)}, u32[]{:S(2)}, u32[]{:S(2)}) %collective-permute-start.7) | collective-permute-done | bytes 196640 | tf_op jit(solution)/shard_map/ppermute | solution.py:493
  35.2 0.1 collective-permute-start.11
  35.2 0.9 %copy-done.1 = f32[4,160,128]{2,1,0:T(8,128)S(1)} copy-done((f32[4,160,128]{2,1,0:T(8,128)S(1)}, f32[4,160,128]{2,1,0:T(8,128)}, u32[]{:S(2)}) %copy-start.1) | copy-done | bytes 327704
  36.1 0.8 %final1.1 = (f32[16,256,128]{2,1,0:T(8,128)S(1)}, f32[256,128]{1,0:T(8,128)S(1)}) custom-call(f32[4,160,128]{2,1,0:T(8,128)S(1)} %open.3.base_ref, f32[4,160,128]{2,1,0:T(8,128)S(1)} %copy-done.1, bf16[16,256,160]{2,1,0:T(8,128)(2,1)S(1)} %get-tuple-element.55.rest_0_, ...), custom_call_target="tpu_custom_call", output_to_operand_aliasing={{0}: (9, {})} | custom-call | flops 1150000000 | tf_op jit(solution)/shard_map/final1/pallas_call | solution.py:141
  36.9 0.0 collective-permute-done.11.base_ref
  36.9 1.1 %final2.1 = (f32[16,256,128]{2,1,0:T(8,128)S(1)}, f32[8,256]{1,0:T(8,128)S(1)}) custom-call(bf16[4,192,128]{2,1,0:T(8,128)(2,1)S(1)} %collective-permute-done.11.base_ref, f32[2,4,160,128]{3,2,1,0:T(8,128)S(1)} %collective-permute-done.9.extra_ref, bf16[16,256,160]{2,1,0:T(8,128)(2,1)S(1)} %get-tuple-element.55.rest_0_, ...), custom_call_target="tpu_custom_call", output_to_operand_aliasing={{0}: (9, {})} | custom-call | flops 1150000000 | tf_op jit(solution)/shard_map/final2/pallas_call | solution.py:141
  38.0 1.5 %collective-permute-start.12 = (f32[8,256]{1,0:T(8,128)S(1)}, f32[8,256]{1,0:T(8,128)S(1)}, u32[]{:S(2)}, u32[]{:S(2)}) collective-permute-start(f32[8,256]{1,0:T(8,128)S(1)} %get-tuple-element.70.sq_ref), channel_id=1, source_target_pairs={{0,1},{1,0},{2,3},{3,2},{4,5},{5,4},{6,7},{7,6},{8,9},{9,8},{10,11... | collective-permute-start | bytes 24584 | tf_op jit(solution)/shard_map/ppermute | solution.py:602
  39.5 2.2 %collective-permute-done.12.rest_0_ = f32[8,256]{1,0:T(8,128)S(1)} collective-permute-done((f32[8,256]{1,0:T(8,128)S(1)}, f32[8,256]{1,0:T(8,128)S(1)}, u32[]{:S(2)}, u32[]{:S(2)}) %collective-permute-start.12) | collective-permute-done | bytes 8224 | tf_op jit(solution)/shard_map/ppermute | solution.py:602
  41.7 1.4 %norm.1 = bf16[256,16,128]{2,1,0:T(8,128)(2,1)} custom-call(f32[16,256,128]{2,1,0:T(8,128)S(1)} %get-tuple-element.69.mixed_ref, f32[8,256]{1,0:T(8,128)S(1)} %get-tuple-element.70.sq_ref, f32[8,256]{1,0:T(8,128)S(1)} %collective-permute-done.12.rest_0_), custom_call_target="tpu_custom_call" | custom-call | flops 1150000000 | tf_op jit(solution)/shard_map/norm/pallas_call | solution.py:141
  (10 shorter events, 0.1 us)
Async XLA Ops:
  0.0 1.4 %copy-start.4 = (bf16[256,16,128]{2,1,0:T(8,128)(2,1)S(1)}, bf16[256,16,128]{2,1,0:T(8,128)(2,1)}, u32[]{:S(2)}) copy-start(bf16[256,16,128]{2,1,0:T(8,128)(2,1)} %v_ref.3) | copy-start | bytes 3145732
  0.0 1.4 %copy-start.7 = (bf16[256,256]{1,0:T(8,128)(2,1)S(1)}, bf16[256,256]{1,0:T(8,128)(2,1)}, u32[]{:S(2)}) copy-start(bf16[256,256]{1,0:T(8,128)(2,1)} %k_ref.1) | copy-start | bytes 393220
  2.1 1.8 %collective-permute-start = (f32[4,160,128]{2,1,0:T(8,128)S(1)}, f32[4,160,128]{2,1,0:T(8,128)S(1)}, u32[]{:S(2)}, u32[]{:S(2)}) collective-permute-start(f32[4,160,128]{2,1,0:T(8,128)S(1)} %get-tuple-element.40.after_ref), channel_id=1, source_target_pairs={{0,2},{2,0},{4,6},{6,4},{8,10},{10,8},{12,14},{14,12},{16,18},{18,... | collective-permute-start | bytes 983048 | tf_op jit(solution)/shard_map/ppermute | solution.py:493
  2.6 11.8 %collective-permute-start.4 = (bf16[2,64,16,128]{3,2,1,0:T(8,128)(2,1)S(1)}, bf16[2,64,16,128]{3,2,1,0:T(8,128)(2,1)S(1)}, u32[]{:S(2)}, u32[]{:S(2)}) collective-permute-start(bf16[2,64,16,128]{3,2,1,0:T(8,128)(2,1)S(1)} %rim.1.after_ref.rim_ref), channel_id=1, source_target_pairs={{6,14},{14,22},{22,30},{0,0},{2,2},{4,4},{8,8},{10,10},{12,12},{16... | collective-permute-start | bytes 1572872 | tf_op jit(solution)/shard_map/ppermute | solution.py:493
  3.9 3.4 %copy-start = (f32[4,160,128]{2,1,0:T(8,128)}, f32[4,160,128]{2,1,0:T(8,128)S(1)}, u32[]{:S(2)}) copy-start(f32[4,160,128]{2,1,0:T(8,128)S(1)} %collective-permute-done.other_ref.extra_ref) | copy-start | bytes 983044
  3.9 8.8 %collective-permute-start.2 = (bf16[4,192,128]{2,1,0:T(8,128)(2,1)S(1)}, bf16[4,192,128]{2,1,0:T(8,128)(2,1)S(1)}, u32[]{:S(2)}, u32[]{:S(2)}) collective-permute-start(bf16[4,192,128]{2,1,0:T(8,128)(2,1)S(1)} %chip.1.after_ref), channel_id=1, source_target_pairs={{0,4},{2,6},{4,0},{6,2},{8,12},{10,14},{12,8},{14,10},{16,20},{18,... | collective-permute-start | bytes 589832 | tf_op jit(solution)/shard_map/ppermute | solution.py:493
  7.3 2.9 %copy-start.8 = (bf16[256,256]{1,0:T(8,128)(2,1)S(1)}, bf16[256,256]{1,0:T(8,128)(2,1)}, u32[]{:S(2)}) copy-start(bf16[256,256]{1,0:T(8,128)(2,1)} %q_ref.3) | copy-start | bytes 393220
  7.3 2.9 %copy-start.9 = (bf16[16,128]{1,0:T(8,128)(2,1)S(1)}, bf16[16,128]{1,0:T(8,128)(2,1)}, u32[]{:S(2)}) copy-start(bf16[16,128]{1,0:T(8,128)(2,1)} %gain_ref.1) | copy-start | bytes 12292
  7.4 2.9 %copy-start.10 = (bf16[4,64,160]{2,1,0:T(8,128)(2,1)S(1)}, bf16[4,64,160]{2,1,0:T(8,128)(2,1)}, u32[]{:S(2)}) copy-start(bf16[4,64,160]{2,1,0:T(8,128)(2,1)} %constant.7.clone.e2_ref) | copy-start | bytes 245764
  7.4 2.9 %copy-start.11 = (bf16[4,64,160]{2,1,0:T(8,128)(2,1)S(1)}, bf16[4,64,160]{2,1,0:T(8,128)(2,1)}, u32[]{:S(2)}) copy-start(bf16[4,64,160]{2,1,0:T(8,128)(2,1)} %constant.6.clone.e1_ref) | copy-start | bytes 245764
  7.4 2.9 %copy-start.12 = (f32[8,160]{1,0:T(8,128)S(1)}, f32[8,160]{1,0:T(8,128)}, u32[]{:S(2)}) copy-start(f32[8,160]{1,0:T(8,128)} %constant.8.clone.add_ref) | copy-start | bytes 15364
  7.9 4.2 %copy-start.5 = (bf16[256,16,128]{2,1,0:T(8,128)(2,1)S(1)}, bf16[256,16,128]{2,1,0:T(8,128)(2,1)}, u32[]{:S(2)}) copy-start(bf16[256,16,128]{2,1,0:T(8,128)(2,1)} %wk_ref.3) | copy-start | bytes 3145732
  7.9 4.2 %copy-start.6 = (bf16[256,16,128]{2,1,0:T(8,128)(2,1)S(1)}, bf16[256,16,128]{2,1,0:T(8,128)(2,1)}, u32[]{:S(2)}) copy-start(bf16[256,16,128]{2,1,0:T(8,128)(2,1)} %wq_ref.1) | copy-start | bytes 3145732
  7.9 4.9 %collective-permute-start.1 = (f32[4,160,128]{2,1,0:T(8,128)S(1)}, f32[4,160,128]{2,1,0:T(8,128)S(1)}, u32[]{:S(2)}, u32[]{:S(2)}) collective-permute-start(f32[4,160,128]{2,1,0:T(8,128)S(1)} %far0.1.after_ref), channel_id=1, source_target_pairs={{0,2},{2,0},{4,6},{6,4},{8,10},{10,8},{12,14},{14,12},{16,18},{18,... | collective-permute-start | bytes 983048 | tf_op jit(solution)/shard_map/ppermute | solution.py:493
  12.1 0.6 %copy-start.2 = (f32[16,1,128]{2,1,0:T(1,128)}, f32[16,1,128]{2,1,0:T(1,128)S(1)}, u32[]{:S(2)}) copy-start(f32[16,1,128]{2,1,0:T(1,128)S(1)} %get-tuple-element.41.after_ref.rest_6_) | copy-start | bytes 24580
  12.8 9.5 %collective-permute-start.3 = (bf16[4,192,128]{2,1,0:T(8,128)(2,1)S(1)}, bf16[4,192,128]{2,1,0:T(8,128)(2,1)S(1)}, u32[]{:S(2)}, u32[]{:S(2)}) collective-permute-start(bf16[4,192,128]{2,1,0:T(8,128)(2,1)S(1)} %get-tuple-element.43.msg_ref.after_ref), channel_id=1, source_target_pairs={{0,8},{2,10},{4,12},{6,14},{8,16},{10,18},{12,20},{14,22},{16,24},... | collective-permute-start | bytes 589832 | tf_op jit(solution)/shard_map/ppermute | solution.py:493
  14.5 13.5 %collective-permute-start.6 = (bf16[4,192,128]{2,1,0:T(8,128)(2,1)S(1)}, bf16[4,192,128]{2,1,0:T(8,128)(2,1)S(1)}, u32[]{:S(2)}, u32[]{:S(2)}) collective-permute-start(bf16[4,192,128]{2,1,0:T(8,128)(2,1)S(1)} %get-tuple-element.48), channel_id=1, source_target_pairs={{0,16},{2,18},{4,20},{6,22},{8,8},{10,10},{12,12},{14,14},{24,24},... | collective-permute-start | bytes 589832 | tf_op jit(solution)/shard_map/ppermute | solution.py:493
  19.4 9.7 %collective-permute-start.10 = (bf16[2,64,16,128]{3,2,1,0:T(8,128)(2,1)S(1)}, bf16[2,64,16,128]{3,2,1,0:T(8,128)(2,1)S(1)}, u32[]{:S(2)}, u32[]{:S(2)}) collective-permute-start(bf16[2,64,16,128]{3,2,1,0:T(8,128)(2,1)S(1)} %get-tuple-element.45.rim_ref), channel_id=1, source_target_pairs={{0,2},{2,4},{4,6},{6,0},{8,10},{10,12},{12,14},{14,8},{16,18},{18,... | collective-permute-start | bytes 1572872 | tf_op jit(solution)/shard_map/ppermute | solution.py:493
  23.1 5.0 %collective-permute-start.5 = (bf16[4,192,128]{2,1,0:T(8,128)(2,1)S(1)}, bf16[4,192,128]{2,1,0:T(8,128)(2,1)S(1)}, u32[]{:S(2)}, u32[]{:S(2)}) collective-permute-start(bf16[4,192,128]{2,1,0:T(8,128)(2,1)S(1)} %get-tuple-element.47.after_ref), channel_id=1, source_target_pairs={{8,24},{10,26},{12,28},{14,30},{0,0},{2,2},{4,4},{6,6},{16,16},{18... | collective-permute-start | bytes 589832 | tf_op jit(solution)/shard_map/ppermute | solution.py:493
  26.6 4.6 %collective-permute-start.9 = (f32[2,4,160,128]{3,2,1,0:T(8,128)S(1)}, f32[2,4,160,128]{3,2,1,0:T(8,128)S(1)}, u32[]{:S(2)}, u32[]{:S(2)}) collective-permute-start(f32[2,4,160,128]{3,2,1,0:T(8,128)S(1)} %get-tuple-element.54), channel_id=1, source_target_pairs={{0,2},{2,0},{4,6},{6,4},{8,10},{10,8},{12,14},{14,12},{16,18},{18,... | collective-permute-start | bytes 1966088 | tf_op jit(solution)/shard_map/ppermute | solution.py:493
  28.2 6.9 %collective-permute-start.7 = (bf16[4,192,128]{2,1,0:T(8,128)(2,1)S(1)}, bf16[4,192,128]{2,1,0:T(8,128)(2,1)S(1)}, u32[]{:S(2)}, u32[]{:S(2)}) collective-permute-start(bf16[4,192,128]{2,1,0:T(8,128)(2,1)S(1)} %get-tuple-element.52.after_ref), channel_id=1, source_target_pairs={{0,4},{2,6},{4,0},{6,2},{8,12},{10,14},{12,8},{14,10},{16,20},{18,... | collective-permute-start | bytes 589832 | tf_op jit(solution)/shard_map/ppermute | solution.py:493
  29.0 2.2 %collective-permute-start.8 = (f32[4,160,128]{2,1,0:T(8,128)S(1)}, f32[4,160,128]{2,1,0:T(8,128)S(1)}, u32[]{:S(2)}, u32[]{:S(2)}) collective-permute-start(f32[4,160,128]{2,1,0:T(8,128)S(1)} %get-tuple-element.53.mine_ref), channel_id=1, source_target_pairs={{0,2},{2,0},{4,6},{6,4},{8,10},{10,8},{12,14},{14,12},{16,18},{18,... | collective-permute-start | bytes 983048 | tf_op jit(solution)/shard_map/ppermute | solution.py:493
  29.2 2.0 %copy-start.3 = (f32[16,1,128]{2,1,0:T(1,128)S(1)}, f32[16,1,128]{2,1,0:T(1,128)}, u32[]{:S(2)}) copy-start(f32[16,1,128]{2,1,0:T(1,128)} %copy-done.2) | copy-start | bytes 24580
  35.1 1.0 %copy-start.1 = (f32[4,160,128]{2,1,0:T(8,128)S(1)}, f32[4,160,128]{2,1,0:T(8,128)}, u32[]{:S(2)}) copy-start(f32[4,160,128]{2,1,0:T(8,128)} %copy-done) | copy-start | bytes 983044
  35.2 1.7 %collective-permute-start.11 = (bf16[4,192,128]{2,1,0:T(8,128)(2,1)S(1)}, bf16[4,192,128]{2,1,0:T(8,128)(2,1)S(1)}, u32[]{:S(2)}, u32[]{:S(2)}) collective-permute-start(bf16[4,192,128]{2,1,0:T(8,128)(2,1)S(1)} %collective-permute-done.7.got_ref), channel_id=1, source_target_pairs={{0,2},{2,0},{4,6},{6,4},{8,10},{10,8},{12,14},{14,12},{16,18},{18,... | collective-permute-start | bytes 589832 | tf_op jit(solution)/shard_map/ppermute | solution.py:493
  38.0 3.7 %collective-permute-start.12 = (f32[8,256]{1,0:T(8,128)S(1)}, f32[8,256]{1,0:T(8,128)S(1)}, u32[]{:S(2)}, u32[]{:S(2)}) collective-permute-start(f32[8,256]{1,0:T(8,128)S(1)} %get-tuple-element.70.sq_ref), channel_id=1, source_target_pairs={{0,1},{1,0},{2,3},{3,2},{4,5},{5,4},{6,7},{7,6},{8,9},{9,8},{10,11... | collective-permute-start | bytes 24584 | tf_op jit(solution)/shard_map/ppermute | solution.py:602

commit v6 on v5

--- a/solution.py
+++ b/solution.py
@@ -126,6 +126,7 @@
 
 
 VMEM_SPEC = pl.BlockSpec(memory_space=pltpu.VMEM)
+HBM_SPEC = pl.BlockSpec(memory_space=pltpu.HBM)
 VMEM_LIMIT = 12 << 20
 FLOPS_PER_US = 1_150_000_000
 EXPECTED_US = {"phi": 1.8, "intra": 2.8, "window": 3.5, "chip": 0.1, "plane": 0.1, "open": 12.0, "pick": 60.0, "turn": 60.0}
@@ -137,7 +138,7 @@
         for x in operands
     ]
     many = isinstance(outs, tuple)
-    spec = pl.BlockSpec(memory_space=pltpu.HBM) if raw else VMEM_SPEC
+    spec = HBM_SPEC if raw else VMEM_SPEC
     return pl.pallas_call(
         body,
         out_shape=outs,
@@ -180,22 +181,33 @@
     each(part, one)
 
 
-def rim_kernel(wk_ref, v_ref, rim_ref, sems):
-    rows = pl.ds(wk_ref.shape[0] - WINDOW, WINDOW)
-    copies = [
-        pltpu.make_async_copy(ref.at[rows], rim_ref.at[i], sems.at[i])
-        for i, ref in enumerate((wk_ref, v_ref))
-    ]
+def first_states_kernel(keys_hbm, v_hbm, wk_hbm, out_ref, vh_ref, kt_ref, rim_ref,
+                        keys_ref, v_ref, sems):
+    toks, heads = v_hbm.shape[:2]
+    pieces = v_ref.shape[0]
+    size = heads // pieces
+    tail = pl.ds(toks - WINDOW, WINDOW)
+    firsts = [pl.multiple_of((1 - core_bit()) * size, size), pl.multiple_of(core_bit() * size, size)]
+    if pieces == 1:
+        firsts = [0]
+    copies = [pltpu.make_async_copy(keys_hbm, keys_ref, sems.at[0])]
+    for i, first in enumerate(firsts):
+        copies.append(
+            pltpu.make_async_copy(v_hbm.at[:, pl.ds(first, size)], v_ref.at[i], sems.at[1 + i])
+        )
+    copies.append(pltpu.make_async_copy(wk_hbm.at[tail], rim_ref.at[0], sems.at[3]))
+    copies.append(pltpu.make_async_copy(v_hbm.at[tail], rim_ref.at[1], sems.at[4]))
     for copy in copies:
         copy.start()
-    for copy in copies:
-        copy.wait()
-
-
-def first_states_kernel(keys_ref, v_ref, after_ref, out_ref, vh_ref, kt_ref):
-    vh_ref[...] = jnp.swapaxes(v_ref[...], 0, 1)
+    copies[0].wait()
     kt_ref[...] = jnp.transpose(keys_ref[...].astype(F32), (1, 0))
-    put_states(out_ref, 1, 1, kt_ref, vh_ref)
+    for i, first in enumerate(firsts):
+        copies[1 + i].wait()
+        vh_ref[pl.ds(first, size)] = jnp.swapaxes(v_ref[i], 0, 1)
+        if i == 0:
+            put_states(out_ref, 1, 1, kt_ref, vh_ref)
+    copies[-2].wait()
+    copies[-1].wait()
 
 
 def states_kernel(far, other, kt_ref, vh_ref, after_ref, out_ref):
@@ -229,13 +241,14 @@
     each(own_ref.shape[0], one)
 
 
-def round_kernel(limits, total_ref, *rest):
-    gots, (next_ref, msg_ref) = rest[: len(limits)], rest[-2:]
+def round_kernel(limits, keep, total_ref, *rest):
+    gots, outs = rest[: len(limits)], rest[len(limits) + 1 :]
 
     def one(j):
         total = total_ref[j] + arrived(gots, limits, j)
-        next_ref[j] = total
-        pack(msg_ref.at[j], total)
+        pack(outs[0].at[j], total)
+        if keep:
+            outs[1][j] = total
 
     each(total_ref.shape[0], one)
 
@@ -350,7 +363,8 @@
     kh_ref[...] = jnp.swapaxes(wk_ref[...], 0, 1)
 
 
-def turn_kernel(rim_ref, after_ref, k_ref, v_ref):
+def turn_kernel(rim_ref, other1_ref, after_ref, k_ref, v_ref, keep_ref):
+    keep_ref[...] = other1_ref[...]
     k_ref[...] = jnp.swapaxes(rim_ref[0], 0, 1)
     v_ref[...] = jnp.swapaxes(rim_ref[1], 0, 1)
 
@@ -390,25 +404,18 @@
 
 def edge_kernel(qh_ref, kh_ref, vh_ref, rk_ref, rv_ref, after_ref, out_ref):
     heads, _, dim = vh_ref.shape
-    part = heads // 4
     band, col = band_mask()
     valid = band & ((col >= WINDOW) | (lax.axis_index("ctx") > 0))
 
-    def one(r, carry):
-        scores = []
-        for j in range(part):
-            head = r * part + j
-            k = jnp.concatenate([rk_ref[head], kh_ref[head, :WINDOW]], axis=0)
-            sc = dot(qh_ref[head, :WINDOW], k, NT)
-            scores.append(jnp.where(valid, sc / math.sqrt(dim), -1e30))
-        weights = softmax_blocks(scores)
-        for j in range(part):
-            head = r * part + j
-            v = jnp.concatenate([rv_ref[head], vh_ref[head, :WINDOW]], axis=0)
-            out_ref[head] = dot(weights[j * WINDOW : (j + 1) * WINDOW], v)
-        return carry
-
-    lax.fori_loop(0, 4, one, 0)
+    scores = []
+    for head in range(heads):
+        k = jnp.concatenate([rk_ref[head], kh_ref[head, :WINDOW]], axis=0)
+        sc = dot(qh_ref[head, :WINDOW], k, NT)
+        scores.append(jnp.where(valid, sc / math.sqrt(dim), -1e30))
+    weights = softmax_blocks(scores)
+    for head in range(heads):
+        v = jnp.concatenate([rv_ref[head], vh_ref[head, :WINDOW]], axis=0)
+        out_ref[head] = dot(weights[head * WINDOW : (head + 1) * WINDOW], v)
 
 
 def first_head(far, other, part):
@@ -460,10 +467,10 @@
     if far == 0:
         sq_ref[...] = squares
     else:
-        sq_ref[...] = lax.dot_general(
-            jnp.ones((8, squares.shape[1]), F32), squares, NT,
-            precision=lax.Precision.HIGHEST, preferred_element_type=F32,
-        )
+        ones = jnp.ones((8, squares.shape[1]), BF16)
+        high, low = split(squares)
+        rest = squares - high.astype(F32) - low.astype(F32)
+        sq_ref[...] = dot(ones, high, NT) + (dot(ones, low, NT) + dot(ones, rest.astype(BF16), NT))
 
 
 def norm_kernel(peers, mixed_ref, sq_ref, *rest):
@@ -492,17 +499,20 @@
     def permute(x, pairs):
         return lax.ppermute(x, "ctx", pairs)
 
-    rim = call(
-        rim_kernel, "rim", pltpu.VMEM((2, WINDOW, heads, dim), BF16), win_k, values,
-        raw=True, scratch=[pltpu.SemaphoreType.DMA((2,))],
-    )
+    pieces = 2 if heads % 16 == 0 else 1
+    far1, values_h, keys_t, rim = call(
+        first_states_kernel, "far1",
+        (state_shape, pltpu.VMEM((heads, toks, dim), BF16), pltpu.VMEM((heads * DK, toks), F32),
+         pltpu.VMEM((2, WINDOW, heads, dim), BF16)),
+        keys, values, win_k, raw=True,
+        scratch=[
+            pltpu.VMEM(keys.shape, BF16),
+            pltpu.VMEM((pieces, toks, heads // pieces, dim), BF16),
+            pltpu.SemaphoreType.DMA((5,)),
+        ],
+    )
+    other1 = permute(far1, core_swap)
     rim_up = permute(rim, full([(i, i + 4) for i in range(3, count - 4, 4)], count))
-    far1, values_h, keys_t = call(
-        first_states_kernel, "far1",
-        (state_shape, pltpu.VMEM((heads, toks, dim), BF16), pltpu.VMEM((heads * DK, toks), F32)),
-        keys, values, rim,
-    )
-    other1 = permute(far1, core_swap)
 
     def states(name, far, other, after):
         return call(functools.partial(states_kernel, far, other), name, state_shape,
@@ -559,17 +569,21 @@
                  pltpu.VMEM((2, part, ROWS, dim), F32), token_shape),
                 wq_h, wk_h, values_h, near0, near1, msg,
             )
-            rim_k, rim_v = call(
-                turn_kernel, "turn", (pltpu.VMEM((heads, WINDOW, dim), BF16),) * 2, rim_prev, token
+            rim_k, rim_v, other1 = call(
+                turn_kernel, "turn",
+                (pltpu.VMEM((heads, WINDOW, dim), BF16),) * 2 + (state_shape,),
+                rim_prev, other1, token,
             )
         gots.extend(got)
         limits.extend(limit)
         step *= 2
         if step < groups:
-            total, msg = call(
-                functools.partial(round_kernel, limit), "round", (state_shape, msg_shape),
-                total, *got, token,
+            keep = 2 * step < groups
+            sums = call(
+                functools.partial(round_kernel, limit, keep), "round",
+                (msg_shape, state_shape) if keep else msg_shape, total, *got, token,
             )
+            msg, total = sums if keep else (sums, None)
     mine, msg = call(
         functools.partial(before_kernel, limits), "before", (state_shape, msg_shape),
         near0, other0, pair, *gots, token,

time: 43.2 us -> 42.1 us (0.975)
  Pallas kernels: 19.2 us -> 17.3 us
  waiting for transfers between devices: 4.83 us -> 6.65 us
  local copies, waits for them, and re-layouts: 1.16 us -> 0.06 us
    pallas_call x22 -> x21, Pallas kernels: 19.2 us -> 17.3 us  [call(): pl.pallas_call(body, out_shape=outs, in_specs=[spec] * len(operands), out...]
    ppermute x12, waiting for transfers between devices: 2.67 us -> 4.48 us  [permute(): return lax.ppermute(x, 'ctx', pairs)]
    unnamed x26 -> x20, local copies, waits for them, and re-layouts: 1.16 us -> 0.06 us
  transfers between devices with their start and end apart: 13 -> 13, of which waited for: 3 -> 5; matrix products, arithmetic and copies ran while one was open for 0% -> 0% of each run, Pallas kernels for 34% -> 31%
where the time goes in v6:
time: 42.1 us; the launch traced here: 41.9 us
  starting transfers between devices  17.5 us (42%)
  Pallas kernels  17.3 us (41%)
  waiting for transfers between devices  6.65 us (16%)
    pallas_call x21, Pallas kernels, call(): pl.pallas_call(body, out_shape=outs, in_specs=[spec] * len(operands), out...  17.3 us
    ppermute x12, starting transfers between devices, permute(): return lax.ppermute(x, 'ctx', pairs)  16 us
    ppermute x12, waiting for transfers between devices, permute(): return lax.ppermute(x, 'ctx', pairs)  4.48 us
    ppermute x1, waiting for transfers between devices, on_device(): lax.ppermute(squares, 'head', [(i, (i + k) % (peers + 1)) for i in range(...  2.17 us
    ppermute x1, starting transfers between devices, on_device(): lax.ppermute(squares, 'head', [(i, (i + k) % (peers + 1)) for i in range(...  1.51 us
  transfers between devices with their start and end apart: 13, of which 5 were waited for; matrix products, arithmetic and copies ran while one was open for 0% of the time, Pallas kernels for 31%

profile of v6, /device:TPU:0, one launch (start us, length us, event | category | flops | bytes accessed | tf_op | source)
XLA Modules:
  0.0 41.9 jit_solution(11622202931015941065)
XLA Ops:
  0.0 1.9 %far1.1 = (f32[4,160,128]{2,1,0:T(8,128)S(1)}, bf16[16,256,128]{2,1,0:T(8,128)(2,1)S(1)}, f32[256,256]{1,0:T(8,128)S(1)}, bf16[2,64,16,128]{3,2,1,0:T(8,128)(2,1)S(1)}) custom-call(bf16[256,256]{1,0:T(8,128)(2,1)} %k_ref.1, bf16[256,16,128]{2,1,0:T(8,128)(2,1)} %v_hbm.1, bf16[256,16,128]{2,1,0:T(8,128)(2,1)} %wk_ref.1), custom_call_target="tpu_custom_call" | custom-call | flops 1150000000 | tf_op jit(solution)/shard_map/far1/pallas_call | solution.py:142
  2.0 0.5 %collective-permute-start = (f32[4,160,128]{2,1,0:T(8,128)S(1)}, f32[4,160,128]{2,1,0:T(8,128)S(1)}, u32[]{:S(2)}, u32[]{:S(2)}) collective-permute-start(f32[4,160,128]{2,1,0:T(8,128)S(1)} %get-tuple-element.41.after_ref), channel_id=1, source_target_pairs={{0,2},{2,0},{4,6},{6,4},{8,10},{10,8},{12,14},{14,12},{16,18},{18,... | collective-permute-start | bytes 983048 | tf_op jit(solution)/shard_map/ppermute | solution.py:500
  2.5 0.7 %collective-permute-start.4 = (bf16[2,64,16,128]{3,2,1,0:T(8,128)(2,1)S(1)}, bf16[2,64,16,128]{3,2,1,0:T(8,128)(2,1)S(1)}, u32[]{:S(2)}, u32[]{:S(2)}) collective-permute-start(bf16[2,64,16,128]{3,2,1,0:T(8,128)(2,1)S(1)} %get-tuple-element.46.rim_ref), channel_id=1, source_target_pairs={{6,14},{14,22},{22,30},{0,0},{2,2},{4,4},{8,8},{10,10},{12,12},{16... | collective-permute-start | bytes 1572872 | tf_op jit(solution)/shard_map/ppermute | solution.py:500
  3.2 0.5 %near1.1.own_ref.near1_ref = f32[4,160,128]{2,1,0:T(8,128)S(1)} custom-call(f32[256,256]{1,0:T(8,128)S(1)} %get-tuple-element.39.kt_ref, bf16[16,256,128]{2,1,0:T(8,128)(2,1)S(1)} %get-tuple-element.40.vh_ref, f32[4,160,128]{2,1,0:T(8,128)S(1)} %get-tuple-element.41.after_ref), custom_call_target="tpu_custom_call" | custom-call | flops 1150000000 | tf_op jit(solution)/shard_map/near1/pallas_call | solution.py:142
  3.6 0.1 collective-permute-done.other_ref.other1_ref
  3.8 2.9 %collective-permute-start.2 = (bf16[4,192,128]{2,1,0:T(8,128)(2,1)S(1)}, bf16[4,192,128]{2,1,0:T(8,128)(2,1)S(1)}, u32[]{:S(2)}, u32[]{:S(2)}) collective-permute-start(bf16[4,192,128]{2,1,0:T(8,128)(2,1)S(1)} %chip.1.after_ref), channel_id=1, source_target_pairs={{0,4},{2,6},{4,0},{6,2},{8,12},{10,14},{12,8},{14,10},{16,20},{18,... | collective-permute-start | bytes 589832 | tf_op jit(solution)/shard_map/ppermute | solution.py:500
  6.7 0.4 %far0.1.after_ref = f32[4,160,128]{2,1,0:T(8,128)S(1)} custom-call(f32[256,256]{1,0:T(8,128)S(1)} %get-tuple-element.39.kt_ref, bf16[16,256,128]{2,1,0:T(8,128)(2,1)S(1)} %get-tuple-element.40.vh_ref, bf16[4,192,128]{2,1,0:T(8,128)(2,1)S(1)} %chip.1.after_ref), custom_call_target="tpu_custom_call" | custom-call | flops 1150000000 | tf_op jit(solution)/shard_map/far0/pallas_call | solution.py:142
  7.2 0.0 copy-start.5
  7.2 0.0 copy-start.6
  7.2 0.0 copy-start.7
  7.2 0.0 copy-start.8
  7.2 0.0 copy-start.9
  7.2 0.5 %near0.1.after_ref.own_ref.near0_ref = f32[4,160,128]{2,1,0:T(8,128)S(1)} custom-call(f32[256,256]{1,0:T(8,128)S(1)} %get-tuple-element.39.kt_ref, bf16[16,256,128]{2,1,0:T(8,128)(2,1)S(1)} %get-tuple-element.40.vh_ref, f32[4,160,128]{2,1,0:T(8,128)S(1)} %far0.1.after_ref), custom_call_target="tpu_custom_call" | custom-call | flops 1150000000 | tf_op jit(solution)/shard_map/near0/pallas_call | solution.py:142
  7.7 0.0 copy-start.2
  7.7 0.0 copy-start.3
  7.7 2.3 %collective-permute-start.1 = (f32[4,160,128]{2,1,0:T(8,128)S(1)}, f32[4,160,128]{2,1,0:T(8,128)S(1)}, u32[]{:S(2)}, u32[]{:S(2)}) collective-permute-start(f32[4,160,128]{2,1,0:T(8,128)S(1)} %far0.1.after_ref), channel_id=1, source_target_pairs={{0,2},{2,0},{4,6},{6,4},{8,10},{10,8},{12,14},{14,12},{16,18},{18,... | collective-permute-start | bytes 983048 | tf_op jit(solution)/shard_map/ppermute | solution.py:500
  10.0 0.0 copy-done.5
  10.1 0.0 copy-done.6
  10.1 0.0 copy-done.7
  10.1 0.0 copy-done.8
  10.1 0.0 copy-done.9
  10.1 1.8 %phi.1 = (bf16[16,256,160]{2,1,0:T(8,128)(2,1)S(1)}, bf16[16,256,160]{2,1,0:T(8,128)(2,1)S(1)}, f32[16,1,128]{2,1,0:T(1,128)S(1)}) custom-call(bf16[256,256]{1,0:T(8,128)(2,1)S(1)} %copy-done.5, bf16[4,64,160]{2,1,0:T(8,128)(2,1)S(1)} %copy-done.8, bf16[4,64,160]{2,1,0:T(8,128)(2,1)S(1)} %copy-done.7, f32[8,160]{1,0:T(8,128)S(1)} %copy-done.9, ...), custom_call_target="tpu_custom_call" | custom-call | flops 2070000000 | tf_op jit(solution)/shard_map/phi/pallas_call | solution.py:142
  11.9 0.0 copy-start
  11.9 0.0 copy-done.2
  11.9 0.0 copy-done.3
  11.9 0.6 %by_head.1 = (bf16[16,256,128]{2,1,0:T(8,128)(2,1)S(1)}, bf16[16,256,128]{2,1,0:T(8,128)(2,1)S(1)}, f32[8,128]{1,0:T(8,128)S(1)}) custom-call(bf16[256,16,128]{2,1,0:T(8,128)(2,1)S(1)} %copy-done.3, bf16[256,16,128]{2,1,0:T(8,128)(2,1)S(1)} %copy-done.2, f32[16,1,128]{2,1,0:T(1,128)S(1)} %get-tuple-element.42.after_ref.rest_6_), custom_call_target="tpu_custom_call" | custom-call | flops 1150000000 | tf_op jit(solution)/shard_map/by_head/pallas_call | solution.py:142
  12.5 0.0 copy-done
  12.5 0.0 collective-permute-done.2.got_ref
  12.6 0.0 collective-permute-done.1.other_ref
  12.6 0.1 plane.1
  12.7 0.0 copy-start.4
  12.7 1.6 %collective-permute-start.3 = (bf16[4,192,128]{2,1,0:T(8,128)(2,1)S(1)}, bf16[4,192,128]{2,1,0:T(8,128)(2,1)S(1)}, u32[]{:S(2)}, u32[]{:S(2)}) collective-permute-start(bf16[4,192,128]{2,1,0:T(8,128)(2,1)S(1)} %get-tuple-element.44.msg_ref.after_ref), channel_id=1, source_target_pairs={{0,8},{2,10},{4,12},{6,14},{8,16},{10,18},{12,20},{14,22},{16,24},... | collective-permute-start | bytes 589832 | tf_op jit(solution)/shard_map/ppermute | solution.py:500
  14.3 0.0 collective-permute-done.4.got_ref
  14.3 0.1 pick.1
  14.4 4.9 %collective-permute-start.6 = (bf16[4,192,128]{2,1,0:T(8,128)(2,1)S(1)}, bf16[4,192,128]{2,1,0:T(8,128)(2,1)S(1)}, u32[]{:S(2)}, u32[]{:S(2)}) collective-permute-start(bf16[4,192,128]{2,1,0:T(8,128)(2,1)S(1)} %get-tuple-element.49), channel_id=1, source_target_pairs={{0,16},{2,18},{4,20},{6,22},{8,8},{10,10},{12,12},{14,14},{24,24},... | collective-permute-start | bytes 589832 | tf_op jit(solution)/shard_map/ppermute | solution.py:500
  19.2 0.1 collective-permute-start.10
  19.3 0.0 copy-done.4
  19.3 2.8 %intra.1 = (f32[16,256,128]{2,1,0:T(8,128)S(1)}, f32[16,256,128]{2,1,0:T(8,128)S(1)}, f32[8,128]{1,0:T(8,128)S(1)}) custom-call(bf16[256,256]{1,0:T(8,128)(2,1)S(1)} %copy-done.5, bf16[256,256]{1,0:T(8,128)(2,1)S(1)} %copy-done.4, bf16[16,256,128]{2,1,0:T(8,128)(2,1)S(1)} %get-tuple-element.40.vh_ref, ...), custom_call_target="tpu_custom_call" | custom-call | flops 3220000000 | tf_op jit(solution)/shard_map/intra/pallas_call | solution.py:142
  22.1 0.0 collective-permute-done.3.rest_0_
  22.2 0.1 round.1.after_ref
  22.2 0.7 %collective-permute-start.5 = (bf16[4,192,128]{2,1,0:T(8,128)(2,1)S(1)}, bf16[4,192,128]{2,1,0:T(8,128)(2,1)S(1)}, u32[]{:S(2)}, u32[]{:S(2)}) collective-permute-start(bf16[4,192,128]{2,1,0:T(8,128)(2,1)S(1)} %round.1.after_ref), channel_id=1, source_target_pairs={{8,24},{10,26},{12,28},{14,30},{0,0},{2,2},{4,4},{6,6},{16,16},{18... | collective-permute-start | bytes 589832 | tf_op jit(solution)/shard_map/ppermute | solution.py:500
  22.9 2.8 %window.1 = (f32[16,192,128]{2,1,0:T(8,128)S(1)}, f32[2,4,160,128]{3,2,1,0:T(8,128)S(1)}, f32[8,128]{1,0:T(8,128)S(1)}) custom-call(bf16[16,256,128]{2,1,0:T(8,128)(2,1)S(1)} %get-tuple-element.50.qh_ref, bf16[16,256,128]{2,1,0:T(8,128)(2,1)S(1)} %get-tuple-element.51.kh_ref, bf16[16,256,128]{2,1,0:T(8,128)(2,1)S(1)} %get-tuple-element.40.vh_ref, ...), custom_call_target="tpu_custom_call" | custom-call | flops 4024999936 | tf_op jit(solution)/shard_map/window/pallas_call | solution.py:142
  25.7 1.5 %collective-permute-start.9 = (f32[2,4,160,128]{3,2,1,0:T(8,128)S(1)}, f32[2,4,160,128]{3,2,1,0:T(8,128)S(1)}, u32[]{:S(2)}, u32[]{:S(2)}) collective-permute-start(f32[2,4,160,128]{3,2,1,0:T(8,128)S(1)} %get-tuple-element.55), channel_id=1, source_target_pairs={{0,2},{2,0},{4,6},{6,4},{8,10},{10,8},{12,14},{14,12},{16,18},{18,... | collective-permute-start | bytes 1966088 | tf_op jit(solution)/shard_map/ppermute | solution.py:500
  27.2 0.0 collective-permute-done.6.rest_2_
  27.2 0.0 collective-permute-done.5.rest_1_
  27.2 0.2 before.1
  27.4 0.8 %collective-permute-start.7 = (bf16[4,192,128]{2,1,0:T(8,128)(2,1)S(1)}, bf16[4,192,128]{2,1,0:T(8,128)(2,1)S(1)}, u32[]{:S(2)}, u32[]{:S(2)}) collective-permute-start(bf16[4,192,128]{2,1,0:T(8,128)(2,1)S(1)} %get-tuple-element.53.after_ref), channel_id=1, source_target_pairs={{0,4},{2,6},{4,0},{6,2},{8,12},{10,14},{12,8},{14,10},{16,20},{18,... | collective-permute-start | bytes 589832 | tf_op jit(solution)/shard_map/ppermute | solution.py:500
  28.2 0.0 collective-permute-start.8
  28.2 0.0 collective-permute-done.10.rim_ref
  28.2 0.2 turn.1
  28.4 0.0 copy-start.1
  28.4 0.8 %edge.1.rest_4_ = f32[16,64,128]{2,1,0:T(8,128)S(1)} custom-call(bf16[16,256,128]{2,1,0:T(8,128)(2,1)S(1)} %get-tuple-element.50.qh_ref, bf16[16,256,128]{2,1,0:T(8,128)(2,1)S(1)} %get-tuple-element.51.kh_ref, bf16[16,256,128]{2,1,0:T(8,128)(2,1)S(1)} %get-tuple-element.40.vh_ref, bf16[16,64,128]{2,1,0:T(8,128)(2,1)S(1)} %get-tuple-element.60.rk_ref, ...), custom_call_target="tpu_custom_call" | custom-call | flops 1150000000 | tf_op jit(solution)/shard_map/edge/pallas_call | solution.py:142
  29.2 0.6 %collective-permute-done.8.far_ref = f32[4,160,128]{2,1,0:T(8,128)S(1)} collective-permute-done((f32[4,160,128]{2,1,0:T(8,128)S(1)}, f32[4,160,128]{2,1,0:T(8,128)S(1)}, u32[]{:S(2)}, u32[]{:S(2)}) %collective-permute-start.8) | collective-permute-done | bytes 327712 | tf_op jit(solution)/shard_map/ppermute | solution.py:500
  29.8 0.0 collective-permute-done.9.extra_ref
  29.8 0.0 copy-done.1
  29.8 1.4 %final0.1 = (f32[16,256,128]{2,1,0:T(8,128)S(1)}, f32[256,128]{1,0:T(8,128)S(1)}) custom-call(f32[4,160,128]{2,1,0:T(8,128)S(1)} %get-tuple-element.54.mine_ref, f32[4,160,128]{2,1,0:T(8,128)S(1)} %collective-permute-done.1.other_ref, f32[4,160,128]{2,1,0:T(8,128)S(1)} %collective-permute-done.8.far_ref, ...), custom_call_target="tpu_custom_call" | custom-call | flops 1150000000 | tf_op jit(solution)/shard_map/final0/pallas_call | solution.py:142
  31.2 3.1 %collective-permute-done.7.got_ref = bf16[4,192,128]{2,1,0:T(8,128)(2,1)S(1)} collective-permute-done((bf16[4,192,128]{2,1,0:T(8,128)(2,1)S(1)}, bf16[4,192,128]{2,1,0:T(8,128)(2,1)S(1)}, u32[]{:S(2)}, u32[]{:S(2)}) %collective-permute-start.7) | collective-permute-done | bytes 196640 | tf_op jit(solution)/shard_map/ppermute | solution.py:500
  34.3 0.1 collective-permute-start.11
  34.4 0.8 %final1.1 = (f32[16,256,128]{2,1,0:T(8,128)S(1)}, f32[256,128]{1,0:T(8,128)S(1)}) custom-call(f32[4,160,128]{2,1,0:T(8,128)S(1)} %open.3.base_ref, f32[4,160,128]{2,1,0:T(8,128)S(1)} %get-tuple-element.66.extra_ref, bf16[16,256,160]{2,1,0:T(8,128)(2,1)S(1)} %get-tuple-element.56.rest_0_, ...), custom_call_target="tpu_custom_call", output_to_operand_aliasing={{0}: (9, {})} | custom-call | flops 1150000000 | tf_op jit(solution)/shard_map/final1/pallas_call | solution.py:142
  35.2 0.7 %collective-permute-done.11.base_ref = bf16[4,192,128]{2,1,0:T(8,128)(2,1)S(1)} collective-permute-done((bf16[4,192,128]{2,1,0:T(8,128)(2,1)S(1)}, bf16[4,192,128]{2,1,0:T(8,128)(2,1)S(1)}, u32[]{:S(2)}, u32[]{:S(2)}) %collective-permute-start.11) | collective-permute-done | bytes 196640 | tf_op jit(solution)/shard_map/ppermute | solution.py:500
  35.8 1.0 %final2.1 = (f32[16,256,128]{2,1,0:T(8,128)S(1)}, f32[8,256]{1,0:T(8,128)S(1)}) custom-call(bf16[4,192,128]{2,1,0:T(8,128)(2,1)S(1)} %collective-permute-done.11.base_ref, f32[2,4,160,128]{3,2,1,0:T(8,128)S(1)} %collective-permute-done.9.extra_ref, bf16[16,256,160]{2,1,0:T(8,128)(2,1)S(1)} %get-tuple-element.56.rest_0_, ...), custom_call_target="tpu_custom_call", output_to_operand_aliasing={{0}: (9, {})} | custom-call | flops 1150000000 | tf_op jit(solution)/shard_map/final2/pallas_call | solution.py:142
  36.8 1.5 %collective-permute-start.12 = (f32[8,256]{1,0:T(8,128)S(1)}, f32[8,256]{1,0:T(8,128)S(1)}, u32[]{:S(2)}, u32[]{:S(2)}) collective-permute-start(f32[8,256]{1,0:T(8,128)S(1)} %get-tuple-element.72.sq_ref), channel_id=1, source_target_pairs={{0,1},{1,0},{2,3},{3,2},{4,5},{5,4},{6,7},{7,6},{8,9},{9,8},{10,11... | collective-permute-start | bytes 24584 | tf_op jit(solution)/shard_map/ppermute | solution.py:616
  38.3 2.2 %collective-permute-done.12.rest_0_ = f32[8,256]{1,0:T(8,128)S(1)} collective-permute-done((f32[8,256]{1,0:T(8,128)S(1)}, f32[8,256]{1,0:T(8,128)S(1)}, u32[]{:S(2)}, u32[]{:S(2)}) %collective-permute-start.12) | collective-permute-done | bytes 8224 | tf_op jit(solution)/shard_map/ppermute | solution.py:616
  40.5 1.4 %norm.1 = bf16[256,16,128]{2,1,0:T(8,128)(2,1)} custom-call(f32[16,256,128]{2,1,0:T(8,128)S(1)} %get-tuple-element.71.mixed_ref, f32[8,256]{1,0:T(8,128)S(1)} %get-tuple-element.72.sq_ref, f32[8,256]{1,0:T(8,128)S(1)} %collective-permute-done.12.rest_0_), custom_call_target="tpu_custom_call" | custom-call | flops 1150000000 | tf_op jit(solution)/shard_map/norm/pallas_call | solution.py:142
  (3 shorter events, 0.1 us)
Async XLA Ops:
  2.0 1.8 %collective-permute-start = (f32[4,160,128]{2,1,0:T(8,128)S(1)}, f32[4,160,128]{2,1,0:T(8,128)S(1)}, u32[]{:S(2)}, u32[]{:S(2)}) collective-permute-start(f32[4,160,128]{2,1,0:T(8,128)S(1)} %get-tuple-element.41.after_ref), channel_id=1, source_target_pairs={{0,2},{2,0},{4,6},{6,4},{8,10},{10,8},{12,14},{14,12},{16,18},{18,... | collective-permute-start | bytes 983048 | tf_op jit(solution)/shard_map/ppermute | solution.py:500
  2.5 11.8 %collective-permute-start.4 = (bf16[2,64,16,128]{3,2,1,0:T(8,128)(2,1)S(1)}, bf16[2,64,16,128]{3,2,1,0:T(8,128)(2,1)S(1)}, u32[]{:S(2)}, u32[]{:S(2)}) collective-permute-start(bf16[2,64,16,128]{3,2,1,0:T(8,128)(2,1)S(1)} %get-tuple-element.46.rim_ref), channel_id=1, source_target_pairs={{6,14},{14,22},{22,30},{0,0},{2,2},{4,4},{8,8},{10,10},{12,12},{16... | collective-permute-start | bytes 1572872 | tf_op jit(solution)/shard_map/ppermute | solution.py:500
  3.8 8.8 %collective-permute-start.2 = (bf16[4,192,128]{2,1,0:T(8,128)(2,1)S(1)}, bf16[4,192,128]{2,1,0:T(8,128)(2,1)S(1)}, u32[]{:S(2)}, u32[]{:S(2)}) collective-permute-start(bf16[4,192,128]{2,1,0:T(8,128)(2,1)S(1)} %chip.1.after_ref), channel_id=1, source_target_pairs={{0,4},{2,6},{4,0},{6,2},{8,12},{10,14},{12,8},{14,10},{16,20},{18,... | collective-permute-start | bytes 589832 | tf_op jit(solution)/shard_map/ppermute | solution.py:500
  7.2 2.9 %copy-start.5 = (bf16[256,256]{1,0:T(8,128)(2,1)S(1)}, bf16[256,256]{1,0:T(8,128)(2,1)}, u32[]{:S(2)}) copy-start(bf16[256,256]{1,0:T(8,128)(2,1)} %q_ref.3) | copy-start | bytes 393220
  7.2 2.9 %copy-start.6 = (bf16[16,128]{1,0:T(8,128)(2,1)S(1)}, bf16[16,128]{1,0:T(8,128)(2,1)}, u32[]{:S(2)}) copy-start(bf16[16,128]{1,0:T(8,128)(2,1)} %gain_ref.1) | copy-start | bytes 12292
  7.2 2.9 %copy-start.7 = (bf16[4,64,160]{2,1,0:T(8,128)(2,1)S(1)}, bf16[4,64,160]{2,1,0:T(8,128)(2,1)}, u32[]{:S(2)}) copy-start(bf16[4,64,160]{2,1,0:T(8,128)(2,1)} %constant.7.clone.e2_ref) | copy-start | bytes 245764
  7.2 2.9 %copy-start.8 = (bf16[4,64,160]{2,1,0:T(8,128)(2,1)S(1)}, bf16[4,64,160]{2,1,0:T(8,128)(2,1)}, u32[]{:S(2)}) copy-start(bf16[4,64,160]{2,1,0:T(8,128)(2,1)} %constant.6.clone.e1_ref) | copy-start | bytes 245764
  7.2 2.9 %copy-start.9 = (f32[8,160]{1,0:T(8,128)S(1)}, f32[8,160]{1,0:T(8,128)}, u32[]{:S(2)}) copy-start(f32[8,160]{1,0:T(8,128)} %constant.8.clone.add_ref) | copy-start | bytes 15364
  7.7 4.2 %copy-start.2 = (bf16[256,16,128]{2,1,0:T(8,128)(2,1)S(1)}, bf16[256,16,128]{2,1,0:T(8,128)(2,1)}, u32[]{:S(2)}) copy-start(bf16[256,16,128]{2,1,0:T(8,128)(2,1)} %wk_ref.1) | copy-start | bytes 3145732
  7.7 4.2 %copy-start.3 = (bf16[256,16,128]{2,1,0:T(8,128)(2,1)S(1)}, bf16[256,16,128]{2,1,0:T(8,128)(2,1)}, u32[]{:S(2)}) copy-start(bf16[256,16,128]{2,1,0:T(8,128)(2,1)} %wq_ref.1) | copy-start | bytes 3145732
  7.7 4.9 %collective-permute-start.1 = (f32[4,160,128]{2,1,0:T(8,128)S(1)}, f32[4,160,128]{2,1,0:T(8,128)S(1)}, u32[]{:S(2)}, u32[]{:S(2)}) collective-permute-start(f32[4,160,128]{2,1,0:T(8,128)S(1)} %far0.1.after_ref), channel_id=1, source_target_pairs={{0,2},{2,0},{4,6},{6,4},{8,10},{10,8},{12,14},{14,12},{16,18},{18,... | collective-permute-start | bytes 983048 | tf_op jit(solution)/shard_map/ppermute | solution.py:500
  11.9 0.6 %copy-start = (f32[16,1,128]{2,1,0:T(1,128)}, f32[16,1,128]{2,1,0:T(1,128)S(1)}, u32[]{:S(2)}) copy-start(f32[16,1,128]{2,1,0:T(1,128)S(1)} %get-tuple-element.42.after_ref.rest_6_) | copy-start | bytes 24580
  12.7 6.6 %copy-start.4 = (bf16[256,256]{1,0:T(8,128)(2,1)S(1)}, bf16[256,256]{1,0:T(8,128)(2,1)}, u32[]{:S(2)}) copy-start(bf16[256,256]{1,0:T(8,128)(2,1)} %k_ref.1) | copy-start | bytes 393220
  12.7 9.5 %collective-permute-start.3 = (bf16[4,192,128]{2,1,0:T(8,128)(2,1)S(1)}, bf16[4,192,128]{2,1,0:T(8,128)(2,1)S(1)}, u32[]{:S(2)}, u32[]{:S(2)}) collective-permute-start(bf16[4,192,128]{2,1,0:T(8,128)(2,1)S(1)} %get-tuple-element.44.msg_ref.after_ref), channel_id=1, source_target_pairs={{0,8},{2,10},{4,12},{6,14},{8,16},{10,18},{12,20},{14,22},{16,24},... | collective-permute-start | bytes 589832 | tf_op jit(solution)/shard_map/ppermute | solution.py:500
  14.4 12.8 %collective-permute-start.6 = (bf16[4,192,128]{2,1,0:T(8,128)(2,1)S(1)}, bf16[4,192,128]{2,1,0:T(8,128)(2,1)S(1)}, u32[]{:S(2)}, u32[]{:S(2)}) collective-permute-start(bf16[4,192,128]{2,1,0:T(8,128)(2,1)S(1)} %get-tuple-element.49), channel_id=1, source_target_pairs={{0,16},{2,18},{4,20},{6,22},{8,8},{10,10},{12,12},{14,14},{24,24},... | collective-permute-start | bytes 589832 | tf_op jit(solution)/shard_map/ppermute | solution.py:500
  19.2 9.0 %collective-permute-start.10 = (bf16[2,64,16,128]{3,2,1,0:T(8,128)(2,1)S(1)}, bf16[2,64,16,128]{3,2,1,0:T(8,128)(2,1)S(1)}, u32[]{:S(2)}, u32[]{:S(2)}) collective-permute-start(bf16[2,64,16,128]{3,2,1,0:T(8,128)(2,1)S(1)} %get-tuple-element.47.rim_ref), channel_id=1, source_target_pairs={{0,2},{2,4},{4,6},{6,0},{8,10},{10,12},{12,14},{14,8},{16,18},{18,... | collective-permute-start | bytes 1572872 | tf_op jit(solution)/shard_map/ppermute | solution.py:500
  22.2 5.0 %collective-permute-start.5 = (bf16[4,192,128]{2,1,0:T(8,128)(2,1)S(1)}, bf16[4,192,128]{2,1,0:T(8,128)(2,1)S(1)}, u32[]{:S(2)}, u32[]{:S(2)}) collective-permute-start(bf16[4,192,128]{2,1,0:T(8,128)(2,1)S(1)} %round.1.after_ref), channel_id=1, source_target_pairs={{8,24},{10,26},{12,28},{14,30},{0,0},{2,2},{4,4},{6,6},{16,16},{18... | collective-permute-start | bytes 589832 | tf_op jit(solution)/shard_map/ppermute | solution.py:500
  25.7 4.1 %collective-permute-start.9 = (f32[2,4,160,128]{3,2,1,0:T(8,128)S(1)}, f32[2,4,160,128]{3,2,1,0:T(8,128)S(1)}, u32[]{:S(2)}, u32[]{:S(2)}) collective-permute-start(f32[2,4,160,128]{3,2,1,0:T(8,128)S(1)} %get-tuple-element.55), channel_id=1, source_target_pairs={{0,2},{2,0},{4,6},{6,4},{8,10},{10,8},{12,14},{14,12},{16,18},{18,... | collective-permute-start | bytes 1966088 | tf_op jit(solution)/shard_map/ppermute | solution.py:500
  27.4 6.9 %collective-permute-start.7 = (bf16[4,192,128]{2,1,0:T(8,128)(2,1)S(1)}, bf16[4,192,128]{2,1,0:T(8,128)(2,1)S(1)}, u32[]{:S(2)}, u32[]{:S(2)}) collective-permute-start(bf16[4,192,128]{2,1,0:T(8,128)(2,1)S(1)} %get-tuple-element.53.after_ref), channel_id=1, source_target_pairs={{0,4},{2,6},{4,0},{6,2},{8,12},{10,14},{12,8},{14,10},{16,20},{18,... | collective-permute-start | bytes 589832 | tf_op jit(solution)/shard_map/ppermute | solution.py:500
  28.2 1.6 %collective-permute-start.8 = (f32[4,160,128]{2,1,0:T(8,128)S(1)}, f32[4,160,128]{2,1,0:T(8,128)S(1)}, u32[]{:S(2)}, u32[]{:S(2)}) collective-permute-start(f32[4,160,128]{2,1,0:T(8,128)S(1)} %get-tuple-element.54.mine_ref), channel_id=1, source_target_pairs={{0,2},{2,0},{4,6},{6,4},{8,10},{10,8},{12,14},{14,12},{16,18},{18,... | collective-permute-start | bytes 983048 | tf_op jit(solution)/shard_map/ppermute | solution.py:500
  28.4 1.4 %copy-start.1 = (f32[16,1,128]{2,1,0:T(1,128)S(1)}, f32[16,1,128]{2,1,0:T(1,128)}, u32[]{:S(2)}) copy-start(f32[16,1,128]{2,1,0:T(1,128)} %copy-done) | copy-start | bytes 24580
  34.3 1.5 %collective-permute-start.11 = (bf16[4,192,128]{2,1,0:T(8,128)(2,1)S(1)}, bf16[4,192,128]{2,1,0:T(8,128)(2,1)S(1)}, u32[]{:S(2)}, u32[]{:S(2)}) collective-permute-start(bf16[4,192,128]{2,1,0:T(8,128)(2,1)S(1)} %collective-permute-done.7.got_ref), channel_id=1, source_target_pairs={{0,2},{2,0},{4,6},{6,4},{8,10},{10,8},{12,14},{14,12},{16,18},{18,... | collective-permute-start | bytes 589832 | tf_op jit(solution)/shard_map/ppermute | solution.py:500
  36.8 3.7 %collective-permute-start.12 = (f32[8,256]{1,0:T(8,128)S(1)}, f32[8,256]{1,0:T(8,128)S(1)}, u32[]{:S(2)}, u32[]{:S(2)}) collective-permute-start(f32[8,256]{1,0:T(8,128)S(1)} %get-tuple-element.72.sq_ref), channel_id=1, source_target_pairs={{0,1},{1,0},{2,3},{3,2},{4,5},{5,4},{6,7},{7,6},{8,9},{9,8},{10,11... | collective-permute-start | bytes 24584 | tf_op jit(solution)/shard_map/ppermute | solution.py:616

commit v7 on v6

--- a/solution.py
+++ b/solution.py
@@ -265,9 +265,12 @@
     each(own_ref.shape[0], one)
 
 
-def pick_kernel(rim_ref, got_ref, msg_ref, out_ref, again_ref):
+def again_kernel(msg_ref, after_ref, again_ref):
+    again_ref[...] = msg_ref[...]
+
+
+def pick_kernel(rim_ref, got_ref, msg_ref, out_ref):
     last = lax.axis_index("ctx") % 4 == 3
-    again_ref[...] = msg_ref[...]
 
     @pl.when(last)
     def _():
@@ -363,19 +366,19 @@
     kh_ref[...] = jnp.swapaxes(wk_ref[...], 0, 1)
 
 
-def turn_kernel(rim_ref, other1_ref, after_ref, k_ref, v_ref, keep_ref):
+def turn_kernel(rim_ref, other1_ref, near0_ref, near1_ref, after_ref,
+                k_ref, v_ref, keep_ref, nears_ref):
     keep_ref[...] = other1_ref[...]
+    nears_ref[0] = near0_ref[...]
+    nears_ref[1] = near1_ref[...]
     k_ref[...] = jnp.swapaxes(rim_ref[0], 0, 1)
     v_ref[...] = jnp.swapaxes(rim_ref[1], 0, 1)
 
 
-def window_kernel(qh_ref, kh_ref, vh_ref, near0_ref, near1_ref, after_ref,
-                  win_ref, nears_ref, token_ref):
+def window_kernel(qh_ref, kh_ref, vh_ref, after_ref, win_ref, token_ref):
     heads, toks, dim = vh_ref.shape
     part = heads // 4
     token_ref[...] = jnp.zeros_like(token_ref)
-    nears_ref[0] = near0_ref[...]
-    nears_ref[1] = near1_ref[...]
     band, _ = band_mask()
     blocks = toks // WINDOW - 1
 
@@ -524,6 +527,7 @@
     far0 = states("far0", 1, 0, msg)
     other0 = permute(far0, core_swap)
     near0 = states("near0", 0, 0, far0)
+    far_near0, far_near1 = permute(near0, core_swap), permute(near1, core_swap)
     first_table, second_table, add_table = pair_tables(part)
     phi_high, phi_low, gain = call(
         phi_kernel, "phi",
@@ -536,9 +540,8 @@
         (pltpu.VMEM((heads, toks, dim), BF16),) * 2 + (token_shape,), win_q, win_k, gain,
     )
     total, msg = call(plane_kernel, "plane", (state_shape, msg_shape), near0, other0, pair, token)
-    rim, again = call(
-        pick_kernel, "pick", (pltpu.VMEM(rim.shape, BF16), msg_shape), rim, rim_up, msg
-    )
+    rim = call(pick_kernel, "pick", pltpu.VMEM(rim.shape, BF16), rim, rim_up, msg)
+    again = call(again_kernel, "again", msg_shape, msg, rim)
     rim_prev = permute(rim, [(i, i - i % 4 + (i + 1) % 4) for i in range(count)])
     groups = count // 4
     gots, limits, early = [], [], {}
@@ -563,16 +566,17 @@
             got = [permute(msg, full(pairs, count)), early[step]]
             limit = [(step + 1, groups), (step, step)]
         if step == 2:
-            win, nears, token = call(
+            win, token = call(
                 window_kernel, "window",
                 (pltpu.VMEM((heads, toks - WINDOW, dim), F32),
-                 pltpu.VMEM((2, part, ROWS, dim), F32), token_shape),
-                wq_h, wk_h, values_h, near0, near1, msg,
+                 token_shape),
+                wq_h, wk_h, values_h, msg,
             )
-            rim_k, rim_v, other1 = call(
+            rim_k, rim_v, other1, far_nears = call(
                 turn_kernel, "turn",
-                (pltpu.VMEM((heads, WINDOW, dim), BF16),) * 2 + (state_shape,),
-                rim_prev, other1, token,
+                (pltpu.VMEM((heads, WINDOW, dim), BF16),) * 2
+                + (state_shape, pltpu.VMEM((2, part, ROWS, dim), F32)),
+                rim_prev, other1, far_near0, far_near1, token,
             )
         gots.extend(got)
         limits.extend(limit)
@@ -590,7 +594,6 @@
     )
     got = permute(msg, pair_swap)
     far_mine = permute(mine, core_swap)
-    far_nears = permute(nears, core_swap)
     edge = call(edge_kernel, "edge", pltpu.VMEM((heads, WINDOW, dim), F32),
                 wq_h, wk_h, values_h, rim_k, rim_v, msg)
 

time: 42.1 us -> 41.8 us (level)
  starting transfers between devices: 17.5 us -> 17 us
    ppermute x12 -> x13, starting transfers between devices: 16 us -> 15.5 us  [permute(): return lax.ppermute(x, 'ctx', pairs)]
    ppermute x12 -> x13, waiting for transfers between devices: 4.48 us -> 4.72 us  [permute(): return lax.ppermute(x, 'ctx', pairs)]
    pallas_call x21 -> x22, Pallas kernels: 17.3 us -> 17.3 us  [call(): pl.pallas_call(body, out_shape=outs, in_specs=[spec] * len(operands), out...]
  transfers between devices with their start and end apart: 13 -> 14, of which waited for: 5 -> 5; matrix products, arithmetic and copies ran while one was open for 0% -> 0% of each run, Pallas kernels for 31% -> 31%
where the time goes in v7:
time: 41.8 us; the launch traced here: 41.6 us
  Pallas kernels  17.3 us (41%)
  starting transfers between devices  17 us (41%)
  waiting for transfers between devices  6.88 us (16%)
    pallas_call x22, Pallas kernels, call(): pl.pallas_call(body, out_shape=outs, in_specs=[spec] * len(operands), out...  17.3 us
    ppermute x13, starting transfers between devices, permute(): return lax.ppermute(x, 'ctx', pairs)  15.5 us
    ppermute x13, waiting for transfers between devices, permute(): return lax.ppermute(x, 'ctx', pairs)  4.72 us
    ppermute x1, waiting for transfers between devices, on_device(): lax.ppermute(squares, 'head', [(i, (i + k) % (peers + 1)) for i in range(...  2.16 us
    ppermute x1, starting transfers between devices, on_device(): lax.ppermute(squares, 'head', [(i, (i + k) % (peers + 1)) for i in range(...  1.52 us
  transfers between devices with their start and end apart: 14, of which 5 were waited for; matrix products, arithmetic and copies ran while one was open for 0% of the time, Pallas kernels for 31%

profile of v7, /device:TPU:0, one launch (start us, length us, event | category | flops | bytes accessed | tf_op | source)
XLA Modules:
  0.0 41.6 jit_solution(9756032104868593083)
XLA Ops:
  0.0 1.9 %far1.1 = (f32[4,160,128]{2,1,0:T(8,128)S(1)}, bf16[16,256,128]{2,1,0:T(8,128)(2,1)S(1)}, f32[256,256]{1,0:T(8,128)S(1)}, bf16[2,64,16,128]{3,2,1,0:T(8,128)(2,1)S(1)}) custom-call(bf16[256,256]{1,0:T(8,128)(2,1)} %k_ref.1, bf16[256,16,128]{2,1,0:T(8,128)(2,1)} %v_hbm.1, bf16[256,16,128]{2,1,0:T(8,128)(2,1)} %wk_ref.1), custom_call_target="tpu_custom_call" | custom-call | flops 1150000000 | tf_op jit(solution)/shard_map/far1/pallas_call | solution.py:142
  2.0 0.5 %collective-permute-start = (f32[4,160,128]{2,1,0:T(8,128)S(1)}, f32[4,160,128]{2,1,0:T(8,128)S(1)}, u32[]{:S(2)}, u32[]{:S(2)}) collective-permute-start(f32[4,160,128]{2,1,0:T(8,128)S(1)} %get-tuple-element.39.after_ref), channel_id=1, source_target_pairs={{0,2},{2,0},{4,6},{6,4},{8,10},{10,8},{12,14},{14,12},{16,18},{18,... | collective-permute-start | bytes 983048 | tf_op jit(solution)/shard_map/ppermute | solution.py:503
  2.5 0.4 %near1.1.own_ref = f32[4,160,128]{2,1,0:T(8,128)S(1)} custom-call(f32[256,256]{1,0:T(8,128)S(1)} %get-tuple-element.37.kt_ref, bf16[16,256,128]{2,1,0:T(8,128)(2,1)S(1)} %get-tuple-element.38.vh_ref, f32[4,160,128]{2,1,0:T(8,128)S(1)} %get-tuple-element.39.after_ref), custom_call_target="tpu_custom_call" | custom-call | flops 1150000000 | tf_op jit(solution)/shard_map/near1/pallas_call | solution.py:142
  2.9 0.1 collective-permute-start.11
  3.0 0.7 %collective-permute-start.4 = (bf16[2,64,16,128]{3,2,1,0:T(8,128)(2,1)S(1)}, bf16[2,64,16,128]{3,2,1,0:T(8,128)(2,1)S(1)}, u32[]{:S(2)}, u32[]{:S(2)}) collective-permute-start(bf16[2,64,16,128]{3,2,1,0:T(8,128)(2,1)S(1)} %get-tuple-element.44.rim_ref), channel_id=1, source_target_pairs={{6,14},{14,22},{22,30},{0,0},{2,2},{4,4},{8,8},{10,10},{12,12},{16... | collective-permute-start | bytes 1572872 | tf_op jit(solution)/shard_map/ppermute | solution.py:503
  3.7 0.0 collective-permute-done.other_ref.other1_ref
  3.7 0.1 chip.1.after_ref
  3.8 3.0 %collective-permute-start.2 = (bf16[4,192,128]{2,1,0:T(8,128)(2,1)S(1)}, bf16[4,192,128]{2,1,0:T(8,128)(2,1)S(1)}, u32[]{:S(2)}, u32[]{:S(2)}) collective-permute-start(bf16[4,192,128]{2,1,0:T(8,128)(2,1)S(1)} %chip.1.after_ref), channel_id=1, source_target_pairs={{0,4},{2,6},{4,0},{6,2},{8,12},{10,14},{12,8},{14,10},{16,20},{18,... | collective-permute-start | bytes 589832 | tf_op jit(solution)/shard_map/ppermute | solution.py:503
  6.8 0.4 %far0.1.after_ref = f32[4,160,128]{2,1,0:T(8,128)S(1)} custom-call(f32[256,256]{1,0:T(8,128)S(1)} %get-tuple-element.37.kt_ref, bf16[16,256,128]{2,1,0:T(8,128)(2,1)S(1)} %get-tuple-element.38.vh_ref, bf16[4,192,128]{2,1,0:T(8,128)(2,1)S(1)} %chip.1.after_ref), custom_call_target="tpu_custom_call" | custom-call | flops 1150000000 | tf_op jit(solution)/shard_map/far0/pallas_call | solution.py:142
  7.3 0.0 copy-start.5
  7.3 0.0 copy-start.6
  7.3 0.0 copy-start.7
  7.3 0.0 copy-start.8
  7.3 0.0 copy-start.9
  7.3 0.5 %near0.1.after_ref.own_ref = f32[4,160,128]{2,1,0:T(8,128)S(1)} custom-call(f32[256,256]{1,0:T(8,128)S(1)} %get-tuple-element.37.kt_ref, bf16[16,256,128]{2,1,0:T(8,128)(2,1)S(1)} %get-tuple-element.38.vh_ref, f32[4,160,128]{2,1,0:T(8,128)S(1)} %far0.1.after_ref), custom_call_target="tpu_custom_call" | custom-call | flops 1150000000 | tf_op jit(solution)/shard_map/near0/pallas_call | solution.py:142
  7.8 0.0 copy-start.2
  7.8 0.0 copy-start.3
  7.8 2.3 %collective-permute-start.1 = (f32[4,160,128]{2,1,0:T(8,128)S(1)}, f32[4,160,128]{2,1,0:T(8,128)S(1)}, u32[]{:S(2)}, u32[]{:S(2)}) collective-permute-start(f32[4,160,128]{2,1,0:T(8,128)S(1)} %far0.1.after_ref), channel_id=1, source_target_pairs={{0,2},{2,0},{4,6},{6,4},{8,10},{10,8},{12,14},{14,12},{16,18},{18,... | collective-permute-start | bytes 983048 | tf_op jit(solution)/shard_map/ppermute | solution.py:503
  10.1 0.1 collective-permute-start.10
  10.2 0.0 copy-done.5
  10.2 0.0 copy-done.6
  10.2 0.0 copy-done.7
  10.2 0.0 copy-done.8
  10.2 0.0 copy-done.9
  10.3 1.8 %phi.1 = (bf16[16,256,160]{2,1,0:T(8,128)(2,1)S(1)}, bf16[16,256,160]{2,1,0:T(8,128)(2,1)S(1)}, f32[16,1,128]{2,1,0:T(1,128)S(1)}) custom-call(bf16[256,256]{1,0:T(8,128)(2,1)S(1)} %copy-done.5, bf16[4,64,160]{2,1,0:T(8,128)(2,1)S(1)} %copy-done.8, bf16[4,64,160]{2,1,0:T(8,128)(2,1)S(1)} %copy-done.7, f32[8,160]{1,0:T(8,128)S(1)} %copy-done.9, ...), custom_call_target="tpu_custom_call" | custom-call | flops 2070000000 | tf_op jit(solution)/shard_map/phi/pallas_call | solution.py:142
  12.1 0.0 copy-start
  12.1 0.0 copy-done.2
  12.1 0.0 copy-done.3
  12.1 0.6 %by_head.1 = (bf16[16,256,128]{2,1,0:T(8,128)(2,1)S(1)}, bf16[16,256,128]{2,1,0:T(8,128)(2,1)S(1)}, f32[8,128]{1,0:T(8,128)S(1)}) custom-call(bf16[256,16,128]{2,1,0:T(8,128)(2,1)S(1)} %copy-done.3, bf16[256,16,128]{2,1,0:T(8,128)(2,1)S(1)} %copy-done.2, f32[16,1,128]{2,1,0:T(1,128)S(1)} %get-tuple-element.40.after_ref.rest_6_), custom_call_target="tpu_custom_call" | custom-call | flops 1150000000 | tf_op jit(solution)/shard_map/by_head/pallas_call | solution.py:142
  12.7 0.0 copy-done
  12.7 0.0 collective-permute-done.2.got_ref
  12.7 0.0 collective-permute-done.1.other_ref
  12.8 0.1 plane.1
  12.8 1.6 %collective-permute-start.3 = (bf16[4,192,128]{2,1,0:T(8,128)(2,1)S(1)}, bf16[4,192,128]{2,1,0:T(8,128)(2,1)S(1)}, u32[]{:S(2)}, u32[]{:S(2)}) collective-permute-start(bf16[4,192,128]{2,1,0:T(8,128)(2,1)S(1)} %get-tuple-element.42.msg_ref.after_ref), channel_id=1, source_target_pairs={{0,8},{2,10},{4,12},{6,14},{8,16},{10,18},{12,20},{14,22},{16,24},... | collective-permute-start | bytes 589832 | tf_op jit(solution)/shard_map/ppermute | solution.py:503
  14.5 0.0 collective-permute-done.4.got_ref
  14.5 0.0 copy-start.4
  14.5 0.2 collective-permute-start.9
  14.7 4.7 %collective-permute-start.6 = (bf16[4,192,128]{2,1,0:T(8,128)(2,1)S(1)}, bf16[4,192,128]{2,1,0:T(8,128)(2,1)S(1)}, u32[]{:S(2)}, u32[]{:S(2)}) collective-permute-start(bf16[4,192,128]{2,1,0:T(8,128)(2,1)S(1)} %again.1), channel_id=1, source_target_pairs={{0,16},{2,18},{4,20},{6,22},{8,8},{10,10},{12,12},{14,14},{24,24},... | collective-permute-start | bytes 589832 | tf_op jit(solution)/shard_map/ppermute | solution.py:503
  19.4 2.8 %intra.1 = (f32[16,256,128]{2,1,0:T(8,128)S(1)}, f32[16,256,128]{2,1,0:T(8,128)S(1)}, f32[8,128]{1,0:T(8,128)S(1)}) custom-call(bf16[256,256]{1,0:T(8,128)(2,1)S(1)} %copy-done.5, bf16[256,256]{1,0:T(8,128)(2,1)S(1)} %copy-done.4, bf16[16,256,128]{2,1,0:T(8,128)(2,1)S(1)} %get-tuple-element.38.vh_ref, bf16[2,64,16,128]{3,2,1,0:T(8,128)(2,1)S(1)} %pick.1.rim_ref.after_ref, ...), custom_call_target="tpu_custom_call" | custom-call | flops 3220000000 | tf_op jit(solution)/shard_map/intra/pallas_call | solution.py:142
  22.3 0.0 collective-permute-done.3.rest_0_
  22.3 0.1 round.1.after_ref
  22.3 0.7 %collective-permute-start.5 = (bf16[4,192,128]{2,1,0:T(8,128)(2,1)S(1)}, bf16[4,192,128]{2,1,0:T(8,128)(2,1)S(1)}, u32[]{:S(2)}, u32[]{:S(2)}) collective-permute-start(bf16[4,192,128]{2,1,0:T(8,128)(2,1)S(1)} %round.1.after_ref), channel_id=1, source_target_pairs={{8,24},{10,26},{12,28},{14,30},{0,0},{2,2},{4,4},{6,6},{16,16},{18... | collective-permute-start | bytes 589832 | tf_op jit(solution)/shard_map/ppermute | solution.py:503
  23.0 2.8 %window.1 = (f32[16,192,128]{2,1,0:T(8,128)S(1)}, f32[8,128]{1,0:T(8,128)S(1)}) custom-call(bf16[16,256,128]{2,1,0:T(8,128)(2,1)S(1)} %get-tuple-element.46.qh_ref, bf16[16,256,128]{2,1,0:T(8,128)(2,1)S(1)} %get-tuple-element.47.kh_ref, bf16[16,256,128]{2,1,0:T(8,128)(2,1)S(1)} %get-tuple-element.38.vh_ref, bf16[4,192,128]{2,1,0:T(8,128)(2,1)S(1)} %round.1.after_ref), custom_call_target="tpu_custom_call" | custom-call | flops 4024999936 | tf_op jit(solution)/shard_map/window/pallas_call | solution.py:142
  25.8 0.3 collective-permute-done.6.rest_2_
  26.1 0.0 collective-permute-done.5.rest_1_
  26.1 0.2 before.1
  26.3 1.5 %collective-permute-start.7 = (bf16[4,192,128]{2,1,0:T(8,128)(2,1)S(1)}, bf16[4,192,128]{2,1,0:T(8,128)(2,1)S(1)}, u32[]{:S(2)}, u32[]{:S(2)}) collective-permute-start(bf16[4,192,128]{2,1,0:T(8,128)(2,1)S(1)} %get-tuple-element.49.after_ref), channel_id=1, source_target_pairs={{0,4},{2,6},{4,0},{6,2},{8,12},{10,14},{12,8},{14,10},{16,20},{18,... | collective-permute-start | bytes 589832 | tf_op jit(solution)/shard_map/ppermute | solution.py:503
  27.8 0.0 collective-permute-start.8
  27.8 0.0 collective-permute-done.11.near1_ref
  27.8 0.0 collective-permute-done.10.near0_ref
  27.8 0.0 collective-permute-done.9.rim_ref
  27.8 0.2 turn.1
  28.1 0.0 copy-start.1
  28.1 0.8 %edge.1.rest_4_ = f32[16,64,128]{2,1,0:T(8,128)S(1)} custom-call(bf16[16,256,128]{2,1,0:T(8,128)(2,1)S(1)} %get-tuple-element.46.qh_ref, bf16[16,256,128]{2,1,0:T(8,128)(2,1)S(1)} %get-tuple-element.47.kh_ref, bf16[16,256,128]{2,1,0:T(8,128)(2,1)S(1)} %get-tuple-element.38.vh_ref, bf16[16,64,128]{2,1,0:T(8,128)(2,1)S(1)} %get-tuple-element.56.rk_ref, ...), custom_call_target="tpu_custom_call" | custom-call | flops 1150000000 | tf_op jit(solution)/shard_map/edge/pallas_call | solution.py:142
  28.9 0.6 %collective-permute-done.8.far_ref = f32[4,160,128]{2,1,0:T(8,128)S(1)} collective-permute-done((f32[4,160,128]{2,1,0:T(8,128)S(1)}, f32[4,160,128]{2,1,0:T(8,128)S(1)}, u32[]{:S(2)}, u32[]{:S(2)}) %collective-permute-start.8) | collective-permute-done | bytes 327712 | tf_op jit(solution)/shard_map/ppermute | solution.py:503
  29.5 1.4 %final0.1 = (f32[16,256,128]{2,1,0:T(8,128)S(1)}, f32[256,128]{1,0:T(8,128)S(1)}) custom-call(f32[4,160,128]{2,1,0:T(8,128)S(1)} %get-tuple-element.50.mine_ref, f32[4,160,128]{2,1,0:T(8,128)S(1)} %collective-permute-done.1.other_ref, f32[4,160,128]{2,1,0:T(8,128)S(1)} %collective-permute-done.8.far_ref, f32[2,4,160,128]{3,2,1,0:T(8,128)S(1)} %get-tuple-element.51.extra_ref, ...), custom_call_target="tpu_custom_call" | custom-call | flops 1150000000 | tf_op jit(solution)/shard_map/final0/pallas_call | solution.py:142
  30.8 3.2 %collective-permute-done.7.got_ref = bf16[4,192,128]{2,1,0:T(8,128)(2,1)S(1)} collective-permute-done((bf16[4,192,128]{2,1,0:T(8,128)(2,1)S(1)}, bf16[4,192,128]{2,1,0:T(8,128)(2,1)S(1)}, u32[]{:S(2)}, u32[]{:S(2)}) %collective-permute-start.7) | collective-permute-done | bytes 196640 | tf_op jit(solution)/shard_map/ppermute | solution.py:503
  34.0 0.1 collective-permute-start.12
  34.1 0.8 %final1.1 = (f32[16,256,128]{2,1,0:T(8,128)S(1)}, f32[256,128]{1,0:T(8,128)S(1)}) custom-call(f32[4,160,128]{2,1,0:T(8,128)S(1)} %open.3.base_ref, f32[4,160,128]{2,1,0:T(8,128)S(1)} %get-tuple-element.62.extra_ref, bf16[16,256,160]{2,1,0:T(8,128)(2,1)S(1)} %get-tuple-element.52.rest_0_, ...), custom_call_target="tpu_custom_call", output_to_operand_aliasing={{0}: (9, {})} | custom-call | flops 1150000000 | tf_op jit(solution)/shard_map/final1/pallas_call | solution.py:142
  34.9 0.7 %collective-permute-done.12.base_ref = bf16[4,192,128]{2,1,0:T(8,128)(2,1)S(1)} collective-permute-done((bf16[4,192,128]{2,1,0:T(8,128)(2,1)S(1)}, bf16[4,192,128]{2,1,0:T(8,128)(2,1)S(1)}, u32[]{:S(2)}, u32[]{:S(2)}) %collective-permute-start.12) | collective-permute-done | bytes 196640 | tf_op jit(solution)/shard_map/ppermute | solution.py:503
  35.5 1.0 %final2.1 = (f32[16,256,128]{2,1,0:T(8,128)S(1)}, f32[8,256]{1,0:T(8,128)S(1)}) custom-call(bf16[4,192,128]{2,1,0:T(8,128)(2,1)S(1)} %collective-permute-done.12.base_ref, f32[2,4,160,128]{3,2,1,0:T(8,128)S(1)} %get-tuple-element.51.extra_ref, bf16[16,256,160]{2,1,0:T(8,128)(2,1)S(1)} %get-tuple-element.52.rest_0_, ...), custom_call_target="tpu_custom_call", output_to_operand_aliasing={{0}: (9, {})} | custom-call | flops 1150000000 | tf_op jit(solution)/shard_map/final2/pallas_call | solution.py:142
  36.5 1.5 %collective-permute-start.13 = (f32[8,256]{1,0:T(8,128)S(1)}, f32[8,256]{1,0:T(8,128)S(1)}, u32[]{:S(2)}, u32[]{:S(2)}) collective-permute-start(f32[8,256]{1,0:T(8,128)S(1)} %get-tuple-element.68.sq_ref), channel_id=1, source_target_pairs={{0,1},{1,0},{2,3},{3,2},{4,5},{5,4},{6,7},{7,6},{8,9},{9,8},{10,11... | collective-permute-start | bytes 24584 | tf_op jit(solution)/shard_map/ppermute | solution.py:619
  38.1 2.2 %collective-permute-done.13.rest_0_ = f32[8,256]{1,0:T(8,128)S(1)} collective-permute-done((f32[8,256]{1,0:T(8,128)S(1)}, f32[8,256]{1,0:T(8,128)S(1)}, u32[]{:S(2)}, u32[]{:S(2)}) %collective-permute-start.13) | collective-permute-done | bytes 8224 | tf_op jit(solution)/shard_map/ppermute | solution.py:619
  40.2 1.4 %norm.1 = bf16[256,16,128]{2,1,0:T(8,128)(2,1)} custom-call(f32[16,256,128]{2,1,0:T(8,128)S(1)} %get-tuple-element.67.mixed_ref, f32[8,256]{1,0:T(8,128)S(1)} %get-tuple-element.68.sq_ref, f32[8,256]{1,0:T(8,128)S(1)} %collective-permute-done.13.rest_0_), custom_call_target="tpu_custom_call" | custom-call | flops 1150000000 | tf_op jit(solution)/shard_map/norm/pallas_call | solution.py:142
  (6 shorter events, 0.1 us)
Async XLA Ops:
  2.0 1.8 %collective-permute-start = (f32[4,160,128]{2,1,0:T(8,128)S(1)}, f32[4,160,128]{2,1,0:T(8,128)S(1)}, u32[]{:S(2)}, u32[]{:S(2)}) collective-permute-start(f32[4,160,128]{2,1,0:T(8,128)S(1)} %get-tuple-element.39.after_ref), channel_id=1, source_target_pairs={{0,2},{2,0},{4,6},{6,4},{8,10},{10,8},{12,14},{14,12},{16,18},{18,... | collective-permute-start | bytes 983048 | tf_op jit(solution)/shard_map/ppermute | solution.py:503
  2.9 24.9 %collective-permute-start.11 = (f32[4,160,128]{2,1,0:T(8,128)S(1)}, f32[4,160,128]{2,1,0:T(8,128)S(1)}, u32[]{:S(2)}, u32[]{:S(2)}) collective-permute-start(f32[4,160,128]{2,1,0:T(8,128)S(1)} %near1.1.own_ref), channel_id=1, source_target_pairs={{0,2},{2,0},{4,6},{6,4},{8,10},{10,8},{12,14},{14,12},{16,18},{18,... | collective-permute-start | bytes 983048 | tf_op jit(solution)/shard_map/ppermute | solution.py:503
  3.0 11.4 %collective-permute-start.4 = (bf16[2,64,16,128]{3,2,1,0:T(8,128)(2,1)S(1)}, bf16[2,64,16,128]{3,2,1,0:T(8,128)(2,1)S(1)}, u32[]{:S(2)}, u32[]{:S(2)}) collective-permute-start(bf16[2,64,16,128]{3,2,1,0:T(8,128)(2,1)S(1)} %get-tuple-element.44.rim_ref), channel_id=1, source_target_pairs={{6,14},{14,22},{22,30},{0,0},{2,2},{4,4},{8,8},{10,10},{12,12},{16... | collective-permute-start | bytes 1572872 | tf_op jit(solution)/shard_map/ppermute | solution.py:503
  3.8 8.9 %collective-permute-start.2 = (bf16[4,192,128]{2,1,0:T(8,128)(2,1)S(1)}, bf16[4,192,128]{2,1,0:T(8,128)(2,1)S(1)}, u32[]{:S(2)}, u32[]{:S(2)}) collective-permute-start(bf16[4,192,128]{2,1,0:T(8,128)(2,1)S(1)} %chip.1.after_ref), channel_id=1, source_target_pairs={{0,4},{2,6},{4,0},{6,2},{8,12},{10,14},{12,8},{14,10},{16,20},{18,... | collective-permute-start | bytes 589832 | tf_op jit(solution)/shard_map/ppermute | solution.py:503
  7.3 3.0 %copy-start.5 = (bf16[256,256]{1,0:T(8,128)(2,1)S(1)}, bf16[256,256]{1,0:T(8,128)(2,1)}, u32[]{:S(2)}) copy-start(bf16[256,256]{1,0:T(8,128)(2,1)} %q_ref.3) | copy-start | bytes 393220
  7.3 2.9 %copy-start.6 = (bf16[16,128]{1,0:T(8,128)(2,1)S(1)}, bf16[16,128]{1,0:T(8,128)(2,1)}, u32[]{:S(2)}) copy-start(bf16[16,128]{1,0:T(8,128)(2,1)} %gain_ref.1) | copy-start | bytes 12292
  7.3 2.9 %copy-start.7 = (bf16[4,64,160]{2,1,0:T(8,128)(2,1)S(1)}, bf16[4,64,160]{2,1,0:T(8,128)(2,1)}, u32[]{:S(2)}) copy-start(bf16[4,64,160]{2,1,0:T(8,128)(2,1)} %constant.7.clone.e2_ref) | copy-start | bytes 245764
  7.3 2.9 %copy-start.8 = (bf16[4,64,160]{2,1,0:T(8,128)(2,1)S(1)}, bf16[4,64,160]{2,1,0:T(8,128)(2,1)}, u32[]{:S(2)}) copy-start(bf16[4,64,160]{2,1,0:T(8,128)(2,1)} %constant.6.clone.e1_ref) | copy-start | bytes 245764
  7.3 2.9 %copy-start.9 = (f32[8,160]{1,0:T(8,128)S(1)}, f32[8,160]{1,0:T(8,128)}, u32[]{:S(2)}) copy-start(f32[8,160]{1,0:T(8,128)} %constant.8.clone.add_ref) | copy-start | bytes 15364
  7.8 4.3 %copy-start.2 = (bf16[256,16,128]{2,1,0:T(8,128)(2,1)S(1)}, bf16[256,16,128]{2,1,0:T(8,128)(2,1)}, u32[]{:S(2)}) copy-start(bf16[256,16,128]{2,1,0:T(8,128)(2,1)} %wk_ref.1) | copy-start | bytes 3145732
  7.8 4.3 %copy-start.3 = (bf16[256,16,128]{2,1,0:T(8,128)(2,1)S(1)}, bf16[256,16,128]{2,1,0:T(8,128)(2,1)}, u32[]{:S(2)}) copy-start(bf16[256,16,128]{2,1,0:T(8,128)(2,1)} %wq_ref.1) | copy-start | bytes 3145732
  7.8 4.9 %collective-permute-start.1 = (f32[4,160,128]{2,1,0:T(8,128)S(1)}, f32[4,160,128]{2,1,0:T(8,128)S(1)}, u32[]{:S(2)}, u32[]{:S(2)}) collective-permute-start(f32[4,160,128]{2,1,0:T(8,128)S(1)} %far0.1.after_ref), channel_id=1, source_target_pairs={{0,2},{2,0},{4,6},{6,4},{8,10},{10,8},{12,14},{14,12},{16,18},{18,... | collective-permute-start | bytes 983048 | tf_op jit(solution)/shard_map/ppermute | solution.py:503
  10.1 17.7 %collective-permute-start.10 = (f32[4,160,128]{2,1,0:T(8,128)S(1)}, f32[4,160,128]{2,1,0:T(8,128)S(1)}, u32[]{:S(2)}, u32[]{:S(2)}) collective-permute-start(f32[4,160,128]{2,1,0:T(8,128)S(1)} %near0.1.after_ref.own_ref), channel_id=1, source_target_pairs={{0,2},{2,0},{4,6},{6,4},{8,10},{10,8},{12,14},{14,12},{16,18},{18,... | collective-permute-start | bytes 983048 | tf_op jit(solution)/shard_map/ppermute | solution.py:503
  12.1 0.6 %copy-start = (f32[16,1,128]{2,1,0:T(1,128)}, f32[16,1,128]{2,1,0:T(1,128)S(1)}, u32[]{:S(2)}) copy-start(f32[16,1,128]{2,1,0:T(1,128)S(1)} %get-tuple-element.40.after_ref.rest_6_) | copy-start | bytes 24580
  12.8 9.4 %collective-permute-start.3 = (bf16[4,192,128]{2,1,0:T(8,128)(2,1)S(1)}, bf16[4,192,128]{2,1,0:T(8,128)(2,1)S(1)}, u32[]{:S(2)}, u32[]{:S(2)}) collective-permute-start(bf16[4,192,128]{2,1,0:T(8,128)(2,1)S(1)} %get-tuple-element.42.msg_ref.after_ref), channel_id=1, source_target_pairs={{0,8},{2,10},{4,12},{6,14},{8,16},{10,18},{12,20},{14,22},{16,24},... | collective-permute-start | bytes 589832 | tf_op jit(solution)/shard_map/ppermute | solution.py:503
  14.5 4.9 %copy-start.4 = (bf16[256,256]{1,0:T(8,128)(2,1)S(1)}, bf16[256,256]{1,0:T(8,128)(2,1)}, u32[]{:S(2)}) copy-start(bf16[256,256]{1,0:T(8,128)(2,1)} %k_ref.1) | copy-start | bytes 393220
  14.5 13.3 %collective-permute-start.9 = (bf16[2,64,16,128]{3,2,1,0:T(8,128)(2,1)S(1)}, bf16[2,64,16,128]{3,2,1,0:T(8,128)(2,1)S(1)}, u32[]{:S(2)}, u32[]{:S(2)}) collective-permute-start(bf16[2,64,16,128]{3,2,1,0:T(8,128)(2,1)S(1)} %pick.1.rim_ref.after_ref), channel_id=1, source_target_pairs={{0,2},{2,4},{4,6},{6,0},{8,10},{10,12},{12,14},{14,8},{16,18},{18,... | collective-permute-start | bytes 1572872 | tf_op jit(solution)/shard_map/ppermute | solution.py:503
  14.7 11.4 %collective-permute-start.6 = (bf16[4,192,128]{2,1,0:T(8,128)(2,1)S(1)}, bf16[4,192,128]{2,1,0:T(8,128)(2,1)S(1)}, u32[]{:S(2)}, u32[]{:S(2)}) collective-permute-start(bf16[4,192,128]{2,1,0:T(8,128)(2,1)S(1)} %again.1), channel_id=1, source_target_pairs={{0,16},{2,18},{4,20},{6,22},{8,8},{10,10},{12,12},{14,14},{24,24},... | collective-permute-start | bytes 589832 | tf_op jit(solution)/shard_map/ppermute | solution.py:503
  22.3 3.8 %collective-permute-start.5 = (bf16[4,192,128]{2,1,0:T(8,128)(2,1)S(1)}, bf16[4,192,128]{2,1,0:T(8,128)(2,1)S(1)}, u32[]{:S(2)}, u32[]{:S(2)}) collective-permute-start(bf16[4,192,128]{2,1,0:T(8,128)(2,1)S(1)} %round.1.after_ref), channel_id=1, source_target_pairs={{8,24},{10,26},{12,28},{14,30},{0,0},{2,2},{4,4},{6,6},{16,16},{18... | collective-permute-start | bytes 589832 | tf_op jit(solution)/shard_map/ppermute | solution.py:503
  26.3 7.7 %collective-permute-start.7 = (bf16[4,192,128]{2,1,0:T(8,128)(2,1)S(1)}, bf16[4,192,128]{2,1,0:T(8,128)(2,1)S(1)}, u32[]{:S(2)}, u32[]{:S(2)}) collective-permute-start(bf16[4,192,128]{2,1,0:T(8,128)(2,1)S(1)} %get-tuple-element.49.after_ref), channel_id=1, source_target_pairs={{0,4},{2,6},{4,0},{6,2},{8,12},{10,14},{12,8},{14,10},{16,20},{18,... | collective-permute-start | bytes 589832 | tf_op jit(solution)/shard_map/ppermute | solution.py:503
  27.8 1.6 %collective-permute-start.8 = (f32[4,160,128]{2,1,0:T(8,128)S(1)}, f32[4,160,128]{2,1,0:T(8,128)S(1)}, u32[]{:S(2)}, u32[]{:S(2)}) collective-permute-start(f32[4,160,128]{2,1,0:T(8,128)S(1)} %get-tuple-element.50.mine_ref), channel_id=1, source_target_pairs={{0,2},{2,0},{4,6},{6,4},{8,10},{10,8},{12,14},{14,12},{16,18},{18,... | collective-permute-start | bytes 983048 | tf_op jit(solution)/shard_map/ppermute | solution.py:503
  28.1 1.4 %copy-start.1 = (f32[16,1,128]{2,1,0:T(1,128)S(1)}, f32[16,1,128]{2,1,0:T(1,128)}, u32[]{:S(2)}) copy-start(f32[16,1,128]{2,1,0:T(1,128)} %copy-done) | copy-start | bytes 24580
  34.0 1.5 %collective-permute-start.12 = (bf16[4,192,128]{2,1,0:T(8,128)(2,1)S(1)}, bf16[4,192,128]{2,1,0:T(8,128)(2,1)S(1)}, u32[]{:S(2)}, u32[]{:S(2)}) collective-permute-start(bf16[4,192,128]{2,1,0:T(8,128)(2,1)S(1)} %collective-permute-done.7.got_ref), channel_id=1, source_target_pairs={{0,2},{2,0},{4,6},{6,4},{8,10},{10,8},{12,14},{14,12},{16,18},{18,... | collective-permute-start | bytes 589832 | tf_op jit(solution)/shard_map/ppermute | solution.py:503
  36.5 3.7 %collective-permute-start.13 = (f32[8,256]{1,0:T(8,128)S(1)}, f32[8,256]{1,0:T(8,128)S(1)}, u32[]{:S(2)}, u32[]{:S(2)}) collective-permute-start(f32[8,256]{1,0:T(8,128)S(1)} %get-tuple-element.68.sq_ref), channel_id=1, source_target_pairs={{0,1},{1,0},{2,3},{3,2},{4,5},{5,4},{6,7},{7,6},{8,9},{9,8},{10,11... | collective-permute-start | bytes 24584 | tf_op jit(solution)/shard_map/ppermute | solution.py:619

commit v8 on v7

--- a/solution.py
+++ b/solution.py
@@ -348,10 +348,10 @@
     lax.fori_loop(0, 4, one, 0)
 
 
-def softmax_blocks(scores):
+def softmax_blocks(scores, dim):
     sc = jnp.concatenate(scores, axis=0)
-    expo = jnp.exp(sc - jnp.max(sc, axis=1, keepdims=True))
-    return (expo / jnp.sum(expo, axis=1, keepdims=True)).astype(BF16)
+    expo = jnp.exp2((sc - jnp.max(sc, axis=1, keepdims=True)) * (math.log2(math.e) / math.sqrt(dim)))
+    return (expo * pl.reciprocal(jnp.sum(expo, axis=1, keepdims=True))).astype(BF16)
 
 
 def band_mask():
@@ -390,8 +390,8 @@
                 lo = b * WINDOW
                 q = qh_ref[head, lo + WINDOW : lo + 2 * WINDOW]
                 sc = dot(q, kh_ref[head, lo : lo + 2 * WINDOW], NT)
-                scores.append(jnp.where(band, sc / math.sqrt(dim), -1e30))
-        weights = softmax_blocks(scores)
+                scores.append(jnp.where(band, sc, -1e30))
+        weights = softmax_blocks(scores, dim)
         for j in range(part):
             head = r * part + j
             for b in range(blocks):
@@ -414,8 +414,8 @@
     for head in range(heads):
         k = jnp.concatenate([rk_ref[head], kh_ref[head, :WINDOW]], axis=0)
         sc = dot(qh_ref[head, :WINDOW], k, NT)
-        scores.append(jnp.where(valid, sc / math.sqrt(dim), -1e30))
-    weights = softmax_blocks(scores)
+        scores.append(jnp.where(valid, sc, -1e30))
+    weights = softmax_blocks(scores, dim)
     for head in range(heads):
         v = jnp.concatenate([rv_ref[head], vh_ref[head, :WINDOW]], axis=0)
         out_ref[head] = dot(weights[head * WINDOW : (head + 1) * WINDOW], v)

time: 41.8 us -> 41.8 us (level)
  no operation moved by 1% of the time
where the time goes in v8:
time: 41.8 us; the launch traced here: 41.6 us
  Pallas kernels  17.3 us (41%)
  starting transfers between devices  17 us (41%)
  waiting for transfers between devices  6.89 us (16%)
    pallas_call x22, Pallas kernels, call(): pl.pallas_call(body, out_shape=outs, in_specs=[spec] * len(operands), out...  17.3 us
    ppermute x13, starting transfers between devices, permute(): return lax.ppermute(x, 'ctx', pairs)  15.5 us
    ppermute x13, waiting for transfers between devices, permute(): return lax.ppermute(x, 'ctx', pairs)  4.72 us
    ppermute x1, waiting for transfers between devices, on_device(): lax.ppermute(squares, 'head', [(i, (i + k) % (peers + 1)) for i in range(...  2.16 us
    ppermute x1, starting transfers between devices, on_device(): lax.ppermute(squares, 'head', [(i, (i + k) % (peers + 1)) for i in range(...  1.52 us
  transfers between devices with their start and end apart: 14, of which 5 were waited for; matrix products, arithmetic and copies ran while one was open for 0% of the time, Pallas kernels for 31%

profile of v8, /device:TPU:0, one launch (start us, length us, event | category | flops | bytes accessed | tf_op | source)
XLA Modules:
  0.0 41.6 jit_solution(8016084412088873965)
XLA Ops:
  0.0 1.9 %far1.1 = (f32[4,160,128]{2,1,0:T(8,128)S(1)}, bf16[16,256,128]{2,1,0:T(8,128)(2,1)S(1)}, f32[256,256]{1,0:T(8,128)S(1)}, bf16[2,64,16,128]{3,2,1,0:T(8,128)(2,1)S(1)}) custom-call(bf16[256,256]{1,0:T(8,128)(2,1)} %k_ref.1, bf16[256,16,128]{2,1,0:T(8,128)(2,1)} %v_hbm.1, bf16[256,16,128]{2,1,0:T(8,128)(2,1)} %wk_ref.1), custom_call_target="tpu_custom_call" | custom-call | flops 1150000000 | tf_op jit(solution)/shard_map/far1/pallas_call | solution.py:142
  2.0 0.5 %collective-permute-start = (f32[4,160,128]{2,1,0:T(8,128)S(1)}, f32[4,160,128]{2,1,0:T(8,128)S(1)}, u32[]{:S(2)}, u32[]{:S(2)}) collective-permute-start(f32[4,160,128]{2,1,0:T(8,128)S(1)} %get-tuple-element.39.after_ref), channel_id=1, source_target_pairs={{0,2},{2,0},{4,6},{6,4},{8,10},{10,8},{12,14},{14,12},{16,18},{18,... | collective-permute-start | bytes 983048 | tf_op jit(solution)/shard_map/ppermute | solution.py:503
  2.5 0.4 %near1.1.own_ref = f32[4,160,128]{2,1,0:T(8,128)S(1)} custom-call(f32[256,256]{1,0:T(8,128)S(1)} %get-tuple-element.37.kt_ref, bf16[16,256,128]{2,1,0:T(8,128)(2,1)S(1)} %get-tuple-element.38.vh_ref, f32[4,160,128]{2,1,0:T(8,128)S(1)} %get-tuple-element.39.after_ref), custom_call_target="tpu_custom_call" | custom-call | flops 1150000000 | tf_op jit(solution)/shard_map/near1/pallas_call | solution.py:142
  2.9 0.1 collective-permute-start.11
  3.0 0.7 %collective-permute-start.4 = (bf16[2,64,16,128]{3,2,1,0:T(8,128)(2,1)S(1)}, bf16[2,64,16,128]{3,2,1,0:T(8,128)(2,1)S(1)}, u32[]{:S(2)}, u32[]{:S(2)}) collective-permute-start(bf16[2,64,16,128]{3,2,1,0:T(8,128)(2,1)S(1)} %get-tuple-element.44.rim_ref), channel_id=1, source_target_pairs={{6,14},{14,22},{22,30},{0,0},{2,2},{4,4},{8,8},{10,10},{12,12},{16... | collective-permute-start | bytes 1572872 | tf_op jit(solution)/shard_map/ppermute | solution.py:503
  3.7 0.0 collective-permute-done.other_ref.other1_ref
  3.7 0.1 chip.1.after_ref
  3.8 3.0 %collective-permute-start.2 = (bf16[4,192,128]{2,1,0:T(8,128)(2,1)S(1)}, bf16[4,192,128]{2,1,0:T(8,128)(2,1)S(1)}, u32[]{:S(2)}, u32[]{:S(2)}) collective-permute-start(bf16[4,192,128]{2,1,0:T(8,128)(2,1)S(1)} %chip.1.after_ref), channel_id=1, source_target_pairs={{0,4},{2,6},{4,0},{6,2},{8,12},{10,14},{12,8},{14,10},{16,20},{18,... | collective-permute-start | bytes 589832 | tf_op jit(solution)/shard_map/ppermute | solution.py:503
  6.8 0.4 %far0.1.after_ref = f32[4,160,128]{2,1,0:T(8,128)S(1)} custom-call(f32[256,256]{1,0:T(8,128)S(1)} %get-tuple-element.37.kt_ref, bf16[16,256,128]{2,1,0:T(8,128)(2,1)S(1)} %get-tuple-element.38.vh_ref, bf16[4,192,128]{2,1,0:T(8,128)(2,1)S(1)} %chip.1.after_ref), custom_call_target="tpu_custom_call" | custom-call | flops 1150000000 | tf_op jit(solution)/shard_map/far0/pallas_call | solution.py:142
  7.3 0.0 copy-start.5
  7.3 0.0 copy-start.6
  7.3 0.0 copy-start.7
  7.3 0.0 copy-start.8
  7.3 0.0 copy-start.9
  7.3 0.5 %near0.1.after_ref.own_ref = f32[4,160,128]{2,1,0:T(8,128)S(1)} custom-call(f32[256,256]{1,0:T(8,128)S(1)} %get-tuple-element.37.kt_ref, bf16[16,256,128]{2,1,0:T(8,128)(2,1)S(1)} %get-tuple-element.38.vh_ref, f32[4,160,128]{2,1,0:T(8,128)S(1)} %far0.1.after_ref), custom_call_target="tpu_custom_call" | custom-call | flops 1150000000 | tf_op jit(solution)/shard_map/near0/pallas_call | solution.py:142
  7.8 0.0 copy-start.2
  7.8 0.0 copy-start.3
  7.8 2.3 %collective-permute-start.1 = (f32[4,160,128]{2,1,0:T(8,128)S(1)}, f32[4,160,128]{2,1,0:T(8,128)S(1)}, u32[]{:S(2)}, u32[]{:S(2)}) collective-permute-start(f32[4,160,128]{2,1,0:T(8,128)S(1)} %far0.1.after_ref), channel_id=1, source_target_pairs={{0,2},{2,0},{4,6},{6,4},{8,10},{10,8},{12,14},{14,12},{16,18},{18,... | collective-permute-start | bytes 983048 | tf_op jit(solution)/shard_map/ppermute | solution.py:503
  10.1 0.1 collective-permute-start.10
  10.2 0.0 copy-done.5
  10.2 0.0 copy-done.6
  10.2 0.0 copy-done.7
  10.2 0.0 copy-done.8
  10.2 0.0 copy-done.9
  10.3 1.8 %phi.1 = (bf16[16,256,160]{2,1,0:T(8,128)(2,1)S(1)}, bf16[16,256,160]{2,1,0:T(8,128)(2,1)S(1)}, f32[16,1,128]{2,1,0:T(1,128)S(1)}) custom-call(bf16[256,256]{1,0:T(8,128)(2,1)S(1)} %copy-done.5, bf16[4,64,160]{2,1,0:T(8,128)(2,1)S(1)} %copy-done.8, bf16[4,64,160]{2,1,0:T(8,128)(2,1)S(1)} %copy-done.7, f32[8,160]{1,0:T(8,128)S(1)} %copy-done.9, ...), custom_call_target="tpu_custom_call" | custom-call | flops 2070000000 | tf_op jit(solution)/shard_map/phi/pallas_call | solution.py:142
  12.1 0.0 copy-start
  12.1 0.0 copy-done.2
  12.1 0.0 copy-done.3
  12.1 0.6 %by_head.1 = (bf16[16,256,128]{2,1,0:T(8,128)(2,1)S(1)}, bf16[16,256,128]{2,1,0:T(8,128)(2,1)S(1)}, f32[8,128]{1,0:T(8,128)S(1)}) custom-call(bf16[256,16,128]{2,1,0:T(8,128)(2,1)S(1)} %copy-done.3, bf16[256,16,128]{2,1,0:T(8,128)(2,1)S(1)} %copy-done.2, f32[16,1,128]{2,1,0:T(1,128)S(1)} %get-tuple-element.40.after_ref.rest_6_), custom_call_target="tpu_custom_call" | custom-call | flops 1150000000 | tf_op jit(solution)/shard_map/by_head/pallas_call | solution.py:142
  12.7 0.0 copy-done
  12.7 0.0 collective-permute-done.2.got_ref
  12.7 0.0 collective-permute-done.1.other_ref
  12.8 0.1 plane.1
  12.8 1.6 %collective-permute-start.3 = (bf16[4,192,128]{2,1,0:T(8,128)(2,1)S(1)}, bf16[4,192,128]{2,1,0:T(8,128)(2,1)S(1)}, u32[]{:S(2)}, u32[]{:S(2)}) collective-permute-start(bf16[4,192,128]{2,1,0:T(8,128)(2,1)S(1)} %get-tuple-element.42.msg_ref.after_ref), channel_id=1, source_target_pairs={{0,8},{2,10},{4,12},{6,14},{8,16},{10,18},{12,20},{14,22},{16,24},... | collective-permute-start | bytes 589832 | tf_op jit(solution)/shard_map/ppermute | solution.py:503
  14.5 0.0 collective-permute-done.4.got_ref
  14.5 0.0 copy-start.4
  14.5 0.2 collective-permute-start.9
  14.7 4.7 %collective-permute-start.6 = (bf16[4,192,128]{2,1,0:T(8,128)(2,1)S(1)}, bf16[4,192,128]{2,1,0:T(8,128)(2,1)S(1)}, u32[]{:S(2)}, u32[]{:S(2)}) collective-permute-start(bf16[4,192,128]{2,1,0:T(8,128)(2,1)S(1)} %again.1), channel_id=1, source_target_pairs={{0,16},{2,18},{4,20},{6,22},{8,8},{10,10},{12,12},{14,14},{24,24},... | collective-permute-start | bytes 589832 | tf_op jit(solution)/shard_map/ppermute | solution.py:503
  19.4 2.8 %intra.1 = (f32[16,256,128]{2,1,0:T(8,128)S(1)}, f32[16,256,128]{2,1,0:T(8,128)S(1)}, f32[8,128]{1,0:T(8,128)S(1)}) custom-call(bf16[256,256]{1,0:T(8,128)(2,1)S(1)} %copy-done.5, bf16[256,256]{1,0:T(8,128)(2,1)S(1)} %copy-done.4, bf16[16,256,128]{2,1,0:T(8,128)(2,1)S(1)} %get-tuple-element.38.vh_ref, bf16[2,64,16,128]{3,2,1,0:T(8,128)(2,1)S(1)} %pick.1.rim_ref.after_ref, ...), custom_call_target="tpu_custom_call" | custom-call | flops 3220000000 | tf_op jit(solution)/shard_map/intra/pallas_call | solution.py:142
  22.3 0.0 collective-permute-done.3.rest_0_
  22.3 0.1 round.1.after_ref
  22.3 0.7 %collective-permute-start.5 = (bf16[4,192,128]{2,1,0:T(8,128)(2,1)S(1)}, bf16[4,192,128]{2,1,0:T(8,128)(2,1)S(1)}, u32[]{:S(2)}, u32[]{:S(2)}) collective-permute-start(bf16[4,192,128]{2,1,0:T(8,128)(2,1)S(1)} %round.1.after_ref), channel_id=1, source_target_pairs={{8,24},{10,26},{12,28},{14,30},{0,0},{2,2},{4,4},{6,6},{16,16},{18... | collective-permute-start | bytes 589832 | tf_op jit(solution)/shard_map/ppermute | solution.py:503
  23.0 2.8 %window.1 = (f32[16,192,128]{2,1,0:T(8,128)S(1)}, f32[8,128]{1,0:T(8,128)S(1)}) custom-call(bf16[16,256,128]{2,1,0:T(8,128)(2,1)S(1)} %get-tuple-element.46.qh_ref, bf16[16,256,128]{2,1,0:T(8,128)(2,1)S(1)} %get-tuple-element.47.kh_ref, bf16[16,256,128]{2,1,0:T(8,128)(2,1)S(1)} %get-tuple-element.38.vh_ref, bf16[4,192,128]{2,1,0:T(8,128)(2,1)S(1)} %round.1.after_ref), custom_call_target="tpu_custom_call" | custom-call | flops 4024999936 | tf_op jit(solution)/shard_map/window/pallas_call | solution.py:142
  25.8 0.3 collective-permute-done.6.rest_2_
  26.1 0.0 collective-permute-done.5.rest_1_
  26.1 0.2 before.1
  26.3 1.5 %collective-permute-start.7 = (bf16[4,192,128]{2,1,0:T(8,128)(2,1)S(1)}, bf16[4,192,128]{2,1,0:T(8,128)(2,1)S(1)}, u32[]{:S(2)}, u32[]{:S(2)}) collective-permute-start(bf16[4,192,128]{2,1,0:T(8,128)(2,1)S(1)} %get-tuple-element.49.after_ref), channel_id=1, source_target_pairs={{0,4},{2,6},{4,0},{6,2},{8,12},{10,14},{12,8},{14,10},{16,20},{18,... | collective-permute-start | bytes 589832 | tf_op jit(solution)/shard_map/ppermute | solution.py:503
  27.8 0.0 collective-permute-start.8
  27.8 0.0 collective-permute-done.11.near1_ref
  27.8 0.0 collective-permute-done.10.near0_ref
  27.8 0.0 collective-permute-done.9.rim_ref
  27.8 0.2 turn.1
  28.1 0.0 copy-start.1
  28.1 0.8 %edge.1.rest_4_ = f32[16,64,128]{2,1,0:T(8,128)S(1)} custom-call(bf16[16,256,128]{2,1,0:T(8,128)(2,1)S(1)} %get-tuple-element.46.qh_ref, bf16[16,256,128]{2,1,0:T(8,128)(2,1)S(1)} %get-tuple-element.47.kh_ref, bf16[16,256,128]{2,1,0:T(8,128)(2,1)S(1)} %get-tuple-element.38.vh_ref, bf16[16,64,128]{2,1,0:T(8,128)(2,1)S(1)} %get-tuple-element.56.rk_ref, ...), custom_call_target="tpu_custom_call" | custom-call | flops 1150000000 | tf_op jit(solution)/shard_map/edge/pallas_call | solution.py:142
  28.9 0.6 %collective-permute-done.8.far_ref = f32[4,160,128]{2,1,0:T(8,128)S(1)} collective-permute-done((f32[4,160,128]{2,1,0:T(8,128)S(1)}, f32[4,160,128]{2,1,0:T(8,128)S(1)}, u32[]{:S(2)}, u32[]{:S(2)}) %collective-permute-start.8) | collective-permute-done | bytes 327712 | tf_op jit(solution)/shard_map/ppermute | solution.py:503
  29.5 1.4 %final0.1 = (f32[16,256,128]{2,1,0:T(8,128)S(1)}, f32[256,128]{1,0:T(8,128)S(1)}) custom-call(f32[4,160,128]{2,1,0:T(8,128)S(1)} %get-tuple-element.50.mine_ref, f32[4,160,128]{2,1,0:T(8,128)S(1)} %collective-permute-done.1.other_ref, f32[4,160,128]{2,1,0:T(8,128)S(1)} %collective-permute-done.8.far_ref, f32[2,4,160,128]{3,2,1,0:T(8,128)S(1)} %get-tuple-element.51.extra_ref, ...), custom_call_target="tpu_custom_call" | custom-call | flops 1150000000 | tf_op jit(solution)/shard_map/final0/pallas_call | solution.py:142
  30.8 3.2 %collective-permute-done.7.got_ref = bf16[4,192,128]{2,1,0:T(8,128)(2,1)S(1)} collective-permute-done((bf16[4,192,128]{2,1,0:T(8,128)(2,1)S(1)}, bf16[4,192,128]{2,1,0:T(8,128)(2,1)S(1)}, u32[]{:S(2)}, u32[]{:S(2)}) %collective-permute-start.7) | collective-permute-done | bytes 196640 | tf_op jit(solution)/shard_map/ppermute | solution.py:503
  34.0 0.1 collective-permute-start.12
  34.1 0.8 %final1.1 = (f32[16,256,128]{2,1,0:T(8,128)S(1)}, f32[256,128]{1,0:T(8,128)S(1)}) custom-call(f32[4,160,128]{2,1,0:T(8,128)S(1)} %open.3.base_ref, f32[4,160,128]{2,1,0:T(8,128)S(1)} %get-tuple-element.62.extra_ref, bf16[16,256,160]{2,1,0:T(8,128)(2,1)S(1)} %get-tuple-element.52.rest_0_, ...), custom_call_target="tpu_custom_call", output_to_operand_aliasing={{0}: (9, {})} | custom-call | flops 1150000000 | tf_op jit(solution)/shard_map/final1/pallas_call | solution.py:142
  34.9 0.7 %collective-permute-done.12.base_ref = bf16[4,192,128]{2,1,0:T(8,128)(2,1)S(1)} collective-permute-done((bf16[4,192,128]{2,1,0:T(8,128)(2,1)S(1)}, bf16[4,192,128]{2,1,0:T(8,128)(2,1)S(1)}, u32[]{:S(2)}, u32[]{:S(2)}) %collective-permute-start.12) | collective-permute-done | bytes 196640 | tf_op jit(solution)/shard_map/ppermute | solution.py:503
  35.5 1.0 %final2.1 = (f32[16,256,128]{2,1,0:T(8,128)S(1)}, f32[8,256]{1,0:T(8,128)S(1)}) custom-call(bf16[4,192,128]{2,1,0:T(8,128)(2,1)S(1)} %collective-permute-done.12.base_ref, f32[2,4,160,128]{3,2,1,0:T(8,128)S(1)} %get-tuple-element.51.extra_ref, bf16[16,256,160]{2,1,0:T(8,128)(2,1)S(1)} %get-tuple-element.52.rest_0_, ...), custom_call_target="tpu_custom_call", output_to_operand_aliasing={{0}: (9, {})} | custom-call | flops 1150000000 | tf_op jit(solution)/shard_map/final2/pallas_call | solution.py:142
  36.5 1.5 %collective-permute-start.13 = (f32[8,256]{1,0:T(8,128)S(1)}, f32[8,256]{1,0:T(8,128)S(1)}, u32[]{:S(2)}, u32[]{:S(2)}) collective-permute-start(f32[8,256]{1,0:T(8,128)S(1)} %get-tuple-element.68.sq_ref), channel_id=1, source_target_pairs={{0,1},{1,0},{2,3},{3,2},{4,5},{5,4},{6,7},{7,6},{8,9},{9,8},{10,11... | collective-permute-start | bytes 24584 | tf_op jit(solution)/shard_map/ppermute | solution.py:619
  38.1 2.2 %collective-permute-done.13.rest_0_ = f32[8,256]{1,0:T(8,128)S(1)} collective-permute-done((f32[8,256]{1,0:T(8,128)S(1)}, f32[8,256]{1,0:T(8,128)S(1)}, u32[]{:S(2)}, u32[]{:S(2)}) %collective-permute-start.13) | collective-permute-done | bytes 8224 | tf_op jit(solution)/shard_map/ppermute | solution.py:619
  40.2 1.4 %norm.1 = bf16[256,16,128]{2,1,0:T(8,128)(2,1)} custom-call(f32[16,256,128]{2,1,0:T(8,128)S(1)} %get-tuple-element.67.mixed_ref, f32[8,256]{1,0:T(8,128)S(1)} %get-tuple-element.68.sq_ref, f32[8,256]{1,0:T(8,128)S(1)} %collective-permute-done.13.rest_0_), custom_call_target="tpu_custom_call" | custom-call | flops 1150000000 | tf_op jit(solution)/shard_map/norm/pallas_call | solution.py:142
  (6 shorter events, 0.1 us)
Async XLA Ops:
  2.0 1.8 %collective-permute-start = (f32[4,160,128]{2,1,0:T(8,128)S(1)}, f32[4,160,128]{2,1,0:T(8,128)S(1)}, u32[]{:S(2)}, u32[]{:S(2)}) collective-permute-start(f32[4,160,128]{2,1,0:T(8,128)S(1)} %get-tuple-element.39.after_ref), channel_id=1, source_target_pairs={{0,2},{2,0},{4,6},{6,4},{8,10},{10,8},{12,14},{14,12},{16,18},{18,... | collective-permute-start | bytes 983048 | tf_op jit(solution)/shard_map/ppermute | solution.py:503
  2.9 24.9 %collective-permute-start.11 = (f32[4,160,128]{2,1,0:T(8,128)S(1)}, f32[4,160,128]{2,1,0:T(8,128)S(1)}, u32[]{:S(2)}, u32[]{:S(2)}) collective-permute-start(f32[4,160,128]{2,1,0:T(8,128)S(1)} %near1.1.own_ref), channel_id=1, source_target_pairs={{0,2},{2,0},{4,6},{6,4},{8,10},{10,8},{12,14},{14,12},{16,18},{18,... | collective-permute-start | bytes 983048 | tf_op jit(solution)/shard_map/ppermute | solution.py:503
  3.0 11.4 %collective-permute-start.4 = (bf16[2,64,16,128]{3,2,1,0:T(8,128)(2,1)S(1)}, bf16[2,64,16,128]{3,2,1,0:T(8,128)(2,1)S(1)}, u32[]{:S(2)}, u32[]{:S(2)}) collective-permute-start(bf16[2,64,16,128]{3,2,1,0:T(8,128)(2,1)S(1)} %get-tuple-element.44.rim_ref), channel_id=1, source_target_pairs={{6,14},{14,22},{22,30},{0,0},{2,2},{4,4},{8,8},{10,10},{12,12},{16... | collective-permute-start | bytes 1572872 | tf_op jit(solution)/shard_map/ppermute | solution.py:503
  3.8 8.9 %collective-permute-start.2 = (bf16[4,192,128]{2,1,0:T(8,128)(2,1)S(1)}, bf16[4,192,128]{2,1,0:T(8,128)(2,1)S(1)}, u32[]{:S(2)}, u32[]{:S(2)}) collective-permute-start(bf16[4,192,128]{2,1,0:T(8,128)(2,1)S(1)} %chip.1.after_ref), channel_id=1, source_target_pairs={{0,4},{2,6},{4,0},{6,2},{8,12},{10,14},{12,8},{14,10},{16,20},{18,... | collective-permute-start | bytes 589832 | tf_op jit(solution)/shard_map/ppermute | solution.py:503
  7.3 3.0 %copy-start.5 = (bf16[256,256]{1,0:T(8,128)(2,1)S(1)}, bf16[256,256]{1,0:T(8,128)(2,1)}, u32[]{:S(2)}) copy-start(bf16[256,256]{1,0:T(8,128)(2,1)} %q_ref.3) | copy-start | bytes 393220
  7.3 2.9 %copy-start.6 = (bf16[16,128]{1,0:T(8,128)(2,1)S(1)}, bf16[16,128]{1,0:T(8,128)(2,1)}, u32[]{:S(2)}) copy-start(bf16[16,128]{1,0:T(8,128)(2,1)} %gain_ref.1) | copy-start | bytes 12292
  7.3 2.9 %copy-start.7 = (bf16[4,64,160]{2,1,0:T(8,128)(2,1)S(1)}, bf16[4,64,160]{2,1,0:T(8,128)(2,1)}, u32[]{:S(2)}) copy-start(bf16[4,64,160]{2,1,0:T(8,128)(2,1)} %constant.7.clone.e2_ref) | copy-start | bytes 245764
  7.3 2.9 %copy-start.8 = (bf16[4,64,160]{2,1,0:T(8,128)(2,1)S(1)}, bf16[4,64,160]{2,1,0:T(8,128)(2,1)}, u32[]{:S(2)}) copy-start(bf16[4,64,160]{2,1,0:T(8,128)(2,1)} %constant.6.clone.e1_ref) | copy-start | bytes 245764
  7.3 2.9 %copy-start.9 = (f32[8,160]{1,0:T(8,128)S(1)}, f32[8,160]{1,0:T(8,128)}, u32[]{:S(2)}) copy-start(f32[8,160]{1,0:T(8,128)} %constant.8.clone.add_ref) | copy-start | bytes 15364
  7.8 4.3 %copy-start.2 = (bf16[256,16,128]{2,1,0:T(8,128)(2,1)S(1)}, bf16[256,16,128]{2,1,0:T(8,128)(2,1)}, u32[]{:S(2)}) copy-start(bf16[256,16,128]{2,1,0:T(8,128)(2,1)} %wk_ref.1) | copy-start | bytes 3145732
  7.8 4.3 %copy-start.3 = (bf16[256,16,128]{2,1,0:T(8,128)(2,1)S(1)}, bf16[256,16,128]{2,1,0:T(8,128)(2,1)}, u32[]{:S(2)}) copy-start(bf16[256,16,128]{2,1,0:T(8,128)(2,1)} %wq_ref.1) | copy-start | bytes 3145732
  7.8 4.9 %collective-permute-start.1 = (f32[4,160,128]{2,1,0:T(8,128)S(1)}, f32[4,160,128]{2,1,0:T(8,128)S(1)}, u32[]{:S(2)}, u32[]{:S(2)}) collective-permute-start(f32[4,160,128]{2,1,0:T(8,128)S(1)} %far0.1.after_ref), channel_id=1, source_target_pairs={{0,2},{2,0},{4,6},{6,4},{8,10},{10,8},{12,14},{14,12},{16,18},{18,... | collective-permute-start | bytes 983048 | tf_op jit(solution)/shard_map/ppermute | solution.py:503
  10.1 17.7 %collective-permute-start.10 = (f32[4,160,128]{2,1,0:T(8,128)S(1)}, f32[4,160,128]{2,1,0:T(8,128)S(1)}, u32[]{:S(2)}, u32[]{:S(2)}) collective-permute-start(f32[4,160,128]{2,1,0:T(8,128)S(1)} %near0.1.after_ref.own_ref), channel_id=1, source_target_pairs={{0,2},{2,0},{4,6},{6,4},{8,10},{10,8},{12,14},{14,12},{16,18},{18,... | collective-permute-start | bytes 983048 | tf_op jit(solution)/shard_map/ppermute | solution.py:503
  12.1 0.6 %copy-start = (f32[16,1,128]{2,1,0:T(1,128)}, f32[16,1,128]{2,1,0:T(1,128)S(1)}, u32[]{:S(2)}) copy-start(f32[16,1,128]{2,1,0:T(1,128)S(1)} %get-tuple-element.40.after_ref.rest_6_) | copy-start | bytes 24580
  12.8 9.4 %collective-permute-start.3 = (bf16[4,192,128]{2,1,0:T(8,128)(2,1)S(1)}, bf16[4,192,128]{2,1,0:T(8,128)(2,1)S(1)}, u32[]{:S(2)}, u32[]{:S(2)}) collective-permute-start(bf16[4,192,128]{2,1,0:T(8,128)(2,1)S(1)} %get-tuple-element.42.msg_ref.after_ref), channel_id=1, source_target_pairs={{0,8},{2,10},{4,12},{6,14},{8,16},{10,18},{12,20},{14,22},{16,24},... | collective-permute-start | bytes 589832 | tf_op jit(solution)/shard_map/ppermute | solution.py:503
  14.5 4.9 %copy-start.4 = (bf16[256,256]{1,0:T(8,128)(2,1)S(1)}, bf16[256,256]{1,0:T(8,128)(2,1)}, u32[]{:S(2)}) copy-start(bf16[256,256]{1,0:T(8,128)(2,1)} %k_ref.1) | copy-start | bytes 393220
  14.5 13.3 %collective-permute-start.9 = (bf16[2,64,16,128]{3,2,1,0:T(8,128)(2,1)S(1)}, bf16[2,64,16,128]{3,2,1,0:T(8,128)(2,1)S(1)}, u32[]{:S(2)}, u32[]{:S(2)}) collective-permute-start(bf16[2,64,16,128]{3,2,1,0:T(8,128)(2,1)S(1)} %pick.1.rim_ref.after_ref), channel_id=1, source_target_pairs={{0,2},{2,4},{4,6},{6,0},{8,10},{10,12},{12,14},{14,8},{16,18},{18,... | collective-permute-start | bytes 1572872 | tf_op jit(solution)/shard_map/ppermute | solution.py:503
  14.7 11.4 %collective-permute-start.6 = (bf16[4,192,128]{2,1,0:T(8,128)(2,1)S(1)}, bf16[4,192,128]{2,1,0:T(8,128)(2,1)S(1)}, u32[]{:S(2)}, u32[]{:S(2)}) collective-permute-start(bf16[4,192,128]{2,1,0:T(8,128)(2,1)S(1)} %again.1), channel_id=1, source_target_pairs={{0,16},{2,18},{4,20},{6,22},{8,8},{10,10},{12,12},{14,14},{24,24},... | collective-permute-start | bytes 589832 | tf_op jit(solution)/shard_map/ppermute | solution.py:503
  22.3 3.8 %collective-permute-start.5 = (bf16[4,192,128]{2,1,0:T(8,128)(2,1)S(1)}, bf16[4,192,128]{2,1,0:T(8,128)(2,1)S(1)}, u32[]{:S(2)}, u32[]{:S(2)}) collective-permute-start(bf16[4,192,128]{2,1,0:T(8,128)(2,1)S(1)} %round.1.after_ref), channel_id=1, source_target_pairs={{8,24},{10,26},{12,28},{14,30},{0,0},{2,2},{4,4},{6,6},{16,16},{18... | collective-permute-start | bytes 589832 | tf_op jit(solution)/shard_map/ppermute | solution.py:503
  26.3 7.7 %collective-permute-start.7 = (bf16[4,192,128]{2,1,0:T(8,128)(2,1)S(1)}, bf16[4,192,128]{2,1,0:T(8,128)(2,1)S(1)}, u32[]{:S(2)}, u32[]{:S(2)}) collective-permute-start(bf16[4,192,128]{2,1,0:T(8,128)(2,1)S(1)} %get-tuple-element.49.after_ref), channel_id=1, source_target_pairs={{0,4},{2,6},{4,0},{6,2},{8,12},{10,14},{12,8},{14,10},{16,20},{18,... | collective-permute-start | bytes 589832 | tf_op jit(solution)/shard_map/ppermute | solution.py:503
  27.8 1.6 %collective-permute-start.8 = (f32[4,160,128]{2,1,0:T(8,128)S(1)}, f32[4,160,128]{2,1,0:T(8,128)S(1)}, u32[]{:S(2)}, u32[]{:S(2)}) collective-permute-start(f32[4,160,128]{2,1,0:T(8,128)S(1)} %get-tuple-element.50.mine_ref), channel_id=1, source_target_pairs={{0,2},{2,0},{4,6},{6,4},{8,10},{10,8},{12,14},{14,12},{16,18},{18,... | collective-permute-start | bytes 983048 | tf_op jit(solution)/shard_map/ppermute | solution.py:503
  28.1 1.4 %copy-start.1 = (f32[16,1,128]{2,1,0:T(1,128)S(1)}, f32[16,1,128]{2,1,0:T(1,128)}, u32[]{:S(2)}) copy-start(f32[16,1,128]{2,1,0:T(1,128)} %copy-done) | copy-start | bytes 24580
  34.0 1.5 %collective-permute-start.12 = (bf16[4,192,128]{2,1,0:T(8,128)(2,1)S(1)}, bf16[4,192,128]{2,1,0:T(8,128)(2,1)S(1)}, u32[]{:S(2)}, u32[]{:S(2)}) collective-permute-start(bf16[4,192,128]{2,1,0:T(8,128)(2,1)S(1)} %collective-permute-done.7.got_ref), channel_id=1, source_target_pairs={{0,2},{2,0},{4,6},{6,4},{8,10},{10,8},{12,14},{14,12},{16,18},{18,... | collective-permute-start | bytes 589832 | tf_op jit(solution)/shard_map/ppermute | solution.py:503
  36.5 3.7 %collective-permute-start.13 = (f32[8,256]{1,0:T(8,128)S(1)}, f32[8,256]{1,0:T(8,128)S(1)}, u32[]{:S(2)}, u32[]{:S(2)}) collective-permute-start(f32[8,256]{1,0:T(8,128)S(1)} %get-tuple-element.68.sq_ref), channel_id=1, source_target_pairs={{0,1},{1,0},{2,3},{3,2},{4,5},{5,4},{6,7},{7,6},{8,9},{9,8},{10,11... | collective-permute-start | bytes 24584 | tf_op jit(solution)/shard_map/ppermute | solution.py:619

commit v9 on v8

--- a/solution.py
+++ b/solution.py
@@ -557,13 +557,11 @@
             )
             while 2 * step < groups:
                 step *= 2
-                early[step] = permute(
-                    again, full([(i, i + 4 * step) for i in range(4)], count)
-                )
+                early[step] = permute(again, [(i, i + 4 * step) for i in range(4)])
             step = 1
         else:
             pairs = [(i, i + 4 * step) for i in range(4, count - 4 * step)]
-            got = [permute(msg, full(pairs, count)), early[step]]
+            got = [permute(msg, pairs), early[step]]
             limit = [(step + 1, groups), (step, step)]
         if step == 2:
             win, token = call(

time: 41.8 us -> 41.8 us (level)
  waiting for transfers between devices: 6.89 us -> 6.4 us
    ppermute x13, waiting for transfers between devices: 4.72 us -> 4.24 us  [permute(): return lax.ppermute(x, 'ctx', pairs)]
  transfers between devices with their start and end apart: 14 -> 14, of which waited for: 5 -> 4; matrix products, arithmetic and copies ran while one was open for 0% -> 0% of each run, Pallas kernels for 31% -> 31%
where the time goes in v9:
time: 41.8 us; the launch traced here: 41.3 us
  Pallas kernels  17.3 us (41%)
  starting transfers between devices  17.3 us (41%)
  waiting for transfers between devices  6.4 us (15%)
    pallas_call x22, Pallas kernels, call(): pl.pallas_call(body, out_shape=outs, in_specs=[spec] * len(operands), out...  17.3 us
    ppermute x13, starting transfers between devices, permute(): return lax.ppermute(x, 'ctx', pairs)  15.7 us
    ppermute x13, waiting for transfers between devices, permute(): return lax.ppermute(x, 'ctx', pairs)  4.24 us
    ppermute x1, waiting for transfers between devices, on_device(): lax.ppermute(squares, 'head', [(i, (i + k) % (peers + 1)) for i in range(...  2.16 us
    ppermute x1, starting transfers between devices, on_device(): lax.ppermute(squares, 'head', [(i, (i + k) % (peers + 1)) for i in range(...  1.52 us
  transfers between devices with their start and end apart: 14, of which 4 were waited for; matrix products, arithmetic and copies ran while one was open for 0% of the time, Pallas kernels for 31%

profile of v9, /device:TPU:0, one launch (start us, length us, event | category | flops | bytes accessed | tf_op | source)
XLA Modules:
  0.0 41.3 jit_solution(7535601151308959186)
XLA Ops:
  0.0 1.9 %far1.1 = (f32[4,160,128]{2,1,0:T(8,128)S(1)}, bf16[16,256,128]{2,1,0:T(8,128)(2,1)S(1)}, f32[256,256]{1,0:T(8,128)S(1)}, bf16[2,64,16,128]{3,2,1,0:T(8,128)(2,1)S(1)}) custom-call(bf16[256,256]{1,0:T(8,128)(2,1)} %k_ref.1, bf16[256,16,128]{2,1,0:T(8,128)(2,1)} %v_hbm.1, bf16[256,16,128]{2,1,0:T(8,128)(2,1)} %wk_ref.1), custom_call_target="tpu_custom_call" | custom-call | flops 1150000000 | tf_op jit(solution)/shard_map/far1/pallas_call | solution.py:142
  2.0 0.5 %collective-permute-start = (f32[4,160,128]{2,1,0:T(8,128)S(1)}, f32[4,160,128]{2,1,0:T(8,128)S(1)}, u32[]{:S(2)}, u32[]{:S(2)}) collective-permute-start(f32[4,160,128]{2,1,0:T(8,128)S(1)} %get-tuple-element.39.after_ref), channel_id=1, source_target_pairs={{0,2},{2,0},{4,6},{6,4},{8,10},{10,8},{12,14},{14,12},{16,18},{18,... | collective-permute-start | bytes 983048 | tf_op jit(solution)/shard_map/ppermute | solution.py:503
  2.5 0.4 %near1.1.own_ref = f32[4,160,128]{2,1,0:T(8,128)S(1)} custom-call(f32[256,256]{1,0:T(8,128)S(1)} %get-tuple-element.37.kt_ref, bf16[16,256,128]{2,1,0:T(8,128)(2,1)S(1)} %get-tuple-element.38.vh_ref, f32[4,160,128]{2,1,0:T(8,128)S(1)} %get-tuple-element.39.after_ref), custom_call_target="tpu_custom_call" | custom-call | flops 1150000000 | tf_op jit(solution)/shard_map/near1/pallas_call | solution.py:142
  2.9 0.1 collective-permute-start.11
  3.0 0.7 %collective-permute-start.4 = (bf16[2,64,16,128]{3,2,1,0:T(8,128)(2,1)S(1)}, bf16[2,64,16,128]{3,2,1,0:T(8,128)(2,1)S(1)}, u32[]{:S(2)}, u32[]{:S(2)}) collective-permute-start(bf16[2,64,16,128]{3,2,1,0:T(8,128)(2,1)S(1)} %get-tuple-element.44.rim_ref), channel_id=1, source_target_pairs={{6,14},{14,22},{22,30},{0,0},{2,2},{4,4},{8,8},{10,10},{12,12},{16... | collective-permute-start | bytes 1572872 | tf_op jit(solution)/shard_map/ppermute | solution.py:503
  3.7 0.0 collective-permute-done.other_ref.other1_ref
  3.7 0.1 chip.1.after_ref
  3.8 3.0 %collective-permute-start.2 = (bf16[4,192,128]{2,1,0:T(8,128)(2,1)S(1)}, bf16[4,192,128]{2,1,0:T(8,128)(2,1)S(1)}, u32[]{:S(2)}, u32[]{:S(2)}) collective-permute-start(bf16[4,192,128]{2,1,0:T(8,128)(2,1)S(1)} %chip.1.after_ref), channel_id=1, source_target_pairs={{0,4},{2,6},{4,0},{6,2},{8,12},{10,14},{12,8},{14,10},{16,20},{18,... | collective-permute-start | bytes 589832 | tf_op jit(solution)/shard_map/ppermute | solution.py:503
  6.8 0.4 %far0.1.after_ref = f32[4,160,128]{2,1,0:T(8,128)S(1)} custom-call(f32[256,256]{1,0:T(8,128)S(1)} %get-tuple-element.37.kt_ref, bf16[16,256,128]{2,1,0:T(8,128)(2,1)S(1)} %get-tuple-element.38.vh_ref, bf16[4,192,128]{2,1,0:T(8,128)(2,1)S(1)} %chip.1.after_ref), custom_call_target="tpu_custom_call" | custom-call | flops 1150000000 | tf_op jit(solution)/shard_map/far0/pallas_call | solution.py:142
  7.3 0.0 copy-start.5
  7.3 0.0 copy-start.6
  7.3 0.0 copy-start.7
  7.3 0.0 copy-start.8
  7.3 0.0 copy-start.9
  7.3 0.5 %near0.1.after_ref.own_ref = f32[4,160,128]{2,1,0:T(8,128)S(1)} custom-call(f32[256,256]{1,0:T(8,128)S(1)} %get-tuple-element.37.kt_ref, bf16[16,256,128]{2,1,0:T(8,128)(2,1)S(1)} %get-tuple-element.38.vh_ref, f32[4,160,128]{2,1,0:T(8,128)S(1)} %far0.1.after_ref), custom_call_target="tpu_custom_call" | custom-call | flops 1150000000 | tf_op jit(solution)/shard_map/near0/pallas_call | solution.py:142
  7.8 0.0 copy-start.2
  7.8 0.0 copy-start.3
  7.8 2.3 %collective-permute-start.1 = (f32[4,160,128]{2,1,0:T(8,128)S(1)}, f32[4,160,128]{2,1,0:T(8,128)S(1)}, u32[]{:S(2)}, u32[]{:S(2)}) collective-permute-start(f32[4,160,128]{2,1,0:T(8,128)S(1)} %far0.1.after_ref), channel_id=1, source_target_pairs={{0,2},{2,0},{4,6},{6,4},{8,10},{10,8},{12,14},{14,12},{16,18},{18,... | collective-permute-start | bytes 983048 | tf_op jit(solution)/shard_map/ppermute | solution.py:503
  10.1 0.1 collective-permute-start.10
  10.2 0.0 copy-done.5
  10.2 0.0 copy-done.6
  10.2 0.0 copy-done.7
  10.2 0.0 copy-done.8
  10.2 0.0 copy-done.9
  10.3 1.8 %phi.1 = (bf16[16,256,160]{2,1,0:T(8,128)(2,1)S(1)}, bf16[16,256,160]{2,1,0:T(8,128)(2,1)S(1)}, f32[16,1,128]{2,1,0:T(1,128)S(1)}) custom-call(bf16[256,256]{1,0:T(8,128)(2,1)S(1)} %copy-done.5, bf16[4,64,160]{2,1,0:T(8,128)(2,1)S(1)} %copy-done.8, bf16[4,64,160]{2,1,0:T(8,128)(2,1)S(1)} %copy-done.7, f32[8,160]{1,0:T(8,128)S(1)} %copy-done.9, ...), custom_call_target="tpu_custom_call" | custom-call | flops 2070000000 | tf_op jit(solution)/shard_map/phi/pallas_call | solution.py:142
  12.1 0.0 copy-start
  12.1 0.0 copy-done.2
  12.1 0.0 copy-done.3
  12.1 0.6 %by_head.1 = (bf16[16,256,128]{2,1,0:T(8,128)(2,1)S(1)}, bf16[16,256,128]{2,1,0:T(8,128)(2,1)S(1)}, f32[8,128]{1,0:T(8,128)S(1)}) custom-call(bf16[256,16,128]{2,1,0:T(8,128)(2,1)S(1)} %copy-done.3, bf16[256,16,128]{2,1,0:T(8,128)(2,1)S(1)} %copy-done.2, f32[16,1,128]{2,1,0:T(1,128)S(1)} %get-tuple-element.40.after_ref.rest_6_), custom_call_target="tpu_custom_call" | custom-call | flops 1150000000 | tf_op jit(solution)/shard_map/by_head/pallas_call | solution.py:142
  12.7 0.0 collective-permute-done.2.got_ref
  12.7 0.0 collective-permute-done.1.other_ref
  12.8 0.1 plane.1
  12.8 1.6 %collective-permute-start.3 = (bf16[4,192,128]{2,1,0:T(8,128)(2,1)S(1)}, bf16[4,192,128]{2,1,0:T(8,128)(2,1)S(1)}, u32[]{:S(2)}, u32[]{:S(2)}) collective-permute-start(bf16[4,192,128]{2,1,0:T(8,128)(2,1)S(1)} %get-tuple-element.42.msg_ref.after_ref), channel_id=1, source_target_pairs={{0,8},{2,10},{4,12},{6,14},{8,16},{10,18},{12,20},{14,22},{16,24},... | collective-permute-start | bytes 589832 | tf_op jit(solution)/shard_map/ppermute | solution.py:503
  14.5 0.0 collective-permute-done.4.got_ref
  14.5 0.0 copy-start.4
  14.5 0.2 collective-permute-start.9
  14.7 4.7 %collective-permute-start.6 = (bf16[4,192,128]{2,1,0:T(8,128)(2,1)S(1)}, bf16[4,192,128]{2,1,0:T(8,128)(2,1)S(1)}, u32[]{:S(2)}, u32[]{:S(2)}) collective-permute-start(bf16[4,192,128]{2,1,0:T(8,128)(2,1)S(1)} %again.1), channel_id=1, source_target_pairs={{0,16},{2,18},{4,20},{6,22},{1,17},{3,19},{5,21},{7,23}} | collective-permute-start | bytes 589832 | tf_op jit(solution)/shard_map/ppermute | solution.py:503
  19.4 2.8 %intra.1 = (f32[16,256,128]{2,1,0:T(8,128)S(1)}, f32[16,256,128]{2,1,0:T(8,128)S(1)}, f32[8,128]{1,0:T(8,128)S(1)}) custom-call(bf16[256,256]{1,0:T(8,128)(2,1)S(1)} %copy-done.5, bf16[256,256]{1,0:T(8,128)(2,1)S(1)} %copy-done.4, bf16[16,256,128]{2,1,0:T(8,128)(2,1)S(1)} %get-tuple-element.38.vh_ref, bf16[2,64,16,128]{3,2,1,0:T(8,128)(2,1)S(1)} %pick.1.rim_ref.after_ref, ...), custom_call_target="tpu_custom_call" | custom-call | flops 3220000000 | tf_op jit(solution)/shard_map/intra/pallas_call | solution.py:142
  22.3 0.0 collective-permute-done.3.rest_0_
  22.3 0.1 round.1.after_ref
  22.3 0.7 %collective-permute-start.5 = (bf16[4,192,128]{2,1,0:T(8,128)(2,1)S(1)}, bf16[4,192,128]{2,1,0:T(8,128)(2,1)S(1)}, u32[]{:S(2)}, u32[]{:S(2)}) collective-permute-start(bf16[4,192,128]{2,1,0:T(8,128)(2,1)S(1)} %round.1.after_ref), channel_id=1, source_target_pairs={{8,24},{10,26},{12,28},{14,30},{9,25},{11,27},{13,29},{15,31}} | collective-permute-start | bytes 589832 | tf_op jit(solution)/shard_map/ppermute | solution.py:503
  23.0 2.8 %window.1 = (f32[16,192,128]{2,1,0:T(8,128)S(1)}, f32[8,128]{1,0:T(8,128)S(1)}) custom-call(bf16[16,256,128]{2,1,0:T(8,128)(2,1)S(1)} %get-tuple-element.46.qh_ref, bf16[16,256,128]{2,1,0:T(8,128)(2,1)S(1)} %get-tuple-element.47.kh_ref, bf16[16,256,128]{2,1,0:T(8,128)(2,1)S(1)} %get-tuple-element.38.vh_ref, bf16[4,192,128]{2,1,0:T(8,128)(2,1)S(1)} %round.1.after_ref), custom_call_target="tpu_custom_call" | custom-call | flops 4024999936 | tf_op jit(solution)/shard_map/window/pallas_call | solution.py:142
  25.8 0.0 collective-permute-done.6.rest_2_
  25.9 0.0 collective-permute-done.5.rest_1_
  25.9 0.2 before.1
  26.0 1.4 %collective-permute-start.7 = (bf16[4,192,128]{2,1,0:T(8,128)(2,1)S(1)}, bf16[4,192,128]{2,1,0:T(8,128)(2,1)S(1)}, u32[]{:S(2)}, u32[]{:S(2)}) collective-permute-start(bf16[4,192,128]{2,1,0:T(8,128)(2,1)S(1)} %get-tuple-element.49.after_ref), channel_id=1, source_target_pairs={{0,4},{2,6},{4,0},{6,2},{8,12},{10,14},{12,8},{14,10},{16,20},{18,... | collective-permute-start | bytes 589832 | tf_op jit(solution)/shard_map/ppermute | solution.py:503
  27.4 0.3 collective-permute-start.8
  27.7 0.0 collective-permute-done.11.near1_ref
  27.7 0.0 collective-permute-done.10.near0_ref
  27.7 0.0 collective-permute-done.9.rim_ref
  27.7 0.2 turn.1
  27.9 0.0 copy-start.1
  27.9 0.8 %edge.1.rest_4_ = f32[16,64,128]{2,1,0:T(8,128)S(1)} custom-call(bf16[16,256,128]{2,1,0:T(8,128)(2,1)S(1)} %get-tuple-element.46.qh_ref, bf16[16,256,128]{2,1,0:T(8,128)(2,1)S(1)} %get-tuple-element.47.kh_ref, bf16[16,256,128]{2,1,0:T(8,128)(2,1)S(1)} %get-tuple-element.38.vh_ref, bf16[16,64,128]{2,1,0:T(8,128)(2,1)S(1)} %get-tuple-element.56.rk_ref, ...), custom_call_target="tpu_custom_call" | custom-call | flops 1150000000 | tf_op jit(solution)/shard_map/edge/pallas_call | solution.py:142
  28.7 0.3 collective-permute-done.8.far_ref
  29.0 0.0 copy-done.1
  29.0 1.4 %final0.1 = (f32[16,256,128]{2,1,0:T(8,128)S(1)}, f32[256,128]{1,0:T(8,128)S(1)}) custom-call(f32[4,160,128]{2,1,0:T(8,128)S(1)} %get-tuple-element.50.mine_ref, f32[4,160,128]{2,1,0:T(8,128)S(1)} %collective-permute-done.1.other_ref, f32[4,160,128]{2,1,0:T(8,128)S(1)} %collective-permute-done.8.far_ref, f32[2,4,160,128]{3,2,1,0:T(8,128)S(1)} %get-tuple-element.51.extra_ref, ...), custom_call_target="tpu_custom_call" | custom-call | flops 1150000000 | tf_op jit(solution)/shard_map/final0/pallas_call | solution.py:142
  30.4 3.4 %collective-permute-done.7.got_ref = bf16[4,192,128]{2,1,0:T(8,128)(2,1)S(1)} collective-permute-done((bf16[4,192,128]{2,1,0:T(8,128)(2,1)S(1)}, bf16[4,192,128]{2,1,0:T(8,128)(2,1)S(1)}, u32[]{:S(2)}, u32[]{:S(2)}) %collective-permute-start.7) | collective-permute-done | bytes 196640 | tf_op jit(solution)/shard_map/ppermute | solution.py:503
  33.8 0.2 collective-permute-start.12
  34.0 0.8 %final1.1 = (f32[16,256,128]{2,1,0:T(8,128)S(1)}, f32[256,128]{1,0:T(8,128)S(1)}) custom-call(f32[4,160,128]{2,1,0:T(8,128)S(1)} %open.3.base_ref, f32[4,160,128]{2,1,0:T(8,128)S(1)} %get-tuple-element.62.extra_ref, bf16[16,256,160]{2,1,0:T(8,128)(2,1)S(1)} %get-tuple-element.52.rest_0_, ...), custom_call_target="tpu_custom_call", output_to_operand_aliasing={{0}: (9, {})} | custom-call | flops 1150000000 | tf_op jit(solution)/shard_map/final1/pallas_call | solution.py:142
  34.7 0.6 %collective-permute-done.12.base_ref = bf16[4,192,128]{2,1,0:T(8,128)(2,1)S(1)} collective-permute-done((bf16[4,192,128]{2,1,0:T(8,128)(2,1)S(1)}, bf16[4,192,128]{2,1,0:T(8,128)(2,1)S(1)}, u32[]{:S(2)}, u32[]{:S(2)}) %collective-permute-start.12) | collective-permute-done | bytes 196640 | tf_op jit(solution)/shard_map/ppermute | solution.py:503
  35.3 1.0 %final2.1 = (f32[16,256,128]{2,1,0:T(8,128)S(1)}, f32[8,256]{1,0:T(8,128)S(1)}) custom-call(bf16[4,192,128]{2,1,0:T(8,128)(2,1)S(1)} %collective-permute-done.12.base_ref, f32[2,4,160,128]{3,2,1,0:T(8,128)S(1)} %get-tuple-element.51.extra_ref, bf16[16,256,160]{2,1,0:T(8,128)(2,1)S(1)} %get-tuple-element.52.rest_0_, ...), custom_call_target="tpu_custom_call", output_to_operand_aliasing={{0}: (9, {})} | custom-call | flops 1150000000 | tf_op jit(solution)/shard_map/final2/pallas_call | solution.py:142
  36.3 1.5 %collective-permute-start.13 = (f32[8,256]{1,0:T(8,128)S(1)}, f32[8,256]{1,0:T(8,128)S(1)}, u32[]{:S(2)}, u32[]{:S(2)}) collective-permute-start(f32[8,256]{1,0:T(8,128)S(1)} %get-tuple-element.68.sq_ref), channel_id=1, source_target_pairs={{0,1},{1,0},{2,3},{3,2},{4,5},{5,4},{6,7},{7,6},{8,9},{9,8},{10,11... | collective-permute-start | bytes 24584 | tf_op jit(solution)/shard_map/ppermute | solution.py:617
  37.8 2.2 %collective-permute-done.13.rest_0_ = f32[8,256]{1,0:T(8,128)S(1)} collective-permute-done((f32[8,256]{1,0:T(8,128)S(1)}, f32[8,256]{1,0:T(8,128)S(1)}, u32[]{:S(2)}, u32[]{:S(2)}) %collective-permute-start.13) | collective-permute-done | bytes 8224 | tf_op jit(solution)/shard_map/ppermute | solution.py:617
  40.0 1.4 %norm.1 = bf16[256,16,128]{2,1,0:T(8,128)(2,1)} custom-call(f32[16,256,128]{2,1,0:T(8,128)S(1)} %get-tuple-element.67.mixed_ref, f32[8,256]{1,0:T(8,128)S(1)} %get-tuple-element.68.sq_ref, f32[8,256]{1,0:T(8,128)S(1)} %collective-permute-done.13.rest_0_), custom_call_target="tpu_custom_call" | custom-call | flops 1150000000 | tf_op jit(solution)/shard_map/norm/pallas_call | solution.py:142
  (6 shorter events, 0.1 us)
Async XLA Ops:
  2.0 1.8 %collective-permute-start = (f32[4,160,128]{2,1,0:T(8,128)S(1)}, f32[4,160,128]{2,1,0:T(8,128)S(1)}, u32[]{:S(2)}, u32[]{:S(2)}) collective-permute-start(f32[4,160,128]{2,1,0:T(8,128)S(1)} %get-tuple-element.39.after_ref), channel_id=1, source_target_pairs={{0,2},{2,0},{4,6},{6,4},{8,10},{10,8},{12,14},{14,12},{16,18},{18,... | collective-permute-start | bytes 983048 | tf_op jit(solution)/shard_map/ppermute | solution.py:503
  2.9 24.8 %collective-permute-start.11 = (f32[4,160,128]{2,1,0:T(8,128)S(1)}, f32[4,160,128]{2,1,0:T(8,128)S(1)}, u32[]{:S(2)}, u32[]{:S(2)}) collective-permute-start(f32[4,160,128]{2,1,0:T(8,128)S(1)} %near1.1.own_ref), channel_id=1, source_target_pairs={{0,2},{2,0},{4,6},{6,4},{8,10},{10,8},{12,14},{14,12},{16,18},{18,... | collective-permute-start | bytes 983048 | tf_op jit(solution)/shard_map/ppermute | solution.py:503
  3.0 11.4 %collective-permute-start.4 = (bf16[2,64,16,128]{3,2,1,0:T(8,128)(2,1)S(1)}, bf16[2,64,16,128]{3,2,1,0:T(8,128)(2,1)S(1)}, u32[]{:S(2)}, u32[]{:S(2)}) collective-permute-start(bf16[2,64,16,128]{3,2,1,0:T(8,128)(2,1)S(1)} %get-tuple-element.44.rim_ref), channel_id=1, source_target_pairs={{6,14},{14,22},{22,30},{0,0},{2,2},{4,4},{8,8},{10,10},{12,12},{16... | collective-permute-start | bytes 1572872 | tf_op jit(solution)/shard_map/ppermute | solution.py:503
  3.8 8.9 %collective-permute-start.2 = (bf16[4,192,128]{2,1,0:T(8,128)(2,1)S(1)}, bf16[4,192,128]{2,1,0:T(8,128)(2,1)S(1)}, u32[]{:S(2)}, u32[]{:S(2)}) collective-permute-start(bf16[4,192,128]{2,1,0:T(8,128)(2,1)S(1)} %chip.1.after_ref), channel_id=1, source_target_pairs={{0,4},{2,6},{4,0},{6,2},{8,12},{10,14},{12,8},{14,10},{16,20},{18,... | collective-permute-start | bytes 589832 | tf_op jit(solution)/shard_map/ppermute | solution.py:503
  7.3 3.0 %copy-start.5 = (bf16[256,256]{1,0:T(8,128)(2,1)S(1)}, bf16[256,256]{1,0:T(8,128)(2,1)}, u32[]{:S(2)}) copy-start(bf16[256,256]{1,0:T(8,128)(2,1)} %q_ref.3) | copy-start | bytes 393220
  7.3 2.9 %copy-start.6 = (bf16[16,128]{1,0:T(8,128)(2,1)S(1)}, bf16[16,128]{1,0:T(8,128)(2,1)}, u32[]{:S(2)}) copy-start(bf16[16,128]{1,0:T(8,128)(2,1)} %gain_ref.1) | copy-start | bytes 12292
  7.3 2.9 %copy-start.7 = (bf16[4,64,160]{2,1,0:T(8,128)(2,1)S(1)}, bf16[4,64,160]{2,1,0:T(8,128)(2,1)}, u32[]{:S(2)}) copy-start(bf16[4,64,160]{2,1,0:T(8,128)(2,1)} %constant.7.clone.e2_ref) | copy-start | bytes 245764
  7.3 2.9 %copy-start.8 = (bf16[4,64,160]{2,1,0:T(8,128)(2,1)S(1)}, bf16[4,64,160]{2,1,0:T(8,128)(2,1)}, u32[]{:S(2)}) copy-start(bf16[4,64,160]{2,1,0:T(8,128)(2,1)} %constant.6.clone.e1_ref) | copy-start | bytes 245764
  7.3 2.9 %copy-start.9 = (f32[8,160]{1,0:T(8,128)S(1)}, f32[8,160]{1,0:T(8,128)}, u32[]{:S(2)}) copy-start(f32[8,160]{1,0:T(8,128)} %constant.8.clone.add_ref) | copy-start | bytes 15364
  7.8 4.3 %copy-start.2 = (bf16[256,16,128]{2,1,0:T(8,128)(2,1)S(1)}, bf16[256,16,128]{2,1,0:T(8,128)(2,1)}, u32[]{:S(2)}) copy-start(bf16[256,16,128]{2,1,0:T(8,128)(2,1)} %wk_ref.1) | copy-start | bytes 3145732
  7.8 4.3 %copy-start.3 = (bf16[256,16,128]{2,1,0:T(8,128)(2,1)S(1)}, bf16[256,16,128]{2,1,0:T(8,128)(2,1)}, u32[]{:S(2)}) copy-start(bf16[256,16,128]{2,1,0:T(8,128)(2,1)} %wq_ref.1) | copy-start | bytes 3145732
  7.8 4.9 %collective-permute-start.1 = (f32[4,160,128]{2,1,0:T(8,128)S(1)}, f32[4,160,128]{2,1,0:T(8,128)S(1)}, u32[]{:S(2)}, u32[]{:S(2)}) collective-permute-start(f32[4,160,128]{2,1,0:T(8,128)S(1)} %far0.1.after_ref), channel_id=1, source_target_pairs={{0,2},{2,0},{4,6},{6,4},{8,10},{10,8},{12,14},{14,12},{16,18},{18,... | collective-permute-start | bytes 983048 | tf_op jit(solution)/shard_map/ppermute | solution.py:503
  10.1 17.5 %collective-permute-start.10 = (f32[4,160,128]{2,1,0:T(8,128)S(1)}, f32[4,160,128]{2,1,0:T(8,128)S(1)}, u32[]{:S(2)}, u32[]{:S(2)}) collective-permute-start(f32[4,160,128]{2,1,0:T(8,128)S(1)} %near0.1.after_ref.own_ref), channel_id=1, source_target_pairs={{0,2},{2,0},{4,6},{6,4},{8,10},{10,8},{12,14},{14,12},{16,18},{18,... | collective-permute-start | bytes 983048 | tf_op jit(solution)/shard_map/ppermute | solution.py:503
  12.1 0.6 %copy-start = (f32[16,1,128]{2,1,0:T(1,128)}, f32[16,1,128]{2,1,0:T(1,128)S(1)}, u32[]{:S(2)}) copy-start(f32[16,1,128]{2,1,0:T(1,128)S(1)} %get-tuple-element.40.after_ref.rest_6_) | copy-start | bytes 24580
  12.8 9.4 %collective-permute-start.3 = (bf16[4,192,128]{2,1,0:T(8,128)(2,1)S(1)}, bf16[4,192,128]{2,1,0:T(8,128)(2,1)S(1)}, u32[]{:S(2)}, u32[]{:S(2)}) collective-permute-start(bf16[4,192,128]{2,1,0:T(8,128)(2,1)S(1)} %get-tuple-element.42.msg_ref.after_ref), channel_id=1, source_target_pairs={{0,8},{2,10},{4,12},{6,14},{8,16},{10,18},{12,20},{14,22},{16,24},... | collective-permute-start | bytes 589832 | tf_op jit(solution)/shard_map/ppermute | solution.py:503
  14.5 4.9 %copy-start.4 = (bf16[256,256]{1,0:T(8,128)(2,1)S(1)}, bf16[256,256]{1,0:T(8,128)(2,1)}, u32[]{:S(2)}) copy-start(bf16[256,256]{1,0:T(8,128)(2,1)} %k_ref.1) | copy-start | bytes 393220
  14.5 13.1 %collective-permute-start.9 = (bf16[2,64,16,128]{3,2,1,0:T(8,128)(2,1)S(1)}, bf16[2,64,16,128]{3,2,1,0:T(8,128)(2,1)S(1)}, u32[]{:S(2)}, u32[]{:S(2)}) collective-permute-start(bf16[2,64,16,128]{3,2,1,0:T(8,128)(2,1)S(1)} %pick.1.rim_ref.after_ref), channel_id=1, source_target_pairs={{0,2},{2,4},{4,6},{6,0},{8,10},{10,12},{12,14},{14,8},{16,18},{18,... | collective-permute-start | bytes 1572872 | tf_op jit(solution)/shard_map/ppermute | solution.py:503
  14.7 11.1 %collective-permute-start.6 = (bf16[4,192,128]{2,1,0:T(8,128)(2,1)S(1)}, bf16[4,192,128]{2,1,0:T(8,128)(2,1)S(1)}, u32[]{:S(2)}, u32[]{:S(2)}) collective-permute-start(bf16[4,192,128]{2,1,0:T(8,128)(2,1)S(1)} %again.1), channel_id=1, source_target_pairs={{0,16},{2,18},{4,20},{6,22},{1,17},{3,19},{5,21},{7,23}} | collective-permute-start | bytes 589832 | tf_op jit(solution)/shard_map/ppermute | solution.py:503
  22.3 3.5 %collective-permute-start.5 = (bf16[4,192,128]{2,1,0:T(8,128)(2,1)S(1)}, bf16[4,192,128]{2,1,0:T(8,128)(2,1)S(1)}, u32[]{:S(2)}, u32[]{:S(2)}) collective-permute-start(bf16[4,192,128]{2,1,0:T(8,128)(2,1)S(1)} %round.1.after_ref), channel_id=1, source_target_pairs={{8,24},{10,26},{12,28},{14,30},{9,25},{11,27},{13,29},{15,31}} | collective-permute-start | bytes 589832 | tf_op jit(solution)/shard_map/ppermute | solution.py:503
  26.0 7.7 %collective-permute-start.7 = (bf16[4,192,128]{2,1,0:T(8,128)(2,1)S(1)}, bf16[4,192,128]{2,1,0:T(8,128)(2,1)S(1)}, u32[]{:S(2)}, u32[]{:S(2)}) collective-permute-start(bf16[4,192,128]{2,1,0:T(8,128)(2,1)S(1)} %get-tuple-element.49.after_ref), channel_id=1, source_target_pairs={{0,4},{2,6},{4,0},{6,2},{8,12},{10,14},{12,8},{14,10},{16,20},{18,... | collective-permute-start | bytes 589832 | tf_op jit(solution)/shard_map/ppermute | solution.py:503
  27.4 1.6 %collective-permute-start.8 = (f32[4,160,128]{2,1,0:T(8,128)S(1)}, f32[4,160,128]{2,1,0:T(8,128)S(1)}, u32[]{:S(2)}, u32[]{:S(2)}) collective-permute-start(f32[4,160,128]{2,1,0:T(8,128)S(1)} %get-tuple-element.50.mine_ref), channel_id=1, source_target_pairs={{0,2},{2,0},{4,6},{6,4},{8,10},{10,8},{12,14},{14,12},{16,18},{18,... | collective-permute-start | bytes 983048 | tf_op jit(solution)/shard_map/ppermute | solution.py:503
  27.9 1.1 %copy-start.1 = (f32[16,1,128]{2,1,0:T(1,128)S(1)}, f32[16,1,128]{2,1,0:T(1,128)}, u32[]{:S(2)}) copy-start(f32[16,1,128]{2,1,0:T(1,128)} %copy-done) | copy-start | bytes 24580
  33.8 1.5 %collective-permute-start.12 = (bf16[4,192,128]{2,1,0:T(8,128)(2,1)S(1)}, bf16[4,192,128]{2,1,0:T(8,128)(2,1)S(1)}, u32[]{:S(2)}, u32[]{:S(2)}) collective-permute-start(bf16[4,192,128]{2,1,0:T(8,128)(2,1)S(1)} %collective-permute-done.7.got_ref), channel_id=1, source_target_pairs={{0,2},{2,0},{4,6},{6,4},{8,10},{10,8},{12,14},{14,12},{16,18},{18,... | collective-permute-start | bytes 589832 | tf_op jit(solution)/shard_map/ppermute | solution.py:503
  36.3 3.7 %collective-permute-start.13 = (f32[8,256]{1,0:T(8,128)S(1)}, f32[8,256]{1,0:T(8,128)S(1)}, u32[]{:S(2)}, u32[]{:S(2)}) collective-permute-start(f32[8,256]{1,0:T(8,128)S(1)} %get-tuple-element.68.sq_ref), channel_id=1, source_target_pairs={{0,1},{1,0},{2,3},{3,2},{4,5},{5,4},{6,7},{7,6},{8,9},{9,8},{10,11... | collective-permute-start | bytes 24584 | tf_op jit(solution)/shard_map/ppermute | solution.py:617
